TPU v7x, 32 devices: a whole 2x2x4 slice. The times are simulated.
32 devices in a mesh: grp: 2 (over y), seq: 4 (over z), sub: 4 (over x, core).
Axes of the slice: x: 2, y: 2, z: 4, core: 2. Of those that a mesh axis runs over, the one named last changes fastest.
Arguments:
- activations: bfloat16 [32768, 384], P(('grp', 'seq', 'sub')), parts along dimension 0, may hold values from -6 to 6
- cotangent: bfloat16 [32768, 384], P(('grp', 'seq', 'sub')), parts along dimension 0, may hold values from -6 to 6
- weights: bfloat16 [2304, 384], P('sub'), may hold values from -0.1875 to 0.1875
Outputs:
- input_grad: bfloat16 [32768, 384], P(('grp', 'seq', 'sub')), parts along dimension 0
- weight_grad: float32 [4608, 384], P(('grp', 'sub')), parts along dimension 0
There are 2 independent parts, one for each index of `grp`. A program takes and returns all parts, laid end to end along the dimension named above; an argument that names none is the same for every part. Nothing has to cross between parts.
All inputs are finite; a program needn't handle non-finite values.
Results may differ from a plain program's by a relative error of at most 0.0053.
Values may be sent and summed in bfloat16 or wider, within the bound.
No kernel may reach another device: no remote copies, remote signals or barrier semaphores. Data moves between devices by JAX's collectives and lax.ppermute only.
A program may use at most 64 MiB of HBM per device.

v0:
```python
import math

import jax
import jax.numpy as jnp
from jax import lax
from jax.sharding import PartitionSpec as P

DILATION_FIRST = 1024
DILATION_SECOND = 2048


def from_behind(block, axis, distance):
    devices = range(lax.axis_size(axis))
    route = [(i - distance, i) for i in devices if i - distance in devices]
    return lax.ppermute(block, axis, route)


def gelu_pair(pre_act):
    coeff = 0.7978845608
    tanh_value = jnp.tanh(coeff * (pre_act + 0.044715 * pre_act * pre_act * pre_act))
    gelu_value = 0.5 * pre_act * (1.0 + tanh_value)
    gelu_slope = 0.5 * (1.0 + tanh_value) + 0.5 * pre_act * (
        1.0 - tanh_value * tanh_value
    ) * coeff * (1.0 + 3.0 * 0.044715 * pre_act * pre_act)
    return (gelu_value, gelu_slope)


def back_product(spread, kernel, count_of_rows, channels):
    spread_three = spread.reshape(count_of_rows, 3, channels)
    kernel_three = kernel.reshape(3, channels, channels)
    return lax.dot_general(
        spread_three, kernel_three, (((1, 2), (0, 2)), ((), ())), preferred_element_type=jnp.float32
    )


def tap_grads(stacked, delta):
    return lax.dot_general(
        stacked, delta, (((0,), (0,)), ((), ())), preferred_element_type=jnp.float32
    )


def per_device(activations, cotangent, weights):
    count_of_rows, channels = activations.shape
    devices = lax.axis_size("seq") * lax.axis_size("sub")
    nearby_jumps = DILATION_FIRST // count_of_rows
    distant_jumps = DILATION_SECOND // count_of_rows
    grad_scale = 1.0 / math.sqrt(count_of_rows * devices)
    all_weights = lax.all_gather(weights, "sub", axis=0, tiled=True)
    first = all_weights[: 3 * channels]
    second = all_weights[3 * channels :]

    def near_rows(source, sign):
        return from_behind(source, ("seq", "sub"), sign * nearby_jumps)

    def far_rows(source, sign):
        return from_behind(source, ("seq", "sub"), sign * distant_jumps)

    first_layer_weights = jnp.concatenate(
        (near_rows(activations, 1), activations, near_rows(activations, -1)), 1
    )
    pre_one = jnp.dot(first_layer_weights, first, preferred_element_type=jnp.float32)
    gelu_one, slope_one = gelu_pair(pre_one)
    middle_state = (activations.astype(jnp.float32) + gelu_one).astype(jnp.bfloat16)
    second_layer_weights = jnp.concatenate(
        (far_rows(middle_state, 1), middle_state, far_rows(middle_state, -1)), 1
    )
    pre_two = jnp.dot(second_layer_weights, second, preferred_element_type=jnp.float32)
    gelu_two, slope_two = gelu_pair(pre_two)
    second_error = (cotangent.astype(jnp.float32) * slope_two).astype(jnp.bfloat16)
    grad_two = tap_grads(second_layer_weights, second_error) * grad_scale
    second_reach = jnp.concatenate(
        (far_rows(second_error, -1), second_error, far_rows(second_error, 1)), 1
    )
    back_one = cotangent.astype(jnp.float32) + back_product(
        second_reach, second, count_of_rows, channels
    )
    first_error = (back_one * slope_one).astype(jnp.bfloat16)
    grad_one = tap_grads(first_layer_weights, first_error) * grad_scale
    first_reach = jnp.concatenate(
        (near_rows(first_error, -1), first_error, near_rows(first_error, 1)), 1
    )
    input_grad = (back_one + back_product(first_reach, first, count_of_rows, channels)).astype(
        jnp.bfloat16
    )
    local_grads = jnp.concatenate((grad_one, grad_two), 0)
    summed = lax.psum(local_grads, "seq")
    weight_grad = lax.psum_scatter(summed, "sub", scatter_dimension=0, tiled=True)
    return (input_grad, weight_grad)


def solution(mesh):
    placed = (P(("grp", "seq", "sub"), None), P(("grp", "seq", "sub"), None), P("sub", None))
    return jax.shard_map(
        per_device,
        mesh=mesh,
        in_specs=placed,
        out_specs=(P(("grp", "seq", "sub"), None), P(("grp", "sub"), None)),
        check_vma=False,
    )
```

profile of v0, /device:TPU:0, one launch (start us, length us, event | category | flops | bytes accessed | tf_op | source)
XLA Modules:
  0.0 237.5 jit_solution(14820011768576403430)
XLA Ops:
  7.2 0.7 all-gather.2.cloned.1.call-update
  8.0 2.4 %collective-permute-start = (bf16[1024,384]{1,0:T(8,128)(2,1)}, bf16[1024,384]{1,0:T(8,128)(2,1)S(1)}, u32[]{:S(2)}, u32[]{:S(2)}) collective-permute-start(bf16[1024,384]{1,0:T(8,128)(2,1)} %param.3), channel_id=1, source_target_pairs={{0,1},{1,2},{2,3},{3,4},{4,5},{5,6},{6,7},{7,8},{8,9},{9,10},{10,1... | collective-permute-start | bytes 2359304 | tf_op jit(solution)/shard_map/ppermute | solution.py:15
  10.4 1.3 collective-permute-start.1
  11.7 1.4 copy.6
  13.1 1.0 constant_dynamic-update-slice_fusion.2
  14.1 1.0 constant_dynamic-update-slice_fusion.1
  15.1 1.7 collective-permute-done.1
  16.8 1.0 constant_dynamic-update-slice_fusion
  17.8 22.2 %all-gather.2.cloned.1.call-done = bf16[2304,384]{1,0:T(8,128)(2,1)} async-done(((bf16[576,384]{1,0:T(8,128)(2,1)}), bf16[2304,384]{1,0:T(8,128)(2,1)}) %all-gather.2.cloned.1.call-update) | async-done | bytes 1769488 | tf_op jit(solution)/shard_map/all_gather | solution.py:48
  40.0 4.9 %add_convert_fusion = (bf16[1024,384]{0,1:T(8,128)(2,1)}, f32[1024,384]{0,1:T(8,128)}) fusion(bf16[1024,384]{0,1:T(8,128)(2,1)S(1)} %copy.6, bf16[1024,1152]{1,0:T(8,128)(2,1)} %constant_dynamic-update-slice_fusion, bf16[2304,384]{1,0:T(8,128)(2,1)} %all-gather.2.cloned.1.call-done), kind=kOutput, calls=%fused_computation.27 | convolution fusion | flops 910295040 | bytes 6389760 | tf_op jit(solution)/shard_map/dot_general | solution.py:61
  44.9 1.3 collective-permute-start.3
  46.2 7.3 %collective-permute-start.2 = (bf16[1024,384]{0,1:T(8,128)(2,1)}, bf16[1024,384]{0,1:T(8,128)(2,1)}, u32[]{:S(2)}, u32[]{:S(2)}) collective-permute-start(bf16[1024,384]{0,1:T(8,128)(2,1)} %get-tuple-element.6), channel_id=1, source_target_pairs={{0,2},{1,3},{2,4},{3,5},{4,6},{5,7},{6,8},{7,9},{8,10},{9,11},{10,... | collective-permute-start | bytes 2359304 | tf_op jit(solution)/shard_map/ppermute | solution.py:15
  53.5 0.3 copy.5
  53.8 15.1 %collective-permute-done.3 = bf16[1024,384]{0,1:T(8,128)(2,1)} collective-permute-done((bf16[1024,384]{0,1:T(8,128)(2,1)}, bf16[1024,384]{0,1:T(8,128)(2,1)}, u32[]{:S(2)}, u32[]{:S(2)}) %collective-permute-start.3) | collective-permute-done | bytes 786464 | tf_op jit(solution)/shard_map/ppermute | solution.py:15
  68.9 17.0 %collective-permute-done.2 = bf16[1024,384]{0,1:T(8,128)(2,1)} collective-permute-done((bf16[1024,384]{0,1:T(8,128)(2,1)}, bf16[1024,384]{0,1:T(8,128)(2,1)}, u32[]{:S(2)}, u32[]{:S(2)}) %collective-permute-start.2) | collective-permute-done | bytes 786464 | tf_op jit(solution)/shard_map/ppermute | solution.py:15
  85.9 3.7 %fusion = bf16[1024,384]{0,1:T(8,128)(2,1)S(1)} fusion(bf16[1024,384]{0,1:T(8,128)(2,1)S(1)} %copy.5, bf16[1024,384]{0,1:T(8,128)(2,1)} %collective-permute-done.3, bf16[1024,384]{0,1:T(8,128)(2,1)} %get-tuple-element.6, bf16[1024,384]{0,1:T(8,128)(2,1)} %collective-permute-done.2, bf16[2304,384]{1,0:T(8,128)(2,1)S(1)} %copy-done.1), kind=kOutput, calls=%fused_computation.12 | convolution fusion | flops 920911872 | bytes 4816896 | tf_op jit(solution)/shard_map/dot_general | solution.py:67
  89.6 4.4 %collective-permute-start.5 = (bf16[1024,384]{0,1:T(8,128)(2,1)S(1)}, bf16[1024,384]{0,1:T(8,128)(2,1)S(1)}, u32[]{:S(2)}, u32[]{:S(2)}) collective-permute-start(bf16[1024,384]{0,1:T(8,128)(2,1)S(1)} %fusion), channel_id=1, source_target_pairs={{0,2},{1,3},{2,4},{3,5},{4,6},{5,7},{6,8},{7,9},{8,10},{9,11},{10,... | collective-permute-start | bytes 2359304 | tf_op jit(solution)/shard_map/ppermute | solution.py:15
  94.0 1.3 collective-permute-start.4
  95.5 3.0 %convolution_multiply_fusion = f32[1152,384]{1,0:T(8,128)S(1)} fusion(bf16[1024,384]{0,1:T(8,128)(2,1)S(1)} %fusion, bf16[1024,384]{0,1:T(8,128)(2,1)} %collective-permute-done.3, bf16[1024,384]{0,1:T(8,128)(2,1)} %get-tuple-element.6, bf16[1024,384]{0,1:T(8,128)(2,1)} %collective-permute-done.2), kind=kOutput, calls=%fused_computation.1 | convolution fusion | flops 913489920 | bytes 4915200 | tf_op jit(solution)/shard_map/dot_general | solution.py:37
  98.6 29.3 %collective-permute-done.5 = bf16[1024,384]{0,1:T(8,128)(2,1)S(1)} collective-permute-done((bf16[1024,384]{0,1:T(8,128)(2,1)S(1)}, bf16[1024,384]{0,1:T(8,128)(2,1)S(1)}, u32[]{:S(2)}, u32[]{:S(2)}) %collective-permute-start.5) | collective-permute-done | bytes 786464 | tf_op jit(solution)/shard_map/ppermute | solution.py:15
  128.1 3.0 %fusion.12 = (bf16[1024,384]{0,1:T(8,128)(2,1)S(1)}, f32[1024,384]{0,1:T(8,128)}) fusion(f32[1024,384]{0,1:T(8,128)S(1)} %copy-done.4, bf16[3,384,384]{2,1,0:T(8,128)(2,1)S(1)} %bitcast.21, bf16[1024,3,384]{0,2,1:T(8,128)(2,1)S(1)} %bitcast.18, bf16[1024,384]{0,1:T(8,128)(2,1)S(1)} %copy.5), kind=kOutput, calls=%fused_computation.24 | convolution fusion | flops 914227200 | bytes 7962624 | tf_op jit(solution)/shard_map/dot_general | solution.py:31
  131.1 3.1 %convolution_multiply_fusion.1 = f32[1152,384]{1,0:T(8,128)S(1)} fusion(bf16[1024,1152]{1,0:T(8,128)(2,1)} %constant_dynamic-update-slice_fusion, bf16[1024,384]{0,1:T(8,128)(2,1)S(1)} %get-tuple-element.8), kind=kOutput, calls=%fused_computation.2 | convolution fusion | flops 906412032 | bytes 4915200 | tf_op jit(solution)/shard_map/dot_general | solution.py:37
  134.2 2.0 pad_maximum_fusion
  136.3 1.3 collective-permute-start.7
  137.6 1.3 collective-permute-start.6
  138.9 39.1 %reduce-scatter.2.cloned.1.call-done = f32[576,384]{1,0:T(8,128)} async-done(((f32[2304,384]{1,0:T(8,128)}), f32[576,384]{1,0:T(8,128)}) %reduce-scatter.2.cloned.1.call-update) | async-done | bytes 884752 | tf_op jit(solution)/shard_map/reduce_scatter | solution.py:87
  178.1 0.2 pad_maximum_fusion.3
  178.3 1.2 copy-done.3
  179.5 1.2 fusion.13
  180.7 1.2 copy.10
  181.8 47.0 %all-reduce.2.cloned.1.call-done = f32[576,384]{1,0:T(8,128)} async-done(((f32[576,384]{1,0:T(8,128)}), f32[576,384]{1,0:T(8,128)}) %all-reduce.2.cloned.1.call-update) | async-done | bytes 884752 | tf_op jit(solution)/shard_map/psum | solution.py:86
  228.8 2.1 copy.18
  (20 shorter events, 0.6 us)
Async XLA Ops:
  7.2 6.9 %copy-start = (bf16[1024,384]{1,0:T(8,128)(2,1)S(1)}, bf16[1024,384]{1,0:T(8,128)(2,1)}, u32[]{:S(2)}) copy-start(bf16[1024,384]{1,0:T(8,128)(2,1)} %param.3) | copy-start | bytes 2359300
  7.2 32.8 %all-gather.2.cloned.1.call-start = ((), (), s32[]{:S(2)}) async-start(), calls=%async_computation.1 | async-start | bytes 2211840 | tf_op jit(solution)/shard_map/all_gather | solution.py:48
  7.9 170.1 %reduce-scatter.2.cloned.1.call-start = ((), (), s32[]{:S(2)}) async-start(), calls=%async_computation.2 | async-start | bytes 4423680 | tf_op jit(solution)/shard_map/reduce_scatter | solution.py:87
  8.0 5.1 %collective-permute-start = (bf16[1024,384]{1,0:T(8,128)(2,1)}, bf16[1024,384]{1,0:T(8,128)(2,1)S(1)}, u32[]{:S(2)}, u32[]{:S(2)}) collective-permute-start(bf16[1024,384]{1,0:T(8,128)(2,1)} %param.3), channel_id=1, source_target_pairs={{0,1},{1,2},{2,3},{3,4},{4,5},{5,6},{6,7},{7,8},{8,9},{9,10},{10,1... | collective-permute-start | bytes 2359304 | tf_op jit(solution)/shard_map/ppermute | solution.py:15
  10.4 6.4 %collective-permute-start.1 = (bf16[1024,384]{1,0:T(8,128)(2,1)}, bf16[1024,384]{1,0:T(8,128)(2,1)S(1)}, u32[]{:S(2)}, u32[]{:S(2)}) collective-permute-start(bf16[1024,384]{1,0:T(8,128)(2,1)} %param.3), channel_id=1, source_target_pairs={{1,0},{2,1},{3,2},{4,3},{5,4},{6,5},{7,6},{8,7},{9,8},{10,9},{11,1... | collective-permute-start | bytes 2359304 | tf_op jit(solution)/shard_map/ppermute | solution.py:15
  17.8 35.7 %copy-start.2 = (bf16[1024,384]{1,0:T(8,128)(2,1)S(1)}, bf16[1024,384]{1,0:T(8,128)(2,1)}, u32[]{:S(2)}) copy-start(bf16[1024,384]{1,0:T(8,128)(2,1)} %param.4) | copy-start | bytes 2359300
  40.0 46.0 %copy-start.1 = (bf16[2304,384]{1,0:T(8,128)(2,1)S(1)}, bf16[2304,384]{1,0:T(8,128)(2,1)}, u32[]{:S(2)}) copy-start(bf16[2304,384]{1,0:T(8,128)(2,1)} %all-gather.2.cloned.1.call-done) | copy-start | bytes 5308420
  44.9 24.0 %collective-permute-start.3 = (bf16[1024,384]{0,1:T(8,128)(2,1)}, bf16[1024,384]{0,1:T(8,128)(2,1)}, u32[]{:S(2)}, u32[]{:S(2)}) collective-permute-start(bf16[1024,384]{0,1:T(8,128)(2,1)} %get-tuple-element.6), channel_id=1, source_target_pairs={{2,0},{3,1},{4,2},{5,3},{6,4},{7,5},{8,6},{9,7},{10,8},{11,9},{12,... | collective-permute-start | bytes 2359304 | tf_op jit(solution)/shard_map/ppermute | solution.py:15
  46.2 39.7 %collective-permute-start.2 = (bf16[1024,384]{0,1:T(8,128)(2,1)}, bf16[1024,384]{0,1:T(8,128)(2,1)}, u32[]{:S(2)}, u32[]{:S(2)}) collective-permute-start(bf16[1024,384]{0,1:T(8,128)(2,1)} %get-tuple-element.6), channel_id=1, source_target_pairs={{0,2},{1,3},{2,4},{3,5},{4,6},{5,7},{6,8},{7,9},{8,10},{9,11},{10,... | collective-permute-start | bytes 2359304 | tf_op jit(solution)/shard_map/ppermute | solution.py:15
  89.6 38.2 %collective-permute-start.5 = (bf16[1024,384]{0,1:T(8,128)(2,1)S(1)}, bf16[1024,384]{0,1:T(8,128)(2,1)S(1)}, u32[]{:S(2)}, u32[]{:S(2)}) collective-permute-start(bf16[1024,384]{0,1:T(8,128)(2,1)S(1)} %fusion), channel_id=1, source_target_pairs={{0,2},{1,3},{2,4},{3,5},{4,6},{5,7},{6,8},{7,9},{8,10},{9,11},{10,... | collective-permute-start | bytes 2359304 | tf_op jit(solution)/shard_map/ppermute | solution.py:15
  94.0 33.8 %collective-permute-start.4 = (bf16[1024,384]{0,1:T(8,128)(2,1)S(1)}, bf16[1024,384]{0,1:T(8,128)(2,1)S(1)}, u32[]{:S(2)}, u32[]{:S(2)}) collective-permute-start(bf16[1024,384]{0,1:T(8,128)(2,1)S(1)} %fusion), channel_id=1, source_target_pairs={{2,0},{3,1},{4,2},{5,3},{6,4},{7,5},{8,6},{9,7},{10,8},{11,9},{12,... | collective-permute-start | bytes 2359304 | tf_op jit(solution)/shard_map/ppermute | solution.py:15
  98.6 29.5 %copy-start.4 = (f32[1024,384]{0,1:T(8,128)S(1)}, f32[1024,384]{0,1:T(8,128)}, u32[]{:S(2)}) copy-start(f32[1024,384]{0,1:T(8,128)} %get-tuple-element.7) | copy-start | bytes 4718596
  136.2 92.6 %all-reduce.2.cloned.1.call-start = ((), (), s32[]{:S(2)}) async-start(), calls=%async_computation.3 | async-start | bytes 1769472 | tf_op jit(solution)/shard_map/psum | solution.py:86
  136.3 41.8 %collective-permute-start.7 = (bf16[1024,384]{0,1:T(8,128)(2,1)S(1)}, bf16[1024,384]{0,1:T(8,128)(2,1)S(1)}, u32[]{:S(2)}, u32[]{:S(2)}) collective-permute-start(bf16[1024,384]{0,1:T(8,128)(2,1)S(1)} %get-tuple-element.8), channel_id=1, source_target_pairs={{0,1},{1,2},{2,3},{3,4},{4,5},{5,6},{6,7},{7,8},{8,9},{9,10},{10,1... | collective-permute-start | bytes 2359304 | tf_op jit(solution)/shard_map/ppermute | solution.py:15
  137.6 40.5 %collective-permute-start.6 = (bf16[1024,384]{0,1:T(8,128)(2,1)S(1)}, bf16[1024,384]{0,1:T(8,128)(2,1)S(1)}, u32[]{:S(2)}, u32[]{:S(2)}) collective-permute-start(bf16[1024,384]{0,1:T(8,128)(2,1)S(1)} %get-tuple-element.8), channel_id=1, source_target_pairs={{1,0},{2,1},{3,2},{4,3},{5,4},{6,5},{7,6},{8,7},{9,8},{10,9},{11,1... | collective-permute-start | bytes 2359304 | tf_op jit(solution)/shard_map/ppermute | solution.py:15
  178.1 1.4 copy-start.3
Sparse Core Ops, SparseCore 0:
  9.6 30.3 all-gather.1
  136.3 41.6 reduce-scatter.1
  180.5 48.2 all-reduce.1
where the time goes:
time: 238 us; the launch traced here: 237 us
  waiting for transfers between devices  172 us (72%)
  starting transfers between devices  20.8 us (9%)
  matrix products  18.9 us (8%)
  between operations  13.9 us (6%)
  local copies, waits for them, and re-layouts  9.33 us (4%)
  other arithmetic  2.4 us (1%)
    ppermute x8, waiting for transfers between devices, from_behind(): return lax.ppermute(block, axis, route)  63.1 us
    psum x1, waiting for transfers between devices, per_device(): summed = lax.psum(local_grads, 'seq')  47 us
    reduce_scatter x1, waiting for transfers between devices, per_device(): lax.psum_scatter(summed, 'sub', scatter_dimension=0, tiled=True)  39.1 us
    all_gather x1, waiting for transfers between devices, per_device(): all_weights = lax.all_gather(weights, 'sub', axis=0, tiled=True)  22.2 us
    ppermute x8, starting transfers between devices, from_behind(): return lax.ppermute(block, axis, route)  20.7 us
    unnamed x16, local copies, waits for them, and re-layouts  8.17 us
    dot_general x2, matrix products, tap_grads(): lax.dot_general(stacked, delta, (((0,), (0,)), ((), ())), preferred_eleme...  6.12 us
    dot_general x1, matrix products, per_device(): jnp.dot(first_layer_weights, first, preferred_element_type=jnp.float32)  4.94 us
  transfers between devices with their start and end apart: 11, of which 7 were waited for; matrix products, arithmetic and copies ran while one was open for 4% of the time, Pallas kernels for 0%

commit v1 on v0

v1 whole, which is shorter than its diff:
```python
import math

import jax
import jax.numpy as jnp
from jax import lax
from jax.sharding import PartitionSpec as P

DILATION_FIRST = 1024
DILATION_SECOND = 2048
F32 = jnp.float32
BF16 = jnp.bfloat16


def shift_route(axis, distance):
    n = lax.axis_size(axis)
    return [(i, i + distance) for i in range(n) if 0 <= i + distance < n]


def xor_swap(block, axis, bits):
    n = lax.axis_size(axis)
    return lax.ppermute(block, axis, [(i, i ^ bits) for i in range(n)])


def by_xor(pieces, j):
    bit = 1
    while bit < len(pieces):
        flip = (j & bit) != 0
        pieces = [jnp.where(flip, pieces[r ^ bit], pieces[r]) for r in range(len(pieces))]
        bit *= 2
    return pieces


def exchange(block, axis):
    n = lax.axis_size(axis)
    j = lax.axis_index(axis)
    rows = block.shape[0] // n
    pieces = [lax.dynamic_slice_in_dim(block, (j ^ r) * rows, rows, 0) for r in range(n)]
    got = [pieces[0]] + [xor_swap(pieces[r], axis, r) for r in range(1, n)]
    return jnp.concatenate(by_xor(got, j), 0)


def gather_rows(block, axis):
    n = lax.axis_size(axis)
    j = lax.axis_index(axis)
    held = [block]
    bit = n // 2
    order = [0]
    while bit:
        held = held + [xor_swap(b, axis, bit) for b in held]
        order = order + [o ^ bit for o in order]
        bit //= 2
    pieces = [held[order.index(r)] for r in range(n)]
    return jnp.concatenate(by_xor(pieces, j), 0)


def gelu_pair(pre_act):
    coeff = 0.7978845608
    tanh_value = jnp.tanh(coeff * (pre_act + 0.044715 * pre_act * pre_act * pre_act))
    gelu_value = 0.5 * pre_act * (1.0 + tanh_value)
    gelu_slope = 0.5 * (1.0 + tanh_value) + 0.5 * pre_act * (
        1.0 - tanh_value * tanh_value
    ) * coeff * (1.0 + 3.0 * 0.044715 * pre_act * pre_act)
    return (gelu_value, gelu_slope)


def tap_stack(ext, step, rows):
    return jnp.concatenate([ext[k * step : k * step + rows] for k in range(3)], 1)


def back_product(spread, kernel):
    channels = kernel.shape[1]
    spread_three = spread.reshape(spread.shape[0], 3, channels)
    kernel_three = kernel.reshape(3, channels, channels)
    return lax.dot_general(
        spread_three, kernel_three, (((1, 2), (0, 2)), ((), ())), preferred_element_type=F32
    )


def tap_grads(stacked, delta):
    return lax.dot_general(stacked, delta, (((0,), (0,)), ((), ())), preferred_element_type=F32)


def halo(block, rows):
    low = lax.ppermute(block[block.shape[0] - rows :], "seq", shift_route("seq", 1))
    high = lax.ppermute(block[:rows], "seq", shift_route("seq", -1))
    return low, high


def sum_over_sub(grad, low_owner):
    n = lax.axis_size("sub")
    j = lax.axis_index("sub")
    owners = n // 2
    parts = grad.reshape(owners, -1, grad.shape[1])
    bit = 1
    kept = parts
    while bit < n:
        mine = (j & bit) != 0
        if kept.shape[0] > 1:
            even, odd = kept[0::2], kept[1::2]
            keep = jnp.where(mine, odd, even)
            send = jnp.where(mine, even, odd)
            wire = F32 if bit == 1 else BF16
            kept = keep + xor_swap(send.astype(wire), "sub", bit).astype(F32)
        else:
            to_high = low_owner > 0
            route = [(i, i ^ bit) for i in range(n) if ((i & bit) == 0) == to_high]
            kept = kept + lax.ppermute(kept.astype(BF16), "sub", route).astype(F32)
        bit *= 2
    return kept[0]


def sum_over_seq(part):
    n = lax.axis_size("seq")
    if n > 4:
        return lax.psum(part, "seq")
    sent = part.astype(BF16)
    total = part
    for turn in range(1, n):
        route = [(i, (i + turn) % n) for i in range(n)]
        total = total + lax.ppermute(sent, "seq", route).astype(F32)
    return total


def per_device(activations, cotangent, weights):
    count_of_rows, channels = activations.shape
    groups, members = lax.axis_size("seq"), lax.axis_size("sub")
    s = lax.axis_index("seq")
    j = lax.axis_index("sub")
    near = DILATION_FIRST // count_of_rows
    far = DILATION_SECOND // count_of_rows
    q = count_of_rows // members
    grad_scale = 1.0 / math.sqrt(count_of_rows * groups * members)

    act = exchange(activations, "sub")
    act_low, act_high = halo(act, (near + far) * q)
    all_weights = gather_rows(weights, "sub")
    first = all_weights[: 3 * channels]
    second = all_weights[3 * channels :]
    cot = exchange(cotangent, "sub")
    cot_low, cot_high = halo(cot, near * q)
    cot_ext = jnp.concatenate((cot_low, cot, cot_high), 0)

    def inside(margin):
        place = lax.broadcasted_iota(jnp.int32, (count_of_rows + 2 * margin * q, 1), 0)
        low_ok = (s > 0) | (place >= margin * q)
        high_ok = (s < groups - 1) | (place < count_of_rows + margin * q)
        return low_ok & high_ok

    act_ext = jnp.concatenate((act_low, act, act_high), 0)
    wide = count_of_rows + 2 * far * q
    act_stack = tap_stack(act_ext, near * q, wide)
    pre_one = jnp.dot(act_stack, first, preferred_element_type=F32)
    gelu_one, slope_one = gelu_pair(pre_one)
    hidden = (act_ext[near * q : near * q + wide].astype(F32) + gelu_one).astype(BF16)
    hidden = jnp.where(inside(far), hidden, jnp.zeros_like(hidden))
    hid_stack = tap_stack(hidden, far * q, count_of_rows)
    pre_two = jnp.dot(hid_stack, second, preferred_element_type=F32)
    _, slope_two = gelu_pair(pre_two)
    delta_two = (cot.astype(F32) * slope_two).astype(BF16)

    two_low, two_high = halo(delta_two, (near + far) * q)
    grad_two = tap_grads(hid_stack, delta_two) * grad_scale
    part_two = sum_over_sub(grad_two, members // 2)

    two_ext = jnp.concatenate((two_low, delta_two, two_high), 0)
    mid = count_of_rows + 2 * near * q
    two_spread = jnp.concatenate(
        [two_ext[k * far * q : k * far * q + mid] for k in (2, 1, 0)], 1
    )
    back_one = cot_ext.astype(F32) + back_product(two_spread, second)
    skip = (far - near) * q
    delta_one = (back_one * slope_one[skip : skip + mid]).astype(BF16)
    delta_one = jnp.where(inside(near), delta_one, jnp.zeros_like(delta_one))
    own_one = delta_one[near * q : near * q + count_of_rows]
    own_stack = act_stack[far * q : far * q + count_of_rows]
    grad_one = tap_grads(own_stack, own_one) * grad_scale
    part_one = sum_over_sub(grad_one, 0)
    one_spread = jnp.concatenate(
        [delta_one[k * near * q : k * near * q + count_of_rows] for k in (2, 1, 0)], 1
    )
    grad_in = back_one[near * q : near * q + count_of_rows] + back_product(one_spread, first)
    input_grad = exchange(grad_in.astype(BF16), "sub")

    part = jnp.where(j >= members // 2, part_two, part_one)
    weight_grad = sum_over_seq(part)
    return (input_grad, weight_grad)


def solution(mesh):
    placed = (P(("grp", "seq", "sub"), None), P(("grp", "seq", "sub"), None), P("sub", None))
    return jax.shard_map(
        per_device,
        mesh=mesh,
        in_specs=placed,
        out_specs=(P(("grp", "seq", "sub"), None), P(("grp", "sub"), None)),
        check_vma=False,
    )
```

time: 238 us -> 169 us (0.71)
  waiting for transfers between devices: 172 us -> 95 us
  other arithmetic: 2.4 us -> 19.6 us
  starting transfers between devices: 20.8 us -> 36.5 us
  between operations: 13.9 us -> 1.17 us
  matrix products: 18.9 us -> 11.3 us
  local copies, waits for them, and re-layouts: 9.33 us -> 5.45 us
    psum x1 -> x0, waiting for transfers between devices: 47 us -> none  [per_device(): summed = lax.psum(local_grads, 'seq')]
    reduce_scatter x1 -> x0, waiting for transfers between devices: 39.1 us -> none  [per_device(): lax.psum_scatter(summed, 'sub', scatter_dimension=0, tiled=True)]
    ppermute x8 -> x25, waiting for transfers between devices: 63.1 us -> 95 us  [the longest x3 33 us: sum_over_seq(): total = total + lax.ppermute(sent, 'seq', route).astype(F32)]
    all_gather x1 -> x0, waiting for transfers between devices: 22.2 us -> none  [per_device(): all_weights = lax.all_gather(weights, 'sub', axis=0, tiled=True)]
    ppermute x8 -> x25, starting transfers between devices: 20.7 us -> 36.5 us  [the longest x3 12 us: halo(): lax.ppermute(block[block.shape[0] - rows:], 'seq', shift_route('seq', 1))]
    concatenate x3 -> x7, other arithmetic: 2.4 us -> 15.6 us  [the longest x1 15 us: per_device(): jnp.concatenate([two_ext[k * far * q:k * far * q + mid] for k in (2, 1, 0...]
    unnamed x16 -> x17, local copies, waits for them, and re-layouts: 8.17 us -> 2.45 us
    dot_general x2, matrix products: 8.61 us -> 4.94 us  [the longest x1 2.86 us: per_device(): pre_one = jnp.dot(act_stack, first, preferred_element_type=F32)]
  transfers between devices with their start and end apart: 11 -> 25, of which waited for: 7 -> 13; matrix products, arithmetic and copies ran while one was open for 4% -> 17% of each run, Pallas kernels for 0% -> 0%
where the time goes in v1:
time: 169 us
  waiting for transfers between devices  95 us (56%)
  starting transfers between devices  36.5 us (22%)
  other arithmetic  19.6 us (12%)
  matrix products  11.3 us (7%)
  local copies, waits for them, and re-layouts  5.45 us (3%)
    ppermute x3, waiting for transfers between devices, sum_over_seq(): total = total + lax.ppermute(sent, 'seq', route).astype(F32)  33 us
    ppermute x3, waiting for transfers between devices, halo(): high = lax.ppermute(block[:rows], 'seq', shift_route('seq', -1))  29.7 us
    ppermute x14, waiting for transfers between devices, xor_swap(): return lax.ppermute(block, axis, [(i, i ^ bits) for i in range(n)])  17.6 us
    concatenate x1, other arithmetic, per_device(): jnp.concatenate([two_ext[k * far * q:k * far * q + mid] for k in (2, 1, 0...  15 us
    ppermute x3, starting transfers between devices, halo(): lax.ppermute(block[block.shape[0] - rows:], 'seq', shift_route('seq', 1))  12 us
    ppermute x14, starting transfers between devices, xor_swap(): return lax.ppermute(block, axis, [(i, i ^ bits) for i in range(n)])  10.5 us
    ppermute x2, waiting for transfers between devices, sum_over_sub(): kept = kept + lax.ppermute(kept.astype(BF16), 'sub', route).astype(F32)  9.39 us
    ppermute x3, starting transfers between devices, sum_over_seq(): total = total + lax.ppermute(sent, 'seq', route).astype(F32)  5.47 us
  transfers between devices with their start and end apart: 25, of which 13 were waited for; matrix products, arithmetic and copies ran while one was open for 17% of the time, Pallas kernels for 0%

profile of v1, /device:TPU:0, one launch (start us, length us, event | category | flops | bytes accessed | tf_op | source)
XLA Modules:
  0.0 169.0 jit_solution(4324829262222430416)
XLA Ops:
  0.6 3.0 %collective-permute-start.10 = (bf16[576,384]{1,0:T(8,128)(2,1)}, bf16[576,384]{1,0:T(8,128)(2,1)S(1)}, u32[]{:S(2)}, u32[]{:S(2)}) collective-permute-start(bf16[576,384]{1,0:T(8,128)(2,1)} %param.5), channel_id=1, source_target_pairs={{0,2},{1,3},{2,0},{3,1},{4,6},{5,7},{6,4},{7,5},{8,10},{9,11},{10,... | collective-permute-start | bytes 1327112 | tf_op jit(solution)/shard_map/ppermute | solution.py:21
  3.6 1.6 constant_dynamic-slice_fusion.3
  5.8 2.0 %collective-permute-start.1 = (bf16[256,384]{0,1:T(8,128)(2,1)S(1)}, bf16[256,384]{0,1:T(8,128)(2,1)S(1)}, u32[]{:S(2)}, u32[]{:S(2)}) collective-permute-start(bf16[256,384]{0,1:T(8,128)(2,1)S(1)} %copy.34), channel_id=1, source_target_pairs={{0,2},{1,3},{2,0},{3,1},{4,6},{5,7},{6,4},{7,5},{8,10},{9,11},{10,... | collective-permute-start | bytes 589832 | tf_op jit(solution)/shard_map/ppermute | solution.py:21
  8.9 9.7 %collective-permute-done.2 = bf16[256,384]{0,1:T(8,128)(2,1)S(1)} collective-permute-done((bf16[256,384]{0,1:T(8,128)(2,1)S(1)}, bf16[256,384]{0,1:T(8,128)(2,1)S(1)}, u32[]{:S(2)}, u32[]{:S(2)}) %collective-permute-start.2) | collective-permute-done | bytes 196640 | tf_op jit(solution)/shard_map/ppermute | solution.py:21
  18.8 4.2 %collective-permute-done.1 = bf16[256,384]{0,1:T(8,128)(2,1)S(1)} collective-permute-done((bf16[256,384]{0,1:T(8,128)(2,1)S(1)}, bf16[256,384]{0,1:T(8,128)(2,1)S(1)}, u32[]{:S(2)}, u32[]{:S(2)}) %collective-permute-start.1) | collective-permute-done | bytes 196640 | tf_op jit(solution)/shard_map/ppermute | solution.py:21
  23.0 1.8 %collective-permute-start.7 = (bf16[256,384]{0,1:T(8,128)(2,1)S(1)}, bf16[256,384]{0,1:T(8,128)(2,1)S(1)}, u32[]{:S(2)}, u32[]{:S(2)}) collective-permute-start(bf16[256,384]{0,1:T(8,128)(2,1)S(1)} %copy.39), channel_id=1, source_target_pairs={{0,1},{1,0},{2,3},{3,2},{4,5},{5,4},{6,7},{7,6},{8,9},{9,8},{10,11... | collective-permute-start | bytes 589832 | tf_op jit(solution)/shard_map/ppermute | solution.py:21
  24.9 2.3 %collective-permute-done.5 = bf16[256,384]{0,1:T(8,128)(2,1)S(1)} collective-permute-done((bf16[256,384]{0,1:T(8,128)(2,1)S(1)}, bf16[256,384]{0,1:T(8,128)(2,1)S(1)}, u32[]{:S(2)}, u32[]{:S(2)}) %collective-permute-start.5) | collective-permute-done | bytes 196640 | tf_op jit(solution)/shard_map/ppermute | solution.py:21
  27.2 3.7 %collective-permute-start.3 = (bf16[256,384]{0,1:T(8,128)(2,1)S(1)}, bf16[256,384]{0,1:T(8,128)(2,1)S(1)}, u32[]{:S(2)}, u32[]{:S(2)}) collective-permute-start(bf16[256,384]{0,1:T(8,128)(2,1)S(1)} %broadcast_select_fusion.32), channel_id=1, source_target_pairs={{0,4},{4,8},{8,12},{1,5},{5,9},{9,13},{2,6},{6,10},{10,14},{3,7},{... | collective-permute-start | bytes 589832 | tf_op jit(solution)/shard_map/ppermute | solution.py:84
  31.1 3.5 %collective-permute-start.8 = (bf16[768,384]{0,1:T(8,128)(2,1)S(1)}, bf16[768,384]{0,1:T(8,128)(2,1)S(1)}, u32[]{:S(2)}, u32[]{:S(2)}) collective-permute-start(bf16[768,384]{0,1:T(8,128)(2,1)S(1)} %pad_maximum_fusion.13), channel_id=1, source_target_pairs={{0,4},{4,8},{8,12},{1,5},{5,9},{9,13},{2,6},{6,10},{10,14},{3,7},{... | collective-permute-start | bytes 1769480 | tf_op jit(solution)/shard_map/ppermute | solution.py:84
  34.8 1.3 collective-permute-start.4
  36.4 6.7 %collective-permute-done.4 = bf16[256,384]{0,1:T(8,128)(2,1)S(1)} collective-permute-done((bf16[256,384]{0,1:T(8,128)(2,1)S(1)}, bf16[256,384]{0,1:T(8,128)(2,1)S(1)}, u32[]{:S(2)}, u32[]{:S(2)}) %collective-permute-start.4) | collective-permute-done | bytes 196640 | tf_op jit(solution)/shard_map/ppermute | solution.py:85
  43.2 4.1 %collective-permute-done.8 = bf16[768,384]{0,1:T(8,128)(2,1)S(1)} collective-permute-done((bf16[768,384]{0,1:T(8,128)(2,1)S(1)}, bf16[768,384]{0,1:T(8,128)(2,1)S(1)}, u32[]{:S(2)}, u32[]{:S(2)}) %collective-permute-start.8) | collective-permute-done | bytes 589856 | tf_op jit(solution)/shard_map/ppermute | solution.py:84
  47.5 1.3 collective-permute-start.9
  49.3 15.1 %collective-permute-done.9 = bf16[768,384]{0,1:T(8,128)(2,1)S(1)} collective-permute-done((bf16[768,384]{0,1:T(8,128)(2,1)S(1)}, bf16[768,384]{0,1:T(8,128)(2,1)S(1)}, u32[]{:S(2)}, u32[]{:S(2)}) %collective-permute-start.9) | collective-permute-done | bytes 589856 | tf_op jit(solution)/shard_map/ppermute | solution.py:85
  65.2 2.9 %broadcast_add_fusion = (f32[2048,384]{0,1:T(8,128)S(1)}, f32[2048,384]{0,1:T(8,128)S(1)}, f32[2048,384]{0,1:T(8,128)S(1)}, f32[2048,384]{0,1:T(8,128)S(1)}) fusion(bf16[576,384]{1,0:T(8,128)(2,1)S(1)} %get-tuple-element.27, bf16[576,384]{1,0:T(8,128)(2,1)S(1)} %get-tuple-element.29, bf16[2048,384]{0,1:T(8,128)(2,1)S(1)} %get-tuple-element.24, ...), kind=kOutput, calls=%fused_computation.50 | convolution fusion | flops 1833369600 | bytes 18186240 | tf_op jit(solution)/shard_map/dot_general | solution.py:152
  69.6 2.1 %fusion.28 = bf16[1024,384]{0,1:T(8,128)(2,1)S(1)} fusion(bf16[1024,384]{0,1:T(8,128)(2,1)S(1)} %get-tuple-element.31, bf16[1024,384]{0,1:T(8,128)(2,1)S(1)} %get-tuple-element.32, bf16[1024,384]{0,1:T(8,128)(2,1)S(1)} %get-tuple-element.30, bf16[256,384]{0,1:T(8,128)(2,1)S(1)} %broadcast_select_fusion.32, bf16[256,384]{0,1:T(8,128)(2,1)S(1)} %get-tuple-element.13, ...), kind=kOutput, calls=%fused_computation.46 | convolution fusion | flops 925433856 | bytes 4816896 | tf_op jit(solution)/shard_map/dot_general | solution.py:157
  71.8 1.3 collective-permute-start.13
  73.1 4.8 %collective-permute-start.14 = (bf16[768,384]{0,1:T(8,128)(2,1)S(1)}, bf16[768,384]{0,1:T(8,128)(2,1)S(1)}, u32[]{:S(2)}, u32[]{:S(2)}) collective-permute-start(bf16[768,384]{0,1:T(8,128)(2,1)S(1)} %get-tuple-element.44), channel_id=1, source_target_pairs={{0,4},{4,8},{8,12},{1,5},{5,9},{9,13},{2,6},{6,10},{10,14},{3,7},{... | collective-permute-start | bytes 1769480 | tf_op jit(solution)/shard_map/ppermute | solution.py:84
  77.8 1.4 convolution_multiply_fusion.1
  79.4 7.9 %collective-permute-done.13 = bf16[768,384]{0,1:T(8,128)(2,1)S(1)} collective-permute-done((bf16[768,384]{0,1:T(8,128)(2,1)S(1)}, bf16[768,384]{0,1:T(8,128)(2,1)S(1)}, u32[]{:S(2)}, u32[]{:S(2)}) %collective-permute-start.13) | collective-permute-done | bytes 589856 | tf_op jit(solution)/shard_map/ppermute | solution.py:85
  88.5 15.0 %fusion.6 = bf16[1536,1152]{0,1:T(8,128)(2,1)S(1)} fusion(bf16[1024,384]{0,1:T(8,128)(2,1)S(1)} %fusion.28, bf16[768,384]{0,1:T(8,128)(2,1)S(1)} %collective-permute-done.14, bf16[768,384]{0,1:T(8,128)(2,1)S(1)} %collective-permute-done.13), kind=kLoop, calls=%fused_computation.8 | loop fusion | flops 24772608 | bytes 5505024 | tf_op jit(solution)/shard_map/concatenate | solution.py:167
  103.5 2.3 %broadcast_select_fusion = (bf16[1536,384]{0,1:T(8,128)(2,1)S(1)}, f32[1536,384]{0,1:T(8,128)S(1)}) fusion(pred[1536]{0:T(1024)(128)(4,1)S(1)} %fusion.38, f32[2048,384]{0,1:T(8,128)S(1)} %get-tuple-element.56, f32[2048,384]{0,1:T(8,128)S(1)} %get-tuple-element.21, f32[2048,384]{0,1:T(8,128)S(1)} %get-tuple-element.22, ...), kind=kOutput, calls=%fused_computation.52 | convolution fusion | flops 1367801856 | bytes 18580992 | tf_op jit(solution)/shard_map/dot_general | solution.py:74
  105.8 1.4 convolution_multiply_fusion
  108.0 3.4 %collective-permute-start.19 = (bf16[1,576,384]{2,1,0:T(8,128)(2,1)S(1)}, bf16[1,576,384]{2,1,0:T(8,128)(2,1)S(1)}, u32[]{:S(2)}, u32[]{:S(2)}) collective-permute-start(bf16[1,576,384]{2,1,0:T(8,128)(2,1)S(1)} %get-tuple-element.6), channel_id=1, source_target_pairs={{0,2},{1,3},{4,6},{5,7},{8,10},{9,11},{12,14},{13,15},{16,18},{17,... | collective-permute-start | bytes 1327112 | tf_op jit(solution)/shard_map/ppermute | solution.py:107
  111.6 1.3 collective-permute-start.21
  114.6 2.5 %collective-permute-start.16 = (bf16[256,384]{0,1:T(8,128)(2,1)S(1)}, bf16[256,384]{0,1:T(8,128)(2,1)S(1)}, u32[]{:S(2)}, u32[]{:S(2)}) collective-permute-start(bf16[256,384]{0,1:T(8,128)(2,1)S(1)} %get-tuple-element.41), channel_id=1, source_target_pairs={{0,2},{1,3},{2,0},{3,1},{4,6},{5,7},{6,4},{7,5},{8,10},{9,11},{10,... | collective-permute-start | bytes 589832 | tf_op jit(solution)/shard_map/ppermute | solution.py:21
  117.2 4.8 %collective-permute-done.19 = bf16[1,576,384]{2,1,0:T(8,128)(2,1)S(1)} collective-permute-done((bf16[1,576,384]{2,1,0:T(8,128)(2,1)S(1)}, bf16[1,576,384]{2,1,0:T(8,128)(2,1)S(1)}, u32[]{:S(2)}, u32[]{:S(2)}) %collective-permute-start.19) | collective-permute-done | bytes 442400 | tf_op jit(solution)/shard_map/ppermute | solution.py:107
  121.9 4.6 %collective-permute-done.21 = bf16[1,576,384]{2,1,0:T(8,128)(2,1)S(1)} collective-permute-done((bf16[1,576,384]{2,1,0:T(8,128)(2,1)S(1)}, bf16[1,576,384]{2,1,0:T(8,128)(2,1)S(1)}, u32[]{:S(2)}, u32[]{:S(2)}) %collective-permute-start.21) | collective-permute-done | bytes 442400 | tf_op jit(solution)/shard_map/ppermute | solution.py:107
  126.8 4.5 %collective-permute-start.24 = (bf16[576,384]{1,0:T(8,128)(2,1)S(1)}, bf16[576,384]{1,0:T(8,128)(2,1)S(1)}, u32[]{:S(2)}, u32[]{:S(2)}) collective-permute-start(bf16[576,384]{1,0:T(8,128)(2,1)S(1)} %get-tuple-element.4), channel_id=1, source_target_pairs={{0,12},{4,0},{8,4},{12,8},{1,13},{5,1},{9,5},{13,9},{2,14},{6,2},{... | collective-permute-start | bytes 1327112 | tf_op jit(solution)/shard_map/ppermute | solution.py:120
  132.2 1.3 collective-permute-done.15
  135.0 6.9 %collective-permute-done.24 = bf16[576,384]{1,0:T(8,128)(2,1)S(1)} collective-permute-done((bf16[576,384]{1,0:T(8,128)(2,1)S(1)}, bf16[576,384]{1,0:T(8,128)(2,1)S(1)}, u32[]{:S(2)}, u32[]{:S(2)}) %collective-permute-start.24) | collective-permute-done | bytes 442400 | tf_op jit(solution)/shard_map/ppermute | solution.py:120
  141.9 26.0 %collective-permute-done.23 = bf16[576,384]{1,0:T(8,128)(2,1)S(1)} collective-permute-done((bf16[576,384]{1,0:T(8,128)(2,1)S(1)}, bf16[576,384]{1,0:T(8,128)(2,1)S(1)}, u32[]{:S(2)}, u32[]{:S(2)}) %collective-permute-start.23) | collective-permute-done | bytes 442400 | tf_op jit(solution)/shard_map/ppermute | solution.py:120
  (73 shorter events, 12.9 us)
Async XLA Ops:
  0.6 35.7 %collective-permute-start.10 = (bf16[576,384]{1,0:T(8,128)(2,1)}, bf16[576,384]{1,0:T(8,128)(2,1)S(1)}, u32[]{:S(2)}, u32[]{:S(2)}) collective-permute-start(bf16[576,384]{1,0:T(8,128)(2,1)} %param.5), channel_id=1, source_target_pairs={{0,2},{1,3},{2,0},{3,1},{4,6},{5,7},{6,4},{7,5},{8,10},{9,11},{10,... | collective-permute-start | bytes 1327112 | tf_op jit(solution)/shard_map/ppermute | solution.py:21
  3.6 45.2 %collective-permute-start.12 = (bf16[576,384]{1,0:T(8,128)(2,1)}, bf16[576,384]{1,0:T(8,128)(2,1)S(1)}, u32[]{:S(2)}, u32[]{:S(2)}) collective-permute-start(bf16[576,384]{1,0:T(8,128)(2,1)} %param.5), channel_id=1, source_target_pairs={{0,1},{1,0},{2,3},{3,2},{4,5},{5,4},{6,7},{7,6},{8,9},{9,8},{10,11... | collective-permute-start | bytes 1327112 | tf_op jit(solution)/shard_map/ppermute | solution.py:21
  5.4 13.2 %collective-permute-start.2 = (bf16[256,384]{0,1:T(8,128)(2,1)S(1)}, bf16[256,384]{0,1:T(8,128)(2,1)S(1)}, u32[]{:S(2)}, u32[]{:S(2)}) collective-permute-start(bf16[256,384]{0,1:T(8,128)(2,1)S(1)} %copy.35), channel_id=1, source_target_pairs={{0,3},{1,2},{2,1},{3,0},{4,7},{5,6},{6,5},{7,4},{8,11},{9,10},{10,... | collective-permute-start | bytes 589832 | tf_op jit(solution)/shard_map/ppermute | solution.py:21
  5.8 17.2 %collective-permute-start.1 = (bf16[256,384]{0,1:T(8,128)(2,1)S(1)}, bf16[256,384]{0,1:T(8,128)(2,1)S(1)}, u32[]{:S(2)}, u32[]{:S(2)}) collective-permute-start(bf16[256,384]{0,1:T(8,128)(2,1)S(1)} %copy.34), channel_id=1, source_target_pairs={{0,2},{1,3},{2,0},{3,1},{4,6},{5,7},{6,4},{7,5},{8,10},{9,11},{10,... | collective-permute-start | bytes 589832 | tf_op jit(solution)/shard_map/ppermute | solution.py:21
  8.0 15.0 %collective-permute-start = (bf16[256,384]{0,1:T(8,128)(2,1)S(1)}, bf16[256,384]{0,1:T(8,128)(2,1)S(1)}, u32[]{:S(2)}, u32[]{:S(2)}) collective-permute-start(bf16[256,384]{0,1:T(8,128)(2,1)S(1)} %copy.33), channel_id=1, source_target_pairs={{0,1},{1,0},{2,3},{3,2},{4,5},{5,4},{6,7},{7,6},{8,9},{9,8},{10,11... | collective-permute-start | bytes 589832 | tf_op jit(solution)/shard_map/ppermute | solution.py:21
  18.6 8.6 %collective-permute-start.5 = (bf16[256,384]{0,1:T(8,128)(2,1)S(1)}, bf16[256,384]{0,1:T(8,128)(2,1)S(1)}, u32[]{:S(2)}, u32[]{:S(2)}) collective-permute-start(bf16[256,384]{0,1:T(8,128)(2,1)S(1)} %copy.36), channel_id=1, source_target_pairs={{0,2},{1,3},{2,0},{3,1},{4,6},{5,7},{6,4},{7,5},{8,10},{9,11},{10,... | collective-permute-start | bytes 589832 | tf_op jit(solution)/shard_map/ppermute | solution.py:21
  23.0 7.9 %collective-permute-start.6 = (bf16[256,384]{0,1:T(8,128)(2,1)S(1)}, bf16[256,384]{0,1:T(8,128)(2,1)S(1)}, u32[]{:S(2)}, u32[]{:S(2)}) collective-permute-start(bf16[256,384]{0,1:T(8,128)(2,1)S(1)} %copy.37), channel_id=1, source_target_pairs={{0,3},{1,2},{2,1},{3,0},{4,7},{5,6},{6,5},{7,4},{8,11},{9,10},{10,... | collective-permute-start | bytes 589832 | tf_op jit(solution)/shard_map/ppermute | solution.py:21
  23.0 8.0 %collective-permute-start.7 = (bf16[256,384]{0,1:T(8,128)(2,1)S(1)}, bf16[256,384]{0,1:T(8,128)(2,1)S(1)}, u32[]{:S(2)}, u32[]{:S(2)}) collective-permute-start(bf16[256,384]{0,1:T(8,128)(2,1)S(1)} %copy.39), channel_id=1, source_target_pairs={{0,1},{1,0},{2,3},{3,2},{4,5},{5,4},{6,7},{7,6},{8,9},{9,8},{10,11... | collective-permute-start | bytes 589832 | tf_op jit(solution)/shard_map/ppermute | solution.py:21
  27.2 7.4 %collective-permute-start.3 = (bf16[256,384]{0,1:T(8,128)(2,1)S(1)}, bf16[256,384]{0,1:T(8,128)(2,1)S(1)}, u32[]{:S(2)}, u32[]{:S(2)}) collective-permute-start(bf16[256,384]{0,1:T(8,128)(2,1)S(1)} %broadcast_select_fusion.32), channel_id=1, source_target_pairs={{0,4},{4,8},{8,12},{1,5},{5,9},{9,13},{2,6},{6,10},{10,14},{3,7},{... | collective-permute-start | bytes 589832 | tf_op jit(solution)/shard_map/ppermute | solution.py:84
  31.1 16.2 %collective-permute-start.8 = (bf16[768,384]{0,1:T(8,128)(2,1)S(1)}, bf16[768,384]{0,1:T(8,128)(2,1)S(1)}, u32[]{:S(2)}, u32[]{:S(2)}) collective-permute-start(bf16[768,384]{0,1:T(8,128)(2,1)S(1)} %pad_maximum_fusion.13), channel_id=1, source_target_pairs={{0,4},{4,8},{8,12},{1,5},{5,9},{9,13},{2,6},{6,10},{10,14},{3,7},{... | collective-permute-start | bytes 1769480 | tf_op jit(solution)/shard_map/ppermute | solution.py:84
  34.8 8.4 %collective-permute-start.4 = (bf16[256,384]{0,1:T(8,128)(2,1)S(1)}, bf16[256,384]{0,1:T(8,128)(2,1)S(1)}, u32[]{:S(2)}, u32[]{:S(2)}) collective-permute-start(bf16[256,384]{0,1:T(8,128)(2,1)S(1)} %get-tuple-element.17), channel_id=1, source_target_pairs={{4,0},{8,4},{12,8},{5,1},{9,5},{13,9},{6,2},{10,6},{14,10},{7,3},{... | collective-permute-start | bytes 589832 | tf_op jit(solution)/shard_map/ppermute | solution.py:85
  36.3 12.5 %collective-permute-start.11 = (bf16[576,384]{1,0:T(8,128)(2,1)S(1)}, bf16[576,384]{1,0:T(8,128)(2,1)S(1)}, u32[]{:S(2)}, u32[]{:S(2)}) collective-permute-start(bf16[576,384]{1,0:T(8,128)(2,1)S(1)} %collective-permute-done.10), channel_id=1, source_target_pairs={{0,1},{1,0},{2,3},{3,2},{4,5},{5,4},{6,7},{7,6},{8,9},{9,8},{10,11... | collective-permute-start | bytes 1327112 | tf_op jit(solution)/shard_map/ppermute | solution.py:21
  47.3 1.6 copy-start
  47.5 17.0 %collective-permute-start.9 = (bf16[768,384]{0,1:T(8,128)(2,1)S(1)}, bf16[768,384]{0,1:T(8,128)(2,1)S(1)}, u32[]{:S(2)}, u32[]{:S(2)}) collective-permute-start(bf16[768,384]{0,1:T(8,128)(2,1)S(1)} %pad_maximum_fusion.14), channel_id=1, source_target_pairs={{4,0},{8,4},{12,8},{5,1},{9,5},{13,9},{6,2},{10,6},{14,10},{7,3},{... | collective-permute-start | bytes 1769480 | tf_op jit(solution)/shard_map/ppermute | solution.py:85
  71.8 15.6 %collective-permute-start.13 = (bf16[768,384]{0,1:T(8,128)(2,1)S(1)}, bf16[768,384]{0,1:T(8,128)(2,1)S(1)}, u32[]{:S(2)}, u32[]{:S(2)}) collective-permute-start(bf16[768,384]{0,1:T(8,128)(2,1)S(1)} %get-tuple-element.43), channel_id=1, source_target_pairs={{4,0},{8,4},{12,8},{5,1},{9,5},{13,9},{6,2},{10,6},{14,10},{7,3},{... | collective-permute-start | bytes 1769480 | tf_op jit(solution)/shard_map/ppermute | solution.py:85
  73.1 15.5 %collective-permute-start.14 = (bf16[768,384]{0,1:T(8,128)(2,1)S(1)}, bf16[768,384]{0,1:T(8,128)(2,1)S(1)}, u32[]{:S(2)}, u32[]{:S(2)}) collective-permute-start(bf16[768,384]{0,1:T(8,128)(2,1)S(1)} %get-tuple-element.44), channel_id=1, source_target_pairs={{0,4},{4,8},{8,12},{1,5},{5,9},{9,13},{2,6},{6,10},{10,14},{3,7},{... | collective-permute-start | bytes 1769480 | tf_op jit(solution)/shard_map/ppermute | solution.py:84
  79.4 28.5 %collective-permute-start.18 = (f32[1,576,384]{2,1,0:T(8,128)S(1)}, f32[1,576,384]{2,1,0:T(8,128)S(1)}, u32[]{:S(2)}, u32[]{:S(2)}) collective-permute-start(f32[1,576,384]{2,1,0:T(8,128)S(1)} %select_bitcast_fusion.1), channel_id=1, source_target_pairs={{0,1},{1,0},{2,3},{3,2},{4,5},{5,4},{6,7},{7,6},{8,9},{9,8},{10,11... | collective-permute-start | bytes 2654216 | tf_op jit(solution)/shard_map/ppermute | solution.py:21
  107.3 4.2 %collective-permute-start.20 = (f32[1,576,384]{2,1,0:T(8,128)S(1)}, f32[1,576,384]{2,1,0:T(8,128)S(1)}, u32[]{:S(2)}, u32[]{:S(2)}) collective-permute-start(f32[1,576,384]{2,1,0:T(8,128)S(1)} %select_bitcast_fusion), channel_id=1, source_target_pairs={{0,1},{1,0},{2,3},{3,2},{4,5},{5,4},{6,7},{7,6},{8,9},{9,8},{10,11... | collective-permute-start | bytes 2654216 | tf_op jit(solution)/shard_map/ppermute | solution.py:21
  108.0 13.9 %collective-permute-start.19 = (bf16[1,576,384]{2,1,0:T(8,128)(2,1)S(1)}, bf16[1,576,384]{2,1,0:T(8,128)(2,1)S(1)}, u32[]{:S(2)}, u32[]{:S(2)}) collective-permute-start(bf16[1,576,384]{2,1,0:T(8,128)(2,1)S(1)} %get-tuple-element.6), channel_id=1, source_target_pairs={{0,2},{1,3},{4,6},{5,7},{8,10},{9,11},{12,14},{13,15},{16,18},{17,... | collective-permute-start | bytes 1327112 | tf_op jit(solution)/shard_map/ppermute | solution.py:107
  111.6 14.9 %collective-permute-start.21 = (bf16[1,576,384]{2,1,0:T(8,128)(2,1)S(1)}, bf16[1,576,384]{2,1,0:T(8,128)(2,1)S(1)}, u32[]{:S(2)}, u32[]{:S(2)}) collective-permute-start(bf16[1,576,384]{2,1,0:T(8,128)(2,1)S(1)} %get-tuple-element.8), channel_id=1, source_target_pairs={{2,0},{3,1},{6,4},{7,5},{10,8},{11,9},{14,12},{15,13},{18,16},{19,... | collective-permute-start | bytes 1327112 | tf_op jit(solution)/shard_map/ppermute | solution.py:107
  114.3 17.0 %collective-permute-start.17 = (bf16[256,384]{0,1:T(8,128)(2,1)S(1)}, bf16[256,384]{0,1:T(8,128)(2,1)S(1)}, u32[]{:S(2)}, u32[]{:S(2)}) collective-permute-start(bf16[256,384]{0,1:T(8,128)(2,1)S(1)} %get-tuple-element.40), channel_id=1, source_target_pairs={{0,1},{1,0},{2,3},{3,2},{4,5},{5,4},{6,7},{7,6},{8,9},{9,8},{10,11... | collective-permute-start | bytes 589832 | tf_op jit(solution)/shard_map/ppermute | solution.py:21
  114.6 17.7 %collective-permute-start.16 = (bf16[256,384]{0,1:T(8,128)(2,1)S(1)}, bf16[256,384]{0,1:T(8,128)(2,1)S(1)}, u32[]{:S(2)}, u32[]{:S(2)}) collective-permute-start(bf16[256,384]{0,1:T(8,128)(2,1)S(1)} %get-tuple-element.41), channel_id=1, source_target_pairs={{0,2},{1,3},{2,0},{3,1},{4,6},{5,7},{6,4},{7,5},{8,10},{9,11},{10,... | collective-permute-start | bytes 589832 | tf_op jit(solution)/shard_map/ppermute | solution.py:21
  117.1 16.5 %collective-permute-start.15 = (bf16[256,384]{0,1:T(8,128)(2,1)S(1)}, bf16[256,384]{0,1:T(8,128)(2,1)S(1)}, u32[]{:S(2)}, u32[]{:S(2)}) collective-permute-start(bf16[256,384]{0,1:T(8,128)(2,1)S(1)} %get-tuple-element.42), channel_id=1, source_target_pairs={{0,3},{1,2},{2,1},{3,0},{4,7},{5,6},{6,5},{7,4},{8,11},{9,10},{10,... | collective-permute-start | bytes 589832 | tf_op jit(solution)/shard_map/ppermute | solution.py:21
  126.8 15.1 %collective-permute-start.24 = (bf16[576,384]{1,0:T(8,128)(2,1)S(1)}, bf16[576,384]{1,0:T(8,128)(2,1)S(1)}, u32[]{:S(2)}, u32[]{:S(2)}) collective-permute-start(bf16[576,384]{1,0:T(8,128)(2,1)S(1)} %get-tuple-element.4), channel_id=1, source_target_pairs={{0,12},{4,0},{8,4},{12,8},{1,13},{5,1},{9,5},{13,9},{2,14},{6,2},{... | collective-permute-start | bytes 1327112 | tf_op jit(solution)/shard_map/ppermute | solution.py:120
  131.3 36.7 %collective-permute-start.23 = (bf16[576,384]{1,0:T(8,128)(2,1)S(1)}, bf16[576,384]{1,0:T(8,128)(2,1)S(1)}, u32[]{:S(2)}, u32[]{:S(2)}) collective-permute-start(bf16[576,384]{1,0:T(8,128)(2,1)S(1)} %get-tuple-element.4), channel_id=1, source_target_pairs={{0,8},{4,12},{8,0},{12,4},{1,9},{5,13},{9,1},{13,5},{2,10},{6,14},... | collective-permute-start | bytes 1327112 | tf_op jit(solution)/shard_map/ppermute | solution.py:120
  131.3 36.7 %collective-permute-start.22 = (bf16[576,384]{1,0:T(8,128)(2,1)S(1)}, bf16[576,384]{1,0:T(8,128)(2,1)S(1)}, u32[]{:S(2)}, u32[]{:S(2)}) collective-permute-start(bf16[576,384]{1,0:T(8,128)(2,1)S(1)} %get-tuple-element.4), channel_id=1, source_target_pairs={{0,4},{4,8},{8,12},{12,0},{1,5},{5,9},{9,13},{13,1},{2,6},{6,10},{... | collective-permute-start | bytes 1327112 | tf_op jit(solution)/shard_map/ppermute | solution.py:120

commit v2 on v0

v2 whole, which is shorter than its diff:
```python
import functools
import math

import jax
import jax.numpy as jnp
from jax import lax
from jax.experimental import pallas as pl
from jax.experimental.pallas import tpu as pltpu
from jax.sharding import PartitionSpec as P

DILATION_FIRST = 1024
DILATION_SECOND = 2048
F32 = jnp.float32
BF16 = jnp.bfloat16
SMEM = pl.BlockSpec(memory_space=pltpu.SMEM)
VMEM = pl.BlockSpec(memory_space=pltpu.VMEM)


def shifted(block, axis, distance):
    n = lax.axis_size(axis)
    route = [(i, i + distance) for i in range(n) if 0 <= i + distance < n]
    return lax.ppermute(block, axis, route)


def turned(block, axis, turn):
    n = lax.axis_size(axis)
    return lax.ppermute(block, axis, [(i, (i + turn) % n) for i in range(n)])


def swapped(block, axis, bits):
    n = lax.axis_size(axis)
    return lax.ppermute(block, axis, [(i, i ^ bits) for i in range(n)])


def after(value, *others):
    return lax.optimization_barrier((value,) + others)[0]


def cut(block, index, rows):
    return lax.dynamic_slice_in_dim(block, index * rows, rows, 0)


def gather_pieces(block, axis, others):
    n = lax.axis_size(axis)
    held = {0: block}
    bit = n // 2
    while bit:
        for r in list(held):
            first_far = r == 0 and bit == n // 2
            source = after(held[r], others) if first_far else held[r]
            held[r ^ bit] = swapped(source, axis, bit)
        bit //= 2
    return [held[r] for r in range(n)]


def slope_of(v, th):
    coeff = 0.7978845608
    return 0.5 * (1.0 + th) + 0.5 * v * (1.0 - th * th) * coeff * (1.0 + 3.0 * 0.044715 * v * v)


def gelu_tanh(v):
    coeff = 0.7978845608
    return jnp.tanh(coeff * (v + 0.044715 * v * v * v))


def dot(a, b):
    return jnp.dot(a, b, preferred_element_type=F32)


def forward_kernel(sizes, place, *refs):
    groups, members, q, near, far = sizes
    own_e, own_l, low_e, low_l, high_e, high_l = refs[:6]
    w_pieces = refs[6 : 6 + members]
    c_pieces = refs[6 + members : 6 + 2 * members]
    outs = refs[6 + 2 * members :]
    act_stack, hid_stack, slope_one, delta, to_high, to_low, cot_out, w_out = outs[:8]
    ext, hid = outs[8:]
    s, j = place[0], place[1]
    rows = w_pieces[0].shape[0]
    for r in range(members):
        at = j ^ r
        for side, (early, late) in enumerate(((low_e, low_l), (own_e, own_l), (high_e, high_l))):
            source = early[r * q : (r + 1) * q] if r < 2 else late[(r - 2) * q : (r - 1) * q]
            ext[side * members + at] = source
        w_out[pl.ds(pl.multiple_of(at * rows, 16), rows), :] = w_pieces[r][...]
        cot_out[pl.ds(pl.multiple_of(at * q, 16), q), :] = c_pieces[r][...]
    taps = w_out.shape[0] // 2
    for b in range(-far, members + far):
        k = members + b
        stack = jnp.concatenate([ext[k - near], ext[k], ext[k + near]], 1)
        pre = dot(stack, w_out[:taps])
        th = gelu_tanh(pre)
        value = (ext[k].astype(F32) + 0.5 * pre * (1.0 + th)).astype(BF16)
        if b < 0:
            value = jnp.where(s > 0, value, jnp.zeros_like(value))
        if b >= members:
            value = jnp.where(s < groups - 1, value, jnp.zeros_like(value))
        hid[b + far] = value
        if 0 <= b < members:
            slope_one[b * q : (b + 1) * q] = slope_of(pre, th)
            act_stack[b * q : (b + 1) * q] = stack
    for b in range(members):
        stack = jnp.concatenate([hid[b], hid[b + far], hid[b + 2 * far]], 1)
        here = slice(b * q, (b + 1) * q)
        hid_stack[here] = stack
        pre = dot(stack, w_out[taps:])
        value = (cot_out[here].astype(F32) * slope_of(pre, gelu_tanh(pre))).astype(BF16)
        delta[here] = value
        if b < far:
            to_low[here] = value
        if b >= members - far:
            at = b - (members - far)
            to_high[at * q : (at + 1) * q] = value


def back_kernel(sizes, low, own, high, cot, slope, w_back, back_one, delta, to_high, to_low):
    members, q, near, far = sizes

    def block(b):
        if b < 0:
            return low[(b + far) * q : (b + far + 1) * q]
        if b >= members:
            return high[(b - members) * q : (b - members + 1) * q]
        return own[b * q : (b + 1) * q]

    for b in range(members):
        here = slice(b * q, (b + 1) * q)
        stack = jnp.concatenate([block(b + far), block(b), block(b - far)], 1)
        back = cot[here].astype(F32) + dot(stack, w_back[...])
        back_one[here] = back
        value = (back * slope[here]).astype(BF16)
        delta[here] = value
        if b < near:
            to_low[here] = value
        if b >= members - near:
            at = b - (members - near)
            to_high[at * q : (at + 1) * q] = value


def input_kernel(sizes, place, low, own, high, back_one, w_back, out):
    members, q, near = sizes
    j = place[1]

    def block(b):
        if b < 0:
            return low[(b + near) * q : (b + near + 1) * q]
        if b >= members:
            return high[(b - members) * q : (b - members + 1) * q]
        return own[b * q : (b + 1) * q]

    for b in range(members):
        here = slice(b * q, (b + 1) * q)
        stack = jnp.concatenate([block(b + near), block(b), block(b - near)], 1)
        value = (back_one[here] + dot(stack, w_back[...])).astype(BF16)
        out[pl.ds(pl.multiple_of((j ^ b) * q, 16), q), :] = value


def call(kernel, out_shapes, scratch=(), scalars=0, operands=()):
    specs = [SMEM] * scalars + [VMEM] * (len(operands) - scalars)
    return pl.pallas_call(
        kernel,
        out_shape=tuple(jax.ShapeDtypeStruct(shape, kind) for shape, kind in out_shapes),
        in_specs=specs,
        out_specs=tuple(VMEM for _ in out_shapes),
        scratch_shapes=list(scratch),
        compiler_params=pltpu.CompilerParams(vmem_limit_bytes=48 * 1024 * 1024),
    )(*operands)


def tap_grads(stacked, delta):
    return lax.dot_general(stacked, delta, (((0,), (0,)), ((), ())), preferred_element_type=F32)


def core_stage(grad, j):
    owners = lax.axis_size("sub") // 2
    parts = grad.reshape(owners, -1, grad.shape[1])
    odd = (j & 1) != 0
    keep = jnp.where(odd, parts[1::2], parts[0::2])
    send = jnp.where(odd, parts[0::2], parts[1::2])
    return keep + swapped(send, "sub", 1)


def seq_stage(part, s):
    n = lax.axis_size("seq")
    if n > 4:
        return lax.psum(part, "seq")
    rows = part.shape[1] // n

    def share(index):
        return lax.dynamic_slice_in_dim(part, index * rows, rows, 1)

    total = share(s)
    for turn in range(1, n):
        piece = share(lax.rem(s + turn, n)).astype(BF16)
        total = total + turned(piece, "seq", turn).astype(F32)
    return total


def chip_stage(part, j, high_layer):
    n = lax.axis_size("sub")
    bit = 2
    while bit < n:
        if part.shape[0] > 1:
            mine = (j & bit) != 0
            keep = jnp.where(mine, part[1::2], part[0::2])
            send = jnp.where(mine, part[0::2], part[1::2])
            part = keep + swapped(send.astype(BF16), "sub", bit).astype(F32)
        else:
            route = [(i, i ^ bit) for i in range(n) if ((i & bit) == 0) == high_layer]
            part = part + lax.ppermute(part.astype(BF16), "sub", route).astype(F32)
        bit *= 2
    return part[0]


def spread_seq(total, s):
    n = lax.axis_size("seq")
    if n > 4:
        return total
    rows, channels = total.shape
    whole = jnp.zeros((n * rows, channels), F32)
    whole = lax.dynamic_update_slice_in_dim(whole, total, s * rows, 0)
    sent = total.astype(BF16)
    for turn in range(1, n):
        got = turned(sent, "seq", turn).astype(F32)
        whole = lax.dynamic_update_slice_in_dim(whole, got, lax.rem(s + n - turn, n) * rows, 0)
    return whole


def per_device(activations, cotangent, weights):
    count, channels = activations.shape
    groups, members = lax.axis_size("seq"), lax.axis_size("sub")
    s, j = lax.axis_index("seq"), lax.axis_index("sub")
    place = jnp.stack([s, j]).astype(jnp.int32)
    near, far = DILATION_FIRST // count, DILATION_SECOND // count
    q = count // members
    taps = 3 * channels
    grad_scale = 1.0 / math.sqrt(count * groups * members)

    pieces = [cut(activations, j ^ r, q) for r in range(members)]
    got = [pieces[0]] + [swapped(pieces[r], "sub", r) for r in range(1, members)]
    own_e = jnp.concatenate(got[:2], 0)
    low_e, high_e = shifted(own_e, "seq", 1), shifted(own_e, "seq", -1)
    own_l = jnp.concatenate(got[2:], 0)
    low_l, high_l = shifted(own_l, "seq", 1), shifted(own_l, "seq", -1)

    w_pieces = gather_pieces(weights, "sub", own_l)
    c_cut = [cut(cotangent, j ^ r, q) for r in range(members)]
    far_weights = w_pieces[members // 2]
    c_pieces = c_cut[:1] + [
        swapped(after(c_cut[r], far_weights) if r > 1 else c_cut[r], "sub", r)
        for r in range(1, members)
    ]

    act_stack, hid_stack, slope_one, delta_two, up_two, down_two, cot, all_weights = call(
        functools.partial(forward_kernel, (groups, members, q, near, far)),
        (
            ((count, taps), BF16),
            ((count, taps), BF16),
            ((count, channels), F32),
            ((count, channels), BF16),
            ((far * q, channels), BF16),
            ((far * q, channels), BF16),
            ((count, channels), BF16),
            ((2 * taps, channels), BF16),
        ),
        (
            pltpu.VMEM((3 * members, q, channels), BF16),
            pltpu.VMEM((members + 2 * far, q, channels), BF16),
        ),
        1,
        (place, own_e, own_l, low_e, low_l, high_e, high_l, *w_pieces, *c_pieces),
    )
    two_low, two_high = shifted(up_two, "seq", 1), shifted(down_two, "seq", -1)
    back = all_weights.reshape(2, 3, channels, channels).transpose(0, 1, 3, 2)
    back = back.reshape(2, taps, channels)
    back_first, back_second = back[0], back[1]

    grad_two = tap_grads(hid_stack, delta_two) * grad_scale
    part_two = chip_stage(seq_stage(core_stage(grad_two, j), s), j, True)

    back_one, delta_one, up_one, down_one = call(
        functools.partial(back_kernel, (members, q, near, far)),
        (
            ((count, channels), F32),
            ((count, channels), BF16),
            ((near * q, channels), BF16),
            ((near * q, channels), BF16),
        ),
        operands=(two_low, delta_two, two_high, cot, slope_one, back_second),
    )
    one_low, one_high = shifted(up_one, "seq", 1), shifted(down_one, "seq", -1)
    grad_one = tap_grads(act_stack, delta_one) * grad_scale
    part_one = chip_stage(seq_stage(core_stage(grad_one, j), s), j, False)

    (grad_in,) = call(
        functools.partial(input_kernel, (members, q, near)),
        (((count, channels), BF16),),
        scalars=1,
        operands=(place, one_low, delta_one, one_high, back_one, back_first),
    )
    input_grad = jnp.zeros((count, channels), BF16)
    for r in range(members):
        piece = grad_in[r * q : (r + 1) * q]
        piece = swapped(piece, "sub", r) if r else piece
        input_grad = lax.dynamic_update_slice_in_dim(input_grad, piece, (j ^ r) * q, 0)

    weight_grad = spread_seq(jnp.where(j >= members // 2, part_two, part_one), s)
    return (input_grad, weight_grad)


def solution(mesh):
    placed = (P(("grp", "seq", "sub"), None), P(("grp", "seq", "sub"), None), P("sub", None))
    return jax.shard_map(
        per_device,
        mesh=mesh,
        in_specs=placed,
        out_specs=(P(("grp", "seq", "sub"), None), P(("grp", "sub"), None)),
        check_vma=False,
    )
```

time: 238 us -> 142 us (0.60)
  waiting for transfers between devices: 172 us -> 54.1 us
  starting transfers between devices: 20.8 us -> 47.8 us
  Pallas kernels: 0 us -> 15.2 us
  matrix products: 18.9 us -> 4.7 us
  between operations: 13.9 us -> 1.01 us
  local copies, waits for them, and re-layouts: 9.33 us -> 13.7 us
  other arithmetic: 2.4 us -> 5.13 us
    psum x1 -> x0, waiting for transfers between devices: 47 us -> none  [per_device(): summed = lax.psum(local_grads, 'seq')]
    reduce_scatter x1 -> x0, waiting for transfers between devices: 39.1 us -> none  [per_device(): lax.psum_scatter(summed, 'sub', scatter_dimension=0, tiled=True)]
    ppermute x8 -> x33, starting transfers between devices: 20.7 us -> 47.8 us  [the longest x8 19.6 us: shifted(): return lax.ppermute(block, axis, route)]
    all_gather x1 -> x0, waiting for transfers between devices: 22.2 us -> none  [per_device(): all_weights = lax.all_gather(weights, 'sub', axis=0, tiled=True)]
    pallas_call x0 -> x3, Pallas kernels: none -> 15.2 us  [call(): pl.pallas_call(kernel, out_shape=tuple((jax.ShapeDtypeStruct(shape, kind)...]
    dot_general x4 -> x0, matrix products: 12.8 us -> none  [the longest x1 4.94 us: per_device(): jnp.dot(first_layer_weights, first, preferred_element_type=jnp.float32)]
    ppermute x8 -> x33, waiting for transfers between devices: 63.1 us -> 54.1 us  [the longest x8 18.9 us: shifted(): return lax.ppermute(block, axis, route)]
    unnamed x16 -> x21, local copies, waits for them, and re-layouts: 8.17 us -> 2.56 us
  transfers between devices with their start and end apart: 11 -> 33, of which waited for: 7 -> 17; matrix products, arithmetic and copies ran while one was open for 4% -> 14% of each run, Pallas kernels for 0% -> 4%
where the time goes in v2:
time: 142 us
  waiting for transfers between devices  54.1 us (38%)
  starting transfers between devices  47.8 us (34%)
  Pallas kernels  15.2 us (11%)
  local copies, waits for them, and re-layouts  13.7 us (10%)
  other arithmetic  5.13 us (4%)
  matrix products  4.7 us (3%)
    ppermute x8, starting transfers between devices, shifted(): return lax.ppermute(block, axis, route)  19.6 us
    ppermute x8, waiting for transfers between devices, shifted(): return lax.ppermute(block, axis, route)  18.9 us
    ppermute x14, waiting for transfers between devices, swapped(): return lax.ppermute(block, axis, [(i, i ^ bits) for i in range(n)])  17.4 us
    pallas_call x3, Pallas kernels, call(): pl.pallas_call(kernel, out_shape=tuple((jax.ShapeDtypeStruct(shape, kind)...  15.2 us
    ppermute x9, starting transfers between devices, turned(): return lax.ppermute(block, axis, [(i, (i + turn) % n) for i in range(n)])  13.8 us
    ppermute x9, waiting for transfers between devices, turned(): return lax.ppermute(block, axis, [(i, (i + turn) % n) for i in range(n)])  13.2 us
    ppermute x14, starting transfers between devices, swapped(): return lax.ppermute(block, axis, [(i, i ^ bits) for i in range(n)])  9.7 us
    ppermute x2, starting transfers between devices, chip_stage(): part = part + lax.ppermute(part.astype(BF16), 'sub', route).astype(F32)  4.81 us
  transfers between devices with their start and end apart: 33, of which 17 were waited for; matrix products, arithmetic and copies ran while one was open for 14% of the time, Pallas kernels for 4%

profile of v2, /device:TPU:0, one launch (start us, length us, event | category | flops | bytes accessed | tf_op | source)
XLA Modules:
  0.0 141.7 jit_solution(7853255273437917172)
XLA Ops:
  2.1 3.0 %collective-permute-start.1 = (bf16[256,384]{1,0:T(8,128)(2,1)S(1)}, bf16[256,384]{1,0:T(8,128)(2,1)S(1)}, u32[]{:S(2)}, u32[]{:S(2)}) collective-permute-start(bf16[256,384]{1,0:T(8,128)(2,1)S(1)} %get-tuple-element.53), channel_id=1, source_target_pairs={{0,2},{1,3},{2,0},{3,1},{4,6},{5,7},{6,4},{7,5},{8,10},{9,11},{10,... | collective-permute-start | bytes 589832 | tf_op jit(solution)/shard_map/ppermute | solution.py:32
  5.1 5.7 %collective-permute-done.1 = bf16[256,384]{1,0:T(8,128)(2,1)S(1)} collective-permute-done((bf16[256,384]{1,0:T(8,128)(2,1)S(1)}, bf16[256,384]{1,0:T(8,128)(2,1)S(1)}, u32[]{:S(2)}, u32[]{:S(2)}) %collective-permute-start.1) | collective-permute-done | bytes 196640 | tf_op jit(solution)/shard_map/ppermute | solution.py:32
  10.8 2.6 %collective-permute-done.2 = bf16[256,384]{1,0:T(8,128)(2,1)S(1)} collective-permute-done((bf16[256,384]{1,0:T(8,128)(2,1)S(1)}, bf16[256,384]{1,0:T(8,128)(2,1)S(1)}, u32[]{:S(2)}, u32[]{:S(2)}) %collective-permute-start.2) | collective-permute-done | bytes 196640 | tf_op jit(solution)/shard_map/ppermute | solution.py:32
  16.9 3.5 %collective-permute-start.4 = (bf16[512,384]{1,0:T(8,128)(2,1)S(1)}, bf16[512,384]{1,0:T(8,128)(2,1)S(1)}, u32[]{:S(2)}, u32[]{:S(2)}) collective-permute-start(bf16[512,384]{1,0:T(8,128)(2,1)S(1)} %constant_dynamic-update-slice_fusion.refs_1_), channel_id=1, source_target_pairs={{0,4},{4,8},{8,12},{1,5},{5,9},{9,13},{2,6},{6,10},{10,14},{3,7},{... | collective-permute-start | bytes 1179656 | tf_op jit(solution)/shard_map/ppermute | solution.py:22
  21.7 4.5 %collective-permute-done.8.refs_8_ = bf16[576,384]{1,0:T(8,128)(2,1)S(1)} collective-permute-done((bf16[576,384]{1,0:T(8,128)(2,1)S(1)}, bf16[576,384]{1,0:T(8,128)(2,1)S(1)}, u32[]{:S(2)}, u32[]{:S(2)}) %collective-permute-start.8) | collective-permute-done | bytes 442400 | tf_op jit(solution)/shard_map/ppermute | solution.py:32
  26.9 4.5 %collective-permute-start.3 = (bf16[512,384]{1,0:T(8,128)(2,1)S(1)}, bf16[512,384]{1,0:T(8,128)(2,1)}, u32[]{:S(2)}, u32[]{:S(2)}) collective-permute-start(bf16[512,384]{1,0:T(8,128)(2,1)S(1)} %pad_maximum_fusion.refs_0_), channel_id=1, source_target_pairs={{0,4},{4,8},{8,12},{1,5},{5,9},{9,13},{2,6},{6,10},{10,14},{3,7},{... | collective-permute-start | bytes 1179656 | tf_op jit(solution)/shard_map/ppermute | solution.py:22
  32.7 1.7 %collective-permute-start.11 = (bf16[256,384]{1,0:T(8,128)(2,1)}, bf16[256,384]{1,0:T(8,128)(2,1)}, u32[]{:S(2)}, u32[]{:S(2)}) collective-permute-start(bf16[256,384]{1,0:T(8,128)(2,1)} %get-tuple-element.18), channel_id=1, source_target_pairs={{0,2},{1,3},{2,0},{3,1},{4,6},{5,7},{6,4},{7,5},{8,10},{9,11},{10,... | collective-permute-start | bytes 589832 | tf_op jit(solution)/shard_map/ppermute | solution.py:32
  34.5 5.2 %collective-permute-done.3.refs_2_ = bf16[512,384]{1,0:T(8,128)(2,1)} collective-permute-done((bf16[512,384]{1,0:T(8,128)(2,1)S(1)}, bf16[512,384]{1,0:T(8,128)(2,1)}, u32[]{:S(2)}, u32[]{:S(2)}) %collective-permute-start.3) | collective-permute-done | bytes 393248 | tf_op jit(solution)/shard_map/ppermute | solution.py:22
  39.7 5.0 %collective-permute-done.5.refs_4_ = bf16[512,384]{1,0:T(8,128)(2,1)} collective-permute-done((bf16[512,384]{1,0:T(8,128)(2,1)S(1)}, bf16[512,384]{1,0:T(8,128)(2,1)}, u32[]{:S(2)}, u32[]{:S(2)}) %collective-permute-start.5) | collective-permute-done | bytes 393248 | tf_op jit(solution)/shard_map/ppermute | solution.py:22
  45.6 10.1 %shard_map.50 = (bf16[1024,1152]{1,0:T(8,128)(2,1)}, bf16[1024,1152]{1,0:T(8,128)(2,1)}, f32[1024,384]{1,0:T(8,128)}, bf16[1024,384]{1,0:T(8,128)(2,1)}, bf16[51...) custom-call(s32[2]{0:T(128)S(1)} %pad_add_fusion.place, ...), custom_call_target="tpu_custom_call" | custom-call | tf_op jit(solution)/shard_map/pallas_call | solution.py:160
  55.7 3.0 %collective-permute-start.13 = (bf16[512,384]{1,0:T(8,128)(2,1)}, bf16[512,384]{1,0:T(8,128)(2,1)S(1)}, u32[]{:S(2)}, u32[]{:S(2)}) collective-permute-start(bf16[512,384]{1,0:T(8,128)(2,1)} %get-tuple-element.20), channel_id=1, source_target_pairs={{0,4},{4,8},{8,12},{1,5},{5,9},{9,13},{2,6},{6,10},{10,14},{3,7},{... | collective-permute-start | bytes 1179656 | tf_op jit(solution)/shard_map/ppermute | solution.py:22
  60.0 3.3 %convolution_multiply_fusion.1 = f32[1152,384]{1,0:T(8,128)S(1)} fusion(bf16[1024,1152]{1,0:T(8,128)(2,1)} %get-tuple-element.30, bf16[1024,384]{1,0:T(8,128)(2,1)} %get-tuple-element.21.own), kind=kOutput, calls=%fused_computation.1 | convolution fusion | flops 906412032 | bytes 4915200 | tf_op jit(solution)/shard_map/dot_general | solution.py:171
  64.9 2.8 %copy.5 = bf16[2,3,384,384]{2,3,1,0:T(8,128)(2,1)S(1)} copy(bf16[2,3,384,384]{3,2,1,0:T(8,128)(2,1)} %bitcast.24) | data formatting | bytes 3538944 | tf_op jit(solution)/shard_map/reshape | solution.py:274
  68.3 4.0 %collective-permute-done.14.high = bf16[512,384]{1,0:T(8,128)(2,1)S(1)} collective-permute-done((bf16[512,384]{1,0:T(8,128)(2,1)}, bf16[512,384]{1,0:T(8,128)(2,1)S(1)}, u32[]{:S(2)}, u32[]{:S(2)}) %collective-permute-start.14) | collective-permute-done | bytes 393248 | tf_op jit(solution)/shard_map/ppermute | solution.py:22
  72.4 3.0 %shard_map.51 = (f32[1024,384]{1,0:T(8,128)S(1)}, bf16[1024,384]{1,0:T(8,128)(2,1)S(1)}, bf16[256,384]{1,0:T(8,128)(2,1)S(1)}, bf16[256,384]{1,0:T(8,128)(2,1)S(1)}) custom-call(bf16[512,384]{1,0:T(8,128)(2,1)S(1)} %collective-permute-done.13.low, bf16[1024,384]{1,0:T(8,128)(2,1)S(1)} %copy-done, bf16[512,384]{1,0:T(8,128)(2,1)S(1)} %collective-permute-done.14.high, ...), custom_call_target="tpu_custom_call" | custom-call | tf_op jit(solution)/shard_map/pallas_call | solution.py:160
  75.4 3.3 %collective-permute-start.15 = (bf16[256,384]{1,0:T(8,128)(2,1)S(1)}, bf16[256,384]{1,0:T(8,128)(2,1)S(1)}, u32[]{:S(2)}, u32[]{:S(2)}) collective-permute-start(bf16[256,384]{1,0:T(8,128)(2,1)S(1)} %get-tuple-element.26), channel_id=1, source_target_pairs={{0,4},{4,8},{8,12},{1,5},{5,9},{9,13},{2,6},{6,10},{10,14},{3,7},{... | collective-permute-start | bytes 589832 | tf_op jit(solution)/shard_map/ppermute | solution.py:22
  82.7 4.1 %collective-permute-done.16.high = bf16[256,384]{1,0:T(8,128)(2,1)S(1)} collective-permute-done((bf16[256,384]{1,0:T(8,128)(2,1)S(1)}, bf16[256,384]{1,0:T(8,128)(2,1)S(1)}, u32[]{:S(2)}, u32[]{:S(2)}) %collective-permute-start.16) | collective-permute-done | bytes 196640 | tf_op jit(solution)/shard_map/ppermute | solution.py:22
  86.9 2.0 %shard_map.52 = bf16[1024,384]{1,0:T(8,128)(2,1)S(1)} custom-call(s32[2]{0:T(128)S(1)} %pad_add_fusion.place, bf16[256,384]{1,0:T(8,128)(2,1)S(1)} %collective-permute-done.15.low, bf16[1024,384]{1,0:T(8,128)(2,1)S(1)} %get-tuple-element.27.own, bf16[256,384]{1,0:T(8,128)(2,1)S(1)} %collective-permute-done.16.high, ...), custom_call_target="tpu_custom_call" | custom-call | tf_op jit(solution)/shard_map/pallas_call | solution.py:160
  92.6 1.6 %constant_dynamic-update-slice_fusion.4 = bf16[1024,384]{1,0:T(8,128)(2,1)} fusion(bf16[1024,384]{1,0:T(8,128)(2,1)} %get-tuple-element.45, bf16[256,384]{1,0:T(8,128)(2,1)} %collective-permute-done.17, s32[]{:T(128)S(6)} %select_n.84), kind=kLoop, calls=%fused_computation.26 | loop fusion | bytes 393220 | tf_op jit(solution)/shard_map/dynamic_update_slice | solution.py:305
  94.2 4.5 %collective-permute-done.18 = bf16[256,384]{1,0:T(8,128)(2,1)} collective-permute-done((bf16[256,384]{1,0:T(8,128)(2,1)}, bf16[256,384]{1,0:T(8,128)(2,1)}, u32[]{:S(2)}, u32[]{:S(2)}) %collective-permute-start.18) | collective-permute-done | bytes 196640 | tf_op jit(solution)/shard_map/ppermute | solution.py:32
  101.7 1.8 %collective-permute-start.21 = (bf16[1,144,384]{2,1,0:T(8,128)(2,1)S(1)}, bf16[1,144,384]{2,1,0:T(8,128)(2,1)S(1)}, u32[]{:S(2)}, u32[]{:S(2)}) collective-permute-start(bf16[1,144,384]{2,1,0:T(8,128)(2,1)S(1)} %get-tuple-element.36), channel_id=1, source_target_pairs={{0,4},{4,8},{8,12},{12,0},{1,5},{5,9},{9,13},{13,1},{2,6},{6,10},{... | collective-permute-start | bytes 331784 | tf_op jit(solution)/shard_map/ppermute | solution.py:27
  103.5 2.7 %collective-permute-start.23 = (bf16[1,144,384]{2,1,0:T(8,128)(2,1)S(1)}, bf16[1,144,384]{2,1,0:T(8,128)(2,1)S(1)}, u32[]{:S(2)}, u32[]{:S(2)}) collective-permute-start(bf16[1,144,384]{2,1,0:T(8,128)(2,1)S(1)} %get-tuple-element.37), channel_id=1, source_target_pairs={{0,12},{4,0},{8,4},{12,8},{1,13},{5,1},{9,5},{13,9},{2,14},{6,2},{... | collective-permute-start | bytes 331784 | tf_op jit(solution)/shard_map/ppermute | solution.py:27
  107.6 2.1 %collective-permute-done.21 = bf16[1,144,384]{2,1,0:T(8,128)(2,1)S(1)} collective-permute-done((bf16[1,144,384]{2,1,0:T(8,128)(2,1)S(1)}, bf16[1,144,384]{2,1,0:T(8,128)(2,1)S(1)}, u32[]{:S(2)}, u32[]{:S(2)}) %collective-permute-start.21) | collective-permute-done | bytes 110624 | tf_op jit(solution)/shard_map/ppermute | solution.py:27
  109.7 2.2 %collective-permute-start.27 = (bf16[1,144,384]{2,1,0:T(8,128)(2,1)S(1)}, bf16[1,144,384]{2,1,0:T(8,128)(2,1)S(1)}, u32[]{:S(2)}, u32[]{:S(2)}) collective-permute-start(bf16[1,144,384]{2,1,0:T(8,128)(2,1)S(1)} %get-tuple-element.41), channel_id=1, source_target_pairs={{0,8},{4,12},{8,0},{12,4},{1,9},{5,13},{9,1},{13,5},{2,10},{6,14},... | collective-permute-start | bytes 331784 | tf_op jit(solution)/shard_map/ppermute | solution.py:27
  111.9 3.9 %collective-permute-done.22 = bf16[1,144,384]{2,1,0:T(8,128)(2,1)S(1)} collective-permute-done((bf16[1,144,384]{2,1,0:T(8,128)(2,1)S(1)}, bf16[1,144,384]{2,1,0:T(8,128)(2,1)S(1)}, u32[]{:S(2)}, u32[]{:S(2)}) %collective-permute-start.22) | collective-permute-done | bytes 110624 | tf_op jit(solution)/shard_map/ppermute | solution.py:27
  115.8 2.2 %collective-permute-start.28 = (bf16[1,144,384]{2,1,0:T(8,128)(2,1)S(1)}, bf16[1,144,384]{2,1,0:T(8,128)(2,1)S(1)}, u32[]{:S(2)}, u32[]{:S(2)}) collective-permute-start(bf16[1,144,384]{2,1,0:T(8,128)(2,1)S(1)} %get-tuple-element.40), channel_id=1, source_target_pairs={{0,12},{4,0},{8,4},{12,8},{1,13},{5,1},{9,5},{13,9},{2,14},{6,2},{... | collective-permute-start | bytes 331784 | tf_op jit(solution)/shard_map/ppermute | solution.py:27
  118.1 3.5 %collective-permute-start.24 = (bf16[1,144,384]{2,1,0:T(8,128)(2,1)S(1)}, bf16[1,144,384]{2,1,0:T(8,128)(2,1)S(1)}, u32[]{:S(2)}, u32[]{:S(2)}) collective-permute-start(bf16[1,144,384]{2,1,0:T(8,128)(2,1)S(1)} %fusion), channel_id=1, source_target_pairs={{0,2},{1,3},{4,6},{5,7},{8,10},{9,11},{12,14},{13,15},{16,18},{17,... | collective-permute-start | bytes 331784 | tf_op jit(solution)/shard_map/ppermute | solution.py:210
  125.0 4.6 %collective-permute-done.29 = bf16[1,144,384]{2,1,0:T(8,128)(2,1)S(1)} collective-permute-done((bf16[1,144,384]{2,1,0:T(8,128)(2,1)S(1)}, bf16[1,144,384]{2,1,0:T(8,128)(2,1)S(1)}, u32[]{:S(2)}, u32[]{:S(2)}) %collective-permute-start.29) | collective-permute-done | bytes 110624 | tf_op jit(solution)/shard_map/ppermute | solution.py:210
  129.8 2.4 %collective-permute-start.30 = (bf16[144,384]{1,0:T(8,128)(2,1)S(1)}, bf16[144,384]{1,0:T(8,128)(2,1)S(1)}, u32[]{:S(2)}, u32[]{:S(2)}) collective-permute-start(bf16[144,384]{1,0:T(8,128)(2,1)S(1)} %get-tuple-element.32), channel_id=1, source_target_pairs={{0,4},{4,8},{8,12},{12,0},{1,5},{5,9},{9,13},{13,1},{2,6},{6,10},{... | collective-permute-start | bytes 331784 | tf_op jit(solution)/shard_map/ppermute | solution.py:27
  133.0 1.7 %collective-permute-start.32 = (bf16[144,384]{1,0:T(8,128)(2,1)S(1)}, bf16[144,384]{1,0:T(8,128)(2,1)S(1)}, u32[]{:S(2)}, u32[]{:S(2)}) collective-permute-start(bf16[144,384]{1,0:T(8,128)(2,1)S(1)} %get-tuple-element.32), channel_id=1, source_target_pairs={{0,12},{4,0},{8,4},{12,8},{1,13},{5,1},{9,5},{13,9},{2,14},{6,2},{... | collective-permute-start | bytes 331784 | tf_op jit(solution)/shard_map/ppermute | solution.py:27
  134.8 2.9 %collective-permute-done.30 = bf16[144,384]{1,0:T(8,128)(2,1)S(1)} collective-permute-done((bf16[144,384]{1,0:T(8,128)(2,1)S(1)}, bf16[144,384]{1,0:T(8,128)(2,1)S(1)}, u32[]{:S(2)}, u32[]{:S(2)}) %collective-permute-start.30) | collective-permute-done | bytes 110624 | tf_op jit(solution)/shard_map/ppermute | solution.py:27
  137.7 3.0 %collective-permute-done.31 = bf16[144,384]{1,0:T(8,128)(2,1)S(1)} collective-permute-done((bf16[144,384]{1,0:T(8,128)(2,1)S(1)}, bf16[144,384]{1,0:T(8,128)(2,1)S(1)}, u32[]{:S(2)}, u32[]{:S(2)}) %collective-permute-start.31) | collective-permute-done | bytes 110624 | tf_op jit(solution)/shard_map/ppermute | solution.py:27
  (86 shorter events, 30.2 us)
Async XLA Ops:
  2.1 8.7 %collective-permute-start.1 = (bf16[256,384]{1,0:T(8,128)(2,1)S(1)}, bf16[256,384]{1,0:T(8,128)(2,1)S(1)}, u32[]{:S(2)}, u32[]{:S(2)}) collective-permute-start(bf16[256,384]{1,0:T(8,128)(2,1)S(1)} %get-tuple-element.53), channel_id=1, source_target_pairs={{0,2},{1,3},{2,0},{3,1},{4,6},{5,7},{6,4},{7,5},{8,10},{9,11},{10,... | collective-permute-start | bytes 589832 | tf_op jit(solution)/shard_map/ppermute | solution.py:32
  5.1 8.4 %collective-permute-start.2 = (bf16[256,384]{1,0:T(8,128)(2,1)S(1)}, bf16[256,384]{1,0:T(8,128)(2,1)S(1)}, u32[]{:S(2)}, u32[]{:S(2)}) collective-permute-start(bf16[256,384]{1,0:T(8,128)(2,1)S(1)} %get-tuple-element.50), channel_id=1, source_target_pairs={{0,3},{1,2},{2,1},{3,0},{4,7},{5,6},{6,5},{7,4},{8,11},{9,10},{10,... | collective-permute-start | bytes 589832 | tf_op jit(solution)/shard_map/ppermute | solution.py:32
  13.5 12.7 %collective-permute-start.8 = (bf16[576,384]{1,0:T(8,128)(2,1)S(1)}, bf16[576,384]{1,0:T(8,128)(2,1)S(1)}, u32[]{:S(2)}, u32[]{:S(2)}) collective-permute-start(bf16[576,384]{1,0:T(8,128)(2,1)S(1)} %copy-done.2), channel_id=1, source_target_pairs={{0,2},{1,3},{2,0},{3,1},{4,6},{5,7},{6,4},{7,5},{8,10},{9,11},{10,... | collective-permute-start | bytes 1327112 | tf_op jit(solution)/shard_map/ppermute | solution.py:32
  14.9 16.5 %collective-permute-start.7 = (bf16[576,384]{1,0:T(8,128)(2,1)S(1)}, bf16[576,384]{1,0:T(8,128)(2,1)S(1)}, u32[]{:S(2)}, u32[]{:S(2)}) collective-permute-start(bf16[576,384]{1,0:T(8,128)(2,1)S(1)} %copy-done.2), channel_id=1, source_target_pairs={{0,1},{1,0},{2,3},{3,2},{4,5},{5,4},{6,7},{7,6},{8,9},{9,8},{10,11... | collective-permute-start | bytes 1327112 | tf_op jit(solution)/shard_map/ppermute | solution.py:32
  15.6 4.8 %collective-permute-start = (bf16[256,384]{1,0:T(8,128)(2,1)S(1)}, bf16[256,384]{1,0:T(8,128)(2,1)S(1)}, u32[]{:S(2)}, u32[]{:S(2)}) collective-permute-start(bf16[256,384]{1,0:T(8,128)(2,1)S(1)} %get-tuple-element.51), channel_id=1, source_target_pairs={{0,1},{1,0},{2,3},{3,2},{4,5},{5,4},{6,7},{7,6},{8,9},{9,8},{10,11... | collective-permute-start | bytes 589832 | tf_op jit(solution)/shard_map/ppermute | solution.py:32
  16.4 9.8 %collective-permute-start.10 = (bf16[256,384]{1,0:T(8,128)(2,1)S(1)}, bf16[256,384]{1,0:T(8,128)(2,1)S(1)}, u32[]{:S(2)}, u32[]{:S(2)}) collective-permute-start(bf16[256,384]{1,0:T(8,128)(2,1)S(1)} %get-tuple-element.47), channel_id=1, source_target_pairs={{0,1},{1,0},{2,3},{3,2},{4,5},{5,4},{6,7},{7,6},{8,9},{9,8},{10,11... | collective-permute-start | bytes 589832 | tf_op jit(solution)/shard_map/ppermute | solution.py:32
  16.9 15.8 %collective-permute-start.4 = (bf16[512,384]{1,0:T(8,128)(2,1)S(1)}, bf16[512,384]{1,0:T(8,128)(2,1)S(1)}, u32[]{:S(2)}, u32[]{:S(2)}) collective-permute-start(bf16[512,384]{1,0:T(8,128)(2,1)S(1)} %constant_dynamic-update-slice_fusion.refs_1_), channel_id=1, source_target_pairs={{0,4},{4,8},{8,12},{1,5},{5,9},{9,13},{2,6},{6,10},{10,14},{3,7},{... | collective-permute-start | bytes 1179656 | tf_op jit(solution)/shard_map/ppermute | solution.py:22
  20.4 14.0 %collective-permute-start.6 = (bf16[512,384]{1,0:T(8,128)(2,1)S(1)}, bf16[512,384]{1,0:T(8,128)(2,1)S(1)}, u32[]{:S(2)}, u32[]{:S(2)}) collective-permute-start(bf16[512,384]{1,0:T(8,128)(2,1)S(1)} %constant_dynamic-update-slice_fusion.refs_1_), channel_id=1, source_target_pairs={{4,0},{8,4},{12,8},{5,1},{9,5},{13,9},{6,2},{10,6},{14,10},{7,3},{... | collective-permute-start | bytes 1179656 | tf_op jit(solution)/shard_map/ppermute | solution.py:22
  26.2 18.5 %collective-permute-start.9 = (bf16[576,384]{1,0:T(8,128)(2,1)S(1)}, bf16[576,384]{1,0:T(8,128)(2,1)S(1)}, u32[]{:S(2)}, u32[]{:S(2)}) collective-permute-start(bf16[576,384]{1,0:T(8,128)(2,1)S(1)} %collective-permute-done.8.refs_8_), channel_id=1, source_target_pairs={{0,1},{1,0},{2,3},{3,2},{4,5},{5,4},{6,7},{7,6},{8,9},{9,8},{10,11... | collective-permute-start | bytes 1327112 | tf_op jit(solution)/shard_map/ppermute | solution.py:32
  26.9 12.8 %collective-permute-start.3 = (bf16[512,384]{1,0:T(8,128)(2,1)S(1)}, bf16[512,384]{1,0:T(8,128)(2,1)}, u32[]{:S(2)}, u32[]{:S(2)}) collective-permute-start(bf16[512,384]{1,0:T(8,128)(2,1)S(1)} %pad_maximum_fusion.refs_0_), channel_id=1, source_target_pairs={{0,4},{4,8},{8,12},{1,5},{5,9},{9,13},{2,6},{6,10},{10,14},{3,7},{... | collective-permute-start | bytes 1179656 | tf_op jit(solution)/shard_map/ppermute | solution.py:22
  31.4 13.2 %collective-permute-start.5 = (bf16[512,384]{1,0:T(8,128)(2,1)S(1)}, bf16[512,384]{1,0:T(8,128)(2,1)}, u32[]{:S(2)}, u32[]{:S(2)}) collective-permute-start(bf16[512,384]{1,0:T(8,128)(2,1)S(1)} %pad_maximum_fusion.refs_0_), channel_id=1, source_target_pairs={{4,0},{8,4},{12,8},{5,1},{9,5},{13,9},{6,2},{10,6},{14,10},{7,3},{... | collective-permute-start | bytes 1179656 | tf_op jit(solution)/shard_map/ppermute | solution.py:22
  32.7 11.9 %collective-permute-start.11 = (bf16[256,384]{1,0:T(8,128)(2,1)}, bf16[256,384]{1,0:T(8,128)(2,1)}, u32[]{:S(2)}, u32[]{:S(2)}) collective-permute-start(bf16[256,384]{1,0:T(8,128)(2,1)} %get-tuple-element.18), channel_id=1, source_target_pairs={{0,2},{1,3},{2,0},{3,1},{4,6},{5,7},{6,4},{7,5},{8,10},{9,11},{10,... | collective-permute-start | bytes 589832 | tf_op jit(solution)/shard_map/ppermute | solution.py:32
  34.4 10.2 %collective-permute-start.12 = (bf16[256,384]{1,0:T(8,128)(2,1)}, bf16[256,384]{1,0:T(8,128)(2,1)}, u32[]{:S(2)}, u32[]{:S(2)}) collective-permute-start(bf16[256,384]{1,0:T(8,128)(2,1)} %get-tuple-element.19), channel_id=1, source_target_pairs={{0,3},{1,2},{2,1},{3,0},{4,7},{5,6},{6,5},{7,4},{8,11},{9,10},{10,... | collective-permute-start | bytes 589832 | tf_op jit(solution)/shard_map/ppermute | solution.py:32
  55.7 12.6 %collective-permute-start.13 = (bf16[512,384]{1,0:T(8,128)(2,1)}, bf16[512,384]{1,0:T(8,128)(2,1)S(1)}, u32[]{:S(2)}, u32[]{:S(2)}) collective-permute-start(bf16[512,384]{1,0:T(8,128)(2,1)} %get-tuple-element.20), channel_id=1, source_target_pairs={{0,4},{4,8},{8,12},{1,5},{5,9},{9,13},{2,6},{6,10},{10,14},{3,7},{... | collective-permute-start | bytes 1179656 | tf_op jit(solution)/shard_map/ppermute | solution.py:22
  58.7 13.7 %collective-permute-start.14 = (bf16[512,384]{1,0:T(8,128)(2,1)}, bf16[512,384]{1,0:T(8,128)(2,1)S(1)}, u32[]{:S(2)}, u32[]{:S(2)}) collective-permute-start(bf16[512,384]{1,0:T(8,128)(2,1)} %get-tuple-element.22), channel_id=1, source_target_pairs={{4,0},{8,4},{12,8},{5,1},{9,5},{13,9},{6,2},{10,6},{14,10},{7,3},{... | collective-permute-start | bytes 1179656 | tf_op jit(solution)/shard_map/ppermute | solution.py:22
  64.4 36.0 %collective-permute-start.20 = (f32[1,576,384]{2,1,0:T(8,128)}, f32[1,576,384]{2,1,0:T(8,128)}, u32[]{:S(2)}, u32[]{:S(2)}) collective-permute-start(f32[1,576,384]{2,1,0:T(8,128)} %select_bitcast_fusion.1), channel_id=1, source_target_pairs={{0,1},{1,0},{2,3},{3,2},{4,5},{5,4},{6,7},{7,6},{8,9},{9,8},{10,11... | collective-permute-start | bytes 2654216 | tf_op jit(solution)/shard_map/ppermute | solution.py:32
  75.4 7.3 %collective-permute-start.15 = (bf16[256,384]{1,0:T(8,128)(2,1)S(1)}, bf16[256,384]{1,0:T(8,128)(2,1)S(1)}, u32[]{:S(2)}, u32[]{:S(2)}) collective-permute-start(bf16[256,384]{1,0:T(8,128)(2,1)S(1)} %get-tuple-element.26), channel_id=1, source_target_pairs={{0,4},{4,8},{8,12},{1,5},{5,9},{9,13},{2,6},{6,10},{10,14},{3,7},{... | collective-permute-start | bytes 589832 | tf_op jit(solution)/shard_map/ppermute | solution.py:22
  78.7 8.2 %collective-permute-start.16 = (bf16[256,384]{1,0:T(8,128)(2,1)S(1)}, bf16[256,384]{1,0:T(8,128)(2,1)S(1)}, u32[]{:S(2)}, u32[]{:S(2)}) collective-permute-start(bf16[256,384]{1,0:T(8,128)(2,1)S(1)} %get-tuple-element.28), channel_id=1, source_target_pairs={{4,0},{8,4},{12,8},{5,1},{9,5},{13,9},{6,2},{10,6},{14,10},{7,3},{... | collective-permute-start | bytes 589832 | tf_op jit(solution)/shard_map/ppermute | solution.py:22
  82.6 23.6 %collective-permute-start.25 = (f32[1,576,384]{2,1,0:T(8,128)}, f32[1,576,384]{2,1,0:T(8,128)}, u32[]{:S(2)}, u32[]{:S(2)}) collective-permute-start(f32[1,576,384]{2,1,0:T(8,128)} %select_bitcast_fusion), channel_id=1, source_target_pairs={{0,1},{1,0},{2,3},{3,2},{4,5},{5,4},{6,7},{7,6},{8,9},{9,8},{10,11... | collective-permute-start | bytes 2654216 | tf_op jit(solution)/shard_map/ppermute | solution.py:32
  90.7 8.0 %collective-permute-start.18 = (bf16[256,384]{1,0:T(8,128)(2,1)}, bf16[256,384]{1,0:T(8,128)(2,1)}, u32[]{:S(2)}, u32[]{:S(2)}) collective-permute-start(bf16[256,384]{1,0:T(8,128)(2,1)} %get-tuple-element.43), channel_id=1, source_target_pairs={{0,2},{1,3},{2,0},{3,1},{4,6},{5,7},{6,4},{7,5},{8,10},{9,11},{10,... | collective-permute-start | bytes 589832 | tf_op jit(solution)/shard_map/ppermute | solution.py:32
  92.3 32.0 %collective-permute-start.19 = (bf16[256,384]{1,0:T(8,128)(2,1)}, bf16[256,384]{1,0:T(8,128)(2,1)S(1)}, u32[]{:S(2)}, u32[]{:S(2)}) collective-permute-start(bf16[256,384]{1,0:T(8,128)(2,1)} %get-tuple-element.42), channel_id=1, source_target_pairs={{0,3},{1,2},{2,1},{3,0},{4,7},{5,6},{6,5},{7,4},{8,11},{9,10},{10,... | collective-permute-start | bytes 589832 | tf_op jit(solution)/shard_map/ppermute | solution.py:32
  101.7 7.9 %collective-permute-start.21 = (bf16[1,144,384]{2,1,0:T(8,128)(2,1)S(1)}, bf16[1,144,384]{2,1,0:T(8,128)(2,1)S(1)}, u32[]{:S(2)}, u32[]{:S(2)}) collective-permute-start(bf16[1,144,384]{2,1,0:T(8,128)(2,1)S(1)} %get-tuple-element.36), channel_id=1, source_target_pairs={{0,4},{4,8},{8,12},{12,0},{1,5},{5,9},{9,13},{13,1},{2,6},{6,10},{... | collective-permute-start | bytes 331784 | tf_op jit(solution)/shard_map/ppermute | solution.py:27
  103.5 12.3 %collective-permute-start.22 = (bf16[1,144,384]{2,1,0:T(8,128)(2,1)S(1)}, bf16[1,144,384]{2,1,0:T(8,128)(2,1)S(1)}, u32[]{:S(2)}, u32[]{:S(2)}) collective-permute-start(bf16[1,144,384]{2,1,0:T(8,128)(2,1)S(1)} %get-tuple-element.38), channel_id=1, source_target_pairs={{0,8},{4,12},{8,0},{12,4},{1,9},{5,13},{9,1},{13,5},{2,10},{6,14},... | collective-permute-start | bytes 331784 | tf_op jit(solution)/shard_map/ppermute | solution.py:27
  103.5 14.5 %collective-permute-start.23 = (bf16[1,144,384]{2,1,0:T(8,128)(2,1)S(1)}, bf16[1,144,384]{2,1,0:T(8,128)(2,1)S(1)}, u32[]{:S(2)}, u32[]{:S(2)}) collective-permute-start(bf16[1,144,384]{2,1,0:T(8,128)(2,1)S(1)} %get-tuple-element.37), channel_id=1, source_target_pairs={{0,12},{4,0},{8,4},{12,8},{1,13},{5,1},{9,5},{13,9},{2,14},{6,2},{... | collective-permute-start | bytes 331784 | tf_op jit(solution)/shard_map/ppermute | solution.py:27
  107.5 14.1 %collective-permute-start.26 = (bf16[1,144,384]{2,1,0:T(8,128)(2,1)S(1)}, bf16[1,144,384]{2,1,0:T(8,128)(2,1)S(1)}, u32[]{:S(2)}, u32[]{:S(2)}) collective-permute-start(bf16[1,144,384]{2,1,0:T(8,128)(2,1)S(1)} %get-tuple-element.39), channel_id=1, source_target_pairs={{0,4},{4,8},{8,12},{12,0},{1,5},{5,9},{9,13},{13,1},{2,6},{6,10},{... | collective-permute-start | bytes 331784 | tf_op jit(solution)/shard_map/ppermute | solution.py:27
  109.7 12.6 %collective-permute-start.27 = (bf16[1,144,384]{2,1,0:T(8,128)(2,1)S(1)}, bf16[1,144,384]{2,1,0:T(8,128)(2,1)S(1)}, u32[]{:S(2)}, u32[]{:S(2)}) collective-permute-start(bf16[1,144,384]{2,1,0:T(8,128)(2,1)S(1)} %get-tuple-element.41), channel_id=1, source_target_pairs={{0,8},{4,12},{8,0},{12,4},{1,9},{5,13},{9,1},{13,5},{2,10},{6,14},... | collective-permute-start | bytes 331784 | tf_op jit(solution)/shard_map/ppermute | solution.py:27
  115.8 7.1 %collective-permute-start.28 = (bf16[1,144,384]{2,1,0:T(8,128)(2,1)S(1)}, bf16[1,144,384]{2,1,0:T(8,128)(2,1)S(1)}, u32[]{:S(2)}, u32[]{:S(2)}) collective-permute-start(bf16[1,144,384]{2,1,0:T(8,128)(2,1)S(1)} %get-tuple-element.40), channel_id=1, source_target_pairs={{0,12},{4,0},{8,4},{12,8},{1,13},{5,1},{9,5},{13,9},{2,14},{6,2},{... | collective-permute-start | bytes 331784 | tf_op jit(solution)/shard_map/ppermute | solution.py:27
  118.1 7.0 %collective-permute-start.24 = (bf16[1,144,384]{2,1,0:T(8,128)(2,1)S(1)}, bf16[1,144,384]{2,1,0:T(8,128)(2,1)S(1)}, u32[]{:S(2)}, u32[]{:S(2)}) collective-permute-start(bf16[1,144,384]{2,1,0:T(8,128)(2,1)S(1)} %fusion), channel_id=1, source_target_pairs={{0,2},{1,3},{4,6},{5,7},{8,10},{9,11},{12,14},{13,15},{16,18},{17,... | collective-permute-start | bytes 331784 | tf_op jit(solution)/shard_map/ppermute | solution.py:210
  123.0 6.6 %collective-permute-start.29 = (bf16[1,144,384]{2,1,0:T(8,128)(2,1)S(1)}, bf16[1,144,384]{2,1,0:T(8,128)(2,1)S(1)}, u32[]{:S(2)}, u32[]{:S(2)}) collective-permute-start(bf16[1,144,384]{2,1,0:T(8,128)(2,1)S(1)} %fusion.1), channel_id=1, source_target_pairs={{2,0},{3,1},{6,4},{7,5},{10,8},{11,9},{14,12},{15,13},{18,16},{19,... | collective-permute-start | bytes 331784 | tf_op jit(solution)/shard_map/ppermute | solution.py:210
  129.8 7.9 %collective-permute-start.30 = (bf16[144,384]{1,0:T(8,128)(2,1)S(1)}, bf16[144,384]{1,0:T(8,128)(2,1)S(1)}, u32[]{:S(2)}, u32[]{:S(2)}) collective-permute-start(bf16[144,384]{1,0:T(8,128)(2,1)S(1)} %get-tuple-element.32), channel_id=1, source_target_pairs={{0,4},{4,8},{8,12},{12,0},{1,5},{5,9},{9,13},{13,1},{2,6},{6,10},{... | collective-permute-start | bytes 331784 | tf_op jit(solution)/shard_map/ppermute | solution.py:27
  132.2 8.4 %collective-permute-start.31 = (bf16[144,384]{1,0:T(8,128)(2,1)S(1)}, bf16[144,384]{1,0:T(8,128)(2,1)S(1)}, u32[]{:S(2)}, u32[]{:S(2)}) collective-permute-start(bf16[144,384]{1,0:T(8,128)(2,1)S(1)} %get-tuple-element.32), channel_id=1, source_target_pairs={{0,8},{4,12},{8,0},{12,4},{1,9},{5,13},{9,1},{13,5},{2,10},{6,14},... | collective-permute-start | bytes 331784 | tf_op jit(solution)/shard_map/ppermute | solution.py:27
  133.0 7.7 %collective-permute-start.32 = (bf16[144,384]{1,0:T(8,128)(2,1)S(1)}, bf16[144,384]{1,0:T(8,128)(2,1)S(1)}, u32[]{:S(2)}, u32[]{:S(2)}) collective-permute-start(bf16[144,384]{1,0:T(8,128)(2,1)S(1)} %get-tuple-element.32), channel_id=1, source_target_pairs={{0,12},{4,0},{8,4},{12,8},{1,13},{5,1},{9,5},{13,9},{2,14},{6,2},{... | collective-permute-start | bytes 331784 | tf_op jit(solution)/shard_map/ppermute | solution.py:27
  (11 other events, 62.5 us)

commit v3 on v2

v3 whole, which is shorter than its diff:
```python
import functools
import math

import jax
import jax.numpy as jnp
from jax import lax
from jax.experimental import pallas as pl
from jax.experimental.pallas import tpu as pltpu
from jax.sharding import PartitionSpec as P

DILATION_FIRST = 1024
DILATION_SECOND = 2048
F32 = jnp.float32
BF16 = jnp.bfloat16
SMEM = pl.BlockSpec(memory_space=pltpu.SMEM)
VMEM = pl.BlockSpec(memory_space=pltpu.VMEM)


def shifted(block, axis, distance):
    n = lax.axis_size(axis)
    route = [(i, i + distance) for i in range(n) if 0 <= i + distance < n]
    return lax.ppermute(block, axis, route)


def turned(block, axis, turn):
    n = lax.axis_size(axis)
    return lax.ppermute(block, axis, [(i, (i + turn) % n) for i in range(n)])


def swapped(block, axis, bits):
    n = lax.axis_size(axis)
    return lax.ppermute(block, axis, [(i, i ^ bits) for i in range(n)])


def after(value, others):
    return lax.optimization_barrier((value, others))[0]


def cut(block, index, rows):
    return lax.dynamic_slice_in_dim(block, index * rows, rows, 0)


def gather_pieces(block, axis, others):
    n = lax.axis_size(axis)
    held = {0: block}
    bit = n // 2
    while bit:
        for r in list(held):
            first_far = r == 0 and bit == n // 2
            source = after(held[r], others) if first_far else held[r]
            held[r ^ bit] = swapped(source, axis, bit)
        bit //= 2
    return [held[r] for r in range(n)]


def slope_of(v, th):
    coeff = 0.7978845608
    return 0.5 * (1.0 + th) + 0.5 * v * (1.0 - th * th) * coeff * (1.0 + 3.0 * 0.044715 * v * v)


def gelu_tanh(v):
    coeff = 0.7978845608
    return jnp.tanh(coeff * (v + 0.044715 * v * v * v))


def dot(a, b):
    return jnp.dot(a, b, preferred_element_type=F32)


def back_dot(blocks, w, first):
    channels = w.shape[1]
    total = None
    for k, block in enumerate(blocks):
        tap = w[first + k * channels : first + (k + 1) * channels]
        part = lax.dot_general(block, tap, (((1,), (1,)), ((), ())), preferred_element_type=F32)
        total = part if total is None else total + part
    return total


def regroup_kernel(sizes, place, block, *refs):
    members, q, reach = sizes
    pieces, (own, to_high, to_low) = refs[: members - 1], refs[members - 1 :]
    j = place[1]

    def rows(index):
        return pl.ds(pl.multiple_of(index * q, 16), q)

    own[rows(j), :] = block[rows(j), :]
    for r in range(1, members):
        own[rows(j ^ r), :] = pieces[r - 1][...]
    to_high[...] = own[(members - reach) * q :]
    to_low[...] = own[: reach * q]


def forward_kernel(sizes, place, low, own, high, *refs):
    groups, members, q, near, far = sizes
    w_pieces, (act_stack, hid_stack, slope_one, slope_two, w_out, hid) = (
        refs[:members],
        refs[members:],
    )
    s, j = place[0], place[1]
    reach = near + far
    rows = w_pieces[0].shape[0]
    for r in range(members):
        w_out[pl.ds(pl.multiple_of((j ^ r) * rows, 16), rows), :] = w_pieces[r][...]
    taps = w_out.shape[0] // 2

    def block(b):
        if b < 0:
            return low[(b + reach) * q : (b + reach + 1) * q]
        if b >= members:
            return high[(b - members) * q : (b - members + 1) * q]
        return own[b * q : (b + 1) * q]

    for b in range(-far, members + far):
        stack = jnp.concatenate([block(b - near), block(b), block(b + near)], 1)
        pre = dot(stack, w_out[:taps])
        th = gelu_tanh(pre)
        value = (block(b).astype(F32) + 0.5 * pre * (1.0 + th)).astype(BF16)
        if b < 0:
            value = jnp.where(s > 0, value, jnp.zeros_like(value))
        if b >= members:
            value = jnp.where(s < groups - 1, value, jnp.zeros_like(value))
        hid[b + far] = value
        if 0 <= b < members:
            slope_one[b * q : (b + 1) * q] = slope_of(pre, th)
            act_stack[b * q : (b + 1) * q] = stack
    for b in range(members):
        stack = jnp.concatenate([hid[b], hid[b + far], hid[b + 2 * far]], 1)
        here = slice(b * q, (b + 1) * q)
        hid_stack[here] = stack
        pre = dot(stack, w_out[taps:])
        slope_two[here] = slope_of(pre, gelu_tanh(pre))


def delta_kernel(sizes, place, slope, cotangent, *refs):
    members, q, far = sizes
    pieces, (delta, to_high, to_low, cot) = refs[: members - 1], refs[members - 1 :]
    j = place[1]

    def rows(index):
        return pl.ds(pl.multiple_of(index * q, 16), q)

    cot[rows(j), :] = cotangent[rows(j), :]
    for r in range(1, members):
        cot[rows(j ^ r), :] = pieces[r - 1][...]
    for b in range(members):
        here = slice(b * q, (b + 1) * q)
        delta[here] = (cot[here].astype(F32) * slope[here]).astype(BF16)
    to_high[...] = delta[(members - far) * q :]
    to_low[...] = delta[: far * q]


def grad_kernel(sizes, scale, place, stack, delta, *refs):
    members, halo = sizes
    keep, send = refs[-2:] if not halo else refs[-4:-2]
    odd = place[1] & 1
    channels = delta.shape[1]
    rows = 3 * channels // (members // 2)
    for k in range(3):
        first = k * channels
        part = scale * lax.dot_general(
            stack[:, first : first + channels],
            delta[...],
            (((0,), (0,)), ((), ())),
            preferred_element_type=F32,
        )
        for owner in range(members // 2):
            start, stop = max(first, owner * rows), min(first + channels, (owner + 1) * rows)
            if start >= stop:
                continue
            at = (owner // 2) * rows + start - owner * rows
            value = part[start - first : stop - first]

            @pl.when(odd == owner % 2)
            def _():
                keep[at : at + stop - start] = value

            @pl.when(odd != owner % 2)
            def _():
                send[at : at + stop - start] = value

    if halo:
        to_high, to_low = refs[-2:]
        to_high[...] = delta[delta.shape[0] - halo :]
        to_low[...] = delta[:halo]


def share_kernel(n, place, keep, other, *refs):
    outs = refs[-n:]
    rows = outs[0].shape[0]
    for turn in range(n):
        at = pl.ds(pl.multiple_of(lax.rem(place[0] + turn, n) * rows, 16), rows)
        outs[turn][...] = (keep[at, :] + other[at, :]).astype(outs[turn].dtype)


def back_kernel(sizes, low, own, high, cot, slope, w, back_one, delta):
    members, q, near, far = sizes

    def block(b):
        if b < 0:
            return low[(b + far) * q : (b + far + 1) * q]
        if b >= members:
            return high[(b - members) * q : (b - members + 1) * q]
        return own[b * q : (b + 1) * q]

    for b in range(members):
        here = slice(b * q, (b + 1) * q)
        product = back_dot((block(b + far), block(b), block(b - far)), w, w.shape[0] // 2)
        back = cot[here].astype(F32) + product
        back_one[here] = back
        delta[here] = (back * slope[here]).astype(BF16)


def input_kernel(sizes, place, low, own, high, back_one, w, out):
    members, q, near = sizes
    j = place[1]

    def block(b):
        if b < 0:
            return low[(b + near) * q : (b + near + 1) * q]
        if b >= members:
            return high[(b - members) * q : (b - members + 1) * q]
        return own[b * q : (b + 1) * q]

    for b in range(members):
        here = slice(b * q, (b + 1) * q)
        product = back_dot((block(b + near), block(b), block(b - near)), w, 0)
        value = (back_one[here] + product).astype(BF16)
        out[pl.ds(pl.multiple_of((j ^ b) * q, 16), q), :] = value


def call(kernel, out_shapes, scratch=(), scalars=0, operands=()):
    specs = [SMEM] * scalars + [VMEM] * (len(operands) - scalars)
    return pl.pallas_call(
        kernel,
        out_shape=tuple(jax.ShapeDtypeStruct(shape, kind) for shape, kind in out_shapes),
        in_specs=specs,
        out_specs=tuple(VMEM for _ in out_shapes),
        scratch_shapes=list(scratch),
        cost_estimate=pl.CostEstimate(flops=1, transcendentals=0, bytes_accessed=1),
        compiler_params=pltpu.CompilerParams(vmem_limit_bytes=16 * 1024 * 1024),
    )(*operands)


def seq_shares(place, keep, other, waits):
    n = lax.axis_size("seq")
    if n > 4:
        return [keep + other]
    shape = (keep.shape[0] // n, keep.shape[1])
    return call(
        functools.partial(share_kernel, n),
        ((shape, F32),) + ((shape, BF16),) * (n - 1),
        scalars=1,
        operands=(place, keep, other, *waits),
    )


def seq_sum(shares):
    if len(shares) == 1:
        return lax.psum(shares[0], "seq")
    total = shares[0]
    for turn in range(1, len(shares)):
        total = total + turned(shares[turn], "seq", turn).astype(F32)
    return total


def chip_sum(total_one, total_two, j):
    n = lax.axis_size("sub")
    owned = n // 4
    one = total_one.reshape(owned, -1, total_one.shape[1])
    two = total_two.reshape(owned, -1, total_two.shape[1])
    high = j >= n // 2
    part, send = jnp.where(high, two, one), jnp.where(high, one, two)
    part = part + swapped(send.astype(BF16), "sub", n // 2).astype(F32)
    bit = 2
    while bit < n // 2:
        mine = (j & bit) != 0
        keep, send = jnp.where(mine, part[1::2], part[0::2]), jnp.where(mine, part[0::2], part[1::2])
        part = keep + swapped(send.astype(BF16), "sub", bit).astype(F32)
        bit *= 2
    return part[0]


def spread_seq(total, sent, s):
    n = lax.axis_size("seq")
    if n > 4:
        return total
    rows, channels = total.shape
    whole = jnp.zeros((n * rows, channels), F32)
    whole = lax.dynamic_update_slice_in_dim(whole, total, s * rows, 0)
    for turn in range(1, n):
        got = turned(sent, "seq", turn).astype(F32)
        whole = lax.dynamic_update_slice_in_dim(whole, got, lax.rem(s + n - turn, n) * rows, 0)
    return whole


def per_device(activations, cotangent, weights):
    count, channels = activations.shape
    groups, members = lax.axis_size("seq"), lax.axis_size("sub")
    s, j = lax.axis_index("seq"), lax.axis_index("sub")
    place = jnp.stack([s, j]).astype(jnp.int32)
    near, far = DILATION_FIRST // count, DILATION_SECOND // count
    q = count // members
    taps = 3 * channels
    grad_scale = 1.0 / math.sqrt(count * groups * members)

    def kernel(body, *shapes, scratch=(), operands=()):
        return call(body, shapes, scratch, 1, (place,) + tuple(operands))

    def regrouped(block, others=None):
        pieces = [cut(block, j ^ r, q) for r in range(1, members)]
        if others is not None:
            pieces[1:] = after(pieces[1:], others)
        return [swapped(piece, "sub", r + 1) for r, piece in enumerate(pieces)]

    reach = near + far
    act, up_act, down_act = kernel(
        functools.partial(regroup_kernel, (members, q, reach)),
        ((count, channels), BF16),
        ((reach * q, channels), BF16),
        ((reach * q, channels), BF16),
        operands=(activations, *regrouped(activations)),
    )
    low, high = shifted(up_act, "seq", 1), shifted(down_act, "seq", -1)
    w_pieces = gather_pieces(weights, "sub", act)
    c_pieces = regrouped(cotangent, w_pieces[members // 2])

    act_stack, hid_stack, slope_one, slope_two, all_weights = kernel(
        functools.partial(forward_kernel, (groups, members, q, near, far)),
        ((count, taps), BF16),
        ((count, taps), BF16),
        ((count, channels), F32),
        ((count, channels), F32),
        ((2 * taps, channels), BF16),
        scratch=(pltpu.VMEM((members + 2 * far, q, channels), BF16),),
        operands=(low, act, high, *w_pieces),
    )
    delta_two, up_two, down_two, cot = kernel(
        functools.partial(delta_kernel, (members, q, far)),
        ((count, channels), BF16),
        ((far * q, channels), BF16),
        ((far * q, channels), BF16),
        ((count, channels), BF16),
        operands=(slope_two, cotangent, *c_pieces),
    )
    two_low, two_high = shifted(up_two, "seq", 1), shifted(down_two, "seq", -1)
    half = ((taps // 2, channels), F32)
    keep_two, send_two = kernel(
        functools.partial(grad_kernel, (members, 0), grad_scale),
        half,
        half,
        operands=(hid_stack, delta_two),
    )
    shares_two = seq_shares(place, keep_two, swapped(send_two, "sub", 1), ())
    back_one, delta_one = call(
        functools.partial(back_kernel, (members, q, near, far)),
        (((count, channels), F32), ((count, channels), BF16)),
        operands=(two_low, delta_two, two_high, cot, slope_one, all_weights),
    )
    keep_one, send_one, up_one, down_one = kernel(
        functools.partial(grad_kernel, (members, near * q), grad_scale),
        half,
        half,
        ((near * q, channels), BF16),
        ((near * q, channels), BF16),
        operands=(act_stack, delta_one, shares_two[0]),
    )
    one_low, one_high = shifted(up_one, "seq", 1), shifted(down_one, "seq", -1)
    total_two = seq_sum(shares_two)
    shares_one = seq_shares(place, keep_one, swapped(send_one, "sub", 1), (total_two,))
    one_low, one_high = after((one_low, one_high), shares_one)
    part = chip_sum(seq_sum(shares_one), total_two, j)
    sent = part.astype(BF16)

    (grad_in,) = call(
        functools.partial(input_kernel, (members, q, near)),
        (((count, channels), BF16),),
        scalars=1,
        operands=(place, one_low, delta_one, one_high, back_one, all_weights),
    )
    got = [grad_in[r * q : (r + 1) * q] for r in range(members)]
    got = got[:1] + [swapped(got[r], "sub", r) for r in range(1, members)]
    got = after(got, sent)
    input_grad = jnp.zeros((count, channels), BF16)
    for r in range(members):
        input_grad = lax.dynamic_update_slice_in_dim(input_grad, got[r], (j ^ r) * q, 0)

    weight_grad = spread_seq(part, sent, s)
    return (input_grad, weight_grad)


def solution(mesh):
    placed = (P(("grp", "seq", "sub"), None), P(("grp", "seq", "sub"), None), P("sub", None))
    return jax.shard_map(
        per_device,
        mesh=mesh,
        in_specs=placed,
        out_specs=(P(("grp", "seq", "sub"), None), P(("grp", "sub"), None)),
        check_vma=False,
    )
```

time: 142 us -> 117 us (0.82)
  starting transfers between devices: 47.8 us -> 37.8 us
  local copies, waits for them, and re-layouts: 13.7 us -> 4.07 us
  Pallas kernels: 15.2 us -> 20.7 us
  matrix products: 4.7 us -> 0 us
  other arithmetic: 5.13 us -> 1.36 us
  waiting for transfers between devices: 54.1 us -> 51.4 us
    ppermute x8 -> x6, starting transfers between devices: 19.6 us -> 12.9 us  [shifted(): return lax.ppermute(block, axis, route)]
    pallas_call x3 -> x9, Pallas kernels: 15.2 us -> 20.7 us  [call(): pl.pallas_call(kernel, out_shape=tuple((jax.ShapeDtypeStruct(shape, kind)...]
    ppermute x2 -> x0, starting transfers between devices: 4.81 us -> none  [chip_stage(): part = part + lax.ppermute(part.astype(BF16), 'sub', route).astype(F32)]
    dot_general x2 -> x0, matrix products: 4.7 us -> none  [tap_grads(): lax.dot_general(stacked, delta, (((0,), (0,)), ((), ())), preferred_eleme...]
    ppermute x2 -> x0, waiting for transfers between devices: 4.63 us -> none  [chip_stage(): part = part + lax.ppermute(part.astype(BF16), 'sub', route).astype(F32)]
    dynamic_update_slice x4, local copies, waits for them, and re-layouts: 3.97 us -> 0.15 us  [per_device(): lax.dynamic_update_slice_in_dim(input_grad, got[r], (j ^ r) * q, 0)]
    reshape x1 -> x0, local copies, waits for them, and re-layouts: 2.77 us -> none  [per_device(): back = all_weights.reshape(2, 3, channels, channels).transpose(0, 1, 3, 2)]
    add x2 -> x1, other arithmetic: 2.58 us -> 0.06 us  [seq_sum(): total = total + turned(shares[turn], 'seq', turn).astype(F32)]
  transfers between devices with their start and end apart: 33 -> 30, of which waited for: 17 -> 14; matrix products, arithmetic and copies ran while one was open for 14% -> 1% of each run, Pallas kernels for 4% -> 11%
where the time goes in v3:
time: 117 us; the launch traced here: 116 us
  waiting for transfers between devices  51.4 us (44%)
  starting transfers between devices  37.8 us (32%)
  Pallas kernels  20.7 us (18%)
  local copies, waits for them, and re-layouts  4.07 us (3%)
  other arithmetic  1.36 us (1%)
    pallas_call x9, Pallas kernels, call(): pl.pallas_call(kernel, out_shape=tuple((jax.ShapeDtypeStruct(shape, kind)...  20.7 us
    ppermute x6, waiting for transfers between devices, shifted(): return lax.ppermute(block, axis, route)  19.8 us
    ppermute x15, waiting for transfers between devices, swapped(): return lax.ppermute(block, axis, [(i, i ^ bits) for i in range(n)])  19.5 us
    ppermute x9, starting transfers between devices, turned(): return lax.ppermute(block, axis, [(i, (i + turn) % n) for i in range(n)])  14.9 us
    ppermute x6, starting transfers between devices, shifted(): return lax.ppermute(block, axis, route)  12.9 us
    ppermute x9, waiting for transfers between devices, turned(): return lax.ppermute(block, axis, [(i, (i + turn) % n) for i in range(n)])  12.1 us
    ppermute x15, starting transfers between devices, swapped(): return lax.ppermute(block, axis, [(i, i ^ bits) for i in range(n)])  10 us
  transfers between devices with their start and end apart: 30, of which 14 were waited for; matrix products, arithmetic and copies ran while one was open for 1% of the time, Pallas kernels for 11%

profile of v3, /device:TPU:0, one launch (start us, length us, event | category | flops | bytes accessed | tf_op | source)
XLA Modules:
  0.0 116.2 jit_solution(1431278704921752234)
XLA Ops:
  2.5 2.6 %collective-permute-start.1 = (bf16[256,384]{1,0:T(8,128)(2,1)S(1)}, bf16[256,384]{1,0:T(8,128)(2,1)S(1)}, u32[]{:S(2)}, u32[]{:S(2)}) collective-permute-start(bf16[256,384]{1,0:T(8,128)(2,1)S(1)} %get-tuple-element.86), channel_id=1, source_target_pairs={{0,2},{1,3},{2,0},{3,1},{4,6},{5,7},{6,4},{7,5},{8,10},{9,11},{10,... | collective-permute-start | bytes 589832 | tf_op jit(solution)/shard_map/ppermute | solution.py:32
  5.2 5.6 %collective-permute-done.1.refs_1_ = bf16[256,384]{1,0:T(8,128)(2,1)S(1)} collective-permute-done((bf16[256,384]{1,0:T(8,128)(2,1)S(1)}, bf16[256,384]{1,0:T(8,128)(2,1)S(1)}, u32[]{:S(2)}, u32[]{:S(2)}) %collective-permute-start.1) | collective-permute-done | bytes 196640 | tf_op jit(solution)/shard_map/ppermute | solution.py:32
  10.8 3.7 %collective-permute-done.2.refs_2_ = bf16[256,384]{1,0:T(8,128)(2,1)S(1)} collective-permute-done((bf16[256,384]{1,0:T(8,128)(2,1)S(1)}, bf16[256,384]{1,0:T(8,128)(2,1)S(1)}, u32[]{:S(2)}, u32[]{:S(2)}) %collective-permute-start.2) | collective-permute-done | bytes 196640 | tf_op jit(solution)/shard_map/ppermute | solution.py:32
  15.3 1.6 %collective-permute-start.6 = (bf16[576,384]{1,0:T(8,128)(2,1)S(1)}, bf16[576,384]{1,0:T(8,128)(2,1)S(1)}, u32[]{:S(2)}, u32[]{:S(2)}) collective-permute-start(bf16[576,384]{1,0:T(8,128)(2,1)S(1)} %copy-done.4), channel_id=1, source_target_pairs={{0,2},{1,3},{2,0},{3,1},{4,6},{5,7},{6,4},{7,5},{8,10},{9,11},{10,... | collective-permute-start | bytes 1327112 | tf_op jit(solution)/shard_map/ppermute | solution.py:32
  16.9 3.5 %collective-permute-start.3 = (bf16[768,384]{1,0:T(8,128)(2,1)S(1)}, bf16[768,384]{1,0:T(8,128)(2,1)S(1)}, u32[]{:S(2)}, u32[]{:S(2)}) collective-permute-start(bf16[768,384]{1,0:T(8,128)(2,1)S(1)} %get-tuple-element.39), channel_id=1, source_target_pairs={{0,4},{4,8},{8,12},{1,5},{5,9},{9,13},{2,6},{6,10},{10,14},{3,7},{... | collective-permute-start | bytes 1769480 | tf_op jit(solution)/shard_map/ppermute | solution.py:22
  21.8 5.7 %collective-permute-done.6.refs_2_ = bf16[576,384]{1,0:T(8,128)(2,1)S(1)} collective-permute-done((bf16[576,384]{1,0:T(8,128)(2,1)S(1)}, bf16[576,384]{1,0:T(8,128)(2,1)S(1)}, u32[]{:S(2)}, u32[]{:S(2)}) %collective-permute-start.6) | collective-permute-done | bytes 442400 | tf_op jit(solution)/shard_map/ppermute | solution.py:32
  28.2 1.4 %collective-permute-start.10 = (bf16[256,384]{1,0:T(8,128)(2,1)S(1)}, bf16[256,384]{1,0:T(8,128)(2,1)S(1)}, u32[]{:S(2)}, u32[]{:S(2)}) collective-permute-start(bf16[256,384]{1,0:T(8,128)(2,1)S(1)} %get-tuple-element.46), channel_id=1, source_target_pairs={{0,3},{1,2},{2,1},{3,0},{4,7},{5,6},{6,5},{7,4},{8,11},{9,10},{10,... | collective-permute-start | bytes 589832 | tf_op jit(solution)/shard_map/ppermute | solution.py:32
  29.6 3.5 %collective-permute-done.3.low = bf16[768,384]{1,0:T(8,128)(2,1)S(1)} collective-permute-done((bf16[768,384]{1,0:T(8,128)(2,1)S(1)}, bf16[768,384]{1,0:T(8,128)(2,1)S(1)}, u32[]{:S(2)}, u32[]{:S(2)}) %collective-permute-start.3) | collective-permute-done | bytes 589856 | tf_op jit(solution)/shard_map/ppermute | solution.py:22
  33.6 4.5 %collective-permute-done.4.high = bf16[768,384]{1,0:T(8,128)(2,1)S(1)} collective-permute-done((bf16[768,384]{1,0:T(8,128)(2,1)S(1)}, bf16[768,384]{1,0:T(8,128)(2,1)S(1)}, u32[]{:S(2)}, u32[]{:S(2)}) %collective-permute-start.4) | collective-permute-done | bytes 589856 | tf_op jit(solution)/shard_map/ppermute | solution.py:22
  38.1 7.0 %shard_map.51 = (bf16[1024,1152]{1,0:T(8,128)(2,1)S(1)}, bf16[1024,1152]{1,0:T(8,128)(2,1)S(1)}, f32[1024,384]{1,0:T(8,128)S(1)}, f32[1024,384]{1,0:T(8,128)S(1)}, bf16[2304,384]{1,0:T(8,128)(2,1)S(1)}) custom-call(s32[2]{0:T(128)S(1)} %pad_add_fusion.place, bf16[768,384]{1,0:T(8,128)(2,1)S(1)} %collective-permute-done.3.low, ...), custom_call_target="tpu_custom_call" | custom-call | flops 1 | bytes 1 | tf_op jit(solution)/shard_map/pallas_call | solution.py:235
  46.1 2.5 %shard_map.54 = (f32[576,384]{1,0:T(8,128)S(1)}, f32[576,384]{1,0:T(8,128)S(1)}) custom-call(s32[2]{0:T(128)S(1)} %pad_add_fusion.place, bf16[1024,1152]{1,0:T(8,128)(2,1)S(1)} %get-tuple-element.54.stack, bf16[1024,384]{1,0:T(8,128)(2,1)S(1)} %get-tuple-element.48.own.delta), custom_call_target="tpu_custom_call" | custom-call | flops 1 | bytes 1 | tf_op jit(solution)/shard_map/pallas_call | solution.py:235
  48.7 3.5 %collective-permute-start.11 = (bf16[512,384]{1,0:T(8,128)(2,1)S(1)}, bf16[512,384]{1,0:T(8,128)(2,1)S(1)}, u32[]{:S(2)}, u32[]{:S(2)}) collective-permute-start(bf16[512,384]{1,0:T(8,128)(2,1)S(1)} %get-tuple-element.47), channel_id=1, source_target_pairs={{0,4},{4,8},{8,12},{1,5},{5,9},{9,13},{2,6},{6,10},{10,14},{3,7},{... | collective-permute-start | bytes 1179656 | tf_op jit(solution)/shard_map/ppermute | solution.py:22
  53.4 7.7 %collective-permute-done.11.low = bf16[512,384]{1,0:T(8,128)(2,1)S(1)} collective-permute-done((bf16[512,384]{1,0:T(8,128)(2,1)S(1)}, bf16[512,384]{1,0:T(8,128)(2,1)S(1)}, u32[]{:S(2)}, u32[]{:S(2)}) %collective-permute-start.11) | collective-permute-done | bytes 393248 | tf_op jit(solution)/shard_map/ppermute | solution.py:22
  61.1 4.1 %collective-permute-done.12.high = bf16[512,384]{1,0:T(8,128)(2,1)S(1)} collective-permute-done((bf16[512,384]{1,0:T(8,128)(2,1)S(1)}, bf16[512,384]{1,0:T(8,128)(2,1)S(1)}, u32[]{:S(2)}, u32[]{:S(2)}) %collective-permute-start.12) | collective-permute-done | bytes 393248 | tf_op jit(solution)/shard_map/ppermute | solution.py:22
  65.3 1.7 %shard_map.53 = (f32[1024,384]{1,0:T(8,128)S(1)}, bf16[1024,384]{1,0:T(8,128)(2,1)S(1)}) custom-call(bf16[512,384]{1,0:T(8,128)(2,1)S(1)} %collective-permute-done.11.low, bf16[1024,384]{1,0:T(8,128)(2,1)S(1)} %get-tuple-element.48.own.delta, bf16[512,384]{1,0:T(8,128)(2,1)S(1)} %collective-permute-done.12.high, ...), custom_call_target="tpu_custom_call" | custom-call | flops 1 | bytes 1 | tf_op jit(solution)/shard_map/pallas_call | solution.py:235
  67.7 3.4 %shard_map.56 = (f32[576,384]{1,0:T(8,128)S(1)}, f32[576,384]{1,0:T(8,128)S(1)}, bf16[256,384]{1,0:T(8,128)(2,1)}, bf16[256,384]{1,0:T(8,128)(2,1)}) custom-call(s32[2]{0:T(128)S(1)} %pad_add_fusion.place, bf16[1024,1152]{1,0:T(8,128)(2,1)S(1)} %get-tuple-element.43.stack, bf16[1024,384]{1,0:T(8,128)(2,1)S(1)} %get-tuple-element.53.delta.own, ...), custom_call_target="tpu_custom_call" | custom-call | flops 1 | bytes 1 | tf_op jit(solution)/shard_map/pallas_call | solution.py:235
  71.1 1.6 %collective-permute-start.17 = (bf16[144,384]{1,0:T(8,128)(2,1)S(1)}, bf16[144,384]{1,0:T(8,128)(2,1)S(1)}, u32[]{:S(2)}, u32[]{:S(2)}) collective-permute-start(bf16[144,384]{1,0:T(8,128)(2,1)S(1)} %get-tuple-element.62), channel_id=1, source_target_pairs={{0,4},{4,8},{8,12},{12,0},{1,5},{5,9},{9,13},{13,1},{2,6},{6,10},{... | collective-permute-start | bytes 331784 | tf_op jit(solution)/shard_map/ppermute | solution.py:27
  72.7 2.7 %collective-permute-start.19 = (bf16[144,384]{1,0:T(8,128)(2,1)S(1)}, bf16[144,384]{1,0:T(8,128)(2,1)S(1)}, u32[]{:S(2)}, u32[]{:S(2)}) collective-permute-start(bf16[144,384]{1,0:T(8,128)(2,1)S(1)} %get-tuple-element.64), channel_id=1, source_target_pairs={{0,12},{4,0},{8,4},{12,8},{1,13},{5,1},{9,5},{13,9},{2,14},{6,2},{... | collective-permute-start | bytes 331784 | tf_op jit(solution)/shard_map/ppermute | solution.py:27
  75.4 2.1 %collective-permute-start.14 = (bf16[256,384]{1,0:T(8,128)(2,1)}, bf16[256,384]{1,0:T(8,128)(2,1)S(1)}, u32[]{:S(2)}, u32[]{:S(2)}) collective-permute-start(bf16[256,384]{1,0:T(8,128)(2,1)} %get-tuple-element.58), channel_id=1, source_target_pairs={{0,4},{4,8},{8,12},{1,5},{5,9},{9,13},{2,6},{6,10},{10,14},{3,7},{... | collective-permute-start | bytes 589832 | tf_op jit(solution)/shard_map/ppermute | solution.py:22
  77.4 1.5 %collective-permute-done.17 = bf16[144,384]{1,0:T(8,128)(2,1)S(1)} collective-permute-done((bf16[144,384]{1,0:T(8,128)(2,1)S(1)}, bf16[144,384]{1,0:T(8,128)(2,1)S(1)}, u32[]{:S(2)}, u32[]{:S(2)}) %collective-permute-start.17) | collective-permute-done | bytes 110624 | tf_op jit(solution)/shard_map/ppermute | solution.py:27
  80.2 3.0 %collective-permute-done.18 = bf16[144,384]{1,0:T(8,128)(2,1)S(1)} collective-permute-done((bf16[144,384]{1,0:T(8,128)(2,1)S(1)}, bf16[144,384]{1,0:T(8,128)(2,1)S(1)}, u32[]{:S(2)}, u32[]{:S(2)}) %collective-permute-start.18) | collective-permute-done | bytes 110624 | tf_op jit(solution)/shard_map/ppermute | solution.py:27
  83.3 1.4 %shard_map.57 = (f32[144,384]{1,0:T(8,128)S(1)}, bf16[144,384]{1,0:T(8,128)(2,1)}, bf16[144,384]{1,0:T(8,128)(2,1)}, bf16[144,384]{1,0:T(8,128)(2,1)S(1)}) custom-call(s32[2]{0:T(128)S(1)} %pad_add_fusion.place, f32[576,384]{1,0:T(8,128)S(1)} %get-tuple-element.60.keep, f32[576,384]{1,0:T(8,128)S(1)} %collective-permute-done.16.other, ...), custom_call_target="tpu_custom_call" | custom-call | flops 1 | bytes 1 | tf_op jit(solution)/shard_map/pallas_call | solution.py:235
  84.7 2.9 %collective-permute-start.23 = (bf16[144,384]{1,0:T(8,128)(2,1)}, bf16[144,384]{1,0:T(8,128)(2,1)}, u32[]{:S(2)}, u32[]{:S(2)}) collective-permute-start(bf16[144,384]{1,0:T(8,128)(2,1)} %get-tuple-element.66), channel_id=1, source_target_pairs={{0,4},{4,8},{8,12},{12,0},{1,5},{5,9},{9,13},{13,1},{2,6},{6,10},{... | collective-permute-start | bytes 331784 | tf_op jit(solution)/shard_map/ppermute | solution.py:27
  88.6 1.4 %collective-permute-start.25 = (bf16[144,384]{1,0:T(8,128)(2,1)S(1)}, bf16[144,384]{1,0:T(8,128)(2,1)}, u32[]{:S(2)}, u32[]{:S(2)}) collective-permute-start(bf16[144,384]{1,0:T(8,128)(2,1)S(1)} %get-tuple-element.68), channel_id=1, source_target_pairs={{0,12},{4,0},{8,4},{12,8},{1,13},{5,1},{9,5},{13,9},{2,14},{6,2},{... | collective-permute-start | bytes 331784 | tf_op jit(solution)/shard_map/ppermute | solution.py:27
  90.0 1.4 %copy-done.3 = f32[1024,384]{1,0:T(8,128)S(1)} copy-done((f32[1024,384]{1,0:T(8,128)S(1)}, f32[1024,384]{1,0:T(8,128)}, u32[]{:S(2)}) %copy-start.3) | copy-done | bytes 1572888
  91.4 2.3 %shard_map.58 = bf16[1024,384]{1,0:T(8,128)(2,1)S(1)} custom-call(s32[2]{0:T(128)S(1)} %pad_add_fusion.place, bf16[256,384]{1,0:T(8,128)(2,1)S(1)} %collective-permute-done.14.low, bf16[1024,384]{1,0:T(8,128)(2,1)S(1)} %get-tuple-element.53.delta.own, bf16[256,384]{1,0:T(8,128)(2,1)S(1)} %collective-permute-done.15.high, f32[1024,384]{1,0:T(8,128)S(1)} %copy-done.3, ...), custom_call_target="tpu_custom_call" | custom-call | flops 1 | bytes 1 | tf_op jit(solution)/shard_map/pallas_call | solution.py:235
  93.7 3.3 %collective-permute-done.24 = bf16[144,384]{1,0:T(8,128)(2,1)} collective-permute-done((bf16[144,384]{1,0:T(8,128)(2,1)}, bf16[144,384]{1,0:T(8,128)(2,1)}, u32[]{:S(2)}, u32[]{:S(2)}) %collective-permute-start.24) | collective-permute-done | bytes 110624 | tf_op jit(solution)/shard_map/ppermute | solution.py:27
  98.9 1.5 %collective-permute-start.21 = (bf16[256,384]{1,0:T(8,128)(2,1)S(1)}, bf16[256,384]{1,0:T(8,128)(2,1)S(1)}, u32[]{:S(2)}, u32[]{:S(2)}) collective-permute-start(bf16[256,384]{1,0:T(8,128)(2,1)S(1)} %get-tuple-element.79), channel_id=1, source_target_pairs={{0,2},{1,3},{2,0},{3,1},{4,6},{5,7},{6,4},{7,5},{8,10},{9,11},{10,... | collective-permute-start | bytes 589832 | tf_op jit(solution)/shard_map/ppermute | solution.py:32
  100.7 3.4 %collective-permute-done.26 = bf16[1,144,384]{2,1,0:T(8,128)(2,1)S(1)} collective-permute-done((bf16[1,144,384]{2,1,0:T(8,128)(2,1)S(1)}, bf16[1,144,384]{2,1,0:T(8,128)(2,1)S(1)}, u32[]{:S(2)}, u32[]{:S(2)}) %collective-permute-start.26) | collective-permute-done | bytes 110624 | tf_op jit(solution)/shard_map/ppermute | solution.py:32
  104.1 2.9 %collective-permute-start.27 = (bf16[144,384]{1,0:T(8,128)(2,1)S(1)}, bf16[144,384]{1,0:T(8,128)(2,1)S(1)}, u32[]{:S(2)}, u32[]{:S(2)}) collective-permute-start(bf16[144,384]{1,0:T(8,128)(2,1)S(1)} %bitcast_convert_fusion), channel_id=1, source_target_pairs={{0,4},{4,8},{8,12},{12,0},{1,5},{5,9},{9,13},{13,1},{2,6},{6,10},{... | collective-permute-start | bytes 331784 | tf_op jit(solution)/shard_map/ppermute | solution.py:27
  108.1 1.4 %collective-permute-start.29 = (bf16[144,384]{1,0:T(8,128)(2,1)S(1)}, bf16[144,384]{1,0:T(8,128)(2,1)S(1)}, u32[]{:S(2)}, u32[]{:S(2)}) collective-permute-start(bf16[144,384]{1,0:T(8,128)(2,1)S(1)} %bitcast_convert_fusion), channel_id=1, source_target_pairs={{0,12},{4,0},{8,4},{12,8},{1,13},{5,1},{9,5},{13,9},{2,14},{6,2},{... | collective-permute-start | bytes 331784 | tf_op jit(solution)/shard_map/ppermute | solution.py:27
  111.8 3.5 %collective-permute-done.28 = bf16[144,384]{1,0:T(8,128)(2,1)S(1)} collective-permute-done((bf16[144,384]{1,0:T(8,128)(2,1)S(1)}, bf16[144,384]{1,0:T(8,128)(2,1)S(1)}, u32[]{:S(2)}, u32[]{:S(2)}) %collective-permute-start.28) | collective-permute-done | bytes 110624 | tf_op jit(solution)/shard_map/ppermute | solution.py:27
  (68 shorter events, 16.9 us)
Async XLA Ops:
  0.6 14.6 %copy-start.4 = (bf16[576,384]{1,0:T(8,128)(2,1)S(1)}, bf16[576,384]{1,0:T(8,128)(2,1)}, u32[]{:S(2)}) copy-start(bf16[576,384]{1,0:T(8,128)(2,1)} %refs_0_.1) | copy-start | bytes 1327108
  0.6 26.9 %copy-start.1 = (bf16[1024,384]{1,0:T(8,128)(2,1)S(1)}, bf16[1024,384]{1,0:T(8,128)(2,1)}, u32[]{:S(2)}) copy-start(bf16[1024,384]{1,0:T(8,128)(2,1)} %cotangent.1) | copy-start | bytes 2359300
  2.0 3.2 %collective-permute-start = (bf16[256,384]{1,0:T(8,128)(2,1)S(1)}, bf16[256,384]{1,0:T(8,128)(2,1)S(1)}, u32[]{:S(2)}, u32[]{:S(2)}) collective-permute-start(bf16[256,384]{1,0:T(8,128)(2,1)S(1)} %get-tuple-element.87), channel_id=1, source_target_pairs={{0,1},{1,0},{2,3},{3,2},{4,5},{5,4},{6,7},{7,6},{8,9},{9,8},{10,11... | collective-permute-start | bytes 589832 | tf_op jit(solution)/shard_map/ppermute | solution.py:32
  2.5 8.3 %collective-permute-start.1 = (bf16[256,384]{1,0:T(8,128)(2,1)S(1)}, bf16[256,384]{1,0:T(8,128)(2,1)S(1)}, u32[]{:S(2)}, u32[]{:S(2)}) collective-permute-start(bf16[256,384]{1,0:T(8,128)(2,1)S(1)} %get-tuple-element.86), channel_id=1, source_target_pairs={{0,2},{1,3},{2,0},{3,1},{4,6},{5,7},{6,4},{7,5},{8,10},{9,11},{10,... | collective-permute-start | bytes 589832 | tf_op jit(solution)/shard_map/ppermute | solution.py:32
  5.1 9.4 %collective-permute-start.2 = (bf16[256,384]{1,0:T(8,128)(2,1)S(1)}, bf16[256,384]{1,0:T(8,128)(2,1)S(1)}, u32[]{:S(2)}, u32[]{:S(2)}) collective-permute-start(bf16[256,384]{1,0:T(8,128)(2,1)S(1)} %get-tuple-element.85), channel_id=1, source_target_pairs={{0,3},{1,2},{2,1},{3,0},{4,7},{5,6},{6,5},{7,4},{8,11},{9,10},{10,... | collective-permute-start | bytes 589832 | tf_op jit(solution)/shard_map/ppermute | solution.py:32
  15.3 12.3 %collective-permute-start.6 = (bf16[576,384]{1,0:T(8,128)(2,1)S(1)}, bf16[576,384]{1,0:T(8,128)(2,1)S(1)}, u32[]{:S(2)}, u32[]{:S(2)}) collective-permute-start(bf16[576,384]{1,0:T(8,128)(2,1)S(1)} %copy-done.4), channel_id=1, source_target_pairs={{0,2},{1,3},{2,0},{3,1},{4,6},{5,7},{6,4},{7,5},{8,10},{9,11},{10,... | collective-permute-start | bytes 1327112 | tf_op jit(solution)/shard_map/ppermute | solution.py:32
  16.9 16.2 %collective-permute-start.3 = (bf16[768,384]{1,0:T(8,128)(2,1)S(1)}, bf16[768,384]{1,0:T(8,128)(2,1)S(1)}, u32[]{:S(2)}, u32[]{:S(2)}) collective-permute-start(bf16[768,384]{1,0:T(8,128)(2,1)S(1)} %get-tuple-element.39), channel_id=1, source_target_pairs={{0,4},{4,8},{8,12},{1,5},{5,9},{9,13},{2,6},{6,10},{10,14},{3,7},{... | collective-permute-start | bytes 1769480 | tf_op jit(solution)/shard_map/ppermute | solution.py:22
  20.4 7.8 %collective-permute-start.5 = (bf16[576,384]{1,0:T(8,128)(2,1)S(1)}, bf16[576,384]{1,0:T(8,128)(2,1)S(1)}, u32[]{:S(2)}, u32[]{:S(2)}) collective-permute-start(bf16[576,384]{1,0:T(8,128)(2,1)S(1)} %copy-done.4), channel_id=1, source_target_pairs={{0,1},{1,0},{2,3},{3,2},{4,5},{5,4},{6,7},{7,6},{8,9},{9,8},{10,11... | collective-permute-start | bytes 1327112 | tf_op jit(solution)/shard_map/ppermute | solution.py:32
  20.5 17.6 %collective-permute-start.4 = (bf16[768,384]{1,0:T(8,128)(2,1)S(1)}, bf16[768,384]{1,0:T(8,128)(2,1)S(1)}, u32[]{:S(2)}, u32[]{:S(2)}) collective-permute-start(bf16[768,384]{1,0:T(8,128)(2,1)S(1)} %get-tuple-element.41), channel_id=1, source_target_pairs={{4,0},{8,4},{12,8},{5,1},{9,5},{13,9},{6,2},{10,6},{14,10},{7,3},{... | collective-permute-start | bytes 1769480 | tf_op jit(solution)/shard_map/ppermute | solution.py:22
  27.5 10.6 %collective-permute-start.7 = (bf16[576,384]{1,0:T(8,128)(2,1)S(1)}, bf16[576,384]{1,0:T(8,128)(2,1)S(1)}, u32[]{:S(2)}, u32[]{:S(2)}) collective-permute-start(bf16[576,384]{1,0:T(8,128)(2,1)S(1)} %collective-permute-done.6.refs_2_), channel_id=1, source_target_pairs={{0,1},{1,0},{2,3},{3,2},{4,5},{5,4},{6,7},{7,6},{8,9},{9,8},{10,11... | collective-permute-start | bytes 1327112 | tf_op jit(solution)/shard_map/ppermute | solution.py:32
  27.6 17.5 %collective-permute-start.8 = (bf16[256,384]{1,0:T(8,128)(2,1)S(1)}, bf16[256,384]{1,0:T(8,128)(2,1)S(1)}, u32[]{:S(2)}, u32[]{:S(2)}) collective-permute-start(bf16[256,384]{1,0:T(8,128)(2,1)S(1)} %get-tuple-element.84), channel_id=1, source_target_pairs={{0,1},{1,0},{2,3},{3,2},{4,5},{5,4},{6,7},{7,6},{8,9},{9,8},{10,11... | collective-permute-start | bytes 589832 | tf_op jit(solution)/shard_map/ppermute | solution.py:32
  28.2 17.0 %collective-permute-start.10 = (bf16[256,384]{1,0:T(8,128)(2,1)S(1)}, bf16[256,384]{1,0:T(8,128)(2,1)S(1)}, u32[]{:S(2)}, u32[]{:S(2)}) collective-permute-start(bf16[256,384]{1,0:T(8,128)(2,1)S(1)} %get-tuple-element.46), channel_id=1, source_target_pairs={{0,3},{1,2},{2,1},{3,0},{4,7},{5,6},{6,5},{7,4},{8,11},{9,10},{10,... | collective-permute-start | bytes 589832 | tf_op jit(solution)/shard_map/ppermute | solution.py:32
  33.1 12.0 %collective-permute-start.9 = (bf16[256,384]{1,0:T(8,128)(2,1)S(1)}, bf16[256,384]{1,0:T(8,128)(2,1)S(1)}, u32[]{:S(2)}, u32[]{:S(2)}) collective-permute-start(bf16[256,384]{1,0:T(8,128)(2,1)S(1)} %get-tuple-element.45), channel_id=1, source_target_pairs={{0,2},{1,3},{2,0},{3,1},{4,6},{5,7},{6,4},{7,5},{8,10},{9,11},{10,... | collective-permute-start | bytes 589832 | tf_op jit(solution)/shard_map/ppermute | solution.py:32
  48.6 18.4 %collective-permute-start.13 = (f32[576,384]{1,0:T(8,128)S(1)}, f32[576,384]{1,0:T(8,128)S(1)}, u32[]{:S(2)}, u32[]{:S(2)}) collective-permute-start(f32[576,384]{1,0:T(8,128)S(1)} %get-tuple-element.56), channel_id=1, source_target_pairs={{0,1},{1,0},{2,3},{3,2},{4,5},{5,4},{6,7},{7,6},{8,9},{9,8},{10,11... | collective-permute-start | bytes 2654216 | tf_op jit(solution)/shard_map/ppermute | solution.py:32
  48.7 12.5 %collective-permute-start.11 = (bf16[512,384]{1,0:T(8,128)(2,1)S(1)}, bf16[512,384]{1,0:T(8,128)(2,1)S(1)}, u32[]{:S(2)}, u32[]{:S(2)}) collective-permute-start(bf16[512,384]{1,0:T(8,128)(2,1)S(1)} %get-tuple-element.47), channel_id=1, source_target_pairs={{0,4},{4,8},{8,12},{1,5},{5,9},{9,13},{2,6},{6,10},{10,14},{3,7},{... | collective-permute-start | bytes 1179656 | tf_op jit(solution)/shard_map/ppermute | solution.py:22
  52.1 13.1 %collective-permute-start.12 = (bf16[512,384]{1,0:T(8,128)(2,1)S(1)}, bf16[512,384]{1,0:T(8,128)(2,1)S(1)}, u32[]{:S(2)}, u32[]{:S(2)}) collective-permute-start(bf16[512,384]{1,0:T(8,128)(2,1)S(1)} %get-tuple-element.49), channel_id=1, source_target_pairs={{4,0},{8,4},{12,8},{5,1},{9,5},{13,9},{6,2},{10,6},{14,10},{7,3},{... | collective-permute-start | bytes 1179656 | tf_op jit(solution)/shard_map/ppermute | solution.py:22
  71.1 12.2 %collective-permute-start.16 = (f32[576,384]{1,0:T(8,128)S(1)}, f32[576,384]{1,0:T(8,128)S(1)}, u32[]{:S(2)}, u32[]{:S(2)}) collective-permute-start(f32[576,384]{1,0:T(8,128)S(1)} %get-tuple-element.61), channel_id=1, source_target_pairs={{0,1},{1,0},{2,3},{3,2},{4,5},{5,4},{6,7},{7,6},{8,9},{9,8},{10,11... | collective-permute-start | bytes 2654216 | tf_op jit(solution)/shard_map/ppermute | solution.py:32
  71.1 7.8 %collective-permute-start.17 = (bf16[144,384]{1,0:T(8,128)(2,1)S(1)}, bf16[144,384]{1,0:T(8,128)(2,1)S(1)}, u32[]{:S(2)}, u32[]{:S(2)}) collective-permute-start(bf16[144,384]{1,0:T(8,128)(2,1)S(1)} %get-tuple-element.62), channel_id=1, source_target_pairs={{0,4},{4,8},{8,12},{12,0},{1,5},{5,9},{9,13},{13,1},{2,6},{6,10},{... | collective-permute-start | bytes 331784 | tf_op jit(solution)/shard_map/ppermute | solution.py:27
  72.7 10.5 %collective-permute-start.18 = (bf16[144,384]{1,0:T(8,128)(2,1)S(1)}, bf16[144,384]{1,0:T(8,128)(2,1)S(1)}, u32[]{:S(2)}, u32[]{:S(2)}) collective-permute-start(bf16[144,384]{1,0:T(8,128)(2,1)S(1)} %get-tuple-element.63), channel_id=1, source_target_pairs={{0,8},{4,12},{8,0},{12,4},{1,9},{5,13},{9,1},{13,5},{2,10},{6,14},... | collective-permute-start | bytes 331784 | tf_op jit(solution)/shard_map/ppermute | solution.py:27
  72.7 10.5 %collective-permute-start.19 = (bf16[144,384]{1,0:T(8,128)(2,1)S(1)}, bf16[144,384]{1,0:T(8,128)(2,1)S(1)}, u32[]{:S(2)}, u32[]{:S(2)}) collective-permute-start(bf16[144,384]{1,0:T(8,128)(2,1)S(1)} %get-tuple-element.64), channel_id=1, source_target_pairs={{0,12},{4,0},{8,4},{12,8},{1,13},{5,1},{9,5},{13,9},{2,14},{6,2},{... | collective-permute-start | bytes 331784 | tf_op jit(solution)/shard_map/ppermute | solution.py:27
  75.4 14.6 %collective-permute-start.14 = (bf16[256,384]{1,0:T(8,128)(2,1)}, bf16[256,384]{1,0:T(8,128)(2,1)S(1)}, u32[]{:S(2)}, u32[]{:S(2)}) collective-permute-start(bf16[256,384]{1,0:T(8,128)(2,1)} %get-tuple-element.58), channel_id=1, source_target_pairs={{0,4},{4,8},{8,12},{1,5},{5,9},{9,13},{2,6},{6,10},{10,14},{3,7},{... | collective-permute-start | bytes 589832 | tf_op jit(solution)/shard_map/ppermute | solution.py:22
  78.9 11.1 %collective-permute-start.15 = (bf16[256,384]{1,0:T(8,128)(2,1)}, bf16[256,384]{1,0:T(8,128)(2,1)S(1)}, u32[]{:S(2)}, u32[]{:S(2)}) collective-permute-start(bf16[256,384]{1,0:T(8,128)(2,1)} %get-tuple-element.59), channel_id=1, source_target_pairs={{4,0},{8,4},{12,8},{5,1},{9,5},{13,9},{6,2},{10,6},{14,10},{7,3},{... | collective-permute-start | bytes 589832 | tf_op jit(solution)/shard_map/ppermute | solution.py:22
  84.7 9.0 %collective-permute-start.23 = (bf16[144,384]{1,0:T(8,128)(2,1)}, bf16[144,384]{1,0:T(8,128)(2,1)}, u32[]{:S(2)}, u32[]{:S(2)}) collective-permute-start(bf16[144,384]{1,0:T(8,128)(2,1)} %get-tuple-element.66), channel_id=1, source_target_pairs={{0,4},{4,8},{8,12},{12,0},{1,5},{5,9},{9,13},{13,1},{2,6},{6,10},{... | collective-permute-start | bytes 331784 | tf_op jit(solution)/shard_map/ppermute | solution.py:27
  87.6 9.4 %collective-permute-start.24 = (bf16[144,384]{1,0:T(8,128)(2,1)}, bf16[144,384]{1,0:T(8,128)(2,1)}, u32[]{:S(2)}, u32[]{:S(2)}) collective-permute-start(bf16[144,384]{1,0:T(8,128)(2,1)} %get-tuple-element.67), channel_id=1, source_target_pairs={{0,8},{4,12},{8,0},{12,4},{1,9},{5,13},{9,1},{13,5},{2,10},{6,14},... | collective-permute-start | bytes 331784 | tf_op jit(solution)/shard_map/ppermute | solution.py:27
  88.6 8.5 %collective-permute-start.25 = (bf16[144,384]{1,0:T(8,128)(2,1)S(1)}, bf16[144,384]{1,0:T(8,128)(2,1)}, u32[]{:S(2)}, u32[]{:S(2)}) collective-permute-start(bf16[144,384]{1,0:T(8,128)(2,1)S(1)} %get-tuple-element.68), channel_id=1, source_target_pairs={{0,12},{4,0},{8,4},{12,8},{1,13},{5,1},{9,5},{13,9},{2,14},{6,2},{... | collective-permute-start | bytes 331784 | tf_op jit(solution)/shard_map/ppermute | solution.py:27
  98.1 6.0 %collective-permute-start.26 = (bf16[1,144,384]{2,1,0:T(8,128)(2,1)S(1)}, bf16[1,144,384]{2,1,0:T(8,128)(2,1)S(1)}, u32[]{:S(2)}, u32[]{:S(2)}) collective-permute-start(bf16[1,144,384]{2,1,0:T(8,128)(2,1)S(1)} %get-tuple-element.76), channel_id=1, source_target_pairs={{0,2},{1,3},{2,0},{3,1},{4,6},{5,7},{6,4},{7,5},{8,10},{9,11},{10,... | collective-permute-start | bytes 331784 | tf_op jit(solution)/shard_map/ppermute | solution.py:32
  98.8 9.3 %collective-permute-start.20 = (bf16[256,384]{1,0:T(8,128)(2,1)S(1)}, bf16[256,384]{1,0:T(8,128)(2,1)S(1)}, u32[]{:S(2)}, u32[]{:S(2)}) collective-permute-start(bf16[256,384]{1,0:T(8,128)(2,1)S(1)} %get-tuple-element.80), channel_id=1, source_target_pairs={{0,1},{1,0},{2,3},{3,2},{4,5},{5,4},{6,7},{7,6},{8,9},{9,8},{10,11... | collective-permute-start | bytes 589832 | tf_op jit(solution)/shard_map/ppermute | solution.py:32
  98.9 10.6 %collective-permute-start.21 = (bf16[256,384]{1,0:T(8,128)(2,1)S(1)}, bf16[256,384]{1,0:T(8,128)(2,1)S(1)}, u32[]{:S(2)}, u32[]{:S(2)}) collective-permute-start(bf16[256,384]{1,0:T(8,128)(2,1)S(1)} %get-tuple-element.79), channel_id=1, source_target_pairs={{0,2},{1,3},{2,0},{3,1},{4,6},{5,7},{6,4},{7,5},{8,10},{9,11},{10,... | collective-permute-start | bytes 589832 | tf_op jit(solution)/shard_map/ppermute | solution.py:32
  100.4 10.1 %collective-permute-start.22 = (bf16[256,384]{1,0:T(8,128)(2,1)S(1)}, bf16[256,384]{1,0:T(8,128)(2,1)S(1)}, u32[]{:S(2)}, u32[]{:S(2)}) collective-permute-start(bf16[256,384]{1,0:T(8,128)(2,1)S(1)} %get-tuple-element.78), channel_id=1, source_target_pairs={{0,3},{1,2},{2,1},{3,0},{4,7},{5,6},{6,5},{7,4},{8,11},{9,10},{10,... | collective-permute-start | bytes 589832 | tf_op jit(solution)/shard_map/ppermute | solution.py:32
  104.1 7.6 %collective-permute-start.27 = (bf16[144,384]{1,0:T(8,128)(2,1)S(1)}, bf16[144,384]{1,0:T(8,128)(2,1)S(1)}, u32[]{:S(2)}, u32[]{:S(2)}) collective-permute-start(bf16[144,384]{1,0:T(8,128)(2,1)S(1)} %bitcast_convert_fusion), channel_id=1, source_target_pairs={{0,4},{4,8},{8,12},{12,0},{1,5},{5,9},{9,13},{13,1},{2,6},{6,10},{... | collective-permute-start | bytes 331784 | tf_op jit(solution)/shard_map/ppermute | solution.py:27
  107.1 8.2 %collective-permute-start.28 = (bf16[144,384]{1,0:T(8,128)(2,1)S(1)}, bf16[144,384]{1,0:T(8,128)(2,1)S(1)}, u32[]{:S(2)}, u32[]{:S(2)}) collective-permute-start(bf16[144,384]{1,0:T(8,128)(2,1)S(1)} %bitcast_convert_fusion), channel_id=1, source_target_pairs={{0,8},{4,12},{8,0},{12,4},{1,9},{5,13},{9,1},{13,5},{2,10},{6,14},... | collective-permute-start | bytes 331784 | tf_op jit(solution)/shard_map/ppermute | solution.py:27
  108.1 7.2 %collective-permute-start.29 = (bf16[144,384]{1,0:T(8,128)(2,1)S(1)}, bf16[144,384]{1,0:T(8,128)(2,1)S(1)}, u32[]{:S(2)}, u32[]{:S(2)}) collective-permute-start(bf16[144,384]{1,0:T(8,128)(2,1)S(1)} %bitcast_convert_fusion), channel_id=1, source_target_pairs={{0,12},{4,0},{8,4},{12,8},{1,13},{5,1},{9,5},{13,9},{2,14},{6,2},{... | collective-permute-start | bytes 331784 | tf_op jit(solution)/shard_map/ppermute | solution.py:27
  (5 other events, 24.7 us)

commit v4 on v3

--- a/solution.py
+++ b/solution.py
@@ -34,6 +34,14 @@
 
 def after(value, others):
     return lax.optimization_barrier((value, others))[0]
+
+
+def share_of(s, n):
+    index, bit = 0, 1
+    while bit < n:
+        index = 2 * index + lax.rem(s // bit, 2)
+        bit *= 2
+    return index
 
 
 def cut(block, index, rows):
@@ -53,14 +61,16 @@
     return [held[r] for r in range(n)]
 
 
-def slope_of(v, th):
+def gelu_parts(v):
     coeff = 0.7978845608
-    return 0.5 * (1.0 + th) + 0.5 * v * (1.0 - th * th) * coeff * (1.0 + 3.0 * 0.044715 * v * v)
-
-
-def gelu_tanh(v):
+    square = v * v
+    return jnp.tanh(v * (coeff + (coeff * 0.044715) * square)), square
+
+
+def slope_of(v, th, square):
     coeff = 0.7978845608
-    return jnp.tanh(coeff * (v + 0.044715 * v * v * v))
+    inner = 0.5 * coeff + (0.5 * coeff * 3.0 * 0.044715) * square
+    return (0.5 + 0.5 * th) + (v * inner) * (1.0 - th * th)
 
 
 def dot(a, b):
@@ -115,22 +125,23 @@
     for b in range(-far, members + far):
         stack = jnp.concatenate([block(b - near), block(b), block(b + near)], 1)
         pre = dot(stack, w_out[:taps])
-        th = gelu_tanh(pre)
-        value = (block(b).astype(F32) + 0.5 * pre * (1.0 + th)).astype(BF16)
+        th, square = gelu_parts(pre)
+        half = 0.5 * pre
+        value = (block(b).astype(F32) + (half + half * th)).astype(BF16)
         if b < 0:
             value = jnp.where(s > 0, value, jnp.zeros_like(value))
         if b >= members:
             value = jnp.where(s < groups - 1, value, jnp.zeros_like(value))
         hid[b + far] = value
         if 0 <= b < members:
-            slope_one[b * q : (b + 1) * q] = slope_of(pre, th)
+            slope_one[b * q : (b + 1) * q] = slope_of(pre, th, square)
             act_stack[b * q : (b + 1) * q] = stack
     for b in range(members):
         stack = jnp.concatenate([hid[b], hid[b + far], hid[b + 2 * far]], 1)
         here = slice(b * q, (b + 1) * q)
         hid_stack[here] = stack
         pre = dot(stack, w_out[taps:])
-        slope_two[here] = slope_of(pre, gelu_tanh(pre))
+        slope_two[here] = slope_of(pre, *gelu_parts(pre))
 
 
 def delta_kernel(sizes, place, slope, cotangent, *refs):
@@ -152,11 +163,13 @@
 
 
 def grad_kernel(sizes, scale, place, stack, delta, *refs):
-    members, halo = sizes
-    keep, send = refs[-2:] if not halo else refs[-4:-2]
+    members, halo, splits = sizes
+    outs = refs[-(1 + splits + (2 if halo else 0)) :]
+    keep, sends = outs[0], outs[1 : 1 + splits]
     odd = place[1] & 1
     channels = delta.shape[1]
     rows = 3 * channels // (members // 2)
+    share = keep.shape[0] // splits
     for k in range(3):
         first = k * channels
         part = scale * lax.dot_general(
@@ -170,28 +183,49 @@
             if start >= stop:
                 continue
             at = (owner // 2) * rows + start - owner * rows
+            end = at + stop - start
             value = part[start - first : stop - first]
 
             @pl.when(odd == owner % 2)
             def _():
-                keep[at : at + stop - start] = value
+                keep[at:end] = value
 
             @pl.when(odd != owner % 2)
             def _():
-                send[at : at + stop - start] = value
+                for i in range(splits):
+                    low, high = max(at, i * share), min(end, (i + 1) * share)
+                    if low < high:
+                        sends[i][low - i * share : high - i * share] = value[low - at : high - at]
 
     if halo:
-        to_high, to_low = refs[-2:]
+        to_high, to_low = outs[-2:]
         to_high[...] = delta[delta.shape[0] - halo :]
         to_low[...] = delta[:halo]
 
 
-def share_kernel(n, place, keep, other, *refs):
-    outs = refs[-n:]
+def share_kernel(n, splits, place, keep, *refs):
+    others, outs, total = refs[:splits], refs[-n - 1 : -1], refs[-1]
     rows = outs[0].shape[0]
+    part = keep.shape[0] // splits
+    for i in range(splits):
+        here = slice(i * part, (i + 1) * part)
+        total[here] = keep[here] + others[i][...]
     for turn in range(n):
-        at = pl.ds(pl.multiple_of(lax.rem(place[0] + turn, n) * rows, 16), rows)
-        outs[turn][...] = (keep[at, :] + other[at, :]).astype(outs[turn].dtype)
+        index = share_of(lax.rem(place[0] + turn, n), n)
+        at = pl.ds(pl.multiple_of(index * rows, 16), rows)
+        outs[turn][...] = total[at, :].astype(outs[turn].dtype)
+
+
+def halve_kernel(bit, place, keep, *refs):
+    others, (kept, sent, total) = refs[:-3], refs[-3:]
+    rows = keep.shape[0] // len(others)
+    for i, other in enumerate(others):
+        here = slice(i * rows, (i + 1) * rows)
+        total[here] = keep[here] + other[...].astype(F32)
+    half = kept.shape[0]
+    mine = lax.rem(place[0] // bit, 2)
+    kept[...] = total[pl.ds(pl.multiple_of(mine * half, 16), half), :]
+    sent[...] = total[pl.ds(pl.multiple_of((1 - mine) * half, 16), half), :].astype(BF16)
 
 
 def back_kernel(sizes, low, own, high, cot, slope, w, back_one, delta):
@@ -239,29 +273,72 @@
         out_specs=tuple(VMEM for _ in out_shapes),
         scratch_shapes=list(scratch),
         cost_estimate=pl.CostEstimate(flops=1, transcendentals=0, bytes_accessed=1),
-        compiler_params=pltpu.CompilerParams(vmem_limit_bytes=16 * 1024 * 1024),
+        compiler_params=pltpu.CompilerParams(vmem_limit_bytes=8 * 1024 * 1024),
     )(*operands)
 
 
-def seq_shares(place, keep, other, waits):
+def core_sum(place, keep, sends, waits):
+    n = lax.axis_size("seq")
+    others = [swapped(send, "sub", 1) for send in sends]
+    if n > 4:
+        return [keep + jnp.concatenate(others, 0)]
+    shape = (keep.shape[0] // n, keep.shape[1])
+    return call(
+        functools.partial(share_kernel, n, len(sends)),
+        ((shape, F32),) + ((shape, BF16),) * (n - 1),
+        scratch=(pltpu.VMEM(keep.shape, F32),),
+        scalars=1,
+        operands=(place, keep, *others, *waits),
+    )
+
+
+def seq_parts(shares):
+    if len(shares) == 1:
+        return [lax.psum(shares[0], "seq")]
+    return [shares[0]] + [turned(shares[t], "seq", t) for t in range(1, len(shares))]
+
+
+def halved(place, keep, others, bit):
+    rows, channels = keep.shape
+    shape = (rows // 2, channels)
+    return call(
+        functools.partial(halve_kernel, bit),
+        ((shape, F32), (shape, BF16)),
+        scratch=(pltpu.VMEM((rows, channels), F32),),
+        scalars=1,
+        operands=(place, keep, *others),
+    )
+
+
+def core_sum_halving(place, keep, sends):
+    others = [swapped(send, "sub", 1) for send in sends]
     n = lax.axis_size("seq")
     if n > 4:
-        return [keep + other]
-    shape = (keep.shape[0] // n, keep.shape[1])
-    return call(
-        functools.partial(share_kernel, n),
-        ((shape, F32),) + ((shape, BF16),) * (n - 1),
-        scalars=1,
-        operands=(place, keep, other, *waits),
-    )
-
-
-def seq_sum(shares):
-    if len(shares) == 1:
-        return lax.psum(shares[0], "seq")
-    total = shares[0]
-    for turn in range(1, len(shares)):
-        total = total + turned(shares[turn], "seq", turn).astype(F32)
+        total = keep + jnp.concatenate(others, 0)
+        return total, total
+    return halved(place, keep, others, 1)
+
+
+def first_half(sent):
+    return sent if lax.axis_size("seq") > 4 else swapped(sent, "seq", 1)
+
+
+def seq_sum_halving(place, kept, got, others):
+    n = lax.axis_size("seq")
+    if n > 4:
+        return lax.psum(kept, "seq")
+    bit = 2
+    while bit < n:
+        kept, sent = halved(place, kept, [after(got, others)], bit)
+        got = swapped(sent, "seq", bit)
+        bit *= 2
+    return added([kept, got])
+
+
+def added(pieces):
+    total = pieces[0]
+    for piece in pieces[1:]:
+        total = total + piece.astype(F32)
     return total
 
 
@@ -288,10 +365,11 @@
         return total
     rows, channels = total.shape
     whole = jnp.zeros((n * rows, channels), F32)
-    whole = lax.dynamic_update_slice_in_dim(whole, total, s * rows, 0)
+    whole = lax.dynamic_update_slice_in_dim(whole, total, share_of(s, n) * rows, 0)
     for turn in range(1, n):
         got = turned(sent, "seq", turn).astype(F32)
-        whole = lax.dynamic_update_slice_in_dim(whole, got, lax.rem(s + n - turn, n) * rows, 0)
+        at = share_of(lax.rem(s + n - turn, n), n) * rows
+        whole = lax.dynamic_update_slice_in_dim(whole, got, at, 0)
     return whole
 
 
@@ -345,32 +423,37 @@
         operands=(slope_two, cotangent, *c_pieces),
     )
     two_low, two_high = shifted(up_two, "seq", 1), shifted(down_two, "seq", -1)
+    splits, more = 8, 8
     half = ((taps // 2, channels), F32)
-    keep_two, send_two = kernel(
-        functools.partial(grad_kernel, (members, 0), grad_scale),
+    share = ((taps // 2 // splits, channels), F32)
+    less = ((taps // 2 // more, channels), F32)
+    keep_two, *send_two = kernel(
+        functools.partial(grad_kernel, (members, 0, splits), grad_scale),
         half,
-        half,
+        *[share] * splits,
         operands=(hid_stack, delta_two),
     )
-    shares_two = seq_shares(place, keep_two, swapped(send_two, "sub", 1), ())
+    kept_two, sent_two = core_sum_halving(place, keep_two, send_two)
     back_one, delta_one = call(
         functools.partial(back_kernel, (members, q, near, far)),
         (((count, channels), F32), ((count, channels), BF16)),
         operands=(two_low, delta_two, two_high, cot, slope_one, all_weights),
     )
-    keep_one, send_one, up_one, down_one = kernel(
-        functools.partial(grad_kernel, (members, near * q), grad_scale),
+    keep_one, *send_one, up_one, down_one = kernel(
+        functools.partial(grad_kernel, (members, near * q, more), grad_scale),
         half,
-        half,
+        *[less] * more,
         ((near * q, channels), BF16),
         ((near * q, channels), BF16),
-        operands=(act_stack, delta_one, shares_two[0]),
-    )
+        operands=(act_stack, delta_one),
+    )
+    got_two = first_half(after(sent_two, (two_low, two_high)))
+    shares_one = core_sum(place, keep_one, send_one, (got_two,))
     one_low, one_high = shifted(up_one, "seq", 1), shifted(down_one, "seq", -1)
-    total_two = seq_sum(shares_two)
-    shares_one = seq_shares(place, keep_one, swapped(send_one, "sub", 1), (total_two,))
-    one_low, one_high = after((one_low, one_high), shares_one)
-    part = chip_sum(seq_sum(shares_one), total_two, j)
+    parts_one = seq_parts(shares_one)
+    total_two = seq_sum_halving(place, kept_two, got_two, shares_one[0])
+    total_one = added(parts_one)
+    part = chip_sum(total_one, total_two, j)
     sent = part.astype(BF16)
 
     (grad_in,) = call(

time: 117 us -> 116 us (level)
  waiting for transfers between devices: 51.4 us -> 48 us
    ppermute x15 -> x31, waiting for transfers between devices: 19.5 us -> 26.1 us  [swapped(): return lax.ppermute(block, axis, [(i, i ^ bits) for i in range(n)])]
    ppermute x15 -> x31, starting transfers between devices: 10 us -> 16.2 us  [swapped(): return lax.ppermute(block, axis, [(i, i ^ bits) for i in range(n)])]
    ppermute x9 -> x6, starting transfers between devices: 14.9 us -> 8.86 us  [turned(): return lax.ppermute(block, axis, [(i, (i + turn) % n) for i in range(n)])]
    ppermute x6, waiting for transfers between devices: 19.8 us -> 14.5 us  [shifted(): return lax.ppermute(block, axis, route)]
    ppermute x9 -> x6, waiting for transfers between devices: 12.1 us -> 7.46 us  [turned(): return lax.ppermute(block, axis, [(i, (i + turn) % n) for i in range(n)])]
    pallas_call x9 -> x10, Pallas kernels: 20.7 us -> 21.6 us  [call(): pl.pallas_call(kernel, out_shape=tuple((jax.ShapeDtypeStruct(shape, kind)...]
  transfers between devices with their start and end apart: 30 -> 43, of which waited for: 14 -> 15; matrix products, arithmetic and copies ran while one was open for 1% -> 1% of each run, Pallas kernels for 11% -> 17%
where the time goes in v4:
time: 116 us; the launch traced here: 115 us
  waiting for transfers between devices  48 us (41%)
  starting transfers between devices  38.3 us (33%)
  Pallas kernels  21.6 us (19%)
  local copies, waits for them, and re-layouts  4.07 us (4%)
  other arithmetic  2.44 us (2%)
    ppermute x31, waiting for transfers between devices, swapped(): return lax.ppermute(block, axis, [(i, i ^ bits) for i in range(n)])  26.1 us
    pallas_call x10, Pallas kernels, call(): pl.pallas_call(kernel, out_shape=tuple((jax.ShapeDtypeStruct(shape, kind)...  21.6 us
    ppermute x31, starting transfers between devices, swapped(): return lax.ppermute(block, axis, [(i, i ^ bits) for i in range(n)])  16.2 us
    ppermute x6, waiting for transfers between devices, shifted(): return lax.ppermute(block, axis, route)  14.5 us
    ppermute x6, starting transfers between devices, shifted(): return lax.ppermute(block, axis, route)  13.2 us
    ppermute x6, starting transfers between devices, turned(): return lax.ppermute(block, axis, [(i, (i + turn) % n) for i in range(n)])  8.86 us
    ppermute x6, waiting for transfers between devices, turned(): return lax.ppermute(block, axis, [(i, (i + turn) % n) for i in range(n)])  7.46 us
    unnamed x14, local copies, waits for them, and re-layouts  2.34 us
  transfers between devices with their start and end apart: 43, of which 15 were waited for; matrix products, arithmetic and copies ran while one was open for 1% of the time, Pallas kernels for 17%

profile of v4, /device:TPU:0, one launch (start us, length us, event | category | flops | bytes accessed | tf_op | source)
XLA Modules:
  0.0 115.5 jit_solution(6351637888586918244)
XLA Ops:
  0.7 1.3 %constant_dynamic-slice_fusion.3 = (bf16[256,384]{1,0:T(8,128)(2,1)S(1)}, bf16[256,384]{1,0:T(8,128)(2,1)S(1)}, bf16[256,384]{1,0:T(8,128)(2,1)S(1)}) fusion(bf16[1024,384]{1,0:T(8,128)(2,1)} %block.1, s32[]{:T(128)S(6)} %select_n.66, s32[]{:T(128)S(6)} %select_n.65, s32[]{:T(128)S(6)} %select_n.64), kind=kLoop, calls=%fused_computation.17 | loop fusion | bytes 1179660 | tf_op jit(solution)/shard_map/dynamic_slice | solution.py:48
  2.5 2.6 %collective-permute-start.1 = (bf16[256,384]{1,0:T(8,128)(2,1)S(1)}, bf16[256,384]{1,0:T(8,128)(2,1)S(1)}, u32[]{:S(2)}, u32[]{:S(2)}) collective-permute-start(bf16[256,384]{1,0:T(8,128)(2,1)S(1)} %get-tuple-element.114), channel_id=1, source_target_pairs={{0,2},{1,3},{2,0},{3,1},{4,6},{5,7},{6,4},{7,5},{8,10},{9,11},{10,... | collective-permute-start | bytes 589832 | tf_op jit(solution)/shard_map/ppermute | solution.py:32
  5.2 5.6 %collective-permute-done.1.refs_1_ = bf16[256,384]{1,0:T(8,128)(2,1)S(1)} collective-permute-done((bf16[256,384]{1,0:T(8,128)(2,1)S(1)}, bf16[256,384]{1,0:T(8,128)(2,1)S(1)}, u32[]{:S(2)}, u32[]{:S(2)}) %collective-permute-start.1) | collective-permute-done | bytes 196640 | tf_op jit(solution)/shard_map/ppermute | solution.py:32
  10.8 3.7 %collective-permute-done.2.refs_2_ = bf16[256,384]{1,0:T(8,128)(2,1)S(1)} collective-permute-done((bf16[256,384]{1,0:T(8,128)(2,1)S(1)}, bf16[256,384]{1,0:T(8,128)(2,1)S(1)}, u32[]{:S(2)}, u32[]{:S(2)}) %collective-permute-start.2) | collective-permute-done | bytes 196640 | tf_op jit(solution)/shard_map/ppermute | solution.py:32
  15.3 1.6 %collective-permute-start.6 = (bf16[576,384]{1,0:T(8,128)(2,1)S(1)}, bf16[576,384]{1,0:T(8,128)(2,1)S(1)}, u32[]{:S(2)}, u32[]{:S(2)}) collective-permute-start(bf16[576,384]{1,0:T(8,128)(2,1)S(1)} %copy-done.4), channel_id=1, source_target_pairs={{0,2},{1,3},{2,0},{3,1},{4,6},{5,7},{6,4},{7,5},{8,10},{9,11},{10,... | collective-permute-start | bytes 1327112 | tf_op jit(solution)/shard_map/ppermute | solution.py:32
  16.9 3.5 %collective-permute-start.3 = (bf16[768,384]{1,0:T(8,128)(2,1)S(1)}, bf16[768,384]{1,0:T(8,128)(2,1)S(1)}, u32[]{:S(2)}, u32[]{:S(2)}) collective-permute-start(bf16[768,384]{1,0:T(8,128)(2,1)S(1)} %get-tuple-element.53), channel_id=1, source_target_pairs={{0,4},{4,8},{8,12},{1,5},{5,9},{9,13},{2,6},{6,10},{10,14},{3,7},{... | collective-permute-start | bytes 1769480 | tf_op jit(solution)/shard_map/ppermute | solution.py:22
  21.8 5.7 %collective-permute-done.6.refs_2_ = bf16[576,384]{1,0:T(8,128)(2,1)S(1)} collective-permute-done((bf16[576,384]{1,0:T(8,128)(2,1)S(1)}, bf16[576,384]{1,0:T(8,128)(2,1)S(1)}, u32[]{:S(2)}, u32[]{:S(2)}) %collective-permute-start.6) | collective-permute-done | bytes 442400 | tf_op jit(solution)/shard_map/ppermute | solution.py:32
  28.2 1.4 %collective-permute-start.10 = (bf16[256,384]{1,0:T(8,128)(2,1)S(1)}, bf16[256,384]{1,0:T(8,128)(2,1)S(1)}, u32[]{:S(2)}, u32[]{:S(2)}) collective-permute-start(bf16[256,384]{1,0:T(8,128)(2,1)S(1)} %get-tuple-element.60), channel_id=1, source_target_pairs={{0,3},{1,2},{2,1},{3,0},{4,7},{5,6},{6,5},{7,4},{8,11},{9,10},{10,... | collective-permute-start | bytes 589832 | tf_op jit(solution)/shard_map/ppermute | solution.py:32
  29.6 3.5 %collective-permute-done.3.low = bf16[768,384]{1,0:T(8,128)(2,1)S(1)} collective-permute-done((bf16[768,384]{1,0:T(8,128)(2,1)S(1)}, bf16[768,384]{1,0:T(8,128)(2,1)S(1)}, u32[]{:S(2)}, u32[]{:S(2)}) %collective-permute-start.3) | collective-permute-done | bytes 589856 | tf_op jit(solution)/shard_map/ppermute | solution.py:22
  33.6 4.5 %collective-permute-done.4.high = bf16[768,384]{1,0:T(8,128)(2,1)S(1)} collective-permute-done((bf16[768,384]{1,0:T(8,128)(2,1)S(1)}, bf16[768,384]{1,0:T(8,128)(2,1)S(1)}, u32[]{:S(2)}, u32[]{:S(2)}) %collective-permute-start.4) | collective-permute-done | bytes 589856 | tf_op jit(solution)/shard_map/ppermute | solution.py:22
  38.1 6.7 %shard_map.51 = (bf16[1024,1152]{1,0:T(8,128)(2,1)S(1)}, bf16[1024,1152]{1,0:T(8,128)(2,1)S(1)}, f32[1024,384]{1,0:T(8,128)S(1)}, f32[1024,384]{1,0:T(8,128)S(1)}, bf16[2304,384]{1,0:T(8,128)(2,1)S(1)}) custom-call(s32[2]{0:T(128)S(1)} %pad_add_fusion.place, bf16[768,384]{1,0:T(8,128)(2,1)S(1)} %collective-permute-done.3.low, ...), custom_call_target="tpu_custom_call" | custom-call | flops 1 | bytes 1 | tf_op jit(solution)/shard_map/pallas_call | solution.py:269
  45.8 3.5 %collective-permute-start.11 = (bf16[512,384]{1,0:T(8,128)(2,1)S(1)}, bf16[512,384]{1,0:T(8,128)(2,1)S(1)}, u32[]{:S(2)}, u32[]{:S(2)}) collective-permute-start(bf16[512,384]{1,0:T(8,128)(2,1)S(1)} %get-tuple-element.61), channel_id=1, source_target_pairs={{0,4},{4,8},{8,12},{1,5},{5,9},{9,13},{2,6},{6,10},{10,14},{3,7},{... | collective-permute-start | bytes 1179656 | tf_op jit(solution)/shard_map/ppermute | solution.py:22
  50.6 2.5 %shard_map.56 = (f32[576,384]{1,0:T(8,128)S(1)}, f32[72,384]{1,0:T(8,128)S(1)}, f32[72,384]{1,0:T(8,128)S(1)}, f32[72,384]{1,0:T(8,128)S(1)}, f32[72,384]{1,0:T(...) custom-call(s32[2]{0:T(128)S(1)} %pad_add_fusion.place, ...), custom_call_target="tpu_custom_call" | custom-call | flops 1 | bytes 1 | tf_op jit(solution)/shard_map/pallas_call | solution.py:269
  55.2 2.3 %collective-permute-done.11.low = bf16[512,384]{1,0:T(8,128)(2,1)S(1)} collective-permute-done((bf16[512,384]{1,0:T(8,128)(2,1)S(1)}, bf16[512,384]{1,0:T(8,128)(2,1)S(1)}, u32[]{:S(2)}, u32[]{:S(2)}) %collective-permute-start.11) | collective-permute-done | bytes 393248 | tf_op jit(solution)/shard_map/ppermute | solution.py:22
  57.5 4.1 %collective-permute-done.12.high = bf16[512,384]{1,0:T(8,128)(2,1)S(1)} collective-permute-done((bf16[512,384]{1,0:T(8,128)(2,1)S(1)}, bf16[512,384]{1,0:T(8,128)(2,1)S(1)}, u32[]{:S(2)}, u32[]{:S(2)}) %collective-permute-start.12) | collective-permute-done | bytes 393248 | tf_op jit(solution)/shard_map/ppermute | solution.py:22
  61.6 1.7 %shard_map.53 = (f32[1024,384]{1,0:T(8,128)S(1)}, bf16[1024,384]{1,0:T(8,128)(2,1)S(1)}) custom-call(bf16[512,384]{1,0:T(8,128)(2,1)S(1)} %collective-permute-done.11.low, bf16[1024,384]{1,0:T(8,128)(2,1)S(1)} %get-tuple-element.62.own.delta, bf16[512,384]{1,0:T(8,128)(2,1)S(1)} %collective-permute-done.12.high, ...), custom_call_target="tpu_custom_call" | custom-call | flops 1 | bytes 1 | tf_op jit(solution)/shard_map/pallas_call | solution.py:269
  63.4 3.4 %shard_map.54 = (f32[576,384]{1,0:T(8,128)S(1)}, f32[72,384]{1,0:T(8,128)S(1)}, f32[72,384]{1,0:T(8,128)S(1)}, f32[72,384]{1,0:T(8,128)S(1)}, f32[72,384]{1,0:T(...) custom-call(s32[2]{0:T(128)S(1)} %pad_add_fusion.place, ...), custom_call_target="tpu_custom_call" | custom-call | flops 1 | bytes 1 | tf_op jit(solution)/shard_map/pallas_call | solution.py:269
  69.1 1.6 %collective-permute-start.26 = (bf16[288,384]{1,0:T(8,128)(2,1)S(1)}, bf16[288,384]{1,0:T(8,128)(2,1)S(1)}, u32[]{:S(2)}, u32[]{:S(2)}) collective-permute-start(bf16[288,384]{1,0:T(8,128)(2,1)S(1)} %get-tuple-element.83), channel_id=1, source_target_pairs={{0,4},{4,0},{8,12},{12,8},{1,5},{5,1},{9,13},{13,9},{2,6},{6,2},{1... | collective-permute-start | bytes 663560 | tf_op jit(solution)/shard_map/ppermute | solution.py:32
  70.7 2.4 %collective-permute-start.13 = (bf16[256,384]{1,0:T(8,128)(2,1)S(1)}, bf16[256,384]{1,0:T(8,128)(2,1)S(1)}, u32[]{:S(2)}, u32[]{:S(2)}) collective-permute-start(bf16[256,384]{1,0:T(8,128)(2,1)S(1)} %get-tuple-element.68), channel_id=1, source_target_pairs={{0,4},{4,8},{8,12},{1,5},{5,9},{9,13},{2,6},{6,10},{10,14},{3,7},{... | collective-permute-start | bytes 589832 | tf_op jit(solution)/shard_map/ppermute | solution.py:22
  75.0 1.5 %collective-permute-done.26.refs_8_.refs_0_ = bf16[288,384]{1,0:T(8,128)(2,1)S(1)} collective-permute-done((bf16[288,384]{1,0:T(8,128)(2,1)S(1)}, bf16[288,384]{1,0:T(8,128)(2,1)S(1)}, u32[]{:S(2)}, u32[]{:S(2)}) %collective-permute-start.26) | collective-permute-done | bytes 221216 | tf_op jit(solution)/shard_map/ppermute | solution.py:32
  76.5 1.4 %shard_map.58 = (f32[144,384]{1,0:T(8,128)S(1)}, bf16[144,384]{1,0:T(8,128)(2,1)}, bf16[144,384]{1,0:T(8,128)(2,1)}, bf16[144,384]{1,0:T(8,128)(2,1)S(1)}) custom-call(s32[2]{0:T(128)S(1)} %pad_add_fusion.place, f32[576,384]{1,0:T(8,128)S(1)} %get-tuple-element.84.keep, f32[72,384]{1,0:T(8,128)S(1)} %collective-permute-done.27.refs_0_, ...), custom_call_target="tpu_custom_call" | custom-call | flops 1 | bytes 1 | tf_op jit(solution)/shard_map/pallas_call | solution.py:269
  81.6 2.9 %collective-permute-start.37 = (bf16[144,384]{1,0:T(8,128)(2,1)}, bf16[144,384]{1,0:T(8,128)(2,1)}, u32[]{:S(2)}, u32[]{:S(2)}) collective-permute-start(bf16[144,384]{1,0:T(8,128)(2,1)} %get-tuple-element.98), channel_id=1, source_target_pairs={{0,8},{4,12},{8,0},{12,4},{1,9},{5,13},{9,1},{13,5},{2,10},{6,14},... | collective-permute-start | bytes 331784 | tf_op jit(solution)/shard_map/ppermute | solution.py:27
  85.1 1.4 %copy-done.3 = f32[1024,384]{1,0:T(8,128)S(1)} copy-done((f32[1024,384]{1,0:T(8,128)S(1)}, f32[1024,384]{1,0:T(8,128)}, u32[]{:S(2)}) %copy-start.3) | copy-done | bytes 1572888
  86.5 2.3 %shard_map.55 = bf16[1024,384]{1,0:T(8,128)(2,1)S(1)} custom-call(s32[2]{0:T(128)S(1)} %pad_add_fusion.place, bf16[256,384]{1,0:T(8,128)(2,1)S(1)} %collective-permute-done.13.low, bf16[1024,384]{1,0:T(8,128)(2,1)S(1)} %get-tuple-element.67.delta.own, bf16[256,384]{1,0:T(8,128)(2,1)S(1)} %collective-permute-done.14.high, f32[1024,384]{1,0:T(8,128)S(1)} %copy-done.3, ...), custom_call_target="tpu_custom_call" | custom-call | flops 1 | bytes 1 | tf_op jit(solution)/shard_map/pallas_call | solution.py:269
  88.7 4.6 %collective-permute-done.35 = bf16[144,384]{1,0:T(8,128)(2,1)} collective-permute-done((bf16[144,384]{1,0:T(8,128)(2,1)}, bf16[144,384]{1,0:T(8,128)(2,1)}, u32[]{:S(2)}, u32[]{:S(2)}) %collective-permute-start.35) | collective-permute-done | bytes 110624 | tf_op jit(solution)/shard_map/ppermute | solution.py:32
  93.3 2.4 %collective-permute-done.37 = bf16[144,384]{1,0:T(8,128)(2,1)} collective-permute-done((bf16[144,384]{1,0:T(8,128)(2,1)}, bf16[144,384]{1,0:T(8,128)(2,1)}, u32[]{:S(2)}, u32[]{:S(2)}) %collective-permute-start.37) | collective-permute-done | bytes 110624 | tf_op jit(solution)/shard_map/ppermute | solution.py:27
  97.6 1.6 %collective-permute-start.16 = (bf16[256,384]{1,0:T(8,128)(2,1)S(1)}, bf16[256,384]{1,0:T(8,128)(2,1)S(1)}, u32[]{:S(2)}, u32[]{:S(2)}) collective-permute-start(bf16[256,384]{1,0:T(8,128)(2,1)S(1)} %get-tuple-element.107), channel_id=1, source_target_pairs={{0,2},{1,3},{2,0},{3,1},{4,6},{5,7},{6,4},{7,5},{8,10},{9,11},{10,... | collective-permute-start | bytes 589832 | tf_op jit(solution)/shard_map/ppermute | solution.py:32
  99.4 3.1 %collective-permute-done.39 = bf16[1,144,384]{2,1,0:T(8,128)(2,1)S(1)} collective-permute-done((bf16[1,144,384]{2,1,0:T(8,128)(2,1)S(1)}, bf16[1,144,384]{2,1,0:T(8,128)(2,1)S(1)}, u32[]{:S(2)}, u32[]{:S(2)}) %collective-permute-start.39) | collective-permute-done | bytes 110624 | tf_op jit(solution)/shard_map/ppermute | solution.py:32
  103.8 1.9 %collective-permute-start.40 = (bf16[144,384]{1,0:T(8,128)(2,1)S(1)}, bf16[144,384]{1,0:T(8,128)(2,1)S(1)}, u32[]{:S(2)}, u32[]{:S(2)}) collective-permute-start(bf16[144,384]{1,0:T(8,128)(2,1)S(1)} %bitcast.11), channel_id=1, source_target_pairs={{0,4},{4,8},{8,12},{12,0},{1,5},{5,9},{9,13},{13,1},{2,6},{6,10},{... | collective-permute-start | bytes 331784 | tf_op jit(solution)/shard_map/ppermute | solution.py:27
  105.6 2.2 %collective-permute-start.41 = (bf16[144,384]{1,0:T(8,128)(2,1)S(1)}, bf16[144,384]{1,0:T(8,128)(2,1)S(1)}, u32[]{:S(2)}, u32[]{:S(2)}) collective-permute-start(bf16[144,384]{1,0:T(8,128)(2,1)S(1)} %bitcast.12), channel_id=1, source_target_pairs={{0,8},{4,12},{8,0},{12,4},{1,9},{5,13},{9,1},{13,5},{2,10},{6,14},... | collective-permute-start | bytes 331784 | tf_op jit(solution)/shard_map/ppermute | solution.py:27
  109.4 1.9 %collective-permute-done.40 = bf16[144,384]{1,0:T(8,128)(2,1)S(1)} collective-permute-done((bf16[144,384]{1,0:T(8,128)(2,1)S(1)}, bf16[144,384]{1,0:T(8,128)(2,1)S(1)}, u32[]{:S(2)}, u32[]{:S(2)}) %collective-permute-start.40) | collective-permute-done | bytes 110624 | tf_op jit(solution)/shard_map/ppermute | solution.py:27
  111.3 3.2 %collective-permute-done.41 = bf16[144,384]{1,0:T(8,128)(2,1)S(1)} collective-permute-done((bf16[144,384]{1,0:T(8,128)(2,1)S(1)}, bf16[144,384]{1,0:T(8,128)(2,1)S(1)}, u32[]{:S(2)}, u32[]{:S(2)}) %collective-permute-start.41) | collective-permute-done | bytes 110624 | tf_op jit(solution)/shard_map/ppermute | solution.py:27
  (93 shorter events, 22.5 us)
Async XLA Ops:
  2.5 8.3 %collective-permute-start.1 = (bf16[256,384]{1,0:T(8,128)(2,1)S(1)}, bf16[256,384]{1,0:T(8,128)(2,1)S(1)}, u32[]{:S(2)}, u32[]{:S(2)}) collective-permute-start(bf16[256,384]{1,0:T(8,128)(2,1)S(1)} %get-tuple-element.114), channel_id=1, source_target_pairs={{0,2},{1,3},{2,0},{3,1},{4,6},{5,7},{6,4},{7,5},{8,10},{9,11},{10,... | collective-permute-start | bytes 589832 | tf_op jit(solution)/shard_map/ppermute | solution.py:32
  5.1 9.4 %collective-permute-start.2 = (bf16[256,384]{1,0:T(8,128)(2,1)S(1)}, bf16[256,384]{1,0:T(8,128)(2,1)S(1)}, u32[]{:S(2)}, u32[]{:S(2)}) collective-permute-start(bf16[256,384]{1,0:T(8,128)(2,1)S(1)} %get-tuple-element.113), channel_id=1, source_target_pairs={{0,3},{1,2},{2,1},{3,0},{4,7},{5,6},{6,5},{7,4},{8,11},{9,10},{10,... | collective-permute-start | bytes 589832 | tf_op jit(solution)/shard_map/ppermute | solution.py:32
  15.3 12.3 %collective-permute-start.6 = (bf16[576,384]{1,0:T(8,128)(2,1)S(1)}, bf16[576,384]{1,0:T(8,128)(2,1)S(1)}, u32[]{:S(2)}, u32[]{:S(2)}) collective-permute-start(bf16[576,384]{1,0:T(8,128)(2,1)S(1)} %copy-done.4), channel_id=1, source_target_pairs={{0,2},{1,3},{2,0},{3,1},{4,6},{5,7},{6,4},{7,5},{8,10},{9,11},{10,... | collective-permute-start | bytes 1327112 | tf_op jit(solution)/shard_map/ppermute | solution.py:32
  16.9 16.2 %collective-permute-start.3 = (bf16[768,384]{1,0:T(8,128)(2,1)S(1)}, bf16[768,384]{1,0:T(8,128)(2,1)S(1)}, u32[]{:S(2)}, u32[]{:S(2)}) collective-permute-start(bf16[768,384]{1,0:T(8,128)(2,1)S(1)} %get-tuple-element.53), channel_id=1, source_target_pairs={{0,4},{4,8},{8,12},{1,5},{5,9},{9,13},{2,6},{6,10},{10,14},{3,7},{... | collective-permute-start | bytes 1769480 | tf_op jit(solution)/shard_map/ppermute | solution.py:22
  20.4 7.8 %collective-permute-start.5 = (bf16[576,384]{1,0:T(8,128)(2,1)S(1)}, bf16[576,384]{1,0:T(8,128)(2,1)S(1)}, u32[]{:S(2)}, u32[]{:S(2)}) collective-permute-start(bf16[576,384]{1,0:T(8,128)(2,1)S(1)} %copy-done.4), channel_id=1, source_target_pairs={{0,1},{1,0},{2,3},{3,2},{4,5},{5,4},{6,7},{7,6},{8,9},{9,8},{10,11... | collective-permute-start | bytes 1327112 | tf_op jit(solution)/shard_map/ppermute | solution.py:32
  20.5 17.6 %collective-permute-start.4 = (bf16[768,384]{1,0:T(8,128)(2,1)S(1)}, bf16[768,384]{1,0:T(8,128)(2,1)S(1)}, u32[]{:S(2)}, u32[]{:S(2)}) collective-permute-start(bf16[768,384]{1,0:T(8,128)(2,1)S(1)} %get-tuple-element.55), channel_id=1, source_target_pairs={{4,0},{8,4},{12,8},{5,1},{9,5},{13,9},{6,2},{10,6},{14,10},{7,3},{... | collective-permute-start | bytes 1769480 | tf_op jit(solution)/shard_map/ppermute | solution.py:22
  27.5 10.6 %collective-permute-start.7 = (bf16[576,384]{1,0:T(8,128)(2,1)S(1)}, bf16[576,384]{1,0:T(8,128)(2,1)S(1)}, u32[]{:S(2)}, u32[]{:S(2)}) collective-permute-start(bf16[576,384]{1,0:T(8,128)(2,1)S(1)} %collective-permute-done.6.refs_2_), channel_id=1, source_target_pairs={{0,1},{1,0},{2,3},{3,2},{4,5},{5,4},{6,7},{7,6},{8,9},{9,8},{10,11... | collective-permute-start | bytes 1327112 | tf_op jit(solution)/shard_map/ppermute | solution.py:32
  27.6 17.3 %collective-permute-start.8 = (bf16[256,384]{1,0:T(8,128)(2,1)S(1)}, bf16[256,384]{1,0:T(8,128)(2,1)S(1)}, u32[]{:S(2)}, u32[]{:S(2)}) collective-permute-start(bf16[256,384]{1,0:T(8,128)(2,1)S(1)} %get-tuple-element.112), channel_id=1, source_target_pairs={{0,1},{1,0},{2,3},{3,2},{4,5},{5,4},{6,7},{7,6},{8,9},{9,8},{10,11... | collective-permute-start | bytes 589832 | tf_op jit(solution)/shard_map/ppermute | solution.py:32
  28.2 16.7 %collective-permute-start.10 = (bf16[256,384]{1,0:T(8,128)(2,1)S(1)}, bf16[256,384]{1,0:T(8,128)(2,1)S(1)}, u32[]{:S(2)}, u32[]{:S(2)}) collective-permute-start(bf16[256,384]{1,0:T(8,128)(2,1)S(1)} %get-tuple-element.60), channel_id=1, source_target_pairs={{0,3},{1,2},{2,1},{3,0},{4,7},{5,6},{6,5},{7,4},{8,11},{9,10},{10,... | collective-permute-start | bytes 589832 | tf_op jit(solution)/shard_map/ppermute | solution.py:32
  33.1 11.8 %collective-permute-start.9 = (bf16[256,384]{1,0:T(8,128)(2,1)S(1)}, bf16[256,384]{1,0:T(8,128)(2,1)S(1)}, u32[]{:S(2)}, u32[]{:S(2)}) collective-permute-start(bf16[256,384]{1,0:T(8,128)(2,1)S(1)} %get-tuple-element.59), channel_id=1, source_target_pairs={{0,2},{1,3},{2,0},{3,1},{4,6},{5,7},{6,4},{7,5},{8,10},{9,11},{10,... | collective-permute-start | bytes 589832 | tf_op jit(solution)/shard_map/ppermute | solution.py:32
  45.8 11.7 %collective-permute-start.11 = (bf16[512,384]{1,0:T(8,128)(2,1)S(1)}, bf16[512,384]{1,0:T(8,128)(2,1)S(1)}, u32[]{:S(2)}, u32[]{:S(2)}) collective-permute-start(bf16[512,384]{1,0:T(8,128)(2,1)S(1)} %get-tuple-element.61), channel_id=1, source_target_pairs={{0,4},{4,8},{8,12},{1,5},{5,9},{9,13},{2,6},{6,10},{10,14},{3,7},{... | collective-permute-start | bytes 1179656 | tf_op jit(solution)/shard_map/ppermute | solution.py:22
  49.3 12.3 %collective-permute-start.12 = (bf16[512,384]{1,0:T(8,128)(2,1)S(1)}, bf16[512,384]{1,0:T(8,128)(2,1)S(1)}, u32[]{:S(2)}, u32[]{:S(2)}) collective-permute-start(bf16[512,384]{1,0:T(8,128)(2,1)S(1)} %get-tuple-element.63), channel_id=1, source_target_pairs={{4,0},{8,4},{12,8},{5,1},{9,5},{13,9},{6,2},{10,6},{14,10},{7,3},{... | collective-permute-start | bytes 1179656 | tf_op jit(solution)/shard_map/ppermute | solution.py:22
  54.5 12.3 %collective-permute-start.21 = (f32[72,384]{1,0:T(8,128)S(1)}, f32[72,384]{1,0:T(8,128)S(1)}, u32[]{:S(2)}, u32[]{:S(2)}) collective-permute-start(f32[72,384]{1,0:T(8,128)S(1)} %get-tuple-element.76), channel_id=1, source_target_pairs={{0,1},{1,0},{2,3},{3,2},{4,5},{5,4},{6,7},{7,6},{8,9},{9,8},{10,11... | collective-permute-start | bytes 331784 | tf_op jit(solution)/shard_map/ppermute | solution.py:32
  54.6 12.7 %collective-permute-start.22 = (f32[72,384]{1,0:T(8,128)S(1)}, f32[72,384]{1,0:T(8,128)S(1)}, u32[]{:S(2)}, u32[]{:S(2)}) collective-permute-start(f32[72,384]{1,0:T(8,128)S(1)} %get-tuple-element.77), channel_id=1, source_target_pairs={{0,1},{1,0},{2,3},{3,2},{4,5},{5,4},{6,7},{7,6},{8,9},{9,8},{10,11... | collective-permute-start | bytes 331784 | tf_op jit(solution)/shard_map/ppermute | solution.py:32
  55.0 12.4 %collective-permute-start.23 = (f32[72,384]{1,0:T(8,128)S(1)}, f32[72,384]{1,0:T(8,128)S(1)}, u32[]{:S(2)}, u32[]{:S(2)}) collective-permute-start(f32[72,384]{1,0:T(8,128)S(1)} %get-tuple-element.78), channel_id=1, source_target_pairs={{0,1},{1,0},{2,3},{3,2},{4,5},{5,4},{6,7},{7,6},{8,9},{9,8},{10,11... | collective-permute-start | bytes 331784 | tf_op jit(solution)/shard_map/ppermute | solution.py:32
  57.5 10.3 %collective-permute-start.24 = (f32[72,384]{1,0:T(8,128)S(1)}, f32[72,384]{1,0:T(8,128)S(1)}, u32[]{:S(2)}, u32[]{:S(2)}) collective-permute-start(f32[72,384]{1,0:T(8,128)S(1)} %get-tuple-element.79), channel_id=1, source_target_pairs={{0,1},{1,0},{2,3},{3,2},{4,5},{5,4},{6,7},{7,6},{8,9},{9,8},{10,11... | collective-permute-start | bytes 331784 | tf_op jit(solution)/shard_map/ppermute | solution.py:32
  61.6 6.2 %collective-permute-start.25 = (f32[72,384]{1,0:T(8,128)S(1)}, f32[72,384]{1,0:T(8,128)S(1)}, u32[]{:S(2)}, u32[]{:S(2)}) collective-permute-start(f32[72,384]{1,0:T(8,128)S(1)} %get-tuple-element.80), channel_id=1, source_target_pairs={{0,1},{1,0},{2,3},{3,2},{4,5},{5,4},{6,7},{7,6},{8,9},{9,8},{10,11... | collective-permute-start | bytes 331784 | tf_op jit(solution)/shard_map/ppermute | solution.py:32
  68.7 4.7 %collective-permute-start.31 = (f32[72,384]{1,0:T(8,128)S(1)}, f32[72,384]{1,0:T(8,128)S(1)}, u32[]{:S(2)}, u32[]{:S(2)}) collective-permute-start(f32[72,384]{1,0:T(8,128)S(1)} %get-tuple-element.89), channel_id=1, source_target_pairs={{0,1},{1,0},{2,3},{3,2},{4,5},{5,4},{6,7},{7,6},{8,9},{9,8},{10,11... | collective-permute-start | bytes 331784 | tf_op jit(solution)/shard_map/ppermute | solution.py:32
  69.1 7.4 %collective-permute-start.26 = (bf16[288,384]{1,0:T(8,128)(2,1)S(1)}, bf16[288,384]{1,0:T(8,128)(2,1)S(1)}, u32[]{:S(2)}, u32[]{:S(2)}) collective-permute-start(bf16[288,384]{1,0:T(8,128)(2,1)S(1)} %get-tuple-element.83), channel_id=1, source_target_pairs={{0,4},{4,0},{8,12},{12,8},{1,5},{5,1},{9,13},{13,9},{2,6},{6,2},{1... | collective-permute-start | bytes 663560 | tf_op jit(solution)/shard_map/ppermute | solution.py:32
  70.7 13.9 %collective-permute-start.13 = (bf16[256,384]{1,0:T(8,128)(2,1)S(1)}, bf16[256,384]{1,0:T(8,128)(2,1)S(1)}, u32[]{:S(2)}, u32[]{:S(2)}) collective-permute-start(bf16[256,384]{1,0:T(8,128)(2,1)S(1)} %get-tuple-element.68), channel_id=1, source_target_pairs={{0,4},{4,8},{8,12},{1,5},{5,9},{9,13},{2,6},{6,10},{10,14},{3,7},{... | collective-permute-start | bytes 589832 | tf_op jit(solution)/shard_map/ppermute | solution.py:22
  73.7 11.4 %collective-permute-start.14 = (bf16[256,384]{1,0:T(8,128)(2,1)}, bf16[256,384]{1,0:T(8,128)(2,1)S(1)}, u32[]{:S(2)}, u32[]{:S(2)}) collective-permute-start(bf16[256,384]{1,0:T(8,128)(2,1)} %get-tuple-element.69), channel_id=1, source_target_pairs={{4,0},{8,4},{12,8},{5,1},{9,5},{13,9},{6,2},{10,6},{14,10},{7,3},{... | collective-permute-start | bytes 589832 | tf_op jit(solution)/shard_map/ppermute | solution.py:22
  79.2 14.1 %collective-permute-start.35 = (bf16[144,384]{1,0:T(8,128)(2,1)}, bf16[144,384]{1,0:T(8,128)(2,1)}, u32[]{:S(2)}, u32[]{:S(2)}) collective-permute-start(bf16[144,384]{1,0:T(8,128)(2,1)} %get-tuple-element.96), channel_id=1, source_target_pairs={{0,8},{4,12},{8,0},{12,4},{1,9},{5,13},{9,1},{13,5},{2,10},{6,14},... | collective-permute-start | bytes 331784 | tf_op jit(solution)/shard_map/ppermute | solution.py:32
  80.5 12.8 %collective-permute-start.36 = (bf16[144,384]{1,0:T(8,128)(2,1)}, bf16[144,384]{1,0:T(8,128)(2,1)}, u32[]{:S(2)}, u32[]{:S(2)}) collective-permute-start(bf16[144,384]{1,0:T(8,128)(2,1)} %get-tuple-element.97), channel_id=1, source_target_pairs={{0,4},{4,8},{8,12},{12,0},{1,5},{5,9},{9,13},{13,1},{2,6},{6,10},{... | collective-permute-start | bytes 331784 | tf_op jit(solution)/shard_map/ppermute | solution.py:27
  81.6 14.0 %collective-permute-start.37 = (bf16[144,384]{1,0:T(8,128)(2,1)}, bf16[144,384]{1,0:T(8,128)(2,1)}, u32[]{:S(2)}, u32[]{:S(2)}) collective-permute-start(bf16[144,384]{1,0:T(8,128)(2,1)} %get-tuple-element.98), channel_id=1, source_target_pairs={{0,8},{4,12},{8,0},{12,4},{1,9},{5,13},{9,1},{13,5},{2,10},{6,14},... | collective-permute-start | bytes 331784 | tf_op jit(solution)/shard_map/ppermute | solution.py:27
  84.6 11.1 %collective-permute-start.38 = (bf16[144,384]{1,0:T(8,128)(2,1)S(1)}, bf16[144,384]{1,0:T(8,128)(2,1)}, u32[]{:S(2)}, u32[]{:S(2)}) collective-permute-start(bf16[144,384]{1,0:T(8,128)(2,1)S(1)} %get-tuple-element.99), channel_id=1, source_target_pairs={{0,12},{4,0},{8,4},{12,8},{1,13},{5,1},{9,5},{13,9},{2,14},{6,2},{... | collective-permute-start | bytes 331784 | tf_op jit(solution)/shard_map/ppermute | solution.py:27
  96.8 5.8 %collective-permute-start.39 = (bf16[1,144,384]{2,1,0:T(8,128)(2,1)S(1)}, bf16[1,144,384]{2,1,0:T(8,128)(2,1)S(1)}, u32[]{:S(2)}, u32[]{:S(2)}) collective-permute-start(bf16[1,144,384]{2,1,0:T(8,128)(2,1)S(1)} %fusion), channel_id=1, source_target_pairs={{0,2},{1,3},{2,0},{3,1},{4,6},{5,7},{6,4},{7,5},{8,10},{9,11},{10,... | collective-permute-start | bytes 331784 | tf_op jit(solution)/shard_map/ppermute | solution.py:32
  97.5 10.4 %collective-permute-start.15 = (bf16[256,384]{1,0:T(8,128)(2,1)S(1)}, bf16[256,384]{1,0:T(8,128)(2,1)S(1)}, u32[]{:S(2)}, u32[]{:S(2)}) collective-permute-start(bf16[256,384]{1,0:T(8,128)(2,1)S(1)} %get-tuple-element.108), channel_id=1, source_target_pairs={{0,1},{1,0},{2,3},{3,2},{4,5},{5,4},{6,7},{7,6},{8,9},{9,8},{10,11... | collective-permute-start | bytes 589832 | tf_op jit(solution)/shard_map/ppermute | solution.py:32
  97.6 10.5 %collective-permute-start.16 = (bf16[256,384]{1,0:T(8,128)(2,1)S(1)}, bf16[256,384]{1,0:T(8,128)(2,1)S(1)}, u32[]{:S(2)}, u32[]{:S(2)}) collective-permute-start(bf16[256,384]{1,0:T(8,128)(2,1)S(1)} %get-tuple-element.107), channel_id=1, source_target_pairs={{0,2},{1,3},{2,0},{3,1},{4,6},{5,7},{6,4},{7,5},{8,10},{9,11},{10,... | collective-permute-start | bytes 589832 | tf_op jit(solution)/shard_map/ppermute | solution.py:32
  99.1 10.0 %collective-permute-start.17 = (bf16[256,384]{1,0:T(8,128)(2,1)S(1)}, bf16[256,384]{1,0:T(8,128)(2,1)S(1)}, u32[]{:S(2)}, u32[]{:S(2)}) collective-permute-start(bf16[256,384]{1,0:T(8,128)(2,1)S(1)} %get-tuple-element.106), channel_id=1, source_target_pairs={{0,3},{1,2},{2,1},{3,0},{4,7},{5,6},{6,5},{7,4},{8,11},{9,10},{10,... | collective-permute-start | bytes 589832 | tf_op jit(solution)/shard_map/ppermute | solution.py:32
  103.8 7.5 %collective-permute-start.40 = (bf16[144,384]{1,0:T(8,128)(2,1)S(1)}, bf16[144,384]{1,0:T(8,128)(2,1)S(1)}, u32[]{:S(2)}, u32[]{:S(2)}) collective-permute-start(bf16[144,384]{1,0:T(8,128)(2,1)S(1)} %bitcast.11), channel_id=1, source_target_pairs={{0,4},{4,8},{8,12},{12,0},{1,5},{5,9},{9,13},{13,1},{2,6},{6,10},{... | collective-permute-start | bytes 331784 | tf_op jit(solution)/shard_map/ppermute | solution.py:27
  105.6 8.8 %collective-permute-start.41 = (bf16[144,384]{1,0:T(8,128)(2,1)S(1)}, bf16[144,384]{1,0:T(8,128)(2,1)S(1)}, u32[]{:S(2)}, u32[]{:S(2)}) collective-permute-start(bf16[144,384]{1,0:T(8,128)(2,1)S(1)} %bitcast.12), channel_id=1, source_target_pairs={{0,8},{4,12},{8,0},{12,4},{1,9},{5,13},{9,1},{13,5},{2,10},{6,14},... | collective-permute-start | bytes 331784 | tf_op jit(solution)/shard_map/ppermute | solution.py:27
  107.9 6.6 %collective-permute-start.42 = (bf16[144,384]{1,0:T(8,128)(2,1)S(1)}, bf16[144,384]{1,0:T(8,128)(2,1)S(1)}, u32[]{:S(2)}, u32[]{:S(2)}) collective-permute-start(bf16[144,384]{1,0:T(8,128)(2,1)S(1)} %bitcast.13), channel_id=1, source_target_pairs={{0,12},{4,0},{8,4},{12,8},{1,13},{5,1},{9,5},{13,9},{2,14},{6,2},{... | collective-permute-start | bytes 331784 | tf_op jit(solution)/shard_map/ppermute | solution.py:27
  (18 other events, 95.5 us)

commit v5 on v4

--- a/solution.py
+++ b/solution.py
@@ -122,26 +122,52 @@
             return high[(b - members) * q : (b - members + 1) * q]
         return own[b * q : (b + 1) * q]
 
-    for b in range(-far, members + far):
-        stack = jnp.concatenate([block(b - near), block(b), block(b + near)], 1)
-        pre = dot(stack, w_out[:taps])
-        th, square = gelu_parts(pre)
-        half = 0.5 * pre
-        value = (block(b).astype(F32) + (half + half * th)).astype(BF16)
-        if b < 0:
-            value = jnp.where(s > 0, value, jnp.zeros_like(value))
-        if b >= members:
-            value = jnp.where(s < groups - 1, value, jnp.zeros_like(value))
-        hid[b + far] = value
-        if 0 <= b < members:
-            slope_one[b * q : (b + 1) * q] = slope_of(pre, th, square)
-            act_stack[b * q : (b + 1) * q] = stack
-    for b in range(members):
-        stack = jnp.concatenate([hid[b], hid[b + far], hid[b + 2 * far]], 1)
-        here = slice(b * q, (b + 1) * q)
-        hid_stack[here] = stack
-        pre = dot(stack, w_out[taps:])
-        slope_two[here] = slope_of(pre, *gelu_parts(pre))
+    wide = 2 if far % 2 == 0 and members % 2 == 0 else 1
+
+    def first_layer(k):
+        stacks = []
+        for b in range(k - far, k - far + wide):
+            stacks.append(jnp.concatenate([block(b - near), block(b), block(b + near)], 1))
+            if 0 <= b < members:
+                act_stack[b * q : (b + 1) * q] = stacks[-1]
+        return dot(jnp.concatenate(stacks, 0), w_out[:taps])
+
+    def first_end(k, pres):
+        for b in range(k - far, k - far + wide):
+            pre = pres[(b + far - k) * q : (b + far - k + 1) * q]
+            th, square = gelu_parts(pre)
+            half = 0.5 * pre
+            value = (block(b).astype(F32) + (half + half * th)).astype(BF16)
+            if b < 0:
+                value = jnp.where(s > 0, value, jnp.zeros_like(value))
+            if b >= members:
+                value = jnp.where(s < groups - 1, value, jnp.zeros_like(value))
+            hid[(b + far) * q : (b + far + 1) * q] = value
+            if 0 <= b < members:
+                slope_one[b * q : (b + 1) * q] = slope_of(pre, th, square)
+
+    def second_layer(b):
+        taken = [hid[(b + k * far) * q : (b + k * far + wide) * q] for k in range(3)]
+        stack = jnp.concatenate(taken, 1)
+        hid_stack[b * q : (b + wide) * q] = stack
+        return dot(stack, w_out[taps:])
+
+    def second_end(b, pre):
+        slope_two[b * q : (b + wide) * q] = slope_of(pre, *gelu_parts(pre))
+
+    order, begun = [], 0
+    for k in range(0, members + 2 * far, wide):
+        order.append((first_layer, first_end, k))
+        if k > 2 * far:
+            order.append((second_layer, second_end, begun))
+            begun += wide
+    order += [(second_layer, second_end, b) for b in range(begun, members, wide)]
+    last = None
+    for product, end, index in order + [(None, None, None)]:
+        value = product(index) if product else None
+        if last:
+            last[0](last[1], last[2])
+        last = (end, index, value)
 
 
 def delta_kernel(sizes, place, slope, cotangent, *refs):
@@ -216,8 +242,8 @@
         outs[turn][...] = total[at, :].astype(outs[turn].dtype)
 
 
-def halve_kernel(bit, place, keep, *refs):
-    others, (kept, sent, total) = refs[:-3], refs[-3:]
+def halve_kernel(bit, count, place, keep, *refs):
+    others, (kept, sent, total) = refs[:count], refs[-3:]
     rows = keep.shape[0] // len(others)
     for i, other in enumerate(others):
         here = slice(i * rows, (i + 1) * rows)
@@ -298,25 +324,25 @@
     return [shares[0]] + [turned(shares[t], "seq", t) for t in range(1, len(shares))]
 
 
-def halved(place, keep, others, bit):
+def halved(place, keep, others, bit, waits=()):
     rows, channels = keep.shape
     shape = (rows // 2, channels)
     return call(
-        functools.partial(halve_kernel, bit),
+        functools.partial(halve_kernel, bit, len(others)),
         ((shape, F32), (shape, BF16)),
         scratch=(pltpu.VMEM((rows, channels), F32),),
         scalars=1,
-        operands=(place, keep, *others),
-    )
-
-
-def core_sum_halving(place, keep, sends):
+        operands=(place, keep, *others, *waits),
+    )
+
+
+def core_sum_halving(place, keep, sends, waits=()):
     others = [swapped(send, "sub", 1) for send in sends]
     n = lax.axis_size("seq")
     if n > 4:
         total = keep + jnp.concatenate(others, 0)
         return total, total
-    return halved(place, keep, others, 1)
+    return halved(place, keep, others, 1, waits)
 
 
 def first_half(sent):
@@ -329,7 +355,8 @@
         return lax.psum(kept, "seq")
     bit = 2
     while bit < n:
-        kept, sent = halved(place, kept, [after(got, others)], bit)
+        came = got if others is None else after(got, others)
+        kept, sent = halved(place, kept, [came], bit)
         got = swapped(sent, "seq", bit)
         bit *= 2
     return added([kept, got])
@@ -411,7 +438,7 @@
         ((count, channels), F32),
         ((count, channels), F32),
         ((2 * taps, channels), BF16),
-        scratch=(pltpu.VMEM((members + 2 * far, q, channels), BF16),),
+        scratch=(pltpu.VMEM(((members + 2 * far) * q, channels), BF16),),
         operands=(low, act, high, *w_pieces),
     )
     delta_two, up_two, down_two, cot = kernel(
@@ -423,7 +450,7 @@
         operands=(slope_two, cotangent, *c_pieces),
     )
     two_low, two_high = shifted(up_two, "seq", 1), shifted(down_two, "seq", -1)
-    splits, more = 8, 8
+    splits, more = 8, 4
     half = ((taps // 2, channels), F32)
     share = ((taps // 2 // splits, channels), F32)
     less = ((taps // 2 // more, channels), F32)
@@ -448,13 +475,12 @@
         operands=(act_stack, delta_one),
     )
     got_two = first_half(after(sent_two, (two_low, two_high)))
-    shares_one = core_sum(place, keep_one, send_one, (got_two,))
+    kept_one, sent_one = core_sum_halving(place, keep_one, send_one, (got_two,))
+    got_one = first_half(sent_one)
+    up_one, down_one = after((up_one, down_one), sent_one)
     one_low, one_high = shifted(up_one, "seq", 1), shifted(down_one, "seq", -1)
-    parts_one = seq_parts(shares_one)
-    total_two = seq_sum_halving(place, kept_two, got_two, shares_one[0])
-    total_one = added(parts_one)
-    part = chip_sum(total_one, total_two, j)
-    sent = part.astype(BF16)
+    total_two = seq_sum_halving(place, kept_two, got_two, sent_one)
+    total_one = seq_sum_halving(place, kept_one, got_one, None)
 
     (grad_in,) = call(
         functools.partial(input_kernel, (members, q, near)),
@@ -462,6 +488,9 @@
         scalars=1,
         operands=(place, one_low, delta_one, one_high, back_one, all_weights),
     )
+    total_one = after(total_one, grad_in)
+    part = chip_sum(total_one, total_two, j)
+    sent = part.astype(BF16)
     got = [grad_in[r * q : (r + 1) * q] for r in range(members)]
     got = got[:1] + [swapped(got[r], "sub", r) for r in range(1, members)]
     got = after(got, sent)

time: 116 us -> 110 us (0.948)
  waiting for transfers between devices: 48 us -> 45 us
  other arithmetic: 2.44 us -> 1.17 us
    ppermute x6 -> x3, starting transfers between devices: 8.86 us -> 4.59 us  [turned(): return lax.ppermute(block, axis, [(i, (i + turn) % n) for i in range(n)])]
    ppermute x6 -> x3, waiting for transfers between devices: 7.46 us -> 3.27 us  [turned(): return lax.ppermute(block, axis, [(i, (i + turn) % n) for i in range(n)])]
    ppermute x31 -> x29, waiting for transfers between devices: 26.1 us -> 28.2 us  [swapped(): return lax.ppermute(block, axis, [(i, i ^ bits) for i in range(n)])]
    ppermute x6, starting transfers between devices: 13.2 us -> 15 us  [shifted(): return lax.ppermute(block, axis, route)]
    ppermute x31 -> x29, starting transfers between devices: 16.2 us -> 17.8 us  [swapped(): return lax.ppermute(block, axis, [(i, i ^ bits) for i in range(n)])]
    pallas_call x10 -> x11, Pallas kernels: 21.6 us -> 21.2 us  [call(): pl.pallas_call(kernel, out_shape=tuple((jax.ShapeDtypeStruct(shape, kind)...]
  transfers between devices with their start and end apart: 43 -> 38, of which waited for: 15 -> 22; matrix products, arithmetic and copies ran while one was open for 1% -> 1% of each run, Pallas kernels for 17% -> 17%
where the time goes in v5:
time: 110 us
  waiting for transfers between devices  45 us (41%)
  starting transfers between devices  37.4 us (34%)
  Pallas kernels  21.2 us (19%)
  local copies, waits for them, and re-layouts  4.07 us (4%)
  other arithmetic  1.17 us (1%)
    ppermute x29, waiting for transfers between devices, swapped(): return lax.ppermute(block, axis, [(i, i ^ bits) for i in range(n)])  28.2 us
    pallas_call x11, Pallas kernels, call(): pl.pallas_call(kernel, out_shape=tuple((jax.ShapeDtypeStruct(shape, kind)...  21.2 us
    ppermute x29, starting transfers between devices, swapped(): return lax.ppermute(block, axis, [(i, i ^ bits) for i in range(n)])  17.8 us
    ppermute x6, starting transfers between devices, shifted(): return lax.ppermute(block, axis, route)  15 us
    ppermute x6, waiting for transfers between devices, shifted(): return lax.ppermute(block, axis, route)  13.5 us
    ppermute x3, starting transfers between devices, turned(): return lax.ppermute(block, axis, [(i, (i + turn) % n) for i in range(n)])  4.59 us
    ppermute x3, waiting for transfers between devices, turned(): return lax.ppermute(block, axis, [(i, (i + turn) % n) for i in range(n)])  3.27 us
    unnamed x14, local copies, waits for them, and re-layouts  2.34 us
  transfers between devices with their start and end apart: 38, of which 22 were waited for; matrix products, arithmetic and copies ran while one was open for 1% of the time, Pallas kernels for 17%

profile of v5, /device:TPU:0, one launch (start us, length us, event | category | flops | bytes accessed | tf_op | source)
XLA Modules:
  0.0 109.9 jit_solution(1688742561926571462)
XLA Ops:
  0.7 1.3 %constant_dynamic-slice_fusion.3 = (bf16[256,384]{1,0:T(8,128)(2,1)S(1)}, bf16[256,384]{1,0:T(8,128)(2,1)S(1)}, bf16[256,384]{1,0:T(8,128)(2,1)S(1)}) fusion(bf16[1024,384]{1,0:T(8,128)(2,1)} %block.1, s32[]{:T(128)S(6)} %select_n.66, s32[]{:T(128)S(6)} %select_n.65, s32[]{:T(128)S(6)} %select_n.64), kind=kLoop, calls=%fused_computation.17 | loop fusion | bytes 1179660 | tf_op jit(solution)/shard_map/dynamic_slice | solution.py:48
  2.5 2.6 %collective-permute-start.1 = (bf16[256,384]{1,0:T(8,128)(2,1)S(1)}, bf16[256,384]{1,0:T(8,128)(2,1)S(1)}, u32[]{:S(2)}, u32[]{:S(2)}) collective-permute-start(bf16[256,384]{1,0:T(8,128)(2,1)S(1)} %get-tuple-element.112), channel_id=1, source_target_pairs={{0,2},{1,3},{2,0},{3,1},{4,6},{5,7},{6,4},{7,5},{8,10},{9,11},{10,... | collective-permute-start | bytes 589832 | tf_op jit(solution)/shard_map/ppermute | solution.py:32
  5.2 5.6 %collective-permute-done.1.refs_1_ = bf16[256,384]{1,0:T(8,128)(2,1)S(1)} collective-permute-done((bf16[256,384]{1,0:T(8,128)(2,1)S(1)}, bf16[256,384]{1,0:T(8,128)(2,1)S(1)}, u32[]{:S(2)}, u32[]{:S(2)}) %collective-permute-start.1) | collective-permute-done | bytes 196640 | tf_op jit(solution)/shard_map/ppermute | solution.py:32
  10.8 3.7 %collective-permute-done.2.refs_2_ = bf16[256,384]{1,0:T(8,128)(2,1)S(1)} collective-permute-done((bf16[256,384]{1,0:T(8,128)(2,1)S(1)}, bf16[256,384]{1,0:T(8,128)(2,1)S(1)}, u32[]{:S(2)}, u32[]{:S(2)}) %collective-permute-start.2) | collective-permute-done | bytes 196640 | tf_op jit(solution)/shard_map/ppermute | solution.py:32
  15.3 1.6 %collective-permute-start.6 = (bf16[576,384]{1,0:T(8,128)(2,1)S(1)}, bf16[576,384]{1,0:T(8,128)(2,1)S(1)}, u32[]{:S(2)}, u32[]{:S(2)}) collective-permute-start(bf16[576,384]{1,0:T(8,128)(2,1)S(1)} %copy-done.4), channel_id=1, source_target_pairs={{0,2},{1,3},{2,0},{3,1},{4,6},{5,7},{6,4},{7,5},{8,10},{9,11},{10,... | collective-permute-start | bytes 1327112 | tf_op jit(solution)/shard_map/ppermute | solution.py:32
  16.9 3.5 %collective-permute-start.3 = (bf16[768,384]{1,0:T(8,128)(2,1)S(1)}, bf16[768,384]{1,0:T(8,128)(2,1)S(1)}, u32[]{:S(2)}, u32[]{:S(2)}) collective-permute-start(bf16[768,384]{1,0:T(8,128)(2,1)S(1)} %get-tuple-element.52), channel_id=1, source_target_pairs={{0,4},{4,8},{8,12},{1,5},{5,9},{9,13},{2,6},{6,10},{10,14},{3,7},{... | collective-permute-start | bytes 1769480 | tf_op jit(solution)/shard_map/ppermute | solution.py:22
  20.5 1.3 %collective-permute-start.4 = (bf16[768,384]{1,0:T(8,128)(2,1)S(1)}, bf16[768,384]{1,0:T(8,128)(2,1)S(1)}, u32[]{:S(2)}, u32[]{:S(2)}) collective-permute-start(bf16[768,384]{1,0:T(8,128)(2,1)S(1)} %get-tuple-element.54), channel_id=1, source_target_pairs={{4,0},{8,4},{12,8},{5,1},{9,5},{13,9},{6,2},{10,6},{14,10},{7,3},{... | collective-permute-start | bytes 1769480 | tf_op jit(solution)/shard_map/ppermute | solution.py:22
  21.8 5.7 %collective-permute-done.6.refs_2_ = bf16[576,384]{1,0:T(8,128)(2,1)S(1)} collective-permute-done((bf16[576,384]{1,0:T(8,128)(2,1)S(1)}, bf16[576,384]{1,0:T(8,128)(2,1)S(1)}, u32[]{:S(2)}, u32[]{:S(2)}) %collective-permute-start.6) | collective-permute-done | bytes 442400 | tf_op jit(solution)/shard_map/ppermute | solution.py:32
  28.2 1.4 %collective-permute-start.10 = (bf16[256,384]{1,0:T(8,128)(2,1)S(1)}, bf16[256,384]{1,0:T(8,128)(2,1)S(1)}, u32[]{:S(2)}, u32[]{:S(2)}) collective-permute-start(bf16[256,384]{1,0:T(8,128)(2,1)S(1)} %get-tuple-element.59), channel_id=1, source_target_pairs={{0,3},{1,2},{2,1},{3,0},{4,7},{5,6},{6,5},{7,4},{8,11},{9,10},{10,... | collective-permute-start | bytes 589832 | tf_op jit(solution)/shard_map/ppermute | solution.py:32
  29.6 3.5 %collective-permute-done.3.low = bf16[768,384]{1,0:T(8,128)(2,1)S(1)} collective-permute-done((bf16[768,384]{1,0:T(8,128)(2,1)S(1)}, bf16[768,384]{1,0:T(8,128)(2,1)S(1)}, u32[]{:S(2)}, u32[]{:S(2)}) %collective-permute-start.3) | collective-permute-done | bytes 589856 | tf_op jit(solution)/shard_map/ppermute | solution.py:22
  33.6 4.5 %collective-permute-done.4.high = bf16[768,384]{1,0:T(8,128)(2,1)S(1)} collective-permute-done((bf16[768,384]{1,0:T(8,128)(2,1)S(1)}, bf16[768,384]{1,0:T(8,128)(2,1)S(1)}, u32[]{:S(2)}, u32[]{:S(2)}) %collective-permute-start.4) | collective-permute-done | bytes 589856 | tf_op jit(solution)/shard_map/ppermute | solution.py:22
  38.1 6.4 %shard_map.51 = (bf16[1024,1152]{1,0:T(8,128)(2,1)S(1)}, bf16[1024,1152]{1,0:T(8,128)(2,1)S(1)}, f32[1024,384]{1,0:T(8,128)S(1)}, f32[1024,384]{1,0:T(8,128)S(1)}, bf16[2304,384]{1,0:T(8,128)(2,1)S(1)}) custom-call(s32[2]{0:T(128)S(1)} %pad_add_fusion.place, bf16[768,384]{1,0:T(8,128)(2,1)S(1)} %collective-permute-done.3.low, ...), custom_call_target="tpu_custom_call" | custom-call | flops 1 | bytes 1 | tf_op jit(solution)/shard_map/pallas_call | solution.py:295
  45.5 3.5 %collective-permute-start.11 = (bf16[512,384]{1,0:T(8,128)(2,1)S(1)}, bf16[512,384]{1,0:T(8,128)(2,1)S(1)}, u32[]{:S(2)}, u32[]{:S(2)}) collective-permute-start(bf16[512,384]{1,0:T(8,128)(2,1)S(1)} %get-tuple-element.60), channel_id=1, source_target_pairs={{0,4},{4,8},{8,12},{1,5},{5,9},{9,13},{2,6},{6,10},{10,14},{3,7},{... | collective-permute-start | bytes 1179656 | tf_op jit(solution)/shard_map/ppermute | solution.py:22
  49.0 1.3 %collective-permute-start.12 = (bf16[512,384]{1,0:T(8,128)(2,1)S(1)}, bf16[512,384]{1,0:T(8,128)(2,1)S(1)}, u32[]{:S(2)}, u32[]{:S(2)}) collective-permute-start(bf16[512,384]{1,0:T(8,128)(2,1)S(1)} %get-tuple-element.62), channel_id=1, source_target_pairs={{4,0},{8,4},{12,8},{5,1},{9,5},{13,9},{6,2},{10,6},{14,10},{7,3},{... | collective-permute-start | bytes 1179656 | tf_op jit(solution)/shard_map/ppermute | solution.py:22
  50.3 2.5 %shard_map.55 = (f32[576,384]{1,0:T(8,128)S(1)}, f32[72,384]{1,0:T(8,128)S(1)}, f32[72,384]{1,0:T(8,128)S(1)}, f32[72,384]{1,0:T(8,128)S(1)}, f32[72,384]{1,0:T(...) custom-call(s32[2]{0:T(128)S(1)} %pad_add_fusion.place, ...), custom_call_target="tpu_custom_call" | custom-call | flops 1 | bytes 1 | tf_op jit(solution)/shard_map/pallas_call | solution.py:295
  57.7 3.6 %collective-permute-done.12.high = bf16[512,384]{1,0:T(8,128)(2,1)S(1)} collective-permute-done((bf16[512,384]{1,0:T(8,128)(2,1)S(1)}, bf16[512,384]{1,0:T(8,128)(2,1)S(1)}, u32[]{:S(2)}, u32[]{:S(2)}) %collective-permute-start.12) | collective-permute-done | bytes 393248 | tf_op jit(solution)/shard_map/ppermute | solution.py:22
  61.3 1.6 %collective-permute-start.25 = (bf16[288,384]{1,0:T(8,128)(2,1)S(1)}, bf16[288,384]{1,0:T(8,128)(2,1)S(1)}, u32[]{:S(2)}, u32[]{:S(2)}) collective-permute-start(bf16[288,384]{1,0:T(8,128)(2,1)S(1)} %get-tuple-element.85), channel_id=1, source_target_pairs={{0,4},{4,0},{8,12},{12,8},{1,5},{5,1},{9,13},{13,9},{2,6},{6,2},{1... | collective-permute-start | bytes 663560 | tf_op jit(solution)/shard_map/ppermute | solution.py:32
  62.9 1.8 %shard_map.53 = (f32[1024,384]{1,0:T(8,128)S(1)}, bf16[1024,384]{1,0:T(8,128)(2,1)S(1)}) custom-call(bf16[512,384]{1,0:T(8,128)(2,1)S(1)} %collective-permute-done.11.low, bf16[1024,384]{1,0:T(8,128)(2,1)S(1)} %get-tuple-element.61.own.delta, bf16[512,384]{1,0:T(8,128)(2,1)S(1)} %collective-permute-done.12.high, ...), custom_call_target="tpu_custom_call" | custom-call | flops 1 | bytes 1 | tf_op jit(solution)/shard_map/pallas_call | solution.py:295
  64.7 3.4 %shard_map.54 = (f32[576,384]{1,0:T(8,128)S(1)}, f32[144,384]{1,0:T(8,128)S(1)}, f32[144,384]{1,0:T(8,128)S(1)}, f32[144,384]{1,0:T(8,128)S(1)}, f32[144,384]{1,...) custom-call(s32[2]{0:T(128)S(1)} %pad_add_fusion.place, ...), custom_call_target="tpu_custom_call" | custom-call | flops 1 | bytes 1 | tf_op jit(solution)/shard_map/pallas_call | solution.py:295
  71.8 4.1 %collective-permute-start.26 = (bf16[256,384]{1,0:T(8,128)(2,1)}, bf16[256,384]{1,0:T(8,128)(2,1)}, u32[]{:S(2)}, u32[]{:S(2)}) collective-permute-start(bf16[256,384]{1,0:T(8,128)(2,1)} %get-tuple-element.87), channel_id=1, source_target_pairs={{0,4},{4,8},{8,12},{1,5},{5,9},{9,13},{2,6},{6,10},{10,14},{3,7},{... | collective-permute-start | bytes 589832 | tf_op jit(solution)/shard_map/ppermute | solution.py:22
  77.2 1.6 %collective-permute-done.32.refs_0_ = bf16[288,384]{1,0:T(8,128)(2,1)S(1)} collective-permute-done((bf16[288,384]{1,0:T(8,128)(2,1)S(1)}, bf16[288,384]{1,0:T(8,128)(2,1)S(1)}, u32[]{:S(2)}, u32[]{:S(2)}) %collective-permute-start.32) | collective-permute-done | bytes 221216 | tf_op jit(solution)/shard_map/ppermute | solution.py:32
  80.3 2.8 %collective-permute-start.31 = (bf16[144,384]{1,0:T(8,128)(2,1)S(1)}, bf16[144,384]{1,0:T(8,128)(2,1)S(1)}, u32[]{:S(2)}, u32[]{:S(2)}) collective-permute-start(bf16[144,384]{1,0:T(8,128)(2,1)S(1)} %get-tuple-element.93), channel_id=1, source_target_pairs={{0,8},{4,12},{8,0},{12,4},{1,9},{5,13},{9,1},{13,5},{2,10},{6,14},... | collective-permute-start | bytes 331784 | tf_op jit(solution)/shard_map/ppermute | solution.py:32
  83.1 1.9 %collective-permute-done.27.high = bf16[256,384]{1,0:T(8,128)(2,1)} collective-permute-done((bf16[256,384]{1,0:T(8,128)(2,1)}, bf16[256,384]{1,0:T(8,128)(2,1)}, u32[]{:S(2)}, u32[]{:S(2)}) %collective-permute-start.27) | collective-permute-done | bytes 196640 | tf_op jit(solution)/shard_map/ppermute | solution.py:22
  85.0 1.4 %copy-done.3 = f32[1024,384]{1,0:T(8,128)S(1)} copy-done((f32[1024,384]{1,0:T(8,128)S(1)}, f32[1024,384]{1,0:T(8,128)}, u32[]{:S(2)}) %copy-start.3) | copy-done | bytes 1572888
  86.4 2.8 %shard_map.58 = bf16[1024,384]{1,0:T(8,128)(2,1)S(1)} custom-call(s32[2]{0:T(128)S(1)} %pad_add_fusion.place, bf16[256,384]{1,0:T(8,128)(2,1)} %collective-permute-done.26.low, bf16[1024,384]{1,0:T(8,128)(2,1)S(1)} %get-tuple-element.66.delta.own, bf16[256,384]{1,0:T(8,128)(2,1)} %collective-permute-done.27.high, f32[1024,384]{1,0:T(8,128)S(1)} %copy-done.3, ...), custom_call_target="tpu_custom_call" | custom-call | flops 1 | bytes 1 | tf_op jit(solution)/shard_map/pallas_call | solution.py:295
  89.2 2.6 %collective-permute-done.33 = bf16[144,384]{1,0:T(8,128)(2,1)} collective-permute-done((bf16[144,384]{1,0:T(8,128)(2,1)S(1)}, bf16[144,384]{1,0:T(8,128)(2,1)}, u32[]{:S(2)}, u32[]{:S(2)}) %collective-permute-start.33) | collective-permute-done | bytes 110624 | tf_op jit(solution)/shard_map/ppermute | solution.py:32
  93.8 1.6 %collective-permute-start.29 = (bf16[256,384]{1,0:T(8,128)(2,1)S(1)}, bf16[256,384]{1,0:T(8,128)(2,1)S(1)}, u32[]{:S(2)}, u32[]{:S(2)}) collective-permute-start(bf16[256,384]{1,0:T(8,128)(2,1)S(1)} %get-tuple-element.105), channel_id=1, source_target_pairs={{0,2},{1,3},{2,0},{3,1},{4,6},{5,7},{6,4},{7,5},{8,10},{9,11},{10,... | collective-permute-start | bytes 589832 | tf_op jit(solution)/shard_map/ppermute | solution.py:32
  95.6 3.2 %collective-permute-done.34 = bf16[1,144,384]{2,1,0:T(8,128)(2,1)S(1)} collective-permute-done((bf16[1,144,384]{2,1,0:T(8,128)(2,1)S(1)}, bf16[1,144,384]{2,1,0:T(8,128)(2,1)S(1)}, u32[]{:S(2)}, u32[]{:S(2)}) %collective-permute-start.34) | collective-permute-done | bytes 110624 | tf_op jit(solution)/shard_map/ppermute | solution.py:32
  98.9 2.1 %collective-permute-start.35 = (bf16[144,384]{1,0:T(8,128)(2,1)S(1)}, bf16[144,384]{1,0:T(8,128)(2,1)S(1)}, u32[]{:S(2)}, u32[]{:S(2)}) collective-permute-start(bf16[144,384]{1,0:T(8,128)(2,1)S(1)} %bitcast.11), channel_id=1, source_target_pairs={{0,4},{4,8},{8,12},{12,0},{1,5},{5,9},{9,13},{13,1},{2,6},{6,10},{... | collective-permute-start | bytes 331784 | tf_op jit(solution)/shard_map/ppermute | solution.py:27
  101.1 2.4 %collective-permute-start.37 = (bf16[144,384]{1,0:T(8,128)(2,1)S(1)}, bf16[144,384]{1,0:T(8,128)(2,1)S(1)}, u32[]{:S(2)}, u32[]{:S(2)}) collective-permute-start(bf16[144,384]{1,0:T(8,128)(2,1)S(1)} %bitcast.13), channel_id=1, source_target_pairs={{0,12},{4,0},{8,4},{12,8},{1,13},{5,1},{9,5},{13,9},{2,14},{6,2},{... | collective-permute-start | bytes 331784 | tf_op jit(solution)/shard_map/ppermute | solution.py:27
  103.5 1.8 %collective-permute-done.30 = bf16[256,384]{1,0:T(8,128)(2,1)S(1)} collective-permute-done((bf16[256,384]{1,0:T(8,128)(2,1)S(1)}, bf16[256,384]{1,0:T(8,128)(2,1)S(1)}, u32[]{:S(2)}, u32[]{:S(2)}) %collective-permute-start.30) | collective-permute-done | bytes 196640 | tf_op jit(solution)/shard_map/ppermute | solution.py:32
  105.7 3.1 %collective-permute-done.36 = bf16[144,384]{1,0:T(8,128)(2,1)S(1)} collective-permute-done((bf16[144,384]{1,0:T(8,128)(2,1)S(1)}, bf16[144,384]{1,0:T(8,128)(2,1)S(1)}, u32[]{:S(2)}, u32[]{:S(2)}) %collective-permute-start.36) | collective-permute-done | bytes 110624 | tf_op jit(solution)/shard_map/ppermute | solution.py:27
  (85 shorter events, 18.6 us)
Async XLA Ops:
  2.0 3.2 %collective-permute-start = (bf16[256,384]{1,0:T(8,128)(2,1)S(1)}, bf16[256,384]{1,0:T(8,128)(2,1)S(1)}, u32[]{:S(2)}, u32[]{:S(2)}) collective-permute-start(bf16[256,384]{1,0:T(8,128)(2,1)S(1)} %get-tuple-element.113), channel_id=1, source_target_pairs={{0,1},{1,0},{2,3},{3,2},{4,5},{5,4},{6,7},{7,6},{8,9},{9,8},{10,11... | collective-permute-start | bytes 589832 | tf_op jit(solution)/shard_map/ppermute | solution.py:32
  2.5 8.3 %collective-permute-start.1 = (bf16[256,384]{1,0:T(8,128)(2,1)S(1)}, bf16[256,384]{1,0:T(8,128)(2,1)S(1)}, u32[]{:S(2)}, u32[]{:S(2)}) collective-permute-start(bf16[256,384]{1,0:T(8,128)(2,1)S(1)} %get-tuple-element.112), channel_id=1, source_target_pairs={{0,2},{1,3},{2,0},{3,1},{4,6},{5,7},{6,4},{7,5},{8,10},{9,11},{10,... | collective-permute-start | bytes 589832 | tf_op jit(solution)/shard_map/ppermute | solution.py:32
  5.1 9.4 %collective-permute-start.2 = (bf16[256,384]{1,0:T(8,128)(2,1)S(1)}, bf16[256,384]{1,0:T(8,128)(2,1)S(1)}, u32[]{:S(2)}, u32[]{:S(2)}) collective-permute-start(bf16[256,384]{1,0:T(8,128)(2,1)S(1)} %get-tuple-element.111), channel_id=1, source_target_pairs={{0,3},{1,2},{2,1},{3,0},{4,7},{5,6},{6,5},{7,4},{8,11},{9,10},{10,... | collective-permute-start | bytes 589832 | tf_op jit(solution)/shard_map/ppermute | solution.py:32
  15.3 12.3 %collective-permute-start.6 = (bf16[576,384]{1,0:T(8,128)(2,1)S(1)}, bf16[576,384]{1,0:T(8,128)(2,1)S(1)}, u32[]{:S(2)}, u32[]{:S(2)}) collective-permute-start(bf16[576,384]{1,0:T(8,128)(2,1)S(1)} %copy-done.4), channel_id=1, source_target_pairs={{0,2},{1,3},{2,0},{3,1},{4,6},{5,7},{6,4},{7,5},{8,10},{9,11},{10,... | collective-permute-start | bytes 1327112 | tf_op jit(solution)/shard_map/ppermute | solution.py:32
  16.9 16.2 %collective-permute-start.3 = (bf16[768,384]{1,0:T(8,128)(2,1)S(1)}, bf16[768,384]{1,0:T(8,128)(2,1)S(1)}, u32[]{:S(2)}, u32[]{:S(2)}) collective-permute-start(bf16[768,384]{1,0:T(8,128)(2,1)S(1)} %get-tuple-element.52), channel_id=1, source_target_pairs={{0,4},{4,8},{8,12},{1,5},{5,9},{9,13},{2,6},{6,10},{10,14},{3,7},{... | collective-permute-start | bytes 1769480 | tf_op jit(solution)/shard_map/ppermute | solution.py:22
  20.4 7.8 %collective-permute-start.5 = (bf16[576,384]{1,0:T(8,128)(2,1)S(1)}, bf16[576,384]{1,0:T(8,128)(2,1)S(1)}, u32[]{:S(2)}, u32[]{:S(2)}) collective-permute-start(bf16[576,384]{1,0:T(8,128)(2,1)S(1)} %copy-done.4), channel_id=1, source_target_pairs={{0,1},{1,0},{2,3},{3,2},{4,5},{5,4},{6,7},{7,6},{8,9},{9,8},{10,11... | collective-permute-start | bytes 1327112 | tf_op jit(solution)/shard_map/ppermute | solution.py:32
  20.5 17.6 %collective-permute-start.4 = (bf16[768,384]{1,0:T(8,128)(2,1)S(1)}, bf16[768,384]{1,0:T(8,128)(2,1)S(1)}, u32[]{:S(2)}, u32[]{:S(2)}) collective-permute-start(bf16[768,384]{1,0:T(8,128)(2,1)S(1)} %get-tuple-element.54), channel_id=1, source_target_pairs={{4,0},{8,4},{12,8},{5,1},{9,5},{13,9},{6,2},{10,6},{14,10},{7,3},{... | collective-permute-start | bytes 1769480 | tf_op jit(solution)/shard_map/ppermute | solution.py:22
  27.5 10.6 %collective-permute-start.7 = (bf16[576,384]{1,0:T(8,128)(2,1)S(1)}, bf16[576,384]{1,0:T(8,128)(2,1)S(1)}, u32[]{:S(2)}, u32[]{:S(2)}) collective-permute-start(bf16[576,384]{1,0:T(8,128)(2,1)S(1)} %collective-permute-done.6.refs_2_), channel_id=1, source_target_pairs={{0,1},{1,0},{2,3},{3,2},{4,5},{5,4},{6,7},{7,6},{8,9},{9,8},{10,11... | collective-permute-start | bytes 1327112 | tf_op jit(solution)/shard_map/ppermute | solution.py:32
  27.6 16.9 %collective-permute-start.8 = (bf16[256,384]{1,0:T(8,128)(2,1)S(1)}, bf16[256,384]{1,0:T(8,128)(2,1)S(1)}, u32[]{:S(2)}, u32[]{:S(2)}) collective-permute-start(bf16[256,384]{1,0:T(8,128)(2,1)S(1)} %get-tuple-element.110), channel_id=1, source_target_pairs={{0,1},{1,0},{2,3},{3,2},{4,5},{5,4},{6,7},{7,6},{8,9},{9,8},{10,11... | collective-permute-start | bytes 589832 | tf_op jit(solution)/shard_map/ppermute | solution.py:32
  28.2 16.4 %collective-permute-start.10 = (bf16[256,384]{1,0:T(8,128)(2,1)S(1)}, bf16[256,384]{1,0:T(8,128)(2,1)S(1)}, u32[]{:S(2)}, u32[]{:S(2)}) collective-permute-start(bf16[256,384]{1,0:T(8,128)(2,1)S(1)} %get-tuple-element.59), channel_id=1, source_target_pairs={{0,3},{1,2},{2,1},{3,0},{4,7},{5,6},{6,5},{7,4},{8,11},{9,10},{10,... | collective-permute-start | bytes 589832 | tf_op jit(solution)/shard_map/ppermute | solution.py:32
  33.1 11.4 %collective-permute-start.9 = (bf16[256,384]{1,0:T(8,128)(2,1)S(1)}, bf16[256,384]{1,0:T(8,128)(2,1)S(1)}, u32[]{:S(2)}, u32[]{:S(2)}) collective-permute-start(bf16[256,384]{1,0:T(8,128)(2,1)S(1)} %get-tuple-element.58), channel_id=1, source_target_pairs={{0,2},{1,3},{2,0},{3,1},{4,6},{5,7},{6,4},{7,5},{8,10},{9,11},{10,... | collective-permute-start | bytes 589832 | tf_op jit(solution)/shard_map/ppermute | solution.py:32
  45.5 12.2 %collective-permute-start.11 = (bf16[512,384]{1,0:T(8,128)(2,1)S(1)}, bf16[512,384]{1,0:T(8,128)(2,1)S(1)}, u32[]{:S(2)}, u32[]{:S(2)}) collective-permute-start(bf16[512,384]{1,0:T(8,128)(2,1)S(1)} %get-tuple-element.60), channel_id=1, source_target_pairs={{0,4},{4,8},{8,12},{1,5},{5,9},{9,13},{2,6},{6,10},{10,14},{3,7},{... | collective-permute-start | bytes 1179656 | tf_op jit(solution)/shard_map/ppermute | solution.py:22
  49.0 12.3 %collective-permute-start.12 = (bf16[512,384]{1,0:T(8,128)(2,1)S(1)}, bf16[512,384]{1,0:T(8,128)(2,1)S(1)}, u32[]{:S(2)}, u32[]{:S(2)}) collective-permute-start(bf16[512,384]{1,0:T(8,128)(2,1)S(1)} %get-tuple-element.62), channel_id=1, source_target_pairs={{4,0},{8,4},{12,8},{5,1},{9,5},{13,9},{6,2},{10,6},{14,10},{7,3},{... | collective-permute-start | bytes 1179656 | tf_op jit(solution)/shard_map/ppermute | solution.py:22
  52.8 1.4 %collective-permute-start.17 = (f32[72,384]{1,0:T(8,128)S(1)}, f32[72,384]{1,0:T(8,128)S(1)}, u32[]{:S(2)}, u32[]{:S(2)}) collective-permute-start(f32[72,384]{1,0:T(8,128)S(1)} %get-tuple-element.76), channel_id=1, source_target_pairs={{0,1},{1,0},{2,3},{3,2},{4,5},{5,4},{6,7},{7,6},{8,9},{9,8},{10,11... | collective-permute-start | bytes 331784 | tf_op jit(solution)/shard_map/ppermute | solution.py:32
  52.9 1.5 %collective-permute-start.18 = (f32[72,384]{1,0:T(8,128)S(1)}, f32[72,384]{1,0:T(8,128)S(1)}, u32[]{:S(2)}, u32[]{:S(2)}) collective-permute-start(f32[72,384]{1,0:T(8,128)S(1)} %get-tuple-element.77), channel_id=1, source_target_pairs={{0,1},{1,0},{2,3},{3,2},{4,5},{5,4},{6,7},{7,6},{8,9},{9,8},{10,11... | collective-permute-start | bytes 331784 | tf_op jit(solution)/shard_map/ppermute | solution.py:32
  61.3 7.8 %collective-permute-start.25 = (bf16[288,384]{1,0:T(8,128)(2,1)S(1)}, bf16[288,384]{1,0:T(8,128)(2,1)S(1)}, u32[]{:S(2)}, u32[]{:S(2)}) collective-permute-start(bf16[288,384]{1,0:T(8,128)(2,1)S(1)} %get-tuple-element.85), channel_id=1, source_target_pairs={{0,4},{4,0},{8,12},{12,8},{1,5},{5,1},{9,13},{13,9},{2,6},{6,2},{1... | collective-permute-start | bytes 663560 | tf_op jit(solution)/shard_map/ppermute | solution.py:32
  68.1 1.5 %collective-permute-start.13 = (f32[144,384]{1,0:T(8,128)S(1)}, f32[144,384]{1,0:T(8,128)S(1)}, u32[]{:S(2)}, u32[]{:S(2)}) collective-permute-start(f32[144,384]{1,0:T(8,128)S(1)} %get-tuple-element.70), channel_id=1, source_target_pairs={{0,1},{1,0},{2,3},{3,2},{4,5},{5,4},{6,7},{7,6},{8,9},{9,8},{10,11... | collective-permute-start | bytes 663560 | tf_op jit(solution)/shard_map/ppermute | solution.py:32
  68.1 1.8 %collective-permute-start.14 = (f32[144,384]{1,0:T(8,128)S(1)}, f32[144,384]{1,0:T(8,128)S(1)}, u32[]{:S(2)}, u32[]{:S(2)}) collective-permute-start(f32[144,384]{1,0:T(8,128)S(1)} %get-tuple-element.71), channel_id=1, source_target_pairs={{0,1},{1,0},{2,3},{3,2},{4,5},{5,4},{6,7},{7,6},{8,9},{9,8},{10,11... | collective-permute-start | bytes 663560 | tf_op jit(solution)/shard_map/ppermute | solution.py:32
  68.6 1.6 %collective-permute-start.15 = (f32[144,384]{1,0:T(8,128)S(1)}, f32[144,384]{1,0:T(8,128)S(1)}, u32[]{:S(2)}, u32[]{:S(2)}) collective-permute-start(f32[144,384]{1,0:T(8,128)S(1)} %get-tuple-element.72), channel_id=1, source_target_pairs={{0,1},{1,0},{2,3},{3,2},{4,5},{5,4},{6,7},{7,6},{8,9},{9,8},{10,11... | collective-permute-start | bytes 663560 | tf_op jit(solution)/shard_map/ppermute | solution.py:32
  68.6 1.9 %collective-permute-start.16 = (f32[144,384]{1,0:T(8,128)S(1)}, f32[144,384]{1,0:T(8,128)S(1)}, u32[]{:S(2)}, u32[]{:S(2)}) collective-permute-start(f32[144,384]{1,0:T(8,128)S(1)} %get-tuple-element.73), channel_id=1, source_target_pairs={{0,1},{1,0},{2,3},{3,2},{4,5},{5,4},{6,7},{7,6},{8,9},{9,8},{10,11... | collective-permute-start | bytes 663560 | tf_op jit(solution)/shard_map/ppermute | solution.py:32
  71.2 7.6 %collective-permute-start.32 = (bf16[288,384]{1,0:T(8,128)(2,1)S(1)}, bf16[288,384]{1,0:T(8,128)(2,1)S(1)}, u32[]{:S(2)}, u32[]{:S(2)}) collective-permute-start(bf16[288,384]{1,0:T(8,128)(2,1)S(1)} %get-tuple-element.86), channel_id=1, source_target_pairs={{0,4},{4,0},{8,12},{12,8},{1,5},{5,1},{9,13},{13,9},{2,6},{6,2},{1... | collective-permute-start | bytes 663560 | tf_op jit(solution)/shard_map/ppermute | solution.py:32
  71.8 11.4 %collective-permute-start.26 = (bf16[256,384]{1,0:T(8,128)(2,1)}, bf16[256,384]{1,0:T(8,128)(2,1)}, u32[]{:S(2)}, u32[]{:S(2)}) collective-permute-start(bf16[256,384]{1,0:T(8,128)(2,1)} %get-tuple-element.87), channel_id=1, source_target_pairs={{0,4},{4,8},{8,12},{1,5},{5,9},{9,13},{2,6},{6,10},{10,14},{3,7},{... | collective-permute-start | bytes 589832 | tf_op jit(solution)/shard_map/ppermute | solution.py:22
  75.9 9.1 %collective-permute-start.27 = (bf16[256,384]{1,0:T(8,128)(2,1)}, bf16[256,384]{1,0:T(8,128)(2,1)}, u32[]{:S(2)}, u32[]{:S(2)}) collective-permute-start(bf16[256,384]{1,0:T(8,128)(2,1)} %get-tuple-element.88), channel_id=1, source_target_pairs={{4,0},{8,4},{12,8},{5,1},{9,5},{13,9},{6,2},{10,6},{14,10},{7,3},{... | collective-permute-start | bytes 589832 | tf_op jit(solution)/shard_map/ppermute | solution.py:22
  79.5 12.3 %collective-permute-start.33 = (bf16[144,384]{1,0:T(8,128)(2,1)S(1)}, bf16[144,384]{1,0:T(8,128)(2,1)}, u32[]{:S(2)}, u32[]{:S(2)}) collective-permute-start(bf16[144,384]{1,0:T(8,128)(2,1)S(1)} %get-tuple-element.96), channel_id=1, source_target_pairs={{0,8},{4,12},{8,0},{12,4},{1,9},{5,13},{9,1},{13,5},{2,10},{6,14},... | collective-permute-start | bytes 331784 | tf_op jit(solution)/shard_map/ppermute | solution.py:32
  80.3 12.7 %collective-permute-start.31 = (bf16[144,384]{1,0:T(8,128)(2,1)S(1)}, bf16[144,384]{1,0:T(8,128)(2,1)S(1)}, u32[]{:S(2)}, u32[]{:S(2)}) collective-permute-start(bf16[144,384]{1,0:T(8,128)(2,1)S(1)} %get-tuple-element.93), channel_id=1, source_target_pairs={{0,8},{4,12},{8,0},{12,4},{1,9},{5,13},{9,1},{13,5},{2,10},{6,14},... | collective-permute-start | bytes 331784 | tf_op jit(solution)/shard_map/ppermute | solution.py:32
  93.0 5.8 %collective-permute-start.34 = (bf16[1,144,384]{2,1,0:T(8,128)(2,1)S(1)}, bf16[1,144,384]{2,1,0:T(8,128)(2,1)S(1)}, u32[]{:S(2)}, u32[]{:S(2)}) collective-permute-start(bf16[1,144,384]{2,1,0:T(8,128)(2,1)S(1)} %fusion), channel_id=1, source_target_pairs={{0,2},{1,3},{2,0},{3,1},{4,6},{5,7},{6,4},{7,5},{8,10},{9,11},{10,... | collective-permute-start | bytes 331784 | tf_op jit(solution)/shard_map/ppermute | solution.py:32
  93.7 7.4 %collective-permute-start.28 = (bf16[256,384]{1,0:T(8,128)(2,1)S(1)}, bf16[256,384]{1,0:T(8,128)(2,1)S(1)}, u32[]{:S(2)}, u32[]{:S(2)}) collective-permute-start(bf16[256,384]{1,0:T(8,128)(2,1)S(1)} %get-tuple-element.106), channel_id=1, source_target_pairs={{0,1},{1,0},{2,3},{3,2},{4,5},{5,4},{6,7},{7,6},{8,9},{9,8},{10,11... | collective-permute-start | bytes 589832 | tf_op jit(solution)/shard_map/ppermute | solution.py:32
  93.8 9.7 %collective-permute-start.29 = (bf16[256,384]{1,0:T(8,128)(2,1)S(1)}, bf16[256,384]{1,0:T(8,128)(2,1)S(1)}, u32[]{:S(2)}, u32[]{:S(2)}) collective-permute-start(bf16[256,384]{1,0:T(8,128)(2,1)S(1)} %get-tuple-element.105), channel_id=1, source_target_pairs={{0,2},{1,3},{2,0},{3,1},{4,6},{5,7},{6,4},{7,5},{8,10},{9,11},{10,... | collective-permute-start | bytes 589832 | tf_op jit(solution)/shard_map/ppermute | solution.py:32
  95.4 10.0 %collective-permute-start.30 = (bf16[256,384]{1,0:T(8,128)(2,1)S(1)}, bf16[256,384]{1,0:T(8,128)(2,1)S(1)}, u32[]{:S(2)}, u32[]{:S(2)}) collective-permute-start(bf16[256,384]{1,0:T(8,128)(2,1)S(1)} %get-tuple-element.104), channel_id=1, source_target_pairs={{0,3},{1,2},{2,1},{3,0},{4,7},{5,6},{6,5},{7,4},{8,11},{9,10},{10,... | collective-permute-start | bytes 589832 | tf_op jit(solution)/shard_map/ppermute | solution.py:32
  98.9 6.8 %collective-permute-start.35 = (bf16[144,384]{1,0:T(8,128)(2,1)S(1)}, bf16[144,384]{1,0:T(8,128)(2,1)S(1)}, u32[]{:S(2)}, u32[]{:S(2)}) collective-permute-start(bf16[144,384]{1,0:T(8,128)(2,1)S(1)} %bitcast.11), channel_id=1, source_target_pairs={{0,4},{4,8},{8,12},{12,0},{1,5},{5,9},{9,13},{13,1},{2,6},{6,10},{... | collective-permute-start | bytes 331784 | tf_op jit(solution)/shard_map/ppermute | solution.py:27
  101.1 7.8 %collective-permute-start.36 = (bf16[144,384]{1,0:T(8,128)(2,1)S(1)}, bf16[144,384]{1,0:T(8,128)(2,1)S(1)}, u32[]{:S(2)}, u32[]{:S(2)}) collective-permute-start(bf16[144,384]{1,0:T(8,128)(2,1)S(1)} %bitcast.12), channel_id=1, source_target_pairs={{0,8},{4,12},{8,0},{12,4},{1,9},{5,13},{9,1},{13,5},{2,10},{6,14},... | collective-permute-start | bytes 331784 | tf_op jit(solution)/shard_map/ppermute | solution.py:27
  101.1 7.8 %collective-permute-start.37 = (bf16[144,384]{1,0:T(8,128)(2,1)S(1)}, bf16[144,384]{1,0:T(8,128)(2,1)S(1)}, u32[]{:S(2)}, u32[]{:S(2)}) collective-permute-start(bf16[144,384]{1,0:T(8,128)(2,1)S(1)} %bitcast.13), channel_id=1, source_target_pairs={{0,12},{4,0},{8,4},{12,8},{1,13},{5,1},{9,5},{13,9},{2,14},{6,2},{... | collective-permute-start | bytes 331784 | tf_op jit(solution)/shard_map/ppermute | solution.py:27
  (13 other events, 75.6 us)

commit v6 on v5

--- a/solution.py
+++ b/solution.py
@@ -48,7 +48,7 @@
     return lax.dynamic_slice_in_dim(block, index * rows, rows, 0)
 
 
-def gather_pieces(block, axis, others):
+def gather_pieces(block, near, axis, others):
     n = lax.axis_size(axis)
     held = {0: block}
     bit = n // 2
@@ -56,7 +56,7 @@
         for r in list(held):
             first_far = r == 0 and bit == n // 2
             source = after(held[r], others) if first_far else held[r]
-            held[r ^ bit] = swapped(source, axis, bit)
+            held[r ^ bit] = near if r ^ bit == 1 else swapped(source, axis, bit)
         bit //= 2
     return [held[r] for r in range(n)]
 
@@ -89,7 +89,7 @@
 
 def regroup_kernel(sizes, place, block, *refs):
     members, q, reach = sizes
-    pieces, (own, to_high, to_low) = refs[: members - 1], refs[members - 1 :]
+    pieces, (own, to_high, to_low) = refs[: members - 1], refs[-3:]
     j = place[1]
 
     def rows(index):
@@ -349,17 +349,17 @@
     return sent if lax.axis_size("seq") > 4 else swapped(sent, "seq", 1)
 
 
-def seq_sum_halving(place, kept, got, others):
+def seq_sum_halving(place, kept, got, others, waits=()):
     n = lax.axis_size("seq")
     if n > 4:
-        return lax.psum(kept, "seq")
+        return [lax.psum(kept, "seq")]
     bit = 2
     while bit < n:
         came = got if others is None else after(got, others)
-        kept, sent = halved(place, kept, [came], bit)
+        kept, sent = halved(place, kept, [came], bit, waits)
         got = swapped(sent, "seq", bit)
         bit *= 2
-    return added([kept, got])
+    return [kept, got]
 
 
 def added(pieces):
@@ -413,23 +413,26 @@
     def kernel(body, *shapes, scratch=(), operands=()):
         return call(body, shapes, scratch, 1, (place,) + tuple(operands))
 
-    def regrouped(block, others=None):
+    def regrouped(block, others=None, first=None):
         pieces = [cut(block, j ^ r, q) for r in range(1, members)]
         if others is not None:
             pieces[1:] = after(pieces[1:], others)
-        return [swapped(piece, "sub", r + 1) for r, piece in enumerate(pieces)]
+        first = swapped(pieces[0], "sub", 1) if first is None else first
+        return [first] + [swapped(piece, "sub", r + 2) for r, piece in enumerate(pieces[1:])]
 
     reach = near + far
+    near_weights = swapped(weights, "sub", 1)
+    near_cot = swapped(cut(cotangent, j ^ 1, q), "sub", 1)
     act, up_act, down_act = kernel(
         functools.partial(regroup_kernel, (members, q, reach)),
         ((count, channels), BF16),
         ((reach * q, channels), BF16),
         ((reach * q, channels), BF16),
-        operands=(activations, *regrouped(activations)),
+        operands=(activations, *regrouped(activations), near_weights),
     )
     low, high = shifted(up_act, "seq", 1), shifted(down_act, "seq", -1)
-    w_pieces = gather_pieces(weights, "sub", act)
-    c_pieces = regrouped(cotangent, w_pieces[members // 2])
+    w_pieces = gather_pieces(weights, near_weights, "sub", act)
+    c_pieces = regrouped(cotangent, w_pieces[members // 2], near_cot)
 
     act_stack, hid_stack, slope_one, slope_two, all_weights = kernel(
         functools.partial(forward_kernel, (groups, members, q, near, far)),
@@ -479,8 +482,8 @@
     got_one = first_half(sent_one)
     up_one, down_one = after((up_one, down_one), sent_one)
     one_low, one_high = shifted(up_one, "seq", 1), shifted(down_one, "seq", -1)
-    total_two = seq_sum_halving(place, kept_two, got_two, sent_one)
-    total_one = seq_sum_halving(place, kept_one, got_one, None)
+    parts_two = seq_sum_halving(place, kept_two, got_two, sent_one)
+    parts_one = seq_sum_halving(place, kept_one, got_one, None, parts_two[1:])
 
     (grad_in,) = call(
         functools.partial(input_kernel, (members, q, near)),
@@ -488,7 +491,8 @@
         scalars=1,
         operands=(place, one_low, delta_one, one_high, back_one, all_weights),
     )
-    total_one = after(total_one, grad_in)
+    total_one = added(after(parts_one, grad_in))
+    total_two = added(parts_two)
     part = chip_sum(total_one, total_two, j)
     sent = part.astype(BF16)
     got = [grad_in[r * q : (r + 1) * q] for r in range(members)]

time: 110 us -> 108 us (0.982)
  starting transfers between devices: 37.4 us -> 35.3 us
  waiting for transfers between devices: 45 us -> 43.3 us
    ppermute x6, waiting for transfers between devices: 13.5 us -> 11.1 us  [shifted(): return lax.ppermute(block, axis, route)]
    ppermute x6, starting transfers between devices: 15 us -> 13.1 us  [shifted(): return lax.ppermute(block, axis, route)]
  transfers between devices with their start and end apart: 38 -> 38, of which waited for: 22 -> 22; matrix products, arithmetic and copies ran while one was open for 1% -> 3% of each run, Pallas kernels for 17% -> 18%
where the time goes in v6:
time: 108 us
  waiting for transfers between devices  43.3 us (40%)
  starting transfers between devices  35.3 us (33%)
  Pallas kernels  21.3 us (20%)
  local copies, waits for them, and re-layouts  4.66 us (4%)
  other arithmetic  2.07 us (2%)
    ppermute x29, waiting for transfers between devices, swapped(): return lax.ppermute(block, axis, [(i, i ^ bits) for i in range(n)])  28.8 us
    pallas_call x11, Pallas kernels, call(): pl.pallas_call(kernel, out_shape=tuple((jax.ShapeDtypeStruct(shape, kind)...  21.3 us
    ppermute x29, starting transfers between devices, swapped(): return lax.ppermute(block, axis, [(i, i ^ bits) for i in range(n)])  17.7 us
    ppermute x6, starting transfers between devices, shifted(): return lax.ppermute(block, axis, route)  13.1 us
    ppermute x6, waiting for transfers between devices, shifted(): return lax.ppermute(block, axis, route)  11.1 us
    ppermute x3, starting transfers between devices, turned(): return lax.ppermute(block, axis, [(i, (i + turn) % n) for i in range(n)])  4.57 us
    ppermute x3, waiting for transfers between devices, turned(): return lax.ppermute(block, axis, [(i, (i + turn) % n) for i in range(n)])  3.36 us
    unnamed x14, local copies, waits for them, and re-layouts  2.34 us
  transfers between devices with their start and end apart: 38, of which 22 were waited for; matrix products, arithmetic and copies ran while one was open for 3% of the time, Pallas kernels for 18%

profile of v6, /device:TPU:0, one launch (start us, length us, event | category | flops | bytes accessed | tf_op | source)
XLA Modules:
  0.0 107.6 jit_solution(17981043800892608707)
XLA Ops:
  1.2 1.9 %constant_dynamic-slice_fusion.3 = (bf16[256,384]{1,0:T(8,128)(2,1)S(1)}, bf16[256,384]{1,0:T(8,128)(2,1)S(1)}, bf16[256,384]{1,0:T(8,128)(2,1)}) fusion(bf16[1024,384]{1,0:T(8,128)(2,1)} %block.1, s32[]{:T(128)S(6)} %select_n.66, s32[]{:T(128)S(6)} %select_n.65, s32[]{:T(128)S(6)} %select_n.64), kind=kLoop, calls=%fused_computation.17 | loop fusion | bytes 1179660 | tf_op jit(solution)/shard_map/dynamic_slice | solution.py:48
  3.2 2.8 %collective-permute-start.1 = (bf16[256,384]{1,0:T(8,128)(2,1)S(1)}, bf16[256,384]{1,0:T(8,128)(2,1)S(1)}, u32[]{:S(2)}, u32[]{:S(2)}) collective-permute-start(bf16[256,384]{1,0:T(8,128)(2,1)S(1)} %get-tuple-element.114), channel_id=1, source_target_pairs={{0,2},{1,3},{2,0},{3,1},{4,6},{5,7},{6,4},{7,5},{8,10},{9,11},{10,... | collective-permute-start | bytes 589832 | tf_op jit(solution)/shard_map/ppermute | solution.py:32
  6.1 5.6 %collective-permute-done.1.refs_1_ = bf16[256,384]{1,0:T(8,128)(2,1)S(1)} collective-permute-done((bf16[256,384]{1,0:T(8,128)(2,1)S(1)}, bf16[256,384]{1,0:T(8,128)(2,1)S(1)}, u32[]{:S(2)}, u32[]{:S(2)}) %collective-permute-start.1) | collective-permute-done | bytes 196640 | tf_op jit(solution)/shard_map/ppermute | solution.py:32
  11.7 3.3 %collective-permute-done.2.refs_2_ = bf16[256,384]{1,0:T(8,128)(2,1)S(1)} collective-permute-done((bf16[256,384]{1,0:T(8,128)(2,1)S(1)}, bf16[256,384]{1,0:T(8,128)(2,1)S(1)}, u32[]{:S(2)}, u32[]{:S(2)}) %collective-permute-start.2) | collective-permute-done | bytes 196640 | tf_op jit(solution)/shard_map/ppermute | solution.py:32
  15.8 1.5 %collective-permute-start.6 = (bf16[576,384]{1,0:T(8,128)(2,1)S(1)}, bf16[576,384]{1,0:T(8,128)(2,1)S(1)}, u32[]{:S(2)}, u32[]{:S(2)}) collective-permute-start(bf16[576,384]{1,0:T(8,128)(2,1)S(1)} %copy-done.4), channel_id=1, source_target_pairs={{0,2},{1,3},{2,0},{3,1},{4,6},{5,7},{6,4},{7,5},{8,10},{9,11},{10,... | collective-permute-start | bytes 1327112 | tf_op jit(solution)/shard_map/ppermute | solution.py:32
  17.2 3.5 %collective-permute-start.4 = (bf16[768,384]{1,0:T(8,128)(2,1)S(1)}, bf16[768,384]{1,0:T(8,128)(2,1)S(1)}, u32[]{:S(2)}, u32[]{:S(2)}) collective-permute-start(bf16[768,384]{1,0:T(8,128)(2,1)S(1)} %get-tuple-element.53), channel_id=1, source_target_pairs={{0,4},{4,8},{8,12},{1,5},{5,9},{9,13},{2,6},{6,10},{10,14},{3,7},{... | collective-permute-start | bytes 1769480 | tf_op jit(solution)/shard_map/ppermute | solution.py:22
  20.8 1.3 %collective-permute-start.5 = (bf16[768,384]{1,0:T(8,128)(2,1)S(1)}, bf16[768,384]{1,0:T(8,128)(2,1)S(1)}, u32[]{:S(2)}, u32[]{:S(2)}) collective-permute-start(bf16[768,384]{1,0:T(8,128)(2,1)S(1)} %get-tuple-element.55), channel_id=1, source_target_pairs={{4,0},{8,4},{12,8},{5,1},{9,5},{13,9},{6,2},{10,6},{14,10},{7,3},{... | collective-permute-start | bytes 1769480 | tf_op jit(solution)/shard_map/ppermute | solution.py:22
  22.1 6.1 %collective-permute-done.6.refs_2_ = bf16[576,384]{1,0:T(8,128)(2,1)S(1)} collective-permute-done((bf16[576,384]{1,0:T(8,128)(2,1)S(1)}, bf16[576,384]{1,0:T(8,128)(2,1)S(1)}, u32[]{:S(2)}, u32[]{:S(2)}) %collective-permute-start.6) | collective-permute-done | bytes 442400 | tf_op jit(solution)/shard_map/ppermute | solution.py:32
  28.8 1.4 %collective-permute-start.10 = (bf16[256,384]{1,0:T(8,128)(2,1)S(1)}, bf16[256,384]{1,0:T(8,128)(2,1)S(1)}, u32[]{:S(2)}, u32[]{:S(2)}) collective-permute-start(bf16[256,384]{1,0:T(8,128)(2,1)S(1)} %get-tuple-element.60), channel_id=1, source_target_pairs={{0,3},{1,2},{2,1},{3,0},{4,7},{5,6},{6,5},{7,4},{8,11},{9,10},{10,... | collective-permute-start | bytes 589832 | tf_op jit(solution)/shard_map/ppermute | solution.py:32
  30.2 3.5 %collective-permute-done.4.low = bf16[768,384]{1,0:T(8,128)(2,1)S(1)} collective-permute-done((bf16[768,384]{1,0:T(8,128)(2,1)S(1)}, bf16[768,384]{1,0:T(8,128)(2,1)S(1)}, u32[]{:S(2)}, u32[]{:S(2)}) %collective-permute-start.4) | collective-permute-done | bytes 589856 | tf_op jit(solution)/shard_map/ppermute | solution.py:22
  34.3 3.6 %collective-permute-done.5.high = bf16[768,384]{1,0:T(8,128)(2,1)S(1)} collective-permute-done((bf16[768,384]{1,0:T(8,128)(2,1)S(1)}, bf16[768,384]{1,0:T(8,128)(2,1)S(1)}, u32[]{:S(2)}, u32[]{:S(2)}) %collective-permute-start.5) | collective-permute-done | bytes 589856 | tf_op jit(solution)/shard_map/ppermute | solution.py:22
  37.9 6.4 %shard_map.51 = (bf16[1024,1152]{1,0:T(8,128)(2,1)S(1)}, bf16[1024,1152]{1,0:T(8,128)(2,1)S(1)}, f32[1024,384]{1,0:T(8,128)S(1)}, f32[1024,384]{1,0:T(8,128)S(1)}, bf16[2304,384]{1,0:T(8,128)(2,1)S(1)}) custom-call(s32[2]{0:T(128)S(1)} %pad_add_fusion.place, bf16[768,384]{1,0:T(8,128)(2,1)S(1)} %collective-permute-done.4.low, ...), custom_call_target="tpu_custom_call" | custom-call | flops 1 | bytes 1 | tf_op jit(solution)/shard_map/pallas_call | solution.py:295
  45.3 3.5 %collective-permute-start.11 = (bf16[512,384]{1,0:T(8,128)(2,1)S(1)}, bf16[512,384]{1,0:T(8,128)(2,1)S(1)}, u32[]{:S(2)}, u32[]{:S(2)}) collective-permute-start(bf16[512,384]{1,0:T(8,128)(2,1)S(1)} %get-tuple-element.61), channel_id=1, source_target_pairs={{0,4},{4,8},{8,12},{1,5},{5,9},{9,13},{2,6},{6,10},{10,14},{3,7},{... | collective-permute-start | bytes 1179656 | tf_op jit(solution)/shard_map/ppermute | solution.py:22
  48.8 1.3 %collective-permute-start.12 = (bf16[512,384]{1,0:T(8,128)(2,1)S(1)}, bf16[512,384]{1,0:T(8,128)(2,1)S(1)}, u32[]{:S(2)}, u32[]{:S(2)}) collective-permute-start(bf16[512,384]{1,0:T(8,128)(2,1)S(1)} %get-tuple-element.63), channel_id=1, source_target_pairs={{4,0},{8,4},{12,8},{5,1},{9,5},{13,9},{6,2},{10,6},{14,10},{7,3},{... | collective-permute-start | bytes 1179656 | tf_op jit(solution)/shard_map/ppermute | solution.py:22
  50.1 2.5 %shard_map.55 = (f32[576,384]{1,0:T(8,128)S(1)}, f32[72,384]{1,0:T(8,128)S(1)}, f32[72,384]{1,0:T(8,128)S(1)}, f32[72,384]{1,0:T(8,128)S(1)}, f32[72,384]{1,0:T(...) custom-call(s32[2]{0:T(128)S(1)} %pad_add_fusion.place, ...), custom_call_target="tpu_custom_call" | custom-call | flops 1 | bytes 1 | tf_op jit(solution)/shard_map/pallas_call | solution.py:295
  57.5 3.1 %collective-permute-done.12.high = bf16[512,384]{1,0:T(8,128)(2,1)S(1)} collective-permute-done((bf16[512,384]{1,0:T(8,128)(2,1)S(1)}, bf16[512,384]{1,0:T(8,128)(2,1)S(1)}, u32[]{:S(2)}, u32[]{:S(2)}) %collective-permute-start.12) | collective-permute-done | bytes 393248 | tf_op jit(solution)/shard_map/ppermute | solution.py:22
  60.6 1.6 %collective-permute-start.25 = (bf16[288,384]{1,0:T(8,128)(2,1)S(1)}, bf16[288,384]{1,0:T(8,128)(2,1)S(1)}, u32[]{:S(2)}, u32[]{:S(2)}) collective-permute-start(bf16[288,384]{1,0:T(8,128)(2,1)S(1)} %get-tuple-element.86), channel_id=1, source_target_pairs={{0,4},{4,0},{8,12},{12,8},{1,5},{5,1},{9,13},{13,9},{2,6},{6,2},{1... | collective-permute-start | bytes 663560 | tf_op jit(solution)/shard_map/ppermute | solution.py:32
  62.2 1.7 %shard_map.53 = (f32[1024,384]{1,0:T(8,128)S(1)}, bf16[1024,384]{1,0:T(8,128)(2,1)S(1)}) custom-call(bf16[512,384]{1,0:T(8,128)(2,1)S(1)} %collective-permute-done.11.low, bf16[1024,384]{1,0:T(8,128)(2,1)S(1)} %get-tuple-element.62.own.delta, bf16[512,384]{1,0:T(8,128)(2,1)S(1)} %collective-permute-done.12.high, ...), custom_call_target="tpu_custom_call" | custom-call | flops 1 | bytes 1 | tf_op jit(solution)/shard_map/pallas_call | solution.py:295
  63.9 3.4 %shard_map.54 = (f32[576,384]{1,0:T(8,128)S(1)}, f32[144,384]{1,0:T(8,128)S(1)}, f32[144,384]{1,0:T(8,128)S(1)}, f32[144,384]{1,0:T(8,128)S(1)}, f32[144,384]{1,...) custom-call(s32[2]{0:T(128)S(1)} %pad_add_fusion.place, ...), custom_call_target="tpu_custom_call" | custom-call | flops 1 | bytes 1 | tf_op jit(solution)/shard_map/pallas_call | solution.py:295
  71.7 1.4 %collective-permute-start.31 = (bf16[144,384]{1,0:T(8,128)(2,1)S(1)}, bf16[144,384]{1,0:T(8,128)(2,1)S(1)}, u32[]{:S(2)}, u32[]{:S(2)}) collective-permute-start(bf16[144,384]{1,0:T(8,128)(2,1)S(1)} %get-tuple-element.94), channel_id=1, source_target_pairs={{0,8},{4,12},{8,0},{12,4},{1,9},{5,13},{9,1},{13,5},{2,10},{6,14},... | collective-permute-start | bytes 331784 | tf_op jit(solution)/shard_map/ppermute | solution.py:32
  73.0 2.2 %collective-permute-start.26 = (bf16[256,384]{1,0:T(8,128)(2,1)}, bf16[256,384]{1,0:T(8,128)(2,1)S(1)}, u32[]{:S(2)}, u32[]{:S(2)}) collective-permute-start(bf16[256,384]{1,0:T(8,128)(2,1)} %get-tuple-element.88), channel_id=1, source_target_pairs={{0,4},{4,8},{8,12},{1,5},{5,9},{9,13},{2,6},{6,10},{10,14},{3,7},{... | collective-permute-start | bytes 589832 | tf_op jit(solution)/shard_map/ppermute | solution.py:22
  76.5 2.7 %collective-permute-done.31.refs_1_ = bf16[144,384]{1,0:T(8,128)(2,1)S(1)} collective-permute-done((bf16[144,384]{1,0:T(8,128)(2,1)S(1)}, bf16[144,384]{1,0:T(8,128)(2,1)S(1)}, u32[]{:S(2)}, u32[]{:S(2)}) %collective-permute-start.31) | collective-permute-done | bytes 110624 | tf_op jit(solution)/shard_map/ppermute | solution.py:32
  79.2 2.0 %collective-permute-done.32.refs_0_ = bf16[288,384]{1,0:T(8,128)(2,1)S(1)} collective-permute-done((bf16[288,384]{1,0:T(8,128)(2,1)S(1)}, bf16[288,384]{1,0:T(8,128)(2,1)S(1)}, u32[]{:S(2)}, u32[]{:S(2)}) %collective-permute-start.32) | collective-permute-done | bytes 221216 | tf_op jit(solution)/shard_map/ppermute | solution.py:32
  82.5 1.4 %collective-permute-start.33 = (bf16[144,384]{1,0:T(8,128)(2,1)}, bf16[144,384]{1,0:T(8,128)(2,1)}, u32[]{:S(2)}, u32[]{:S(2)}) collective-permute-start(bf16[144,384]{1,0:T(8,128)(2,1)} %get-tuple-element.97), channel_id=1, source_target_pairs={{0,8},{4,12},{8,0},{12,4},{1,9},{5,13},{9,1},{13,5},{2,10},{6,14},... | collective-permute-start | bytes 331784 | tf_op jit(solution)/shard_map/ppermute | solution.py:32
  84.7 1.4 %copy-done.3 = f32[1024,384]{1,0:T(8,128)S(1)} copy-done((f32[1024,384]{1,0:T(8,128)S(1)}, f32[1024,384]{1,0:T(8,128)}, u32[]{:S(2)}) %copy-start.3) | copy-done | bytes 1572888
  86.1 2.3 %shard_map.58 = bf16[1024,384]{1,0:T(8,128)(2,1)S(1)} custom-call(s32[2]{0:T(128)S(1)} %pad_add_fusion.place, bf16[256,384]{1,0:T(8,128)(2,1)S(1)} %collective-permute-done.26.low, bf16[1024,384]{1,0:T(8,128)(2,1)S(1)} %get-tuple-element.67.delta.own, bf16[256,384]{1,0:T(8,128)(2,1)S(1)} %collective-permute-done.27.high, f32[1024,384]{1,0:T(8,128)S(1)} %copy-done.3, ...), custom_call_target="tpu_custom_call" | custom-call | flops 1 | bytes 1 | tf_op jit(solution)/shard_map/pallas_call | solution.py:295
  88.4 1.3 %collective-permute-done.33 = bf16[144,384]{1,0:T(8,128)(2,1)} collective-permute-done((bf16[144,384]{1,0:T(8,128)(2,1)}, bf16[144,384]{1,0:T(8,128)(2,1)}, u32[]{:S(2)}, u32[]{:S(2)}) %collective-permute-start.33) | collective-permute-done | bytes 110624 | tf_op jit(solution)/shard_map/ppermute | solution.py:32
  91.4 1.6 %collective-permute-start.29 = (bf16[256,384]{1,0:T(8,128)(2,1)S(1)}, bf16[256,384]{1,0:T(8,128)(2,1)S(1)}, u32[]{:S(2)}, u32[]{:S(2)}) collective-permute-start(bf16[256,384]{1,0:T(8,128)(2,1)S(1)} %get-tuple-element.107), channel_id=1, source_target_pairs={{0,2},{1,3},{2,0},{3,1},{4,6},{5,7},{6,4},{7,5},{8,10},{9,11},{10,... | collective-permute-start | bytes 589832 | tf_op jit(solution)/shard_map/ppermute | solution.py:32
  93.3 3.1 %collective-permute-done.34 = bf16[1,144,384]{2,1,0:T(8,128)(2,1)S(1)} collective-permute-done((bf16[1,144,384]{2,1,0:T(8,128)(2,1)S(1)}, bf16[1,144,384]{2,1,0:T(8,128)(2,1)S(1)}, u32[]{:S(2)}, u32[]{:S(2)}) %collective-permute-start.34) | collective-permute-done | bytes 110624 | tf_op jit(solution)/shard_map/ppermute | solution.py:32
  97.5 2.1 %collective-permute-start.36 = (bf16[144,384]{1,0:T(8,128)(2,1)S(1)}, bf16[144,384]{1,0:T(8,128)(2,1)S(1)}, u32[]{:S(2)}, u32[]{:S(2)}) collective-permute-start(bf16[144,384]{1,0:T(8,128)(2,1)S(1)} %bitcast.12), channel_id=1, source_target_pairs={{0,8},{4,12},{8,0},{12,4},{1,9},{5,13},{9,1},{13,5},{2,10},{6,14},... | collective-permute-start | bytes 331784 | tf_op jit(solution)/shard_map/ppermute | solution.py:27
  99.6 2.5 %collective-permute-start.37 = (bf16[144,384]{1,0:T(8,128)(2,1)S(1)}, bf16[144,384]{1,0:T(8,128)(2,1)S(1)}, u32[]{:S(2)}, u32[]{:S(2)}) collective-permute-start(bf16[144,384]{1,0:T(8,128)(2,1)S(1)} %bitcast.13), channel_id=1, source_target_pairs={{0,12},{4,0},{8,4},{12,8},{1,13},{5,1},{9,5},{13,9},{2,14},{6,2},{... | collective-permute-start | bytes 331784 | tf_op jit(solution)/shard_map/ppermute | solution.py:27
  104.2 2.3 %collective-permute-done.36 = bf16[144,384]{1,0:T(8,128)(2,1)S(1)} collective-permute-done((bf16[144,384]{1,0:T(8,128)(2,1)S(1)}, bf16[144,384]{1,0:T(8,128)(2,1)S(1)}, u32[]{:S(2)}, u32[]{:S(2)}) %collective-permute-start.36) | collective-permute-done | bytes 110624 | tf_op jit(solution)/shard_map/ppermute | solution.py:27
  (84 shorter events, 22.4 us)
Async XLA Ops:
  0.7 14.4 %collective-permute-start.3 = (bf16[576,384]{1,0:T(8,128)(2,1)}, bf16[576,384]{1,0:T(8,128)(2,1)S(1)}, u32[]{:S(2)}, u32[]{:S(2)}) collective-permute-start(bf16[576,384]{1,0:T(8,128)(2,1)} %refs_0_.1), channel_id=1, source_target_pairs={{0,1},{1,0},{2,3},{3,2},{4,5},{5,4},{6,7},{7,6},{8,9},{9,8},{10,11... | collective-permute-start | bytes 1327112 | tf_op jit(solution)/shard_map/ppermute | solution.py:32
  3.1 3.0 %collective-permute-start = (bf16[256,384]{1,0:T(8,128)(2,1)}, bf16[256,384]{1,0:T(8,128)(2,1)S(1)}, u32[]{:S(2)}, u32[]{:S(2)}) collective-permute-start(bf16[256,384]{1,0:T(8,128)(2,1)} %get-tuple-element.115), channel_id=1, source_target_pairs={{0,1},{1,0},{2,3},{3,2},{4,5},{5,4},{6,7},{7,6},{8,9},{9,8},{10,11... | collective-permute-start | bytes 589832 | tf_op jit(solution)/shard_map/ppermute | solution.py:32
  3.2 8.5 %collective-permute-start.1 = (bf16[256,384]{1,0:T(8,128)(2,1)S(1)}, bf16[256,384]{1,0:T(8,128)(2,1)S(1)}, u32[]{:S(2)}, u32[]{:S(2)}) collective-permute-start(bf16[256,384]{1,0:T(8,128)(2,1)S(1)} %get-tuple-element.114), channel_id=1, source_target_pairs={{0,2},{1,3},{2,0},{3,1},{4,6},{5,7},{6,4},{7,5},{8,10},{9,11},{10,... | collective-permute-start | bytes 589832 | tf_op jit(solution)/shard_map/ppermute | solution.py:32
  6.0 9.0 %collective-permute-start.2 = (bf16[256,384]{1,0:T(8,128)(2,1)S(1)}, bf16[256,384]{1,0:T(8,128)(2,1)S(1)}, u32[]{:S(2)}, u32[]{:S(2)}) collective-permute-start(bf16[256,384]{1,0:T(8,128)(2,1)S(1)} %get-tuple-element.113), channel_id=1, source_target_pairs={{0,3},{1,2},{2,1},{3,0},{4,7},{5,6},{6,5},{7,4},{8,11},{9,10},{10,... | collective-permute-start | bytes 589832 | tf_op jit(solution)/shard_map/ppermute | solution.py:32
  15.8 12.4 %collective-permute-start.6 = (bf16[576,384]{1,0:T(8,128)(2,1)S(1)}, bf16[576,384]{1,0:T(8,128)(2,1)S(1)}, u32[]{:S(2)}, u32[]{:S(2)}) collective-permute-start(bf16[576,384]{1,0:T(8,128)(2,1)S(1)} %copy-done.4), channel_id=1, source_target_pairs={{0,2},{1,3},{2,0},{3,1},{4,6},{5,7},{6,4},{7,5},{8,10},{9,11},{10,... | collective-permute-start | bytes 1327112 | tf_op jit(solution)/shard_map/ppermute | solution.py:32
  17.2 16.5 %collective-permute-start.4 = (bf16[768,384]{1,0:T(8,128)(2,1)S(1)}, bf16[768,384]{1,0:T(8,128)(2,1)S(1)}, u32[]{:S(2)}, u32[]{:S(2)}) collective-permute-start(bf16[768,384]{1,0:T(8,128)(2,1)S(1)} %get-tuple-element.53), channel_id=1, source_target_pairs={{0,4},{4,8},{8,12},{1,5},{5,9},{9,13},{2,6},{6,10},{10,14},{3,7},{... | collective-permute-start | bytes 1769480 | tf_op jit(solution)/shard_map/ppermute | solution.py:22
  20.8 17.2 %collective-permute-start.5 = (bf16[768,384]{1,0:T(8,128)(2,1)S(1)}, bf16[768,384]{1,0:T(8,128)(2,1)S(1)}, u32[]{:S(2)}, u32[]{:S(2)}) collective-permute-start(bf16[768,384]{1,0:T(8,128)(2,1)S(1)} %get-tuple-element.55), channel_id=1, source_target_pairs={{4,0},{8,4},{12,8},{5,1},{9,5},{13,9},{6,2},{10,6},{14,10},{7,3},{... | collective-permute-start | bytes 1769480 | tf_op jit(solution)/shard_map/ppermute | solution.py:22
  28.2 9.8 %collective-permute-start.7 = (bf16[576,384]{1,0:T(8,128)(2,1)S(1)}, bf16[576,384]{1,0:T(8,128)(2,1)S(1)}, u32[]{:S(2)}, u32[]{:S(2)}) collective-permute-start(bf16[576,384]{1,0:T(8,128)(2,1)S(1)} %collective-permute-done.6.refs_2_), channel_id=1, source_target_pairs={{0,1},{1,0},{2,3},{3,2},{4,5},{5,4},{6,7},{7,6},{8,9},{9,8},{10,11... | collective-permute-start | bytes 1327112 | tf_op jit(solution)/shard_map/ppermute | solution.py:32
  28.2 16.1 %collective-permute-start.8 = (bf16[256,384]{1,0:T(8,128)(2,1)S(1)}, bf16[256,384]{1,0:T(8,128)(2,1)S(1)}, u32[]{:S(2)}, u32[]{:S(2)}) collective-permute-start(bf16[256,384]{1,0:T(8,128)(2,1)S(1)} %get-tuple-element.112), channel_id=1, source_target_pairs={{0,1},{1,0},{2,3},{3,2},{4,5},{5,4},{6,7},{7,6},{8,9},{9,8},{10,11... | collective-permute-start | bytes 589832 | tf_op jit(solution)/shard_map/ppermute | solution.py:32
  28.8 15.5 %collective-permute-start.10 = (bf16[256,384]{1,0:T(8,128)(2,1)S(1)}, bf16[256,384]{1,0:T(8,128)(2,1)S(1)}, u32[]{:S(2)}, u32[]{:S(2)}) collective-permute-start(bf16[256,384]{1,0:T(8,128)(2,1)S(1)} %get-tuple-element.60), channel_id=1, source_target_pairs={{0,3},{1,2},{2,1},{3,0},{4,7},{5,6},{6,5},{7,4},{8,11},{9,10},{10,... | collective-permute-start | bytes 589832 | tf_op jit(solution)/shard_map/ppermute | solution.py:32
  33.8 10.6 %collective-permute-start.9 = (bf16[256,384]{1,0:T(8,128)(2,1)S(1)}, bf16[256,384]{1,0:T(8,128)(2,1)S(1)}, u32[]{:S(2)}, u32[]{:S(2)}) collective-permute-start(bf16[256,384]{1,0:T(8,128)(2,1)S(1)} %get-tuple-element.59), channel_id=1, source_target_pairs={{0,2},{1,3},{2,0},{3,1},{4,6},{5,7},{6,4},{7,5},{8,10},{9,11},{10,... | collective-permute-start | bytes 589832 | tf_op jit(solution)/shard_map/ppermute | solution.py:32
  45.3 12.2 %collective-permute-start.11 = (bf16[512,384]{1,0:T(8,128)(2,1)S(1)}, bf16[512,384]{1,0:T(8,128)(2,1)S(1)}, u32[]{:S(2)}, u32[]{:S(2)}) collective-permute-start(bf16[512,384]{1,0:T(8,128)(2,1)S(1)} %get-tuple-element.61), channel_id=1, source_target_pairs={{0,4},{4,8},{8,12},{1,5},{5,9},{9,13},{2,6},{6,10},{10,14},{3,7},{... | collective-permute-start | bytes 1179656 | tf_op jit(solution)/shard_map/ppermute | solution.py:22
  48.8 11.8 %collective-permute-start.12 = (bf16[512,384]{1,0:T(8,128)(2,1)S(1)}, bf16[512,384]{1,0:T(8,128)(2,1)S(1)}, u32[]{:S(2)}, u32[]{:S(2)}) collective-permute-start(bf16[512,384]{1,0:T(8,128)(2,1)S(1)} %get-tuple-element.63), channel_id=1, source_target_pairs={{4,0},{8,4},{12,8},{5,1},{9,5},{13,9},{6,2},{10,6},{14,10},{7,3},{... | collective-permute-start | bytes 1179656 | tf_op jit(solution)/shard_map/ppermute | solution.py:22
  52.6 1.4 %collective-permute-start.17 = (f32[72,384]{1,0:T(8,128)S(1)}, f32[72,384]{1,0:T(8,128)S(1)}, u32[]{:S(2)}, u32[]{:S(2)}) collective-permute-start(f32[72,384]{1,0:T(8,128)S(1)} %get-tuple-element.77), channel_id=1, source_target_pairs={{0,1},{1,0},{2,3},{3,2},{4,5},{5,4},{6,7},{7,6},{8,9},{9,8},{10,11... | collective-permute-start | bytes 331784 | tf_op jit(solution)/shard_map/ppermute | solution.py:32
  52.7 1.5 %collective-permute-start.18 = (f32[72,384]{1,0:T(8,128)S(1)}, f32[72,384]{1,0:T(8,128)S(1)}, u32[]{:S(2)}, u32[]{:S(2)}) collective-permute-start(f32[72,384]{1,0:T(8,128)S(1)} %get-tuple-element.78), channel_id=1, source_target_pairs={{0,1},{1,0},{2,3},{3,2},{4,5},{5,4},{6,7},{7,6},{8,9},{9,8},{10,11... | collective-permute-start | bytes 331784 | tf_op jit(solution)/shard_map/ppermute | solution.py:32
  60.6 7.8 %collective-permute-start.25 = (bf16[288,384]{1,0:T(8,128)(2,1)S(1)}, bf16[288,384]{1,0:T(8,128)(2,1)S(1)}, u32[]{:S(2)}, u32[]{:S(2)}) collective-permute-start(bf16[288,384]{1,0:T(8,128)(2,1)S(1)} %get-tuple-element.86), channel_id=1, source_target_pairs={{0,4},{4,0},{8,12},{12,8},{1,5},{5,1},{9,13},{13,9},{2,6},{6,2},{1... | collective-permute-start | bytes 663560 | tf_op jit(solution)/shard_map/ppermute | solution.py:32
  67.4 1.5 %collective-permute-start.13 = (f32[144,384]{1,0:T(8,128)S(1)}, f32[144,384]{1,0:T(8,128)S(1)}, u32[]{:S(2)}, u32[]{:S(2)}) collective-permute-start(f32[144,384]{1,0:T(8,128)S(1)} %get-tuple-element.71), channel_id=1, source_target_pairs={{0,1},{1,0},{2,3},{3,2},{4,5},{5,4},{6,7},{7,6},{8,9},{9,8},{10,11... | collective-permute-start | bytes 663560 | tf_op jit(solution)/shard_map/ppermute | solution.py:32
  67.4 1.8 %collective-permute-start.14 = (f32[144,384]{1,0:T(8,128)S(1)}, f32[144,384]{1,0:T(8,128)S(1)}, u32[]{:S(2)}, u32[]{:S(2)}) collective-permute-start(f32[144,384]{1,0:T(8,128)S(1)} %get-tuple-element.72), channel_id=1, source_target_pairs={{0,1},{1,0},{2,3},{3,2},{4,5},{5,4},{6,7},{7,6},{8,9},{9,8},{10,11... | collective-permute-start | bytes 663560 | tf_op jit(solution)/shard_map/ppermute | solution.py:32
  67.9 1.6 %collective-permute-start.15 = (f32[144,384]{1,0:T(8,128)S(1)}, f32[144,384]{1,0:T(8,128)S(1)}, u32[]{:S(2)}, u32[]{:S(2)}) collective-permute-start(f32[144,384]{1,0:T(8,128)S(1)} %get-tuple-element.73), channel_id=1, source_target_pairs={{0,1},{1,0},{2,3},{3,2},{4,5},{5,4},{6,7},{7,6},{8,9},{9,8},{10,11... | collective-permute-start | bytes 663560 | tf_op jit(solution)/shard_map/ppermute | solution.py:32
  67.9 1.9 %collective-permute-start.16 = (f32[144,384]{1,0:T(8,128)S(1)}, f32[144,384]{1,0:T(8,128)S(1)}, u32[]{:S(2)}, u32[]{:S(2)}) collective-permute-start(f32[144,384]{1,0:T(8,128)S(1)} %get-tuple-element.74), channel_id=1, source_target_pairs={{0,1},{1,0},{2,3},{3,2},{4,5},{5,4},{6,7},{7,6},{8,9},{9,8},{10,11... | collective-permute-start | bytes 663560 | tf_op jit(solution)/shard_map/ppermute | solution.py:32
  70.5 10.7 %collective-permute-start.32 = (bf16[288,384]{1,0:T(8,128)(2,1)S(1)}, bf16[288,384]{1,0:T(8,128)(2,1)S(1)}, u32[]{:S(2)}, u32[]{:S(2)}) collective-permute-start(bf16[288,384]{1,0:T(8,128)(2,1)S(1)} %get-tuple-element.87), channel_id=1, source_target_pairs={{0,4},{4,0},{8,12},{12,8},{1,5},{5,1},{9,13},{13,9},{2,6},{6,2},{1... | collective-permute-start | bytes 663560 | tf_op jit(solution)/shard_map/ppermute | solution.py:32
  71.7 7.5 %collective-permute-start.31 = (bf16[144,384]{1,0:T(8,128)(2,1)S(1)}, bf16[144,384]{1,0:T(8,128)(2,1)S(1)}, u32[]{:S(2)}, u32[]{:S(2)}) collective-permute-start(bf16[144,384]{1,0:T(8,128)(2,1)S(1)} %get-tuple-element.94), channel_id=1, source_target_pairs={{0,8},{4,12},{8,0},{12,4},{1,9},{5,13},{9,1},{13,5},{2,10},{6,14},... | collective-permute-start | bytes 331784 | tf_op jit(solution)/shard_map/ppermute | solution.py:32
  73.0 10.8 %collective-permute-start.26 = (bf16[256,384]{1,0:T(8,128)(2,1)}, bf16[256,384]{1,0:T(8,128)(2,1)S(1)}, u32[]{:S(2)}, u32[]{:S(2)}) collective-permute-start(bf16[256,384]{1,0:T(8,128)(2,1)} %get-tuple-element.88), channel_id=1, source_target_pairs={{0,4},{4,8},{8,12},{1,5},{5,9},{9,13},{2,6},{6,10},{10,14},{3,7},{... | collective-permute-start | bytes 589832 | tf_op jit(solution)/shard_map/ppermute | solution.py:22
  75.2 9.5 %collective-permute-start.27 = (bf16[256,384]{1,0:T(8,128)(2,1)}, bf16[256,384]{1,0:T(8,128)(2,1)S(1)}, u32[]{:S(2)}, u32[]{:S(2)}) collective-permute-start(bf16[256,384]{1,0:T(8,128)(2,1)} %get-tuple-element.89), channel_id=1, source_target_pairs={{4,0},{8,4},{12,8},{5,1},{9,5},{13,9},{6,2},{10,6},{14,10},{7,3},{... | collective-permute-start | bytes 589832 | tf_op jit(solution)/shard_map/ppermute | solution.py:22
  82.5 7.2 %collective-permute-start.33 = (bf16[144,384]{1,0:T(8,128)(2,1)}, bf16[144,384]{1,0:T(8,128)(2,1)}, u32[]{:S(2)}, u32[]{:S(2)}) collective-permute-start(bf16[144,384]{1,0:T(8,128)(2,1)} %get-tuple-element.97), channel_id=1, source_target_pairs={{0,8},{4,12},{8,0},{12,4},{1,9},{5,13},{9,1},{13,5},{2,10},{6,14},... | collective-permute-start | bytes 331784 | tf_op jit(solution)/shard_map/ppermute | solution.py:32
  90.6 5.8 %collective-permute-start.34 = (bf16[1,144,384]{2,1,0:T(8,128)(2,1)S(1)}, bf16[1,144,384]{2,1,0:T(8,128)(2,1)S(1)}, u32[]{:S(2)}, u32[]{:S(2)}) collective-permute-start(bf16[1,144,384]{2,1,0:T(8,128)(2,1)S(1)} %fusion), channel_id=1, source_target_pairs={{0,2},{1,3},{2,0},{3,1},{4,6},{5,7},{6,4},{7,5},{8,10},{9,11},{10,... | collective-permute-start | bytes 331784 | tf_op jit(solution)/shard_map/ppermute | solution.py:32
  91.3 8.2 %collective-permute-start.28 = (bf16[256,384]{1,0:T(8,128)(2,1)S(1)}, bf16[256,384]{1,0:T(8,128)(2,1)S(1)}, u32[]{:S(2)}, u32[]{:S(2)}) collective-permute-start(bf16[256,384]{1,0:T(8,128)(2,1)S(1)} %get-tuple-element.108), channel_id=1, source_target_pairs={{0,1},{1,0},{2,3},{3,2},{4,5},{5,4},{6,7},{7,6},{8,9},{9,8},{10,11... | collective-permute-start | bytes 589832 | tf_op jit(solution)/shard_map/ppermute | solution.py:32
  91.4 10.6 %collective-permute-start.29 = (bf16[256,384]{1,0:T(8,128)(2,1)S(1)}, bf16[256,384]{1,0:T(8,128)(2,1)S(1)}, u32[]{:S(2)}, u32[]{:S(2)}) collective-permute-start(bf16[256,384]{1,0:T(8,128)(2,1)S(1)} %get-tuple-element.107), channel_id=1, source_target_pairs={{0,2},{1,3},{2,0},{3,1},{4,6},{5,7},{6,4},{7,5},{8,10},{9,11},{10,... | collective-permute-start | bytes 589832 | tf_op jit(solution)/shard_map/ppermute | solution.py:32
  93.0 10.0 %collective-permute-start.30 = (bf16[256,384]{1,0:T(8,128)(2,1)S(1)}, bf16[256,384]{1,0:T(8,128)(2,1)S(1)}, u32[]{:S(2)}, u32[]{:S(2)}) collective-permute-start(bf16[256,384]{1,0:T(8,128)(2,1)S(1)} %get-tuple-element.106), channel_id=1, source_target_pairs={{0,3},{1,2},{2,1},{3,0},{4,7},{5,6},{6,5},{7,4},{8,11},{9,10},{10,... | collective-permute-start | bytes 589832 | tf_op jit(solution)/shard_map/ppermute | solution.py:32
  97.4 6.8 %collective-permute-start.35 = (bf16[144,384]{1,0:T(8,128)(2,1)S(1)}, bf16[144,384]{1,0:T(8,128)(2,1)S(1)}, u32[]{:S(2)}, u32[]{:S(2)}) collective-permute-start(bf16[144,384]{1,0:T(8,128)(2,1)S(1)} %bitcast.11), channel_id=1, source_target_pairs={{0,4},{4,8},{8,12},{12,0},{1,5},{5,9},{9,13},{13,1},{2,6},{6,10},{... | collective-permute-start | bytes 331784 | tf_op jit(solution)/shard_map/ppermute | solution.py:27
  97.5 9.1 %collective-permute-start.36 = (bf16[144,384]{1,0:T(8,128)(2,1)S(1)}, bf16[144,384]{1,0:T(8,128)(2,1)S(1)}, u32[]{:S(2)}, u32[]{:S(2)}) collective-permute-start(bf16[144,384]{1,0:T(8,128)(2,1)S(1)} %bitcast.12), channel_id=1, source_target_pairs={{0,8},{4,12},{8,0},{12,4},{1,9},{5,13},{9,1},{13,5},{2,10},{6,14},... | collective-permute-start | bytes 331784 | tf_op jit(solution)/shard_map/ppermute | solution.py:27
  99.6 7.0 %collective-permute-start.37 = (bf16[144,384]{1,0:T(8,128)(2,1)S(1)}, bf16[144,384]{1,0:T(8,128)(2,1)S(1)}, u32[]{:S(2)}, u32[]{:S(2)}) collective-permute-start(bf16[144,384]{1,0:T(8,128)(2,1)S(1)} %bitcast.13), channel_id=1, source_target_pairs={{0,12},{4,0},{8,4},{12,8},{1,13},{5,1},{9,5},{13,9},{2,14},{6,2},{... | collective-permute-start | bytes 331784 | tf_op jit(solution)/shard_map/ppermute | solution.py:27
  (13 other events, 77.3 us)

commit v7 on v6

--- a/solution.py
+++ b/solution.py
@@ -104,7 +104,7 @@
 
 def forward_kernel(sizes, place, low, own, high, *refs):
     groups, members, q, near, far = sizes
-    w_pieces, (act_stack, hid_stack, slope_one, slope_two, w_out, hid) = (
+    w_pieces, (hid, slope_one, slope_two, w_out) = (
         refs[:members],
         refs[members:],
     )
@@ -128,8 +128,6 @@
         stacks = []
         for b in range(k - far, k - far + wide):
             stacks.append(jnp.concatenate([block(b - near), block(b), block(b + near)], 1))
-            if 0 <= b < members:
-                act_stack[b * q : (b + 1) * q] = stacks[-1]
         return dot(jnp.concatenate(stacks, 0), w_out[:taps])
 
     def first_end(k, pres):
@@ -149,7 +147,6 @@
     def second_layer(b):
         taken = [hid[(b + k * far) * q : (b + k * far + wide) * q] for k in range(3)]
         stack = jnp.concatenate(taken, 1)
-        hid_stack[b * q : (b + wide) * q] = stack
         return dot(stack, w_out[taps:])
 
     def second_end(b, pre):
@@ -188,8 +185,17 @@
     to_low[...] = delta[: far * q]
 
 
-def grad_kernel(sizes, scale, place, stack, delta, *refs):
-    members, halo, splits = sizes
+def window(low, own, high, shift):
+    rows = own.shape[0]
+    if shift < 0:
+        return jnp.concatenate([low[low.shape[0] + shift :], own[: rows + shift]], 0)
+    if shift > 0:
+        return jnp.concatenate([own[shift:], high[:shift]], 0)
+    return own[...]
+
+
+def grad_kernel(sizes, scale, place, low, own, high, delta, *refs):
+    members, halo, splits, step = sizes
     outs = refs[-(1 + splits + (2 if halo else 0)) :]
     keep, sends = outs[0], outs[1 : 1 + splits]
     odd = place[1] & 1
@@ -199,7 +205,7 @@
     for k in range(3):
         first = k * channels
         part = scale * lax.dot_general(
-            stack[:, first : first + channels],
+            window(low, own, high, (k - 1) * step),
             delta[...],
             (((0,), (0,)), ((), ())),
             preferred_element_type=F32,
@@ -227,6 +233,12 @@
         to_high, to_low = outs[-2:]
         to_high[...] = delta[delta.shape[0] - halo :]
         to_low[...] = delta[:halo]
+
+
+def grad_two_kernel(sizes, scale, place, hidden, delta, *refs):
+    step, rows = sizes[3], delta.shape[0]
+    low, own, high = hidden.at[:step], hidden.at[step : step + rows], hidden.at[step + rows :]
+    grad_kernel(sizes, scale, place, low, own, high, delta, *refs)
 
 
 def share_kernel(n, splits, place, keep, *refs):
@@ -434,14 +446,12 @@
     w_pieces = gather_pieces(weights, near_weights, "sub", act)
     c_pieces = regrouped(cotangent, w_pieces[members // 2], near_cot)
 
-    act_stack, hid_stack, slope_one, slope_two, all_weights = kernel(
+    hidden, slope_one, slope_two, all_weights = kernel(
         functools.partial(forward_kernel, (groups, members, q, near, far)),
-        ((count, taps), BF16),
-        ((count, taps), BF16),
+        ((count + 2 * far * q, channels), BF16),
         ((count, channels), F32),
         ((count, channels), F32),
         ((2 * taps, channels), BF16),
-        scratch=(pltpu.VMEM(((members + 2 * far) * q, channels), BF16),),
         operands=(low, act, high, *w_pieces),
     )
     delta_two, up_two, down_two, cot = kernel(
@@ -458,10 +468,10 @@
     share = ((taps // 2 // splits, channels), F32)
     less = ((taps // 2 // more, channels), F32)
     keep_two, *send_two = kernel(
-        functools.partial(grad_kernel, (members, 0, splits), grad_scale),
+        functools.partial(grad_two_kernel, (members, 0, splits, far * q), grad_scale),
         half,
         *[share] * splits,
-        operands=(hid_stack, delta_two),
+        operands=(hidden, delta_two),
     )
     kept_two, sent_two = core_sum_halving(place, keep_two, send_two)
     back_one, delta_one = call(
@@ -470,12 +480,12 @@
         operands=(two_low, delta_two, two_high, cot, slope_one, all_weights),
     )
     keep_one, *send_one, up_one, down_one = kernel(
-        functools.partial(grad_kernel, (members, near * q, more), grad_scale),
+        functools.partial(grad_kernel, (members, near * q, more, near * q), grad_scale),
         half,
         *[less] * more,
         ((near * q, channels), BF16),
         ((near * q, channels), BF16),
-        operands=(act_stack, delta_one),
+        operands=(low, act, high, delta_one),
     )
     got_two = first_half(after(sent_two, (two_low, two_high)))
     kept_one, sent_one = core_sum_halving(place, keep_one, send_one, (got_two,))
@@ -491,7 +501,7 @@
         scalars=1,
         operands=(place, one_low, delta_one, one_high, back_one, all_weights),
     )
-    total_one = added(after(parts_one, grad_in))
+    total_one = added(after(parts_one, (one_low, one_high)))
     total_two = added(parts_two)
     part = chip_sum(total_one, total_two, j)
     sent = part.astype(BF16)

time: 108 us -> 107 us (level)
  transfers between devices with their start and end apart: 38 -> 38, of which waited for: 22 -> 22; matrix products, arithmetic and copies ran while one was open for 3% -> 3% of each run, Pallas kernels for 18% -> 17%
where the time goes in v7:
time: 107 us
  waiting for transfers between devices  43.3 us (40%)
  starting transfers between devices  35.3 us (33%)
  Pallas kernels  20.8 us (19%)
  local copies, waits for them, and re-layouts  4.66 us (4%)
  other arithmetic  2.07 us (2%)
    ppermute x29, waiting for transfers between devices, swapped(): return lax.ppermute(block, axis, [(i, i ^ bits) for i in range(n)])  28.8 us
    pallas_call x11, Pallas kernels, call(): pl.pallas_call(kernel, out_shape=tuple((jax.ShapeDtypeStruct(shape, kind)...  20.8 us
    ppermute x29, starting transfers between devices, swapped(): return lax.ppermute(block, axis, [(i, i ^ bits) for i in range(n)])  17.7 us
    ppermute x6, starting transfers between devices, shifted(): return lax.ppermute(block, axis, route)  13.1 us
    ppermute x6, waiting for transfers between devices, shifted(): return lax.ppermute(block, axis, route)  11.1 us
    ppermute x3, starting transfers between devices, turned(): return lax.ppermute(block, axis, [(i, (i + turn) % n) for i in range(n)])  4.56 us
    ppermute x3, waiting for transfers between devices, turned(): return lax.ppermute(block, axis, [(i, (i + turn) % n) for i in range(n)])  3.36 us
    unnamed x14, local copies, waits for them, and re-layouts  2.34 us
  transfers between devices with their start and end apart: 38, of which 22 were waited for; matrix products, arithmetic and copies ran while one was open for 3% of the time, Pallas kernels for 17%

profile of v7, /device:TPU:0, one launch (start us, length us, event | category | flops | bytes accessed | tf_op | source)
XLA Modules:
  0.0 107.1 jit_solution(18195356661703891709)
XLA Ops:
  1.2 1.9 %constant_dynamic-slice_fusion.3 = (bf16[256,384]{1,0:T(8,128)(2,1)S(1)}, bf16[256,384]{1,0:T(8,128)(2,1)S(1)}, bf16[256,384]{1,0:T(8,128)(2,1)}) fusion(bf16[1024,384]{1,0:T(8,128)(2,1)} %block.1, s32[]{:T(128)S(6)} %select_n.66, s32[]{:T(128)S(6)} %select_n.65, s32[]{:T(128)S(6)} %select_n.64), kind=kLoop, calls=%fused_computation.17 | loop fusion | bytes 1179660 | tf_op jit(solution)/shard_map/dynamic_slice | solution.py:48
  3.2 2.8 %collective-permute-start.1 = (bf16[256,384]{1,0:T(8,128)(2,1)S(1)}, bf16[256,384]{1,0:T(8,128)(2,1)S(1)}, u32[]{:S(2)}, u32[]{:S(2)}) collective-permute-start(bf16[256,384]{1,0:T(8,128)(2,1)S(1)} %get-tuple-element.112), channel_id=1, source_target_pairs={{0,2},{1,3},{2,0},{3,1},{4,6},{5,7},{6,4},{7,5},{8,10},{9,11},{10,... | collective-permute-start | bytes 589832 | tf_op jit(solution)/shard_map/ppermute | solution.py:32
  6.1 5.6 %collective-permute-done.1.refs_1_ = bf16[256,384]{1,0:T(8,128)(2,1)S(1)} collective-permute-done((bf16[256,384]{1,0:T(8,128)(2,1)S(1)}, bf16[256,384]{1,0:T(8,128)(2,1)S(1)}, u32[]{:S(2)}, u32[]{:S(2)}) %collective-permute-start.1) | collective-permute-done | bytes 196640 | tf_op jit(solution)/shard_map/ppermute | solution.py:32
  11.7 3.3 %collective-permute-done.2.refs_2_ = bf16[256,384]{1,0:T(8,128)(2,1)S(1)} collective-permute-done((bf16[256,384]{1,0:T(8,128)(2,1)S(1)}, bf16[256,384]{1,0:T(8,128)(2,1)S(1)}, u32[]{:S(2)}, u32[]{:S(2)}) %collective-permute-start.2) | collective-permute-done | bytes 196640 | tf_op jit(solution)/shard_map/ppermute | solution.py:32
  15.8 1.5 %collective-permute-start.6 = (bf16[576,384]{1,0:T(8,128)(2,1)S(1)}, bf16[576,384]{1,0:T(8,128)(2,1)S(1)}, u32[]{:S(2)}, u32[]{:S(2)}) collective-permute-start(bf16[576,384]{1,0:T(8,128)(2,1)S(1)} %copy-done.4), channel_id=1, source_target_pairs={{0,2},{1,3},{2,0},{3,1},{4,6},{5,7},{6,4},{7,5},{8,10},{9,11},{10,... | collective-permute-start | bytes 1327112 | tf_op jit(solution)/shard_map/ppermute | solution.py:32
  17.2 3.5 %collective-permute-start.4 = (bf16[768,384]{1,0:T(8,128)(2,1)S(1)}, bf16[768,384]{1,0:T(8,128)(2,1)S(1)}, u32[]{:S(2)}, u32[]{:S(2)}) collective-permute-start(bf16[768,384]{1,0:T(8,128)(2,1)S(1)} %get-tuple-element.52), channel_id=1, source_target_pairs={{0,4},{4,8},{8,12},{1,5},{5,9},{9,13},{2,6},{6,10},{10,14},{3,7},{... | collective-permute-start | bytes 1769480 | tf_op jit(solution)/shard_map/ppermute | solution.py:22
  22.1 6.1 %collective-permute-done.6.refs_2_ = bf16[576,384]{1,0:T(8,128)(2,1)S(1)} collective-permute-done((bf16[576,384]{1,0:T(8,128)(2,1)S(1)}, bf16[576,384]{1,0:T(8,128)(2,1)S(1)}, u32[]{:S(2)}, u32[]{:S(2)}) %collective-permute-start.6) | collective-permute-done | bytes 442400 | tf_op jit(solution)/shard_map/ppermute | solution.py:32
  28.8 1.4 %collective-permute-start.10 = (bf16[256,384]{1,0:T(8,128)(2,1)S(1)}, bf16[256,384]{1,0:T(8,128)(2,1)S(1)}, u32[]{:S(2)}, u32[]{:S(2)}) collective-permute-start(bf16[256,384]{1,0:T(8,128)(2,1)S(1)} %get-tuple-element.58), channel_id=1, source_target_pairs={{0,3},{1,2},{2,1},{3,0},{4,7},{5,6},{6,5},{7,4},{8,11},{9,10},{10,... | collective-permute-start | bytes 589832 | tf_op jit(solution)/shard_map/ppermute | solution.py:32
  30.2 3.5 %collective-permute-done.4.low = bf16[768,384]{1,0:T(8,128)(2,1)S(1)} collective-permute-done((bf16[768,384]{1,0:T(8,128)(2,1)S(1)}, bf16[768,384]{1,0:T(8,128)(2,1)S(1)}, u32[]{:S(2)}, u32[]{:S(2)}) %collective-permute-start.4) | collective-permute-done | bytes 589856 | tf_op jit(solution)/shard_map/ppermute | solution.py:22
  34.3 3.6 %collective-permute-done.5.high = bf16[768,384]{1,0:T(8,128)(2,1)S(1)} collective-permute-done((bf16[768,384]{1,0:T(8,128)(2,1)S(1)}, bf16[768,384]{1,0:T(8,128)(2,1)S(1)}, u32[]{:S(2)}, u32[]{:S(2)}) %collective-permute-start.5) | collective-permute-done | bytes 589856 | tf_op jit(solution)/shard_map/ppermute | solution.py:22
  37.9 6.0 %shard_map.51 = (bf16[2048,384]{1,0:T(8,128)(2,1)S(1)}, f32[1024,384]{1,0:T(8,128)S(1)}, f32[1024,384]{1,0:T(8,128)S(1)}, bf16[2304,384]{1,0:T(8,128)(2,1)S(1)}) custom-call(s32[2]{0:T(128)S(1)} %pad_add_fusion.place, bf16[768,384]{1,0:T(8,128)(2,1)S(1)} %collective-permute-done.4.low, bf16[1024,384]{1,0:T(8,128)(2,1)S(1)} %get-tuple-element.53.own, ...), custom_call_target="tpu_custom_call" | custom-call | flops 1 | bytes 1 | tf_op jit(solution)/shard_map/pallas_call | solution.py:307
  44.9 3.5 %collective-permute-start.11 = (bf16[512,384]{1,0:T(8,128)(2,1)S(1)}, bf16[512,384]{1,0:T(8,128)(2,1)S(1)}, u32[]{:S(2)}, u32[]{:S(2)}) collective-permute-start(bf16[512,384]{1,0:T(8,128)(2,1)S(1)} %get-tuple-element.59), channel_id=1, source_target_pairs={{0,4},{4,8},{8,12},{1,5},{5,9},{9,13},{2,6},{6,10},{10,14},{3,7},{... | collective-permute-start | bytes 1179656 | tf_op jit(solution)/shard_map/ppermute | solution.py:22
  48.4 1.3 %collective-permute-start.12 = (bf16[512,384]{1,0:T(8,128)(2,1)S(1)}, bf16[512,384]{1,0:T(8,128)(2,1)S(1)}, u32[]{:S(2)}, u32[]{:S(2)}) collective-permute-start(bf16[512,384]{1,0:T(8,128)(2,1)S(1)} %get-tuple-element.61), channel_id=1, source_target_pairs={{4,0},{8,4},{12,8},{5,1},{9,5},{13,9},{6,2},{10,6},{14,10},{7,3},{... | collective-permute-start | bytes 1179656 | tf_op jit(solution)/shard_map/ppermute | solution.py:22
  49.7 2.5 %shard_map.55 = (f32[576,384]{1,0:T(8,128)S(1)}, f32[72,384]{1,0:T(8,128)S(1)}, f32[72,384]{1,0:T(8,128)S(1)}, f32[72,384]{1,0:T(8,128)S(1)}, f32[72,384]{1,0:T(...) custom-call(s32[2]{0:T(128)S(1)} %pad_add_fusion.place, ...), custom_call_target="tpu_custom_call" | custom-call | flops 1 | bytes 1 | tf_op jit(solution)/shard_map/pallas_call | solution.py:307
  57.1 3.2 %collective-permute-done.12.high = bf16[512,384]{1,0:T(8,128)(2,1)S(1)} collective-permute-done((bf16[512,384]{1,0:T(8,128)(2,1)S(1)}, bf16[512,384]{1,0:T(8,128)(2,1)S(1)}, u32[]{:S(2)}, u32[]{:S(2)}) %collective-permute-start.12) | collective-permute-done | bytes 393248 | tf_op jit(solution)/shard_map/ppermute | solution.py:22
  60.2 1.6 %collective-permute-start.25 = (bf16[288,384]{1,0:T(8,128)(2,1)S(1)}, bf16[288,384]{1,0:T(8,128)(2,1)S(1)}, u32[]{:S(2)}, u32[]{:S(2)}) collective-permute-start(bf16[288,384]{1,0:T(8,128)(2,1)S(1)} %get-tuple-element.84), channel_id=1, source_target_pairs={{0,4},{4,0},{8,12},{12,8},{1,5},{5,1},{9,13},{13,9},{2,6},{6,2},{1... | collective-permute-start | bytes 663560 | tf_op jit(solution)/shard_map/ppermute | solution.py:32
  61.8 1.7 %shard_map.53 = (f32[1024,384]{1,0:T(8,128)S(1)}, bf16[1024,384]{1,0:T(8,128)(2,1)S(1)}) custom-call(bf16[512,384]{1,0:T(8,128)(2,1)S(1)} %collective-permute-done.11.low, bf16[1024,384]{1,0:T(8,128)(2,1)S(1)} %get-tuple-element.60.own.delta, bf16[512,384]{1,0:T(8,128)(2,1)S(1)} %collective-permute-done.12.high, ...), custom_call_target="tpu_custom_call" | custom-call | flops 1 | bytes 1 | tf_op jit(solution)/shard_map/pallas_call | solution.py:307
  63.5 3.4 %shard_map.54 = (f32[576,384]{1,0:T(8,128)S(1)}, f32[144,384]{1,0:T(8,128)S(1)}, f32[144,384]{1,0:T(8,128)S(1)}, f32[144,384]{1,0:T(8,128)S(1)}, f32[144,384]{1,...) custom-call(s32[2]{0:T(128)S(1)} %pad_add_fusion.place, ...), custom_call_target="tpu_custom_call" | custom-call | flops 1 | bytes 1 | tf_op jit(solution)/shard_map/pallas_call | solution.py:307
  71.2 1.3 %collective-permute-start.31 = (bf16[144,384]{1,0:T(8,128)(2,1)S(1)}, bf16[144,384]{1,0:T(8,128)(2,1)S(1)}, u32[]{:S(2)}, u32[]{:S(2)}) collective-permute-start(bf16[144,384]{1,0:T(8,128)(2,1)S(1)} %get-tuple-element.92), channel_id=1, source_target_pairs={{0,8},{4,12},{8,0},{12,4},{1,9},{5,13},{9,1},{13,5},{2,10},{6,14},... | collective-permute-start | bytes 331784 | tf_op jit(solution)/shard_map/ppermute | solution.py:32
  72.6 2.2 %collective-permute-start.26 = (bf16[256,384]{1,0:T(8,128)(2,1)}, bf16[256,384]{1,0:T(8,128)(2,1)S(1)}, u32[]{:S(2)}, u32[]{:S(2)}) collective-permute-start(bf16[256,384]{1,0:T(8,128)(2,1)} %get-tuple-element.86), channel_id=1, source_target_pairs={{0,4},{4,8},{8,12},{1,5},{5,9},{9,13},{2,6},{6,10},{10,14},{3,7},{... | collective-permute-start | bytes 589832 | tf_op jit(solution)/shard_map/ppermute | solution.py:22
  74.8 1.3 %collective-permute-start.27 = (bf16[256,384]{1,0:T(8,128)(2,1)}, bf16[256,384]{1,0:T(8,128)(2,1)S(1)}, u32[]{:S(2)}, u32[]{:S(2)}) collective-permute-start(bf16[256,384]{1,0:T(8,128)(2,1)} %get-tuple-element.87), channel_id=1, source_target_pairs={{4,0},{8,4},{12,8},{5,1},{9,5},{13,9},{6,2},{10,6},{14,10},{7,3},{... | collective-permute-start | bytes 589832 | tf_op jit(solution)/shard_map/ppermute | solution.py:22
  76.1 2.7 %collective-permute-done.31.refs_1_ = bf16[144,384]{1,0:T(8,128)(2,1)S(1)} collective-permute-done((bf16[144,384]{1,0:T(8,128)(2,1)S(1)}, bf16[144,384]{1,0:T(8,128)(2,1)S(1)}, u32[]{:S(2)}, u32[]{:S(2)}) %collective-permute-start.31) | collective-permute-done | bytes 110624 | tf_op jit(solution)/shard_map/ppermute | solution.py:32
  78.7 2.0 %collective-permute-done.32.refs_0_ = bf16[288,384]{1,0:T(8,128)(2,1)S(1)} collective-permute-done((bf16[288,384]{1,0:T(8,128)(2,1)S(1)}, bf16[288,384]{1,0:T(8,128)(2,1)S(1)}, u32[]{:S(2)}, u32[]{:S(2)}) %collective-permute-start.32) | collective-permute-done | bytes 221216 | tf_op jit(solution)/shard_map/ppermute | solution.py:32
  82.0 1.4 %collective-permute-start.33 = (bf16[144,384]{1,0:T(8,128)(2,1)}, bf16[144,384]{1,0:T(8,128)(2,1)}, u32[]{:S(2)}, u32[]{:S(2)}) collective-permute-start(bf16[144,384]{1,0:T(8,128)(2,1)} %get-tuple-element.95), channel_id=1, source_target_pairs={{0,8},{4,12},{8,0},{12,4},{1,9},{5,13},{9,1},{13,5},{2,10},{6,14},... | collective-permute-start | bytes 331784 | tf_op jit(solution)/shard_map/ppermute | solution.py:32
  84.2 1.4 %copy-done.3 = f32[1024,384]{1,0:T(8,128)S(1)} copy-done((f32[1024,384]{1,0:T(8,128)S(1)}, f32[1024,384]{1,0:T(8,128)}, u32[]{:S(2)}) %copy-start.3) | copy-done | bytes 1572888
  85.6 2.3 %shard_map.58 = bf16[1024,384]{1,0:T(8,128)(2,1)S(1)} custom-call(s32[2]{0:T(128)S(1)} %pad_add_fusion.place, bf16[256,384]{1,0:T(8,128)(2,1)S(1)} %collective-permute-done.26.low, bf16[1024,384]{1,0:T(8,128)(2,1)S(1)} %get-tuple-element.65.delta.own, bf16[256,384]{1,0:T(8,128)(2,1)S(1)} %collective-permute-done.27.high, f32[1024,384]{1,0:T(8,128)S(1)} %copy-done.3, ...), custom_call_target="tpu_custom_call" | custom-call | flops 1 | bytes 1 | tf_op jit(solution)/shard_map/pallas_call | solution.py:307
  87.9 1.3 %collective-permute-done.33 = bf16[144,384]{1,0:T(8,128)(2,1)} collective-permute-done((bf16[144,384]{1,0:T(8,128)(2,1)}, bf16[144,384]{1,0:T(8,128)(2,1)}, u32[]{:S(2)}, u32[]{:S(2)}) %collective-permute-start.33) | collective-permute-done | bytes 110624 | tf_op jit(solution)/shard_map/ppermute | solution.py:32
  90.9 1.6 %collective-permute-start.29 = (bf16[256,384]{1,0:T(8,128)(2,1)S(1)}, bf16[256,384]{1,0:T(8,128)(2,1)S(1)}, u32[]{:S(2)}, u32[]{:S(2)}) collective-permute-start(bf16[256,384]{1,0:T(8,128)(2,1)S(1)} %get-tuple-element.105), channel_id=1, source_target_pairs={{0,2},{1,3},{2,0},{3,1},{4,6},{5,7},{6,4},{7,5},{8,10},{9,11},{10,... | collective-permute-start | bytes 589832 | tf_op jit(solution)/shard_map/ppermute | solution.py:32
  92.8 3.1 %collective-permute-done.34 = bf16[1,144,384]{2,1,0:T(8,128)(2,1)S(1)} collective-permute-done((bf16[1,144,384]{2,1,0:T(8,128)(2,1)S(1)}, bf16[1,144,384]{2,1,0:T(8,128)(2,1)S(1)}, u32[]{:S(2)}, u32[]{:S(2)}) %collective-permute-start.34) | collective-permute-done | bytes 110624 | tf_op jit(solution)/shard_map/ppermute | solution.py:32
  97.1 2.1 %collective-permute-start.36 = (bf16[144,384]{1,0:T(8,128)(2,1)S(1)}, bf16[144,384]{1,0:T(8,128)(2,1)S(1)}, u32[]{:S(2)}, u32[]{:S(2)}) collective-permute-start(bf16[144,384]{1,0:T(8,128)(2,1)S(1)} %bitcast.12), channel_id=1, source_target_pairs={{0,8},{4,12},{8,0},{12,4},{1,9},{5,13},{9,1},{13,5},{2,10},{6,14},... | collective-permute-start | bytes 331784 | tf_op jit(solution)/shard_map/ppermute | solution.py:27
  99.1 2.4 %collective-permute-start.37 = (bf16[144,384]{1,0:T(8,128)(2,1)S(1)}, bf16[144,384]{1,0:T(8,128)(2,1)S(1)}, u32[]{:S(2)}, u32[]{:S(2)}) collective-permute-start(bf16[144,384]{1,0:T(8,128)(2,1)S(1)} %bitcast.13), channel_id=1, source_target_pairs={{0,12},{4,0},{8,4},{12,8},{1,13},{5,1},{9,5},{13,9},{2,14},{6,2},{... | collective-permute-start | bytes 331784 | tf_op jit(solution)/shard_map/ppermute | solution.py:27
  103.8 2.3 %collective-permute-done.36 = bf16[144,384]{1,0:T(8,128)(2,1)S(1)} collective-permute-done((bf16[144,384]{1,0:T(8,128)(2,1)S(1)}, bf16[144,384]{1,0:T(8,128)(2,1)S(1)}, u32[]{:S(2)}, u32[]{:S(2)}) %collective-permute-start.36) | collective-permute-done | bytes 110624 | tf_op jit(solution)/shard_map/ppermute | solution.py:27
  (84 shorter events, 22.3 us)
Async XLA Ops:
  0.7 14.4 %collective-permute-start.3 = (bf16[576,384]{1,0:T(8,128)(2,1)}, bf16[576,384]{1,0:T(8,128)(2,1)S(1)}, u32[]{:S(2)}, u32[]{:S(2)}) collective-permute-start(bf16[576,384]{1,0:T(8,128)(2,1)} %refs_0_.1), channel_id=1, source_target_pairs={{0,1},{1,0},{2,3},{3,2},{4,5},{5,4},{6,7},{7,6},{8,9},{9,8},{10,11... | collective-permute-start | bytes 1327112 | tf_op jit(solution)/shard_map/ppermute | solution.py:32
  3.1 3.0 %collective-permute-start = (bf16[256,384]{1,0:T(8,128)(2,1)}, bf16[256,384]{1,0:T(8,128)(2,1)S(1)}, u32[]{:S(2)}, u32[]{:S(2)}) collective-permute-start(bf16[256,384]{1,0:T(8,128)(2,1)} %get-tuple-element.113), channel_id=1, source_target_pairs={{0,1},{1,0},{2,3},{3,2},{4,5},{5,4},{6,7},{7,6},{8,9},{9,8},{10,11... | collective-permute-start | bytes 589832 | tf_op jit(solution)/shard_map/ppermute | solution.py:32
  3.2 8.5 %collective-permute-start.1 = (bf16[256,384]{1,0:T(8,128)(2,1)S(1)}, bf16[256,384]{1,0:T(8,128)(2,1)S(1)}, u32[]{:S(2)}, u32[]{:S(2)}) collective-permute-start(bf16[256,384]{1,0:T(8,128)(2,1)S(1)} %get-tuple-element.112), channel_id=1, source_target_pairs={{0,2},{1,3},{2,0},{3,1},{4,6},{5,7},{6,4},{7,5},{8,10},{9,11},{10,... | collective-permute-start | bytes 589832 | tf_op jit(solution)/shard_map/ppermute | solution.py:32
  6.0 9.0 %collective-permute-start.2 = (bf16[256,384]{1,0:T(8,128)(2,1)S(1)}, bf16[256,384]{1,0:T(8,128)(2,1)S(1)}, u32[]{:S(2)}, u32[]{:S(2)}) collective-permute-start(bf16[256,384]{1,0:T(8,128)(2,1)S(1)} %get-tuple-element.111), channel_id=1, source_target_pairs={{0,3},{1,2},{2,1},{3,0},{4,7},{5,6},{6,5},{7,4},{8,11},{9,10},{10,... | collective-permute-start | bytes 589832 | tf_op jit(solution)/shard_map/ppermute | solution.py:32
  15.8 12.4 %collective-permute-start.6 = (bf16[576,384]{1,0:T(8,128)(2,1)S(1)}, bf16[576,384]{1,0:T(8,128)(2,1)S(1)}, u32[]{:S(2)}, u32[]{:S(2)}) collective-permute-start(bf16[576,384]{1,0:T(8,128)(2,1)S(1)} %copy-done.4), channel_id=1, source_target_pairs={{0,2},{1,3},{2,0},{3,1},{4,6},{5,7},{6,4},{7,5},{8,10},{9,11},{10,... | collective-permute-start | bytes 1327112 | tf_op jit(solution)/shard_map/ppermute | solution.py:32
  17.2 16.5 %collective-permute-start.4 = (bf16[768,384]{1,0:T(8,128)(2,1)S(1)}, bf16[768,384]{1,0:T(8,128)(2,1)S(1)}, u32[]{:S(2)}, u32[]{:S(2)}) collective-permute-start(bf16[768,384]{1,0:T(8,128)(2,1)S(1)} %get-tuple-element.52), channel_id=1, source_target_pairs={{0,4},{4,8},{8,12},{1,5},{5,9},{9,13},{2,6},{6,10},{10,14},{3,7},{... | collective-permute-start | bytes 1769480 | tf_op jit(solution)/shard_map/ppermute | solution.py:22
  20.8 17.2 %collective-permute-start.5 = (bf16[768,384]{1,0:T(8,128)(2,1)S(1)}, bf16[768,384]{1,0:T(8,128)(2,1)S(1)}, u32[]{:S(2)}, u32[]{:S(2)}) collective-permute-start(bf16[768,384]{1,0:T(8,128)(2,1)S(1)} %get-tuple-element.54), channel_id=1, source_target_pairs={{4,0},{8,4},{12,8},{5,1},{9,5},{13,9},{6,2},{10,6},{14,10},{7,3},{... | collective-permute-start | bytes 1769480 | tf_op jit(solution)/shard_map/ppermute | solution.py:22
  28.2 9.8 %collective-permute-start.7 = (bf16[576,384]{1,0:T(8,128)(2,1)S(1)}, bf16[576,384]{1,0:T(8,128)(2,1)S(1)}, u32[]{:S(2)}, u32[]{:S(2)}) collective-permute-start(bf16[576,384]{1,0:T(8,128)(2,1)S(1)} %collective-permute-done.6.refs_2_), channel_id=1, source_target_pairs={{0,1},{1,0},{2,3},{3,2},{4,5},{5,4},{6,7},{7,6},{8,9},{9,8},{10,11... | collective-permute-start | bytes 1327112 | tf_op jit(solution)/shard_map/ppermute | solution.py:32
  28.2 15.7 %collective-permute-start.8 = (bf16[256,384]{1,0:T(8,128)(2,1)S(1)}, bf16[256,384]{1,0:T(8,128)(2,1)S(1)}, u32[]{:S(2)}, u32[]{:S(2)}) collective-permute-start(bf16[256,384]{1,0:T(8,128)(2,1)S(1)} %get-tuple-element.110), channel_id=1, source_target_pairs={{0,1},{1,0},{2,3},{3,2},{4,5},{5,4},{6,7},{7,6},{8,9},{9,8},{10,11... | collective-permute-start | bytes 589832 | tf_op jit(solution)/shard_map/ppermute | solution.py:32
  28.8 15.1 %collective-permute-start.10 = (bf16[256,384]{1,0:T(8,128)(2,1)S(1)}, bf16[256,384]{1,0:T(8,128)(2,1)S(1)}, u32[]{:S(2)}, u32[]{:S(2)}) collective-permute-start(bf16[256,384]{1,0:T(8,128)(2,1)S(1)} %get-tuple-element.58), channel_id=1, source_target_pairs={{0,3},{1,2},{2,1},{3,0},{4,7},{5,6},{6,5},{7,4},{8,11},{9,10},{10,... | collective-permute-start | bytes 589832 | tf_op jit(solution)/shard_map/ppermute | solution.py:32
  33.8 10.2 %collective-permute-start.9 = (bf16[256,384]{1,0:T(8,128)(2,1)S(1)}, bf16[256,384]{1,0:T(8,128)(2,1)S(1)}, u32[]{:S(2)}, u32[]{:S(2)}) collective-permute-start(bf16[256,384]{1,0:T(8,128)(2,1)S(1)} %get-tuple-element.57), channel_id=1, source_target_pairs={{0,2},{1,3},{2,0},{3,1},{4,6},{5,7},{6,4},{7,5},{8,10},{9,11},{10,... | collective-permute-start | bytes 589832 | tf_op jit(solution)/shard_map/ppermute | solution.py:32
  44.9 12.1 %collective-permute-start.11 = (bf16[512,384]{1,0:T(8,128)(2,1)S(1)}, bf16[512,384]{1,0:T(8,128)(2,1)S(1)}, u32[]{:S(2)}, u32[]{:S(2)}) collective-permute-start(bf16[512,384]{1,0:T(8,128)(2,1)S(1)} %get-tuple-element.59), channel_id=1, source_target_pairs={{0,4},{4,8},{8,12},{1,5},{5,9},{9,13},{2,6},{6,10},{10,14},{3,7},{... | collective-permute-start | bytes 1179656 | tf_op jit(solution)/shard_map/ppermute | solution.py:22
  48.4 11.8 %collective-permute-start.12 = (bf16[512,384]{1,0:T(8,128)(2,1)S(1)}, bf16[512,384]{1,0:T(8,128)(2,1)S(1)}, u32[]{:S(2)}, u32[]{:S(2)}) collective-permute-start(bf16[512,384]{1,0:T(8,128)(2,1)S(1)} %get-tuple-element.61), channel_id=1, source_target_pairs={{4,0},{8,4},{12,8},{5,1},{9,5},{13,9},{6,2},{10,6},{14,10},{7,3},{... | collective-permute-start | bytes 1179656 | tf_op jit(solution)/shard_map/ppermute | solution.py:22
  52.1 1.4 %collective-permute-start.17 = (f32[72,384]{1,0:T(8,128)S(1)}, f32[72,384]{1,0:T(8,128)S(1)}, u32[]{:S(2)}, u32[]{:S(2)}) collective-permute-start(f32[72,384]{1,0:T(8,128)S(1)} %get-tuple-element.75), channel_id=1, source_target_pairs={{0,1},{1,0},{2,3},{3,2},{4,5},{5,4},{6,7},{7,6},{8,9},{9,8},{10,11... | collective-permute-start | bytes 331784 | tf_op jit(solution)/shard_map/ppermute | solution.py:32
  52.2 1.5 %collective-permute-start.18 = (f32[72,384]{1,0:T(8,128)S(1)}, f32[72,384]{1,0:T(8,128)S(1)}, u32[]{:S(2)}, u32[]{:S(2)}) collective-permute-start(f32[72,384]{1,0:T(8,128)S(1)} %get-tuple-element.76), channel_id=1, source_target_pairs={{0,1},{1,0},{2,3},{3,2},{4,5},{5,4},{6,7},{7,6},{8,9},{9,8},{10,11... | collective-permute-start | bytes 331784 | tf_op jit(solution)/shard_map/ppermute | solution.py:32
  60.2 7.7 %collective-permute-start.25 = (bf16[288,384]{1,0:T(8,128)(2,1)S(1)}, bf16[288,384]{1,0:T(8,128)(2,1)S(1)}, u32[]{:S(2)}, u32[]{:S(2)}) collective-permute-start(bf16[288,384]{1,0:T(8,128)(2,1)S(1)} %get-tuple-element.84), channel_id=1, source_target_pairs={{0,4},{4,0},{8,12},{12,8},{1,5},{5,1},{9,13},{13,9},{2,6},{6,2},{1... | collective-permute-start | bytes 663560 | tf_op jit(solution)/shard_map/ppermute | solution.py:32
  66.9 1.5 %collective-permute-start.13 = (f32[144,384]{1,0:T(8,128)S(1)}, f32[144,384]{1,0:T(8,128)S(1)}, u32[]{:S(2)}, u32[]{:S(2)}) collective-permute-start(f32[144,384]{1,0:T(8,128)S(1)} %get-tuple-element.69), channel_id=1, source_target_pairs={{0,1},{1,0},{2,3},{3,2},{4,5},{5,4},{6,7},{7,6},{8,9},{9,8},{10,11... | collective-permute-start | bytes 663560 | tf_op jit(solution)/shard_map/ppermute | solution.py:32
  66.9 1.8 %collective-permute-start.14 = (f32[144,384]{1,0:T(8,128)S(1)}, f32[144,384]{1,0:T(8,128)S(1)}, u32[]{:S(2)}, u32[]{:S(2)}) collective-permute-start(f32[144,384]{1,0:T(8,128)S(1)} %get-tuple-element.70), channel_id=1, source_target_pairs={{0,1},{1,0},{2,3},{3,2},{4,5},{5,4},{6,7},{7,6},{8,9},{9,8},{10,11... | collective-permute-start | bytes 663560 | tf_op jit(solution)/shard_map/ppermute | solution.py:32
  67.4 1.6 %collective-permute-start.15 = (f32[144,384]{1,0:T(8,128)S(1)}, f32[144,384]{1,0:T(8,128)S(1)}, u32[]{:S(2)}, u32[]{:S(2)}) collective-permute-start(f32[144,384]{1,0:T(8,128)S(1)} %get-tuple-element.71), channel_id=1, source_target_pairs={{0,1},{1,0},{2,3},{3,2},{4,5},{5,4},{6,7},{7,6},{8,9},{9,8},{10,11... | collective-permute-start | bytes 663560 | tf_op jit(solution)/shard_map/ppermute | solution.py:32
  67.4 1.9 %collective-permute-start.16 = (f32[144,384]{1,0:T(8,128)S(1)}, f32[144,384]{1,0:T(8,128)S(1)}, u32[]{:S(2)}, u32[]{:S(2)}) collective-permute-start(f32[144,384]{1,0:T(8,128)S(1)} %get-tuple-element.72), channel_id=1, source_target_pairs={{0,1},{1,0},{2,3},{3,2},{4,5},{5,4},{6,7},{7,6},{8,9},{9,8},{10,11... | collective-permute-start | bytes 663560 | tf_op jit(solution)/shard_map/ppermute | solution.py:32
  70.1 10.7 %collective-permute-start.32 = (bf16[288,384]{1,0:T(8,128)(2,1)S(1)}, bf16[288,384]{1,0:T(8,128)(2,1)S(1)}, u32[]{:S(2)}, u32[]{:S(2)}) collective-permute-start(bf16[288,384]{1,0:T(8,128)(2,1)S(1)} %get-tuple-element.85), channel_id=1, source_target_pairs={{0,4},{4,0},{8,12},{12,8},{1,5},{5,1},{9,13},{13,9},{2,6},{6,2},{1... | collective-permute-start | bytes 663560 | tf_op jit(solution)/shard_map/ppermute | solution.py:32
  71.2 7.5 %collective-permute-start.31 = (bf16[144,384]{1,0:T(8,128)(2,1)S(1)}, bf16[144,384]{1,0:T(8,128)(2,1)S(1)}, u32[]{:S(2)}, u32[]{:S(2)}) collective-permute-start(bf16[144,384]{1,0:T(8,128)(2,1)S(1)} %get-tuple-element.92), channel_id=1, source_target_pairs={{0,8},{4,12},{8,0},{12,4},{1,9},{5,13},{9,1},{13,5},{2,10},{6,14},... | collective-permute-start | bytes 331784 | tf_op jit(solution)/shard_map/ppermute | solution.py:32
  72.6 10.8 %collective-permute-start.26 = (bf16[256,384]{1,0:T(8,128)(2,1)}, bf16[256,384]{1,0:T(8,128)(2,1)S(1)}, u32[]{:S(2)}, u32[]{:S(2)}) collective-permute-start(bf16[256,384]{1,0:T(8,128)(2,1)} %get-tuple-element.86), channel_id=1, source_target_pairs={{0,4},{4,8},{8,12},{1,5},{5,9},{9,13},{2,6},{6,10},{10,14},{3,7},{... | collective-permute-start | bytes 589832 | tf_op jit(solution)/shard_map/ppermute | solution.py:22
  74.8 9.5 %collective-permute-start.27 = (bf16[256,384]{1,0:T(8,128)(2,1)}, bf16[256,384]{1,0:T(8,128)(2,1)S(1)}, u32[]{:S(2)}, u32[]{:S(2)}) collective-permute-start(bf16[256,384]{1,0:T(8,128)(2,1)} %get-tuple-element.87), channel_id=1, source_target_pairs={{4,0},{8,4},{12,8},{5,1},{9,5},{13,9},{6,2},{10,6},{14,10},{7,3},{... | collective-permute-start | bytes 589832 | tf_op jit(solution)/shard_map/ppermute | solution.py:22
  82.0 7.2 %collective-permute-start.33 = (bf16[144,384]{1,0:T(8,128)(2,1)}, bf16[144,384]{1,0:T(8,128)(2,1)}, u32[]{:S(2)}, u32[]{:S(2)}) collective-permute-start(bf16[144,384]{1,0:T(8,128)(2,1)} %get-tuple-element.95), channel_id=1, source_target_pairs={{0,8},{4,12},{8,0},{12,4},{1,9},{5,13},{9,1},{13,5},{2,10},{6,14},... | collective-permute-start | bytes 331784 | tf_op jit(solution)/shard_map/ppermute | solution.py:32
  90.2 5.8 %collective-permute-start.34 = (bf16[1,144,384]{2,1,0:T(8,128)(2,1)S(1)}, bf16[1,144,384]{2,1,0:T(8,128)(2,1)S(1)}, u32[]{:S(2)}, u32[]{:S(2)}) collective-permute-start(bf16[1,144,384]{2,1,0:T(8,128)(2,1)S(1)} %fusion), channel_id=1, source_target_pairs={{0,2},{1,3},{2,0},{3,1},{4,6},{5,7},{6,4},{7,5},{8,10},{9,11},{10,... | collective-permute-start | bytes 331784 | tf_op jit(solution)/shard_map/ppermute | solution.py:32
  90.9 8.3 %collective-permute-start.28 = (bf16[256,384]{1,0:T(8,128)(2,1)S(1)}, bf16[256,384]{1,0:T(8,128)(2,1)S(1)}, u32[]{:S(2)}, u32[]{:S(2)}) collective-permute-start(bf16[256,384]{1,0:T(8,128)(2,1)S(1)} %get-tuple-element.106), channel_id=1, source_target_pairs={{0,1},{1,0},{2,3},{3,2},{4,5},{5,4},{6,7},{7,6},{8,9},{9,8},{10,11... | collective-permute-start | bytes 589832 | tf_op jit(solution)/shard_map/ppermute | solution.py:32
  90.9 10.6 %collective-permute-start.29 = (bf16[256,384]{1,0:T(8,128)(2,1)S(1)}, bf16[256,384]{1,0:T(8,128)(2,1)S(1)}, u32[]{:S(2)}, u32[]{:S(2)}) collective-permute-start(bf16[256,384]{1,0:T(8,128)(2,1)S(1)} %get-tuple-element.105), channel_id=1, source_target_pairs={{0,2},{1,3},{2,0},{3,1},{4,6},{5,7},{6,4},{7,5},{8,10},{9,11},{10,... | collective-permute-start | bytes 589832 | tf_op jit(solution)/shard_map/ppermute | solution.py:32
  92.5 10.0 %collective-permute-start.30 = (bf16[256,384]{1,0:T(8,128)(2,1)S(1)}, bf16[256,384]{1,0:T(8,128)(2,1)S(1)}, u32[]{:S(2)}, u32[]{:S(2)}) collective-permute-start(bf16[256,384]{1,0:T(8,128)(2,1)S(1)} %get-tuple-element.104), channel_id=1, source_target_pairs={{0,3},{1,2},{2,1},{3,0},{4,7},{5,6},{6,5},{7,4},{8,11},{9,10},{10,... | collective-permute-start | bytes 589832 | tf_op jit(solution)/shard_map/ppermute | solution.py:32
  97.0 6.8 %collective-permute-start.35 = (bf16[144,384]{1,0:T(8,128)(2,1)S(1)}, bf16[144,384]{1,0:T(8,128)(2,1)S(1)}, u32[]{:S(2)}, u32[]{:S(2)}) collective-permute-start(bf16[144,384]{1,0:T(8,128)(2,1)S(1)} %bitcast.11), channel_id=1, source_target_pairs={{0,4},{4,8},{8,12},{12,0},{1,5},{5,9},{9,13},{13,1},{2,6},{6,10},{... | collective-permute-start | bytes 331784 | tf_op jit(solution)/shard_map/ppermute | solution.py:27
  97.1 9.1 %collective-permute-start.36 = (bf16[144,384]{1,0:T(8,128)(2,1)S(1)}, bf16[144,384]{1,0:T(8,128)(2,1)S(1)}, u32[]{:S(2)}, u32[]{:S(2)}) collective-permute-start(bf16[144,384]{1,0:T(8,128)(2,1)S(1)} %bitcast.12), channel_id=1, source_target_pairs={{0,8},{4,12},{8,0},{12,4},{1,9},{5,13},{9,1},{13,5},{2,10},{6,14},... | collective-permute-start | bytes 331784 | tf_op jit(solution)/shard_map/ppermute | solution.py:27
  99.1 7.0 %collective-permute-start.37 = (bf16[144,384]{1,0:T(8,128)(2,1)S(1)}, bf16[144,384]{1,0:T(8,128)(2,1)S(1)}, u32[]{:S(2)}, u32[]{:S(2)}) collective-permute-start(bf16[144,384]{1,0:T(8,128)(2,1)S(1)} %bitcast.13), channel_id=1, source_target_pairs={{0,12},{4,0},{8,4},{12,8},{1,13},{5,1},{9,5},{13,9},{2,14},{6,2},{... | collective-permute-start | bytes 331784 | tf_op jit(solution)/shard_map/ppermute | solution.py:27
  (13 other events, 77.3 us)

commit v8 on v7

--- a/solution.py
+++ b/solution.py
@@ -227,7 +227,8 @@
                 for i in range(splits):
                     low, high = max(at, i * share), min(end, (i + 1) * share)
                     if low < high:
-                        sends[i][low - i * share : high - i * share] = value[low - at : high - at]
+                        piece = value[low - at : high - at].astype(sends[i].dtype)
+                        sends[i][low - i * share : high - i * share] = piece
 
     if halo:
         to_high, to_low = outs[-2:]
@@ -463,10 +464,10 @@
         operands=(slope_two, cotangent, *c_pieces),
     )
     two_low, two_high = shifted(up_two, "seq", 1), shifted(down_two, "seq", -1)
-    splits, more = 8, 4
+    splits, more = 4, 2
     half = ((taps // 2, channels), F32)
-    share = ((taps // 2 // splits, channels), F32)
-    less = ((taps // 2 // more, channels), F32)
+    share = ((taps // 2 // splits, channels), BF16)
+    less = ((taps // 2 // more, channels), BF16)
     keep_two, *send_two = kernel(
         functools.partial(grad_two_kernel, (members, 0, splits, far * q), grad_scale),
         half,

time: 107 us -> 107 us (level)
  starting transfers between devices: 35.3 us -> 34 us
    ppermute x6, waiting for transfers between devices: 11.1 us -> 12.7 us  [shifted(): return lax.ppermute(block, axis, route)]
    ppermute x29 -> x23, starting transfers between devices: 17.7 us -> 16.2 us  [swapped(): return lax.ppermute(block, axis, [(i, i ^ bits) for i in range(n)])]
    ppermute x29 -> x23, waiting for transfers between devices: 28.8 us -> 28.2 us  [swapped(): return lax.ppermute(block, axis, [(i, i ^ bits) for i in range(n)])]
  transfers between devices with their start and end apart: 38 -> 32, of which waited for: 22 -> 20; matrix products, arithmetic and copies ran while one was open for 3% -> 3% of each run, Pallas kernels for 17% -> 17%
where the time goes in v8:
time: 107 us
  waiting for transfers between devices  44.2 us (41%)
  starting transfers between devices  34 us (32%)
  Pallas kernels  20.6 us (19%)
  local copies, waits for them, and re-layouts  4.66 us (4%)
  other arithmetic  2.07 us (2%)
    ppermute x23, waiting for transfers between devices, swapped(): return lax.ppermute(block, axis, [(i, i ^ bits) for i in range(n)])  28.2 us
    pallas_call x11, Pallas kernels, call(): pl.pallas_call(kernel, out_shape=tuple((jax.ShapeDtypeStruct(shape, kind)...  20.6 us
    ppermute x23, starting transfers between devices, swapped(): return lax.ppermute(block, axis, [(i, i ^ bits) for i in range(n)])  16.2 us
    ppermute x6, starting transfers between devices, shifted(): return lax.ppermute(block, axis, route)  13.2 us
    ppermute x6, waiting for transfers between devices, shifted(): return lax.ppermute(block, axis, route)  12.7 us
    ppermute x3, starting transfers between devices, turned(): return lax.ppermute(block, axis, [(i, (i + turn) % n) for i in range(n)])  4.56 us
    ppermute x3, waiting for transfers between devices, turned(): return lax.ppermute(block, axis, [(i, (i + turn) % n) for i in range(n)])  3.36 us
    unnamed x14, local copies, waits for them, and re-layouts  2.34 us
  transfers between devices with their start and end apart: 32, of which 20 were waited for; matrix products, arithmetic and copies ran while one was open for 3% of the time, Pallas kernels for 17%

profile of v8, /device:TPU:0, one launch (start us, length us, event | category | flops | bytes accessed | tf_op | source)
XLA Modules:
  0.0 106.5 jit_solution(10195580641530495105)
XLA Ops:
  1.2 1.9 %constant_dynamic-slice_fusion.3 = (bf16[256,384]{1,0:T(8,128)(2,1)S(1)}, bf16[256,384]{1,0:T(8,128)(2,1)S(1)}, bf16[256,384]{1,0:T(8,128)(2,1)}) fusion(bf16[1024,384]{1,0:T(8,128)(2,1)} %block.1, s32[]{:T(128)S(6)} %select_n.66, s32[]{:T(128)S(6)} %select_n.65, s32[]{:T(128)S(6)} %select_n.64), kind=kLoop, calls=%fused_computation.17 | loop fusion | bytes 1179660 | tf_op jit(solution)/shard_map/dynamic_slice | solution.py:48
  3.2 2.8 %collective-permute-start.1 = (bf16[256,384]{1,0:T(8,128)(2,1)S(1)}, bf16[256,384]{1,0:T(8,128)(2,1)S(1)}, u32[]{:S(2)}, u32[]{:S(2)}) collective-permute-start(bf16[256,384]{1,0:T(8,128)(2,1)S(1)} %get-tuple-element.100), channel_id=1, source_target_pairs={{0,2},{1,3},{2,0},{3,1},{4,6},{5,7},{6,4},{7,5},{8,10},{9,11},{10,... | collective-permute-start | bytes 589832 | tf_op jit(solution)/shard_map/ppermute | solution.py:32
  6.1 5.6 %collective-permute-done.1.refs_1_ = bf16[256,384]{1,0:T(8,128)(2,1)S(1)} collective-permute-done((bf16[256,384]{1,0:T(8,128)(2,1)S(1)}, bf16[256,384]{1,0:T(8,128)(2,1)S(1)}, u32[]{:S(2)}, u32[]{:S(2)}) %collective-permute-start.1) | collective-permute-done | bytes 196640 | tf_op jit(solution)/shard_map/ppermute | solution.py:32
  11.7 3.3 %collective-permute-done.2.refs_2_ = bf16[256,384]{1,0:T(8,128)(2,1)S(1)} collective-permute-done((bf16[256,384]{1,0:T(8,128)(2,1)S(1)}, bf16[256,384]{1,0:T(8,128)(2,1)S(1)}, u32[]{:S(2)}, u32[]{:S(2)}) %collective-permute-start.2) | collective-permute-done | bytes 196640 | tf_op jit(solution)/shard_map/ppermute | solution.py:32
  15.8 1.5 %collective-permute-start.6 = (bf16[576,384]{1,0:T(8,128)(2,1)S(1)}, bf16[576,384]{1,0:T(8,128)(2,1)S(1)}, u32[]{:S(2)}, u32[]{:S(2)}) collective-permute-start(bf16[576,384]{1,0:T(8,128)(2,1)S(1)} %copy-done.4), channel_id=1, source_target_pairs={{0,2},{1,3},{2,0},{3,1},{4,6},{5,7},{6,4},{7,5},{8,10},{9,11},{10,... | collective-permute-start | bytes 1327112 | tf_op jit(solution)/shard_map/ppermute | solution.py:32
  17.2 3.5 %collective-permute-start.4 = (bf16[768,384]{1,0:T(8,128)(2,1)S(1)}, bf16[768,384]{1,0:T(8,128)(2,1)S(1)}, u32[]{:S(2)}, u32[]{:S(2)}) collective-permute-start(bf16[768,384]{1,0:T(8,128)(2,1)S(1)} %get-tuple-element.46), channel_id=1, source_target_pairs={{0,4},{4,8},{8,12},{1,5},{5,9},{9,13},{2,6},{6,10},{10,14},{3,7},{... | collective-permute-start | bytes 1769480 | tf_op jit(solution)/shard_map/ppermute | solution.py:22
  20.8 1.3 %collective-permute-start.5 = (bf16[768,384]{1,0:T(8,128)(2,1)S(1)}, bf16[768,384]{1,0:T(8,128)(2,1)S(1)}, u32[]{:S(2)}, u32[]{:S(2)}) collective-permute-start(bf16[768,384]{1,0:T(8,128)(2,1)S(1)} %get-tuple-element.48), channel_id=1, source_target_pairs={{4,0},{8,4},{12,8},{5,1},{9,5},{13,9},{6,2},{10,6},{14,10},{7,3},{... | collective-permute-start | bytes 1769480 | tf_op jit(solution)/shard_map/ppermute | solution.py:22
  22.1 6.1 %collective-permute-done.6.refs_2_ = bf16[576,384]{1,0:T(8,128)(2,1)S(1)} collective-permute-done((bf16[576,384]{1,0:T(8,128)(2,1)S(1)}, bf16[576,384]{1,0:T(8,128)(2,1)S(1)}, u32[]{:S(2)}, u32[]{:S(2)}) %collective-permute-start.6) | collective-permute-done | bytes 442400 | tf_op jit(solution)/shard_map/ppermute | solution.py:32
  28.8 1.4 %collective-permute-start.10 = (bf16[256,384]{1,0:T(8,128)(2,1)S(1)}, bf16[256,384]{1,0:T(8,128)(2,1)S(1)}, u32[]{:S(2)}, u32[]{:S(2)}) collective-permute-start(bf16[256,384]{1,0:T(8,128)(2,1)S(1)} %get-tuple-element.52), channel_id=1, source_target_pairs={{0,3},{1,2},{2,1},{3,0},{4,7},{5,6},{6,5},{7,4},{8,11},{9,10},{10,... | collective-permute-start | bytes 589832 | tf_op jit(solution)/shard_map/ppermute | solution.py:32
  30.2 3.5 %collective-permute-done.4.low = bf16[768,384]{1,0:T(8,128)(2,1)S(1)} collective-permute-done((bf16[768,384]{1,0:T(8,128)(2,1)S(1)}, bf16[768,384]{1,0:T(8,128)(2,1)S(1)}, u32[]{:S(2)}, u32[]{:S(2)}) %collective-permute-start.4) | collective-permute-done | bytes 589856 | tf_op jit(solution)/shard_map/ppermute | solution.py:22
  34.3 3.6 %collective-permute-done.5.high = bf16[768,384]{1,0:T(8,128)(2,1)S(1)} collective-permute-done((bf16[768,384]{1,0:T(8,128)(2,1)S(1)}, bf16[768,384]{1,0:T(8,128)(2,1)S(1)}, u32[]{:S(2)}, u32[]{:S(2)}) %collective-permute-start.5) | collective-permute-done | bytes 589856 | tf_op jit(solution)/shard_map/ppermute | solution.py:22
  37.9 6.0 %shard_map.51 = (bf16[2048,384]{1,0:T(8,128)(2,1)S(1)}, f32[1024,384]{1,0:T(8,128)S(1)}, f32[1024,384]{1,0:T(8,128)S(1)}, bf16[2304,384]{1,0:T(8,128)(2,1)S(1)}) custom-call(s32[2]{0:T(128)S(1)} %pad_add_fusion.place, bf16[768,384]{1,0:T(8,128)(2,1)S(1)} %collective-permute-done.4.low, bf16[1024,384]{1,0:T(8,128)(2,1)S(1)} %get-tuple-element.47.own, ...), custom_call_target="tpu_custom_call" | custom-call | flops 1 | bytes 1 | tf_op jit(solution)/shard_map/pallas_call | solution.py:308
  44.9 3.5 %collective-permute-start.11 = (bf16[512,384]{1,0:T(8,128)(2,1)S(1)}, bf16[512,384]{1,0:T(8,128)(2,1)S(1)}, u32[]{:S(2)}, u32[]{:S(2)}) collective-permute-start(bf16[512,384]{1,0:T(8,128)(2,1)S(1)} %get-tuple-element.53), channel_id=1, source_target_pairs={{0,4},{4,8},{8,12},{1,5},{5,9},{9,13},{2,6},{6,10},{10,14},{3,7},{... | collective-permute-start | bytes 1179656 | tf_op jit(solution)/shard_map/ppermute | solution.py:22
  49.7 2.5 %shard_map.55 = (f32[576,384]{1,0:T(8,128)S(1)}, bf16[144,384]{1,0:T(8,128)(2,1)S(1)}, bf16[144,384]{1,0:T(8,128)(2,1)S(1)}, bf16[144,384]{1,0:T(8,128)(2,1)S(1)}, bf16[144,384]{1,0:T(8,128)(2,1)S(1)}) custom-call(s32[2]{0:T(128)S(1)} %pad_add_fusion.place, bf16[2048,384]{1,0:T(8,128)(2,1)S(1)} %get-tuple-element.65.hidden, ...), custom_call_target="tpu_custom_call" | custom-call | flops 1 | bytes 1 | tf_op jit(solution)/shard_map/pallas_call | solution.py:308
  56.1 4.1 %collective-permute-done.12.high = bf16[512,384]{1,0:T(8,128)(2,1)S(1)} collective-permute-done((bf16[512,384]{1,0:T(8,128)(2,1)S(1)}, bf16[512,384]{1,0:T(8,128)(2,1)S(1)}, u32[]{:S(2)}, u32[]{:S(2)}) %collective-permute-start.12) | collective-permute-done | bytes 393248 | tf_op jit(solution)/shard_map/ppermute | solution.py:22
  60.2 1.6 %collective-permute-start.19 = (bf16[288,384]{1,0:T(8,128)(2,1)S(1)}, bf16[288,384]{1,0:T(8,128)(2,1)S(1)}, u32[]{:S(2)}, u32[]{:S(2)}) collective-permute-start(bf16[288,384]{1,0:T(8,128)(2,1)S(1)} %get-tuple-element.72), channel_id=1, source_target_pairs={{0,4},{4,0},{8,12},{12,8},{1,5},{5,1},{9,13},{13,9},{2,6},{6,2},{1... | collective-permute-start | bytes 663560 | tf_op jit(solution)/shard_map/ppermute | solution.py:32
  61.8 1.7 %shard_map.53 = (f32[1024,384]{1,0:T(8,128)S(1)}, bf16[1024,384]{1,0:T(8,128)(2,1)S(1)}) custom-call(bf16[512,384]{1,0:T(8,128)(2,1)S(1)} %collective-permute-done.11.low, bf16[1024,384]{1,0:T(8,128)(2,1)S(1)} %get-tuple-element.54.own.delta, bf16[512,384]{1,0:T(8,128)(2,1)S(1)} %collective-permute-done.12.high, ...), custom_call_target="tpu_custom_call" | custom-call | flops 1 | bytes 1 | tf_op jit(solution)/shard_map/pallas_call | solution.py:308
  63.5 3.2 %shard_map.54 = (f32[576,384]{1,0:T(8,128)S(1)}, bf16[288,384]{1,0:T(8,128)(2,1)S(1)}, bf16[288,384]{1,0:T(8,128)(2,1)S(1)}, bf16[256,384]{1,0:T(8,128)(2,1)}, bf16[256,384]{1,0:T(8,128)(2,1)}) custom-call(s32[2]{0:T(128)S(1)} %pad_add_fusion.place, bf16[768,384]{1,0:T(8,128)(2,1)S(1)} %collective-permute-done.4.low, ...), custom_call_target="tpu_custom_call" | custom-call | flops 1 | bytes 1 | tf_op jit(solution)/shard_map/pallas_call | solution.py:308
  70.4 1.3 %collective-permute-start.25 = (bf16[144,384]{1,0:T(8,128)(2,1)S(1)}, bf16[144,384]{1,0:T(8,128)(2,1)S(1)}, u32[]{:S(2)}, u32[]{:S(2)}) collective-permute-start(bf16[144,384]{1,0:T(8,128)(2,1)S(1)} %get-tuple-element.80), channel_id=1, source_target_pairs={{0,8},{4,12},{8,0},{12,4},{1,9},{5,13},{9,1},{13,5},{2,10},{6,14},... | collective-permute-start | bytes 331784 | tf_op jit(solution)/shard_map/ppermute | solution.py:32
  71.8 2.4 %collective-permute-start.20 = (bf16[256,384]{1,0:T(8,128)(2,1)}, bf16[256,384]{1,0:T(8,128)(2,1)S(1)}, u32[]{:S(2)}, u32[]{:S(2)}) collective-permute-start(bf16[256,384]{1,0:T(8,128)(2,1)} %get-tuple-element.74), channel_id=1, source_target_pairs={{0,4},{4,8},{8,12},{1,5},{5,9},{9,13},{2,6},{6,10},{10,14},{3,7},{... | collective-permute-start | bytes 589832 | tf_op jit(solution)/shard_map/ppermute | solution.py:22
  74.2 1.3 %collective-permute-start.21 = (bf16[256,384]{1,0:T(8,128)(2,1)}, bf16[256,384]{1,0:T(8,128)(2,1)S(1)}, u32[]{:S(2)}, u32[]{:S(2)}) collective-permute-start(bf16[256,384]{1,0:T(8,128)(2,1)} %get-tuple-element.75), channel_id=1, source_target_pairs={{4,0},{8,4},{12,8},{5,1},{9,5},{13,9},{6,2},{10,6},{14,10},{7,3},{... | collective-permute-start | bytes 589832 | tf_op jit(solution)/shard_map/ppermute | solution.py:22
  75.5 2.5 %collective-permute-done.25.refs_1_ = bf16[144,384]{1,0:T(8,128)(2,1)S(1)} collective-permute-done((bf16[144,384]{1,0:T(8,128)(2,1)S(1)}, bf16[144,384]{1,0:T(8,128)(2,1)S(1)}, u32[]{:S(2)}, u32[]{:S(2)}) %collective-permute-start.25) | collective-permute-done | bytes 110624 | tf_op jit(solution)/shard_map/ppermute | solution.py:32
  78.0 1.9 %collective-permute-done.26.refs_0_ = bf16[288,384]{1,0:T(8,128)(2,1)S(1)} collective-permute-done((bf16[288,384]{1,0:T(8,128)(2,1)S(1)}, bf16[288,384]{1,0:T(8,128)(2,1)S(1)}, u32[]{:S(2)}, u32[]{:S(2)}) %collective-permute-start.26) | collective-permute-done | bytes 221216 | tf_op jit(solution)/shard_map/ppermute | solution.py:32
  81.2 1.5 %collective-permute-start.27 = (bf16[144,384]{1,0:T(8,128)(2,1)}, bf16[144,384]{1,0:T(8,128)(2,1)}, u32[]{:S(2)}, u32[]{:S(2)}) collective-permute-start(bf16[144,384]{1,0:T(8,128)(2,1)} %get-tuple-element.83), channel_id=1, source_target_pairs={{0,8},{4,12},{8,0},{12,4},{1,9},{5,13},{9,1},{13,5},{2,10},{6,14},... | collective-permute-start | bytes 331784 | tf_op jit(solution)/shard_map/ppermute | solution.py:32
  83.5 1.4 %copy-done.3 = f32[1024,384]{1,0:T(8,128)S(1)} copy-done((f32[1024,384]{1,0:T(8,128)S(1)}, f32[1024,384]{1,0:T(8,128)}, u32[]{:S(2)}) %copy-start.3) | copy-done | bytes 1572888
  84.9 2.3 %shard_map.58 = bf16[1024,384]{1,0:T(8,128)(2,1)S(1)} custom-call(s32[2]{0:T(128)S(1)} %pad_add_fusion.place, bf16[256,384]{1,0:T(8,128)(2,1)S(1)} %collective-permute-done.20.low, bf16[1024,384]{1,0:T(8,128)(2,1)S(1)} %get-tuple-element.59.delta.own, bf16[256,384]{1,0:T(8,128)(2,1)S(1)} %collective-permute-done.21.high, f32[1024,384]{1,0:T(8,128)S(1)} %copy-done.3, ...), custom_call_target="tpu_custom_call" | custom-call | flops 1 | bytes 1 | tf_op jit(solution)/shard_map/pallas_call | solution.py:308
  87.1 1.5 %collective-permute-done.27 = bf16[144,384]{1,0:T(8,128)(2,1)} collective-permute-done((bf16[144,384]{1,0:T(8,128)(2,1)}, bf16[144,384]{1,0:T(8,128)(2,1)}, u32[]{:S(2)}, u32[]{:S(2)}) %collective-permute-start.27) | collective-permute-done | bytes 110624 | tf_op jit(solution)/shard_map/ppermute | solution.py:32
  90.3 1.6 %collective-permute-start.23 = (bf16[256,384]{1,0:T(8,128)(2,1)S(1)}, bf16[256,384]{1,0:T(8,128)(2,1)S(1)}, u32[]{:S(2)}, u32[]{:S(2)}) collective-permute-start(bf16[256,384]{1,0:T(8,128)(2,1)S(1)} %get-tuple-element.93), channel_id=1, source_target_pairs={{0,2},{1,3},{2,0},{3,1},{4,6},{5,7},{6,4},{7,5},{8,10},{9,11},{10,... | collective-permute-start | bytes 589832 | tf_op jit(solution)/shard_map/ppermute | solution.py:32
  92.2 3.1 %collective-permute-done.28 = bf16[1,144,384]{2,1,0:T(8,128)(2,1)S(1)} collective-permute-done((bf16[1,144,384]{2,1,0:T(8,128)(2,1)S(1)}, bf16[1,144,384]{2,1,0:T(8,128)(2,1)S(1)}, u32[]{:S(2)}, u32[]{:S(2)}) %collective-permute-start.28) | collective-permute-done | bytes 110624 | tf_op jit(solution)/shard_map/ppermute | solution.py:32
  96.8 1.5 %collective-permute-start.30 = (bf16[144,384]{1,0:T(8,128)(2,1)S(1)}, bf16[144,384]{1,0:T(8,128)(2,1)S(1)}, u32[]{:S(2)}, u32[]{:S(2)}) collective-permute-start(bf16[144,384]{1,0:T(8,128)(2,1)S(1)} %bitcast.12), channel_id=1, source_target_pairs={{0,8},{4,12},{8,0},{12,4},{1,9},{5,13},{9,1},{13,5},{2,10},{6,14},... | collective-permute-start | bytes 331784 | tf_op jit(solution)/shard_map/ppermute | solution.py:27
  98.3 2.6 %collective-permute-start.31 = (bf16[144,384]{1,0:T(8,128)(2,1)S(1)}, bf16[144,384]{1,0:T(8,128)(2,1)S(1)}, u32[]{:S(2)}, u32[]{:S(2)}) collective-permute-start(bf16[144,384]{1,0:T(8,128)(2,1)S(1)} %bitcast.13), channel_id=1, source_target_pairs={{0,12},{4,0},{8,4},{12,8},{1,13},{5,1},{9,5},{13,9},{2,14},{6,2},{... | collective-permute-start | bytes 331784 | tf_op jit(solution)/shard_map/ppermute | solution.py:27
  103.2 2.3 %collective-permute-done.30 = bf16[144,384]{1,0:T(8,128)(2,1)S(1)} collective-permute-done((bf16[144,384]{1,0:T(8,128)(2,1)S(1)}, bf16[144,384]{1,0:T(8,128)(2,1)S(1)}, u32[]{:S(2)}, u32[]{:S(2)}) %collective-permute-start.30) | collective-permute-done | bytes 110624 | tf_op jit(solution)/shard_map/ppermute | solution.py:27
  (72 shorter events, 21.2 us)
Async XLA Ops:
  0.7 14.4 %collective-permute-start.3 = (bf16[576,384]{1,0:T(8,128)(2,1)}, bf16[576,384]{1,0:T(8,128)(2,1)S(1)}, u32[]{:S(2)}, u32[]{:S(2)}) collective-permute-start(bf16[576,384]{1,0:T(8,128)(2,1)} %refs_0_.1), channel_id=1, source_target_pairs={{0,1},{1,0},{2,3},{3,2},{4,5},{5,4},{6,7},{7,6},{8,9},{9,8},{10,11... | collective-permute-start | bytes 1327112 | tf_op jit(solution)/shard_map/ppermute | solution.py:32
  3.1 3.0 %collective-permute-start = (bf16[256,384]{1,0:T(8,128)(2,1)}, bf16[256,384]{1,0:T(8,128)(2,1)S(1)}, u32[]{:S(2)}, u32[]{:S(2)}) collective-permute-start(bf16[256,384]{1,0:T(8,128)(2,1)} %get-tuple-element.101), channel_id=1, source_target_pairs={{0,1},{1,0},{2,3},{3,2},{4,5},{5,4},{6,7},{7,6},{8,9},{9,8},{10,11... | collective-permute-start | bytes 589832 | tf_op jit(solution)/shard_map/ppermute | solution.py:32
  3.2 8.5 %collective-permute-start.1 = (bf16[256,384]{1,0:T(8,128)(2,1)S(1)}, bf16[256,384]{1,0:T(8,128)(2,1)S(1)}, u32[]{:S(2)}, u32[]{:S(2)}) collective-permute-start(bf16[256,384]{1,0:T(8,128)(2,1)S(1)} %get-tuple-element.100), channel_id=1, source_target_pairs={{0,2},{1,3},{2,0},{3,1},{4,6},{5,7},{6,4},{7,5},{8,10},{9,11},{10,... | collective-permute-start | bytes 589832 | tf_op jit(solution)/shard_map/ppermute | solution.py:32
  6.0 9.0 %collective-permute-start.2 = (bf16[256,384]{1,0:T(8,128)(2,1)S(1)}, bf16[256,384]{1,0:T(8,128)(2,1)S(1)}, u32[]{:S(2)}, u32[]{:S(2)}) collective-permute-start(bf16[256,384]{1,0:T(8,128)(2,1)S(1)} %get-tuple-element.99), channel_id=1, source_target_pairs={{0,3},{1,2},{2,1},{3,0},{4,7},{5,6},{6,5},{7,4},{8,11},{9,10},{10,... | collective-permute-start | bytes 589832 | tf_op jit(solution)/shard_map/ppermute | solution.py:32
  15.8 12.4 %collective-permute-start.6 = (bf16[576,384]{1,0:T(8,128)(2,1)S(1)}, bf16[576,384]{1,0:T(8,128)(2,1)S(1)}, u32[]{:S(2)}, u32[]{:S(2)}) collective-permute-start(bf16[576,384]{1,0:T(8,128)(2,1)S(1)} %copy-done.4), channel_id=1, source_target_pairs={{0,2},{1,3},{2,0},{3,1},{4,6},{5,7},{6,4},{7,5},{8,10},{9,11},{10,... | collective-permute-start | bytes 1327112 | tf_op jit(solution)/shard_map/ppermute | solution.py:32
  17.2 16.5 %collective-permute-start.4 = (bf16[768,384]{1,0:T(8,128)(2,1)S(1)}, bf16[768,384]{1,0:T(8,128)(2,1)S(1)}, u32[]{:S(2)}, u32[]{:S(2)}) collective-permute-start(bf16[768,384]{1,0:T(8,128)(2,1)S(1)} %get-tuple-element.46), channel_id=1, source_target_pairs={{0,4},{4,8},{8,12},{1,5},{5,9},{9,13},{2,6},{6,10},{10,14},{3,7},{... | collective-permute-start | bytes 1769480 | tf_op jit(solution)/shard_map/ppermute | solution.py:22
  20.8 17.2 %collective-permute-start.5 = (bf16[768,384]{1,0:T(8,128)(2,1)S(1)}, bf16[768,384]{1,0:T(8,128)(2,1)S(1)}, u32[]{:S(2)}, u32[]{:S(2)}) collective-permute-start(bf16[768,384]{1,0:T(8,128)(2,1)S(1)} %get-tuple-element.48), channel_id=1, source_target_pairs={{4,0},{8,4},{12,8},{5,1},{9,5},{13,9},{6,2},{10,6},{14,10},{7,3},{... | collective-permute-start | bytes 1769480 | tf_op jit(solution)/shard_map/ppermute | solution.py:22
  28.2 9.8 %collective-permute-start.7 = (bf16[576,384]{1,0:T(8,128)(2,1)S(1)}, bf16[576,384]{1,0:T(8,128)(2,1)S(1)}, u32[]{:S(2)}, u32[]{:S(2)}) collective-permute-start(bf16[576,384]{1,0:T(8,128)(2,1)S(1)} %collective-permute-done.6.refs_2_), channel_id=1, source_target_pairs={{0,1},{1,0},{2,3},{3,2},{4,5},{5,4},{6,7},{7,6},{8,9},{9,8},{10,11... | collective-permute-start | bytes 1327112 | tf_op jit(solution)/shard_map/ppermute | solution.py:32
  28.2 15.7 %collective-permute-start.8 = (bf16[256,384]{1,0:T(8,128)(2,1)S(1)}, bf16[256,384]{1,0:T(8,128)(2,1)S(1)}, u32[]{:S(2)}, u32[]{:S(2)}) collective-permute-start(bf16[256,384]{1,0:T(8,128)(2,1)S(1)} %get-tuple-element.98), channel_id=1, source_target_pairs={{0,1},{1,0},{2,3},{3,2},{4,5},{5,4},{6,7},{7,6},{8,9},{9,8},{10,11... | collective-permute-start | bytes 589832 | tf_op jit(solution)/shard_map/ppermute | solution.py:32
  28.8 15.1 %collective-permute-start.10 = (bf16[256,384]{1,0:T(8,128)(2,1)S(1)}, bf16[256,384]{1,0:T(8,128)(2,1)S(1)}, u32[]{:S(2)}, u32[]{:S(2)}) collective-permute-start(bf16[256,384]{1,0:T(8,128)(2,1)S(1)} %get-tuple-element.52), channel_id=1, source_target_pairs={{0,3},{1,2},{2,1},{3,0},{4,7},{5,6},{6,5},{7,4},{8,11},{9,10},{10,... | collective-permute-start | bytes 589832 | tf_op jit(solution)/shard_map/ppermute | solution.py:32
  33.8 10.2 %collective-permute-start.9 = (bf16[256,384]{1,0:T(8,128)(2,1)S(1)}, bf16[256,384]{1,0:T(8,128)(2,1)S(1)}, u32[]{:S(2)}, u32[]{:S(2)}) collective-permute-start(bf16[256,384]{1,0:T(8,128)(2,1)S(1)} %get-tuple-element.51), channel_id=1, source_target_pairs={{0,2},{1,3},{2,0},{3,1},{4,6},{5,7},{6,4},{7,5},{8,10},{9,11},{10,... | collective-permute-start | bytes 589832 | tf_op jit(solution)/shard_map/ppermute | solution.py:32
  44.9 11.2 %collective-permute-start.11 = (bf16[512,384]{1,0:T(8,128)(2,1)S(1)}, bf16[512,384]{1,0:T(8,128)(2,1)S(1)}, u32[]{:S(2)}, u32[]{:S(2)}) collective-permute-start(bf16[512,384]{1,0:T(8,128)(2,1)S(1)} %get-tuple-element.53), channel_id=1, source_target_pairs={{0,4},{4,8},{8,12},{1,5},{5,9},{9,13},{2,6},{6,10},{10,14},{3,7},{... | collective-permute-start | bytes 1179656 | tf_op jit(solution)/shard_map/ppermute | solution.py:22
  48.4 11.8 %collective-permute-start.12 = (bf16[512,384]{1,0:T(8,128)(2,1)S(1)}, bf16[512,384]{1,0:T(8,128)(2,1)S(1)}, u32[]{:S(2)}, u32[]{:S(2)}) collective-permute-start(bf16[512,384]{1,0:T(8,128)(2,1)S(1)} %get-tuple-element.55), channel_id=1, source_target_pairs={{4,0},{8,4},{12,8},{5,1},{9,5},{13,9},{6,2},{10,6},{14,10},{7,3},{... | collective-permute-start | bytes 1179656 | tf_op jit(solution)/shard_map/ppermute | solution.py:22
  52.1 1.4 %collective-permute-start.15 = (bf16[144,384]{1,0:T(8,128)(2,1)S(1)}, bf16[144,384]{1,0:T(8,128)(2,1)S(1)}, u32[]{:S(2)}, u32[]{:S(2)}) collective-permute-start(bf16[144,384]{1,0:T(8,128)(2,1)S(1)} %get-tuple-element.67), channel_id=1, source_target_pairs={{0,1},{1,0},{2,3},{3,2},{4,5},{5,4},{6,7},{7,6},{8,9},{9,8},{10,11... | collective-permute-start | bytes 331784 | tf_op jit(solution)/shard_map/ppermute | solution.py:32
  52.2 1.5 %collective-permute-start.16 = (bf16[144,384]{1,0:T(8,128)(2,1)S(1)}, bf16[144,384]{1,0:T(8,128)(2,1)S(1)}, u32[]{:S(2)}, u32[]{:S(2)}) collective-permute-start(bf16[144,384]{1,0:T(8,128)(2,1)S(1)} %get-tuple-element.68), channel_id=1, source_target_pairs={{0,1},{1,0},{2,3},{3,2},{4,5},{5,4},{6,7},{7,6},{8,9},{9,8},{10,11... | collective-permute-start | bytes 331784 | tf_op jit(solution)/shard_map/ppermute | solution.py:32
  52.7 1.3 %collective-permute-start.17 = (bf16[144,384]{1,0:T(8,128)(2,1)S(1)}, bf16[144,384]{1,0:T(8,128)(2,1)S(1)}, u32[]{:S(2)}, u32[]{:S(2)}) collective-permute-start(bf16[144,384]{1,0:T(8,128)(2,1)S(1)} %get-tuple-element.69), channel_id=1, source_target_pairs={{0,1},{1,0},{2,3},{3,2},{4,5},{5,4},{6,7},{7,6},{8,9},{9,8},{10,11... | collective-permute-start | bytes 331784 | tf_op jit(solution)/shard_map/ppermute | solution.py:32
  53.5 1.3 %collective-permute-start.18 = (bf16[144,384]{1,0:T(8,128)(2,1)S(1)}, bf16[144,384]{1,0:T(8,128)(2,1)S(1)}, u32[]{:S(2)}, u32[]{:S(2)}) collective-permute-start(bf16[144,384]{1,0:T(8,128)(2,1)S(1)} %get-tuple-element.70), channel_id=1, source_target_pairs={{0,1},{1,0},{2,3},{3,2},{4,5},{5,4},{6,7},{7,6},{8,9},{9,8},{10,11... | collective-permute-start | bytes 331784 | tf_op jit(solution)/shard_map/ppermute | solution.py:32
  60.2 7.0 %collective-permute-start.19 = (bf16[288,384]{1,0:T(8,128)(2,1)S(1)}, bf16[288,384]{1,0:T(8,128)(2,1)S(1)}, u32[]{:S(2)}, u32[]{:S(2)}) collective-permute-start(bf16[288,384]{1,0:T(8,128)(2,1)S(1)} %get-tuple-element.72), channel_id=1, source_target_pairs={{0,4},{4,0},{8,12},{12,8},{1,5},{5,1},{9,13},{13,9},{2,6},{6,2},{1... | collective-permute-start | bytes 663560 | tf_op jit(solution)/shard_map/ppermute | solution.py:32
  66.7 1.5 %collective-permute-start.13 = (bf16[288,384]{1,0:T(8,128)(2,1)S(1)}, bf16[288,384]{1,0:T(8,128)(2,1)S(1)}, u32[]{:S(2)}, u32[]{:S(2)}) collective-permute-start(bf16[288,384]{1,0:T(8,128)(2,1)S(1)} %get-tuple-element.63), channel_id=1, source_target_pairs={{0,1},{1,0},{2,3},{3,2},{4,5},{5,4},{6,7},{7,6},{8,9},{9,8},{10,11... | collective-permute-start | bytes 663560 | tf_op jit(solution)/shard_map/ppermute | solution.py:32
  66.8 1.8 %collective-permute-start.14 = (bf16[288,384]{1,0:T(8,128)(2,1)S(1)}, bf16[288,384]{1,0:T(8,128)(2,1)S(1)}, u32[]{:S(2)}, u32[]{:S(2)}) collective-permute-start(bf16[288,384]{1,0:T(8,128)(2,1)S(1)} %get-tuple-element.64), channel_id=1, source_target_pairs={{0,1},{1,0},{2,3},{3,2},{4,5},{5,4},{6,7},{7,6},{8,9},{9,8},{10,11... | collective-permute-start | bytes 663560 | tf_op jit(solution)/shard_map/ppermute | solution.py:32
  69.3 10.6 %collective-permute-start.26 = (bf16[288,384]{1,0:T(8,128)(2,1)S(1)}, bf16[288,384]{1,0:T(8,128)(2,1)S(1)}, u32[]{:S(2)}, u32[]{:S(2)}) collective-permute-start(bf16[288,384]{1,0:T(8,128)(2,1)S(1)} %get-tuple-element.73), channel_id=1, source_target_pairs={{0,4},{4,0},{8,12},{12,8},{1,5},{5,1},{9,13},{13,9},{2,6},{6,2},{1... | collective-permute-start | bytes 663560 | tf_op jit(solution)/shard_map/ppermute | solution.py:32
  70.4 7.5 %collective-permute-start.25 = (bf16[144,384]{1,0:T(8,128)(2,1)S(1)}, bf16[144,384]{1,0:T(8,128)(2,1)S(1)}, u32[]{:S(2)}, u32[]{:S(2)}) collective-permute-start(bf16[144,384]{1,0:T(8,128)(2,1)S(1)} %get-tuple-element.80), channel_id=1, source_target_pairs={{0,8},{4,12},{8,0},{12,4},{1,9},{5,13},{9,1},{13,5},{2,10},{6,14},... | collective-permute-start | bytes 331784 | tf_op jit(solution)/shard_map/ppermute | solution.py:32
  71.8 10.8 %collective-permute-start.20 = (bf16[256,384]{1,0:T(8,128)(2,1)}, bf16[256,384]{1,0:T(8,128)(2,1)S(1)}, u32[]{:S(2)}, u32[]{:S(2)}) collective-permute-start(bf16[256,384]{1,0:T(8,128)(2,1)} %get-tuple-element.74), channel_id=1, source_target_pairs={{0,4},{4,8},{8,12},{1,5},{5,9},{9,13},{2,6},{6,10},{10,14},{3,7},{... | collective-permute-start | bytes 589832 | tf_op jit(solution)/shard_map/ppermute | solution.py:22
  74.2 9.3 %collective-permute-start.21 = (bf16[256,384]{1,0:T(8,128)(2,1)}, bf16[256,384]{1,0:T(8,128)(2,1)S(1)}, u32[]{:S(2)}, u32[]{:S(2)}) collective-permute-start(bf16[256,384]{1,0:T(8,128)(2,1)} %get-tuple-element.75), channel_id=1, source_target_pairs={{4,0},{8,4},{12,8},{5,1},{9,5},{13,9},{6,2},{10,6},{14,10},{7,3},{... | collective-permute-start | bytes 589832 | tf_op jit(solution)/shard_map/ppermute | solution.py:22
  81.2 7.5 %collective-permute-start.27 = (bf16[144,384]{1,0:T(8,128)(2,1)}, bf16[144,384]{1,0:T(8,128)(2,1)}, u32[]{:S(2)}, u32[]{:S(2)}) collective-permute-start(bf16[144,384]{1,0:T(8,128)(2,1)} %get-tuple-element.83), channel_id=1, source_target_pairs={{0,8},{4,12},{8,0},{12,4},{1,9},{5,13},{9,1},{13,5},{2,10},{6,14},... | collective-permute-start | bytes 331784 | tf_op jit(solution)/shard_map/ppermute | solution.py:32
  89.6 5.8 %collective-permute-start.28 = (bf16[1,144,384]{2,1,0:T(8,128)(2,1)S(1)}, bf16[1,144,384]{2,1,0:T(8,128)(2,1)S(1)}, u32[]{:S(2)}, u32[]{:S(2)}) collective-permute-start(bf16[1,144,384]{2,1,0:T(8,128)(2,1)S(1)} %fusion), channel_id=1, source_target_pairs={{0,2},{1,3},{2,0},{3,1},{4,6},{5,7},{6,4},{7,5},{8,10},{9,11},{10,... | collective-permute-start | bytes 331784 | tf_op jit(solution)/shard_map/ppermute | solution.py:32
  90.3 8.1 %collective-permute-start.22 = (bf16[256,384]{1,0:T(8,128)(2,1)S(1)}, bf16[256,384]{1,0:T(8,128)(2,1)S(1)}, u32[]{:S(2)}, u32[]{:S(2)}) collective-permute-start(bf16[256,384]{1,0:T(8,128)(2,1)S(1)} %get-tuple-element.94), channel_id=1, source_target_pairs={{0,1},{1,0},{2,3},{3,2},{4,5},{5,4},{6,7},{7,6},{8,9},{9,8},{10,11... | collective-permute-start | bytes 589832 | tf_op jit(solution)/shard_map/ppermute | solution.py:32
  90.3 10.6 %collective-permute-start.23 = (bf16[256,384]{1,0:T(8,128)(2,1)S(1)}, bf16[256,384]{1,0:T(8,128)(2,1)S(1)}, u32[]{:S(2)}, u32[]{:S(2)}) collective-permute-start(bf16[256,384]{1,0:T(8,128)(2,1)S(1)} %get-tuple-element.93), channel_id=1, source_target_pairs={{0,2},{1,3},{2,0},{3,1},{4,6},{5,7},{6,4},{7,5},{8,10},{9,11},{10,... | collective-permute-start | bytes 589832 | tf_op jit(solution)/shard_map/ppermute | solution.py:32
  91.9 10.0 %collective-permute-start.24 = (bf16[256,384]{1,0:T(8,128)(2,1)S(1)}, bf16[256,384]{1,0:T(8,128)(2,1)S(1)}, u32[]{:S(2)}, u32[]{:S(2)}) collective-permute-start(bf16[256,384]{1,0:T(8,128)(2,1)S(1)} %get-tuple-element.92), channel_id=1, source_target_pairs={{0,3},{1,2},{2,1},{3,0},{4,7},{5,6},{6,5},{7,4},{8,11},{9,10},{10,... | collective-permute-start | bytes 589832 | tf_op jit(solution)/shard_map/ppermute | solution.py:32
  96.4 6.8 %collective-permute-start.29 = (bf16[144,384]{1,0:T(8,128)(2,1)S(1)}, bf16[144,384]{1,0:T(8,128)(2,1)S(1)}, u32[]{:S(2)}, u32[]{:S(2)}) collective-permute-start(bf16[144,384]{1,0:T(8,128)(2,1)S(1)} %bitcast.11), channel_id=1, source_target_pairs={{0,4},{4,8},{8,12},{12,0},{1,5},{5,9},{9,13},{13,1},{2,6},{6,10},{... | collective-permute-start | bytes 331784 | tf_op jit(solution)/shard_map/ppermute | solution.py:27
  96.8 8.7 %collective-permute-start.30 = (bf16[144,384]{1,0:T(8,128)(2,1)S(1)}, bf16[144,384]{1,0:T(8,128)(2,1)S(1)}, u32[]{:S(2)}, u32[]{:S(2)}) collective-permute-start(bf16[144,384]{1,0:T(8,128)(2,1)S(1)} %bitcast.12), channel_id=1, source_target_pairs={{0,8},{4,12},{8,0},{12,4},{1,9},{5,13},{9,1},{13,5},{2,10},{6,14},... | collective-permute-start | bytes 331784 | tf_op jit(solution)/shard_map/ppermute | solution.py:27
  98.3 7.2 %collective-permute-start.31 = (bf16[144,384]{1,0:T(8,128)(2,1)S(1)}, bf16[144,384]{1,0:T(8,128)(2,1)S(1)}, u32[]{:S(2)}, u32[]{:S(2)}) collective-permute-start(bf16[144,384]{1,0:T(8,128)(2,1)S(1)} %bitcast.13), channel_id=1, source_target_pairs={{0,12},{4,0},{8,4},{12,8},{1,13},{5,1},{9,5},{13,9},{2,14},{6,2},{... | collective-permute-start | bytes 331784 | tf_op jit(solution)/shard_map/ppermute | solution.py:27
  (7 other events, 68.6 us)
